TPU v7x, 32 devices: a whole 2x2x4 slice. The times are simulated.
32 devices in a mesh: dp: 8 (over y, x, core), tensor: 4 (over z).
Axes of the slice: x: 2, y: 2, z: 4, core: 2. Of those that a mesh axis runs over, the one named last changes fastest.
Arguments:
- hidden_in: bfloat16 [16384, 1024], P(('dp', 'tensor')), may hold values from -6 to 6
- cotangent: bfloat16 [16384, 1024], P(('dp', 'tensor')), may hold values from -6 to 6
- segments: int32 [16384], P('dp'), may hold values from 0 to 63, as said below
- attn_weight: float32 [4, 1024, 1024], P(None, 'dp', 'tensor'), may hold values from -0.1875 to 0.1875
- mlp_weight: float32 [3, 1024, 4096], P(None, 'dp', 'tensor'), may hold values from -0.1875 to 0.1875
- rates: float32 [2, 1024], replicated, may hold values from 0.2 to 0.6
- qk_scale: float32 [1024], P('tensor'), may hold values from 0.9 to 1.5
- mlp_scales: float32 [2, 4096], P(None, 'tensor'), may hold values from 0.5 to 1.5
- attn_moment_one: float32 [4, 1024, 1024], P(None, 'dp', 'tensor'), may hold values from -112 to 112
- attn_moment_two: float32 [4, 1024, 1024], P(None, 'dp', 'tensor'), may hold values from 163 to 1638
- mlp_moment_one: float32 [3, 1024, 4096], P(None, 'dp', 'tensor'), may hold values from -48 to 48
- mlp_moment_two: float32 [3, 1024, 4096], P(None, 'dp', 'tensor'), may hold values from 25 to 256
Outputs:
- hidden_out: bfloat16 [16384, 1024], P(('dp', 'tensor'))
- input_grad: bfloat16 [16384, 1024], P(('dp', 'tensor'))
- attn_weight_grad: float32 [4, 1024, 1024], P(None, 'dp', 'tensor')
- mlp_weight_grad: float32 [3, 1024, 4096], P(None, 'dp', 'tensor')
- rates_grad: float32 [2, 1024], replicated
- qk_scale_grad: float32 [1024], replicated
- mlp_scales_grad: float32 [2, 4096], replicated
- attn_moment_one_new: float32 [4, 1024, 1024], P(None, 'dp', 'tensor')
- attn_moment_two_new: float32 [4, 1024, 1024], P(None, 'dp', 'tensor')
- mlp_moment_one_new: float32 [3, 1024, 4096], P(None, 'dp', 'tensor')
- mlp_moment_two_new: float32 [3, 1024, 4096], P(None, 'dp', 'tensor')
- attn_weight_new: float32 [4, 1024, 1024], P(None, 'dp', 'tensor')
- mlp_weight_new: float32 [3, 1024, 4096], P(None, 'dp', 'tensor')
Inputs may be any that keep to these rules, and one draw needn't show every extreme that they name: `segments`: each index of dp holds one packed row of 2048 tokens: whole documents in order, numbered 0, 1, 2, ... from the row's start, each 2048 // 32 times a power of two tokens long (short ones far more common), then padding with id 63 where the row is not full. The first row is a single document of 2048 tokens; the last row ends with padding.
All inputs are finite; a program needn't handle non-finite values.
Results may differ from a plain program's by a relative error of at most 0.018.
Values may be sent and summed in bfloat16 or wider, within the bound.
No kernel may reach another device: no remote copies, remote signals or barrier semaphores. Data moves between devices by JAX's collectives and lax.ppermute only.
A program may use at most 192 MiB of HBM per device.

v0:
```python
import math

import jax
import jax.numpy as jnp
from jax import lax
from jax.sharding import PartitionSpec as P

HEADS = 16
HEAD_DIM = 64
FF = 4096
QBLOCK = 512


norm_eps = 1e-06
pad_segment = 63
masked_score = -1e30
beta_one = 0.9
beta_two = 0.95
learning_rate = 0.01
adam_eps = 1e-08
bias_one = 1.0 - 0.9**10
bias_two = 1.0 - 0.95**10


def rms_norm(vector):
    return vector * lax.rsqrt(jnp.mean(vector * vector, axis=-1, keepdims=True) + norm_eps)


def unit_norm(vector):
    return vector * lax.rsqrt(jnp.sum(vector * vector, axis=-1, keepdims=True) + norm_eps)


def sphere_mix(base, branch, rate):
    return rms_norm(base + rate * (rms_norm(branch) - base))


def gated_unit(up_part, gate_part, up_gain, gate_gain):
    scaled = gate_part * gate_gain
    return up_part * up_gain * (scaled * jax.nn.sigmoid(scaled))


def positions_of(segment_row):
    length = segment_row.shape[0]
    indices = jnp.arange(length, dtype=jnp.int32)
    changed = jnp.concatenate(
        [jnp.ones((1,), dtype=jnp.bool_), segment_row[1:] != segment_row[:-1]]
    )
    starts = lax.cummax(jnp.where(changed, indices, jnp.zeros_like(indices)), axis=0)
    return indices - starts


def rotary(vector, positions):
    half_dim = vector.shape[-1] // 2
    frequency = 10000.0 ** (-jnp.arange(half_dim, dtype=jnp.float32) / half_dim)
    angles = positions.astype(jnp.float32)[:, None] * frequency[None, :]
    cosine_table = jnp.cos(angles)[:, None, :]
    sine_table = jnp.sin(angles)[:, None, :]
    first_half = vector[..., :half_dim]
    second_half = vector[..., half_dim:]
    return jnp.concatenate(
        [
            first_half * cosine_table - second_half * sine_table,
            second_half * cosine_table + first_half * sine_table,
        ],
        axis=-1,
    )


def allowed_block(segment_row, offset):
    length = segment_row.shape[0]
    query_segments = lax.dynamic_slice_in_dim(segment_row, offset, QBLOCK, 0)
    query_index = offset + jnp.arange(QBLOCK, dtype=jnp.int32)
    key_index = jnp.arange(length, dtype=jnp.int32)
    return (query_segments[:, None] == segment_row[None, :]) & (
        key_index[None, :] <= query_index[:, None]
    )


def adam_moved(weight, gradient, moment_one, moment_two):
    moment_one_new = beta_one * moment_one + (1.0 - beta_one) * gradient
    moment_two_new = beta_two * moment_two + (1.0 - beta_two) * gradient * gradient
    moved = weight - learning_rate * (moment_one_new / bias_one) / (
        jnp.sqrt(moment_two_new / bias_two) + adam_eps
    )
    return (moment_one_new, moment_two_new, moved)


def local(
    hidden_in,
    cotangent,
    segments,
    attn_weight,
    mlp_weight,
    rates,
    qk_scale,
    mlp_scales,
    attn_moment_one,
    attn_moment_two,
    mlp_moment_one,
    mlp_moment_two,
):
    row_count = hidden_in.shape[0]
    length = segments.shape[0]
    heads_width = attn_weight.shape[2]
    hidden_width = mlp_weight.shape[2]
    local_heads = heads_width // HEAD_DIM
    block_count = length // QBLOCK
    scale_factor = math.sqrt(HEAD_DIM)
    attn_full, mlp_full = (
        lax.all_gather(attn_weight.astype(jnp.bfloat16), "dp", axis=1, tiled=True),
        lax.all_gather(mlp_weight.astype(jnp.bfloat16), "dp", axis=1, tiled=True),
    )
    qkv_matrix = jnp.concatenate([attn_full[0], attn_full[1], attn_full[2]], axis=1)
    out_matrix = attn_full[3]
    in_matrix = jnp.concatenate([mlp_full[0], mlp_full[1]], axis=1)
    down_matrix = mlp_full[2]
    projected = jnp.dot(
        lax.all_gather(hidden_in, "tensor", axis=0, tiled=True),
        qkv_matrix,
        preferred_element_type=jnp.float32,
    )
    qkv_values = projected
    positions = positions_of(segments)

    def prepare_flat(raw, gain_flat):
        rotated = rotary(raw.reshape(length, local_heads, HEAD_DIM), positions)
        return unit_norm(rotated) * gain_flat.reshape(local_heads, HEAD_DIM)

    query_raw = qkv_values[:, :heads_width]
    key_raw = qkv_values[:, heads_width : 2 * heads_width]
    value_raw = qkv_values[:, 2 * heads_width :]
    query_hat = prepare_flat(query_raw, qk_scale).astype(jnp.bfloat16)
    key_hat = prepare_flat(key_raw, qk_scale).astype(jnp.bfloat16)
    value_hat = value_raw.reshape(length, local_heads, HEAD_DIM).astype(jnp.bfloat16)

    def attend_block(block_index):
        offset = block_index * QBLOCK
        queries = lax.dynamic_slice_in_dim(query_hat, offset, QBLOCK, 0)
        allowed = allowed_block(segments, offset)
        scores = (
            jnp.einsum("qhd,khd->hqk", queries, key_hat, preferred_element_type=jnp.float32)
            * scale_factor
        )
        scores = jnp.where(allowed[None], scores, masked_score)
        row_peak = jnp.max(scores, axis=-1, keepdims=True)
        weights = jnp.exp(scores - row_peak)
        summed = jnp.sum(weights, axis=-1, keepdims=True)
        attention_probs = weights / summed
        block_out = jnp.einsum(
            "hqk,khd->qhd",
            attention_probs.astype(jnp.bfloat16),
            value_hat,
            preferred_element_type=jnp.float32,
        )
        return (block_out, (row_peak + jnp.log(summed))[..., 0])

    block_outs, log_sums = lax.map(attend_block, jnp.arange(block_count, dtype=jnp.int32))
    attended = block_outs.reshape(length, heads_width).astype(jnp.bfloat16)
    fragment = attended
    branch = lax.psum_scatter(
        jnp.einsum("th,dh->td", fragment, out_matrix, preferred_element_type=jnp.float32),
        "tensor",
        scatter_dimension=0,
        tiled=True,
    )
    tokens = hidden_in.astype(jnp.float32)
    middle = sphere_mix(tokens, branch, rates[0])
    middle_low = middle.astype(jnp.bfloat16)
    projected = jnp.dot(
        lax.all_gather(middle_low, "tensor", axis=0, tiled=True),
        in_matrix,
        preferred_element_type=jnp.float32,
    )
    mlp_parts = (projected,)
    up_part = mlp_parts[0][:, :hidden_width]
    gate_part = mlp_parts[0][:, hidden_width:]
    hidden_units = gated_unit(up_part, gate_part, mlp_scales[0], mlp_scales[1]).astype(jnp.bfloat16)
    fragment = hidden_units
    mlp_out = lax.psum_scatter(
        jnp.einsum("tf,df->td", fragment, down_matrix, preferred_element_type=jnp.float32),
        "tensor",
        scatter_dimension=0,
        tiled=True,
    )
    result = sphere_mix(middle, mlp_out, rates[1])
    tensor_index = lax.axis_index("tensor")
    row_segments = lax.dynamic_slice_in_dim(segments, tensor_index * row_count, row_count, 0)
    upstream = (
        cotangent.astype(jnp.float32) * (row_segments < pad_segment).astype(jnp.float32)[:, None]
    )
    unused_mix, mlp_pull = jax.vjp(sphere_mix, middle, mlp_out, rates[1])
    middle_direct, mlp_out_grad, rate_mlp_grad = mlp_pull(upstream)
    fragment = lax.all_gather(mlp_out_grad.astype(jnp.bfloat16), "tensor", axis=0, tiled=True)
    hidden_grad = jnp.dot(fragment, down_matrix, preferred_element_type=jnp.float32)
    mlp_grad_full = fragment
    down_grad = jnp.einsum(
        "td,tf->df", mlp_grad_full, hidden_units, preferred_element_type=jnp.float32
    )
    unused_gate, gate_pull = jax.vjp(gated_unit, up_part, gate_part, mlp_scales[0], mlp_scales[1])
    up_grad, gate_grad, up_scale_grad, gate_scale_grad = gate_pull(hidden_grad)
    in_grad = jnp.concatenate([up_grad, gate_grad], axis=1).astype(jnp.bfloat16)
    grad_rows = in_grad
    in_weight_grad = jnp.einsum(
        "td,tk->dk",
        lax.all_gather(middle_low, "tensor", axis=0, tiled=True),
        grad_rows,
        preferred_element_type=jnp.float32,
    )
    fragment = in_grad
    middle_grad = middle_direct + lax.psum_scatter(
        jnp.einsum("tk,dk->td", fragment, in_matrix, preferred_element_type=jnp.float32),
        "tensor",
        scatter_dimension=0,
        tiled=True,
    )
    unused_attn, attn_pull = jax.vjp(sphere_mix, tokens, branch, rates[0])
    token_direct, branch_grad, rate_attn_grad = attn_pull(middle_grad)
    fragment = lax.all_gather(branch_grad.astype(jnp.bfloat16), "tensor", axis=0, tiled=True)
    attended_grad = jnp.einsum(
        "td,dh->th", fragment, out_matrix, preferred_element_type=jnp.float32
    )
    branch_grad_full = fragment
    out_grad = jnp.einsum(
        "td,th->dh", branch_grad_full, attended, preferred_element_type=jnp.float32
    )
    attended_low = attended_grad.astype(jnp.bfloat16).reshape(length, local_heads, HEAD_DIM)

    def back_block(running, block_index):
        key_acc, value_acc = running
        offset = block_index * QBLOCK
        queries = lax.dynamic_slice_in_dim(query_hat, offset, QBLOCK, 0)
        allowed = allowed_block(segments, offset)
        scores = (
            jnp.einsum("qhd,khd->hqk", queries, key_hat, preferred_element_type=jnp.float32)
            * scale_factor
        )
        scores = jnp.where(allowed[None], scores, masked_score)
        attention_probs = jnp.exp(scores - log_sums[block_index][..., None])
        grad_block = lax.dynamic_slice_in_dim(attended_low, offset, QBLOCK, 0)
        prob_grad = jnp.einsum(
            "qhd,khd->hqk", grad_block, value_hat, preferred_element_type=jnp.float32
        )
        row_delta = jnp.sum(attention_probs * prob_grad, axis=-1, keepdims=True)
        score_grad = (attention_probs * (prob_grad - row_delta)).astype(jnp.bfloat16)
        query_grad = (
            jnp.einsum("hqk,khd->qhd", score_grad, key_hat, preferred_element_type=jnp.float32)
            * scale_factor
        )
        key_acc = (
            key_acc
            + jnp.einsum("hqk,qhd->khd", score_grad, queries, preferred_element_type=jnp.float32)
            * scale_factor
        )
        value_acc = value_acc + jnp.einsum(
            "hqk,qhd->khd",
            attention_probs.astype(jnp.bfloat16),
            grad_block,
            preferred_element_type=jnp.float32,
        )
        return ((key_acc, value_acc), query_grad)

    zero_heads = jnp.zeros((length, local_heads, HEAD_DIM), jnp.float32)
    (key_hat_grad, value_grad), query_blocks = lax.scan(
        back_block, (zero_heads, zero_heads), jnp.arange(block_count, dtype=jnp.int32)
    )
    query_hat_grad = query_blocks.reshape(length, local_heads, HEAD_DIM)
    unused_query, query_pull = jax.vjp(prepare_flat, query_raw, qk_scale)
    query_raw_grad, gain_query = query_pull(query_hat_grad)
    unused_key, key_pull = jax.vjp(prepare_flat, key_raw, qk_scale)
    key_raw_grad, gain_key = key_pull(key_hat_grad)
    qkv_grad = jnp.concatenate(
        [query_raw_grad, key_raw_grad, value_grad.reshape(length, heads_width)], axis=1
    ).astype(jnp.bfloat16)
    grad_rows = qkv_grad
    qkv_weight_grad = jnp.einsum(
        "td,tk->dk",
        lax.all_gather(hidden_in, "tensor", axis=0, tiled=True),
        grad_rows,
        preferred_element_type=jnp.float32,
    )
    fragment = qkv_grad
    input_grad = (
        token_direct
        + lax.psum_scatter(
            jnp.einsum(
                "tk,dk->td", fragment, qkv_matrix, preferred_element_type=jnp.float32
            ).astype(jnp.bfloat16),
            "tensor",
            scatter_dimension=0,
            tiled=True,
        ).astype(jnp.float32)
    ).astype(jnp.bfloat16)
    attn_local = jnp.stack(
        [
            qkv_weight_grad[:, :heads_width],
            qkv_weight_grad[:, heads_width : 2 * heads_width],
            qkv_weight_grad[:, 2 * heads_width :],
            out_grad,
        ]
    )
    mlp_local = jnp.stack(
        [in_weight_grad[:, :hidden_width], in_weight_grad[:, hidden_width:], down_grad]
    )
    attn_weight_grad, mlp_weight_grad = (
        lax.psum_scatter(
            attn_local.astype(jnp.bfloat16), "dp", scatter_dimension=1, tiled=True
        ).astype(jnp.float32),
        lax.psum_scatter(
            mlp_local.astype(jnp.bfloat16), "dp", scatter_dimension=1, tiled=True
        ).astype(jnp.float32),
    )
    rate_part = jnp.stack([rate_attn_grad, rate_mlp_grad])
    gain_part = lax.dynamic_update_slice(
        jnp.zeros((HEADS * HEAD_DIM,), jnp.float32),
        gain_query + gain_key,
        (tensor_index * heads_width,),
    )
    scale_part = lax.dynamic_update_slice(
        jnp.zeros((2, FF), jnp.float32),
        jnp.stack([up_scale_grad, gate_scale_grad]),
        (jnp.zeros((), jnp.int32), tensor_index * hidden_width),
    )
    rates_grad, qk_scale_grad, mlp_scales_grad = lax.psum(
        (rate_part, gain_part, scale_part), ("dp", "tensor")
    )
    attn_one, attn_two, attn_moved = adam_moved(
        attn_weight, attn_weight_grad, attn_moment_one, attn_moment_two
    )
    mlp_one, mlp_two, mlp_moved = adam_moved(
        mlp_weight, mlp_weight_grad, mlp_moment_one, mlp_moment_two
    )
    attn_square = jnp.sum(attn_moved * attn_moved, axis=1, keepdims=True)
    mlp_square = jnp.sum(mlp_moved * mlp_moved, axis=1, keepdims=True)
    attn_square, mlp_square = lax.psum((attn_square, mlp_square), "dp")
    attn_new = attn_moved * lax.rsqrt(attn_square + norm_eps)
    mlp_new = mlp_moved * lax.rsqrt(mlp_square + norm_eps)
    return (
        result.astype(jnp.bfloat16),
        input_grad,
        attn_weight_grad,
        mlp_weight_grad,
        rates_grad,
        qk_scale_grad,
        mlp_scales_grad,
        attn_one,
        attn_two,
        mlp_one,
        mlp_two,
        attn_new,
        mlp_new,
    )


def solution(mesh):
    return jax.shard_map(
        local,
        mesh=mesh,
        in_specs=(
            P(("dp", "tensor"), None),
            P(("dp", "tensor"), None),
            P("dp"),
            P(None, "dp", "tensor"),
            P(None, "dp", "tensor"),
            P(),
            P("tensor"),
            P(None, "tensor"),
            P(None, "dp", "tensor"),
            P(None, "dp", "tensor"),
            P(None, "dp", "tensor"),
            P(None, "dp", "tensor"),
        ),
        out_specs=(
            P(("dp", "tensor"), None),
            P(("dp", "tensor"), None),
            P(None, "dp", "tensor"),
            P(None, "dp", "tensor"),
            P(),
            P(),
            P(),
            P(None, "dp", "tensor"),
            P(None, "dp", "tensor"),
            P(None, "dp", "tensor"),
            P(None, "dp", "tensor"),
            P(None, "dp", "tensor"),
            P(None, "dp", "tensor"),
        ),
        check_vma=False,
    )
```

profile of v0, /device:TPU:0, one launch (start us, length us, event | category | flops | bytes accessed | tf_op | source)
XLA Modules:
  0.0 1517.3 jit_solution(7430998798819704375)
XLA Ops:
  12.5 28.5 %all-gather.7.cloned.1.call-done = bf16[4,1024,256]{2,1,0:T(8,128)(2,1)} async-done(((bf16[4,128,256]{2,1,0:T(8,128)(2,1)}), bf16[4,1024,256]{2,1,0:T(8,128)(2,1)}) %all-gather.7.cloned.1.call-update) | async-done | bytes 2097168 | tf_op jit(solution)/shard_map/all_gather | solution.py:110
  42.5 80.8 %all-gather.9.cloned.1.call-done = bf16[2048,1024]{1,0:T(8,128)(2,1)} async-done(((bf16[512,1024]{1,0:T(8,128)(2,1)}), bf16[2048,1024]{1,0:T(8,128)(2,1)}) %all-gather.9.cloned.1.call-update) | async-done | bytes 4194320 | tf_op jit(solution)/shard_map/all_gather | solution.py:118
  133.9 72.5 %while.27 = (s32[]{:T(128)}, bf16[4,512,4,64]{1,3,2,0:T(8,128)(2,1)S(1)}, f32[4,4,512]{2,1,0:T(4,128)}, s32[4]{0:T(128)S(1)}, s32[2048]{0:T(1024)}, /*index=5*/b...) while((s32[]{:T(128)}, ...), condition=%wide.region_7.8_spmd, body=%wide.region_4.7_spmd.sunk | while | flops 1127217664 | bytes 57494204 | solution.py:157
  216.9 140.8 %reduce-scatter.9.cloned.1.call-done = f32[512,1024]{1,0:T(8,128)} async-done(((f32[2048,1024]{1,0:T(8,128)}), f32[512,1024]{1,0:T(8,128)}) %reduce-scatter.9.cloned.1.call-update) | async-done | bytes 2097168 | tf_op jit(solution)/shard_map/reduce_scatter | solution.py:160
  362.0 44.1 %all-gather.13.cloned.1.call-done = bf16[3,1024,1024]{2,1,0:T(8,128)(2,1)} async-done(((bf16[3,128,1024]{2,1,0:T(8,128)(2,1)}), bf16[3,1024,1024]{2,1,0:T(8,128)(2,1)}) %all-gather.13.cloned.1.call-update) | async-done | bytes 6291472 | tf_op jit(solution)/shard_map/all_gather | solution.py:111
  410.8 78.0 %all-gather.11.cloned.1.call-done = bf16[2048,1024]{1,0:T(8,128)(2,1)} async-done(((bf16[512,1024]{1,0:T(8,128)(2,1)}), bf16[2048,1024]{1,0:T(8,128)(2,1)}) %all-gather.11.cloned.1.call-update) | async-done | bytes 4194320 | tf_op jit(solution)/shard_map/all_gather | solution.py:170
  527.4 133.0 %reduce-scatter.11.cloned.1.call-done = f32[512,1024]{1,0:T(8,128)} async-done(((f32[2048,1024]{1,0:T(8,128)}), f32[512,1024]{1,0:T(8,128)}) %reduce-scatter.11.cloned.1.call-update) | async-done | bytes 2097168 | tf_op jit(solution)/shard_map/reduce_scatter | solution.py:179
  667.4 81.5 %all-gather.15.cloned.1.call-done = bf16[2048,1024]{1,0:T(8,128)(2,1)} async-done(((bf16[512,1024]{1,0:T(8,128)(2,1)}), bf16[2048,1024]{1,0:T(8,128)(2,1)}) %all-gather.15.cloned.1.call-update) | async-done | bytes 4194320 | tf_op jit(solution)/shard_map/all_gather | solution.py:193
  748.9 21.6 %multiply_reduce_fusion.2 = (f32[1024]{0:T(1024)}, f32[1024]{0:T(1024)}, f32[2048,1024]{1,0:T(8,128)S(1)}, bf16[2048,1024]{1,0:T(8,128)(2,1)}) fusion(f32[2048,2048]{1,0:T(8,128)} %copy-done.24, f32[1024]{0:T(1024)S(1)} %bitcast.193, f32[1024]{0:T(1024)S(1)} %bitcast.199, bf16[2048,1024]{1,0:T(8,128)(2,1)} %all-gather.15.cloned.1.call-done, ...), kind=kOutput, calls=%fused_computation.51 | convolution fusion | flops 4336908288 | bytes 35667968 | tf_op jit(solution)/shard_map/dot_general | solution.py:194
  773.9 13.3 fusion.41
  787.7 142.8 %reduce-scatter.13.cloned.1.call-done = f32[512,1024]{1,0:T(8,128)} async-done(((f32[2048,1024]{1,0:T(8,128)}), f32[512,1024]{1,0:T(8,128)}) %reduce-scatter.13.cloned.1.call-update) | async-done | bytes 2097168 | tf_op jit(solution)/shard_map/reduce_scatter | solution.py:210
  946.2 13.6 fusion.42
  971.4 51.9 %all-gather.17.cloned.1.call-done = bf16[2048,1024]{1,0:T(8,128)(2,1)} async-done(((bf16[512,1024]{1,0:T(8,128)(2,1)}), bf16[2048,1024]{1,0:T(8,128)(2,1)}) %all-gather.17.cloned.1.call-update) | async-done | bytes 4194320 | tf_op jit(solution)/shard_map/all_gather | solution.py:218
  1027.8 329.2 %while.28 = (s32[]{:T(128)}, f32[2048,4,64]{0,2,1:T(8,128)}, f32[2048,4,64]{0,2,1:T(8,128)}, f32[4,512,4,64]{1,0,3,2:T(4,128)}, s32[4]{0:T(128)S(1)}, /*index=5*...) while((s32[]{:T(128)}, f32[2048,4,64]{0,2,1:T(8,128)}, ...), condition=%wide.region_21.22_spmd.clone, body=%wide.region_19.21_spmd.clone.sunk | while | flops 2753165824 | bytes 216607184 | solution.py:263
  1045.5 16.5 %multiply_reduce_fusion.22 = (f32[4,512]{1,0:T(4,128)}, f32[4,512,2048]{2,1,0:T(8,128)}) fusion(f32[4,512,2048]{2,1,0:T(8,128)} %fusion.125, f32[4,512]{1,0:T(4,128)S(1)} %dynamic-slice_bitcast_fusion.2, pred[512,2048]{1,0:T(8,128)(4,1)} %fusion.126, bf16[2048,4,64]{0,2,1:T(8,128)(2,1)} %get-tuple-element.509, ...), kind=kOutput, calls=%fused_computation.18.clone.1 | convolution fusion | flops 557840384 | bytes 35930116 | tf_op jit(solution)/shard_map/while/body/eval_jaxpr/qhd,khd->hqk/dot_general | solution.py:240
  1127.9 15.8 %multiply_reduce_fusion.22 = (f32[4,512]{1,0:T(4,128)}, f32[4,512,2048]{2,1,0:T(8,128)}) fusion(f32[4,512,2048]{2,1,0:T(8,128)} %fusion.125, f32[4,512]{1,0:T(4,128)S(1)} %dynamic-slice_bitcast_fusion.2, pred[512,2048]{1,0:T(8,128)(4,1)} %fusion.126, bf16[2048,4,64]{0,2,1:T(8,128)(2,1)} %get-tuple-element.509, ...), kind=kOutput, calls=%fused_computation.18.clone.1 | convolution fusion | flops 557840384 | bytes 35930116 | tf_op jit(solution)/shard_map/while/body/eval_jaxpr/qhd,khd->hqk/dot_general | solution.py:240
  1180.0 13.1 fusion.128
  1209.8 15.8 %multiply_reduce_fusion.22 = (f32[4,512]{1,0:T(4,128)}, f32[4,512,2048]{2,1,0:T(8,128)}) fusion(f32[4,512,2048]{2,1,0:T(8,128)} %fusion.125, f32[4,512]{1,0:T(4,128)S(1)} %dynamic-slice_bitcast_fusion.2, pred[512,2048]{1,0:T(8,128)(4,1)} %fusion.126, bf16[2048,4,64]{0,2,1:T(8,128)(2,1)} %get-tuple-element.509, ...), kind=kOutput, calls=%fused_computation.18.clone.1 | convolution fusion | flops 557840384 | bytes 35930116 | tf_op jit(solution)/shard_map/while/body/eval_jaxpr/qhd,khd->hqk/dot_general | solution.py:240
  1261.8 13.1 fusion.128
  1291.6 15.8 %multiply_reduce_fusion.22 = (f32[4,512]{1,0:T(4,128)}, f32[4,512,2048]{2,1,0:T(8,128)}) fusion(f32[4,512,2048]{2,1,0:T(8,128)} %fusion.125, f32[4,512]{1,0:T(4,128)S(1)} %dynamic-slice_bitcast_fusion.2, pred[512,2048]{1,0:T(8,128)(4,1)} %fusion.126, bf16[2048,4,64]{0,2,1:T(8,128)(2,1)} %get-tuple-element.509, ...), kind=kOutput, calls=%fused_computation.18.clone.1 | convolution fusion | flops 557840384 | bytes 35930116 | tf_op jit(solution)/shard_map/while/body/eval_jaxpr/qhd,khd->hqk/dot_general | solution.py:240
  1343.6 13.1 fusion.128
  1403.7 41.3 %all-reduce.4 = (f32[2,1024]{1,0:T(2,128)}, f32[1024]{0:T(1024)}, f32[2,4096]{1,0:T(2,128)}) all-reduce(f32[2,1024]{1,0:T(2,128)S(1)} %pad_maximum_fusion.18, f32[1024]{0:T(1024)S(1)} %dynamic_update_slice.17, f32[2,4096]{1,0:T(2,128)S(1)} %maximum_dynamic-update-slice_fusion), channel_id=1, replica_groups=mesh['dp'=8,'tensor'=4] {'dp','tensor'}, use_global_device_ids=true, to_apply=%region_29.30 | all-reduce | flops 11264 | bytes 90112 | tf_op jit(solution)/shard_map/psum | solution.py:323
  1448.6 24.8 %all-reduce.5 = (f32[4,1,256]{2,0,1:T(4,128)S(1)}, f32[3,1,1024]{2,0,1:T(4,128)S(1)}) all-reduce(f32[4,1,256]{2,0,1:T(4,128)S(1)} %bitcast.195, f32[3,1,1024]{2,0,1:T(4,128)S(1)} %bitcast.191), channel_id=1, replica_groups=mesh['dp'=8,'tensor'=4] {'dp'}, use_global_device_ids=true, to_apply=%region_37.38 | all-reduce | flops 4096 | bytes 32768 | tf_op jit(solution)/shard_map/psum | solution.py:334
  1479.4 28.0 %reduce-scatter.15.cloned.1.call-done = bf16[512,1024]{1,0:T(8,128)(2,1)} async-done(((bf16[2048,1024]{1,0:T(8,128)(2,1)}), bf16[512,1024]{1,0:T(8,128)(2,1)}) %reduce-scatter.15.cloned.1.call-update) | async-done | bytes 1048592 | tf_op jit(solution)/shard_map/reduce_scatter | solution.py:284
  (415 shorter events, 460.5 us)
Async XLA Ops:
  7.2 33.8 %all-gather.7.cloned.1.call-start = ((), (), s32[]{:S(2)}) async-start(), calls=%async_computation.6 | async-start | bytes 2359296 | tf_op jit(solution)/shard_map/all_gather | solution.py:110
  9.0 114.3 %all-gather.9.cloned.1.call-start = ((), (), s32[]{:S(2)}) async-start(), calls=%async_computation.7 | async-start | bytes 5242880 | tf_op jit(solution)/shard_map/all_gather | solution.py:118
  9.8 347.9 %reduce-scatter.9.cloned.1.call-start = ((), (), s32[]{:S(2)}) async-start(), calls=%async_computation.8 | async-start | bytes 10485760 | tf_op jit(solution)/shard_map/reduce_scatter | solution.py:160
  11.3 120.7 %copy-start.64 = (f32[4,64]{1,0:T(4,128)}, f32[4,64]{1,0:T(4,128)S(1)}, u32[]{:S(2)}) copy-start(f32[4,64]{1,0:T(4,128)S(1)} %mul.730) | copy-start | bytes 3076
  12.5 116.8 %copy-start.37 = (f32[2048,32]{0,1:T(8,128)}, f32[2048,32]{0,1:T(8,128)S(1)}, u32[]{:S(2)}) copy-start(f32[2048,32]{0,1:T(8,128)S(1)} %get-tuple-element.293) | copy-start | bytes 786436
  12.5 116.8 %copy-start.39 = (f32[2048,32]{0,1:T(8,128)}, f32[2048,32]{0,1:T(8,128)S(1)}, u32[]{:S(2)}) copy-start(f32[2048,32]{0,1:T(8,128)S(1)} %get-tuple-element.294) | copy-start | bytes 786436
  42.5 86.2 %copy-start.54 = (bf16[1024,256]{1,0:T(8,128)(2,1)}, bf16[1024,256]{1,0:T(8,128)(2,1)S(1)}, u32[]{:S(2)}) copy-start(bf16[1024,256]{1,0:T(8,128)(2,1)S(1)} %get-tuple-element.283) | copy-start | bytes 1572868
  42.5 86.2 %copy-start.55 = (bf16[1024,256]{1,0:T(8,128)(2,1)}, bf16[1024,256]{1,0:T(8,128)(2,1)S(1)}, u32[]{:S(2)}) copy-start(bf16[1024,256]{1,0:T(8,128)(2,1)S(1)} %get-tuple-element.284) | copy-start | bytes 1572868
  42.5 86.2 %copy-start.56 = (bf16[1024,256]{1,0:T(8,128)(2,1)}, bf16[1024,256]{1,0:T(8,128)(2,1)S(1)}, u32[]{:S(2)}) copy-start(bf16[1024,256]{1,0:T(8,128)(2,1)S(1)} %get-tuple-element.285) | copy-start | bytes 1572868
  214.4 145.2 %copy-start.25 = (bf16[512,1024]{1,0:T(8,128)(2,1)S(1)}, bf16[512,1024]{1,0:T(8,128)(2,1)}, u32[]{:S(2)}) copy-start(bf16[512,1024]{1,0:T(8,128)(2,1)} %param.16) | copy-start | bytes 3145732
  214.4 191.6 %all-gather.13.cloned.1.call-start = ((), (), s32[]{:S(2)}) async-start(), calls=%async_computation.10 | async-start | bytes 7077888 | tf_op jit(solution)/shard_map/all_gather | solution.py:111
  216.8 272.0 %all-gather.11.cloned.1.call-start = ((), (), s32[]{:S(2)}) async-start(), calls=%async_computation.9 | async-start | bytes 5242880 | tf_op jit(solution)/shard_map/all_gather | solution.py:170
  216.9 722.0 %copy-start.62 = (f32[1,1024]{1,0:T(1,128)}, f32[1,1024]{1,0:T(1,128)S(1)}, u32[]{:S(2)}) copy-start(f32[1,1024]{1,0:T(1,128)S(1)} %get-tuple-element.296) | copy-start | bytes 12292
  361.9 298.5 %reduce-scatter.11.cloned.1.call-start = ((), (), s32[]{:S(2)}) async-start(), calls=%async_computation.11 | async-start | bytes 10485760 | tf_op jit(solution)/shard_map/reduce_scatter | solution.py:179
  517.1 145.2 %copy-start.11 = (bf16[512,1024]{1,0:T(8,128)(2,1)S(1)}, bf16[512,1024]{1,0:T(8,128)(2,1)}, u32[]{:S(2)}) copy-start(bf16[512,1024]{1,0:T(8,128)(2,1)} %param.17) | copy-start | bytes 3145732
  517.1 231.8 %all-gather.15.cloned.1.call-start = ((), (), s32[]{:S(2)}) async-start(), calls=%async_computation.12 | async-start | bytes 5242880 | tf_op jit(solution)/shard_map/all_gather | solution.py:193
  667.4 263.1 %reduce-scatter.13.cloned.1.call-start = ((), (), s32[]{:S(2)}) async-start(), calls=%async_computation.13 | async-start | bytes 10485760 | tf_op jit(solution)/shard_map/reduce_scatter | solution.py:210
  787.2 236.0 %all-gather.17.cloned.1.call-start = ((), (), s32[]{:S(2)}) async-start(), calls=%async_computation.14 | async-start | bytes 5242880 | tf_op jit(solution)/shard_map/all_gather | solution.py:218
  941.7 456.2 %reduce-scatter.17.cloned.1.call-start = ((), (), s32[]{:S(2)}) async-start(), calls=%async_computation.16 | async-start | bytes 7077888 | tf_op jit(solution)/shard_map/reduce_scatter | solution.py:308
  971.3 56.5 %copy-start.1 = (bf16[2048,4,64]{0,2,1:T(8,128)(2,1)S(1)}, bf16[2048,4,64]{0,2,1:T(8,128)(2,1)}, u32[]{:S(2)}) copy-start(bf16[2048,4,64]{0,2,1:T(8,128)(2,1)} %copy-done) | copy-start | bytes 3145732
  971.3 473.7 %reduce-scatter.19.cloned.1.call-start = ((), (), s32[]{:S(2)}) async-start(), calls=%async_computation.17 | async-start | bytes 2359296
  1386.7 120.7 %reduce-scatter.15.cloned.1.call-start = ((), (), s32[]{:S(2)}) async-start(), calls=%async_computation.15 | async-start | bytes 5242880 | tf_op jit(solution)/shard_map/reduce_scatter | solution.py:284
  1475.6 31.8 %copy-start.23 = (f32[512,1024]{1,0:T(8,128)S(1)}, f32[512,1024]{1,0:T(8,128)}, u32[]{:S(2)}) copy-start(f32[512,1024]{1,0:T(8,128)} %copy-done.22) | copy-start | bytes 6291460
  1475.6 31.8 %copy-start.63 = (f32[1,1024]{1,0:T(1,128)S(1)}, f32[1,1024]{1,0:T(1,128)}, u32[]{:S(2)}) copy-start(f32[1,1024]{1,0:T(1,128)} %copy-done.62) | copy-start | bytes 12292
  (89 other events, 566.6 us)
Sparse Core Ops, SparseCore 0:
  10.5 30.4 all-gather.6
  42.6 80.7 all-gather.8
  214.5 143.0 reduce-scatter.8
  360.0 45.9 all-gather.12
  408.0 80.7 all-gather.10
  517.3 143.0 reduce-scatter.10
  667.5 81.3 all-gather.14
  787.3 143.0 reduce-scatter.12
  941.9 81.3 all-gather.16
  1026.5 60.1 reduce-scatter.16
  1386.8 41.5 reduce-scatter.18
  1430.6 76.7 reduce-scatter.14
where the time goes:
time: 1530 us; the launch traced here: 1520 us
  waiting for transfers between devices  810 us (53%)
  matrix products  336 us (22%)
  other arithmetic  141 us (9%)
  local copies, waits for them, and re-layouts  124 us (8%)
  blocking collectives  66.1 us (4%)
  between operations  15.7 us (1%)
    reduce_scatter x1, waiting for transfers between devices, local(): lax.psum_scatter(jnp.einsum('tk,dk->td', fragment, in_matrix, preferred_e...  143 us
    reduce_scatter x1, waiting for transfers between devices, local(): lax.psum_scatter(jnp.einsum('th,dh->td', fragment, out_matrix, preferred_...  141 us
    reduce_scatter x1, waiting for transfers between devices, local(): lax.psum_scatter(jnp.einsum('tf,df->td', fragment, down_matrix, preferred...  133 us
    all_gather x1, waiting for transfers between devices, local(): lax.all_gather(mlp_out_grad.astype(jnp.bfloat16), 'tensor', axis=0, tiled...  81.5 us
    all_gather x1, waiting for transfers between devices, local(): lax.all_gather(hidden_in, 'tensor', axis=0, tiled=True)  80.8 us
    all_gather x1, waiting for transfers between devices, local(): lax.all_gather(middle_low, 'tensor', axis=0, tiled=True)  78 us
    dot_general x4, matrix products, back_block(): jnp.einsum('qhd,khd->hqk', grad_block, value_hat, preferred_element_type=...  63.8 us
    dot_general x4, matrix products, back_block(): jnp.einsum('hqk,qhd->khd', attention_probs.astype(jnp.bfloat16), grad_blo...  52 us
  transfers between devices with their start and end apart: 12, of which 10 were waited for; matrix products, arithmetic and copies ran while one was open for 27% of the time, Pallas kernels for 0%

commit v1 on v0

v1 whole, which is shorter than its diff:
```python
import functools
import math

import jax
import jax.numpy as jnp
from jax import lax
from jax.experimental import pallas as pl
from jax.experimental.pallas import tpu as pltpu
from jax.sharding import PartitionSpec as P

HEAD_DIM = 64
LOG2E = 1.4426950408889634

norm_eps = 1e-06
pad_segment = 63
beta_one = 0.9
beta_two = 0.95
learning_rate = 0.01
adam_eps = 1e-08
bias_one = 1.0 - 0.9**10
bias_two = 1.0 - 0.95**10
scale_factor = math.sqrt(HEAD_DIM)
f32 = jnp.float32
bf16 = jnp.bfloat16


def rms_norm(vector):
    return vector * lax.rsqrt(jnp.mean(vector * vector, axis=-1, keepdims=True) + norm_eps)


def unit_norm(vector):
    return vector * lax.rsqrt(jnp.sum(vector * vector, axis=-1, keepdims=True) + norm_eps)


def sphere_mix(base, branch, rate):
    return rms_norm(base + rate * (rms_norm(branch) - base))


def starts_of(segment_row):
    indices = jnp.arange(segment_row.shape[0], dtype=jnp.int32)
    changed = jnp.concatenate(
        [jnp.ones((1,), dtype=jnp.bool_), segment_row[1:] != segment_row[:-1]]
    )
    return lax.cummax(jnp.where(changed, indices, jnp.zeros_like(indices)), axis=0)


def rotary(vector, positions):
    half_dim = vector.shape[-1] // 2
    frequency = 10000.0 ** (-jnp.arange(half_dim, dtype=jnp.float32) / half_dim)
    angles = positions.astype(jnp.float32)[:, None] * frequency[None, :]
    cosine_table = jnp.cos(angles)[:, None, :]
    sine_table = jnp.sin(angles)[:, None, :]
    first_half = vector[..., :half_dim]
    second_half = vector[..., half_dim:]
    return jnp.concatenate(
        [
            first_half * cosine_table - second_half * sine_table,
            second_half * cosine_table + first_half * sine_table,
        ],
        axis=-1,
    )


def adam_moved(weight, gradient, moment_one, moment_two):
    moment_one_new = beta_one * moment_one + (1.0 - beta_one) * gradient
    moment_two_new = beta_two * moment_two + (1.0 - beta_two) * gradient * gradient
    moved = weight - learning_rate * (moment_one_new / bias_one) / (
        jnp.sqrt(moment_two_new / bias_two) + adam_eps
    )
    return (moment_one_new, moment_two_new, moved)


def dot_nt(a, b):
    return lax.dot_general(a, b, (((1,), (1,)), ((), ())), preferred_element_type=f32)


def dot_nn(a, b):
    return lax.dot_general(a, b, (((1,), (0,)), ((), ())), preferred_element_type=f32)


def dot_tn(a, b):
    return lax.dot_general(a, b, (((0,), (0,)), ((), ())), preferred_element_type=f32)


def head_stack(x, heads):
    lane = lax.broadcasted_iota(jnp.int32, x.shape, 1) // HEAD_DIM
    zero = jnp.zeros_like(x)
    return jnp.concatenate([jnp.where(lane == h, x, zero) for h in range(heads)], axis=0)


def head_pick(stacked, heads, rows):
    width = stacked.shape[1]
    lane = lax.broadcasted_iota(jnp.int32, (rows, width), 1) // HEAD_DIM
    picked = jnp.zeros((rows, width), f32)
    for h in range(heads):
        picked = jnp.where(lane == h, stacked[h * rows : (h + 1) * rows], picked)
    return picked


def attend_kernel(heads, bq, bk, q_ref, k_ref, v_ref, start_ref, o_ref, of_ref, l_ref, acc, lsum):
    i = pl.program_id(0)
    qs = head_stack(q_ref[...], heads)
    acc[...] = jnp.zeros_like(acc)
    lsum[...] = jnp.zeros_like(lsum)
    start = jnp.concatenate([start_ref[...]] * heads, axis=0)

    def step(j, diagonal):
        offset = pl.multiple_of(j * bk, bk)
        keys = k_ref[pl.ds(offset, bk), :]
        values = v_ref[pl.ds(offset, bk), :]
        scores = dot_nt(qs, keys)
        key_index = offset + lax.broadcasted_iota(jnp.int32, scores.shape, 1)
        allowed = key_index >= start
        if diagonal:
            row = lax.rem(lax.broadcasted_iota(jnp.int32, scores.shape, 0), bq)
            allowed = allowed & (key_index <= i * bq + row)
        weights = jnp.where(allowed, jnp.exp2(scores * (scale_factor * LOG2E)), 0.0)
        total = weights[:, :128]
        for part in range(1, bk // 128):
            total = total + weights[:, part * 128 : (part + 1) * 128]
        lsum[...] += total
        acc[...] += dot_nn(weights.astype(bf16), values)

    def body(j, carry):
        step(j, False)
        return carry

    lax.fori_loop(0, i, body, 0)
    step(i, True)
    summed = jnp.sum(lsum[...], axis=1, keepdims=True)
    out = head_pick(acc[...] * (1.0 / summed), heads, bq)
    of_ref[...] = out
    o_ref[...] = out.astype(bf16)
    l_ref[...] = jnp.log2(summed).reshape(heads, bq)


def attend(q, k, v, start, block):
    length, width = q.shape
    heads = width // HEAD_DIM
    whole = pl.BlockSpec((length, width), lambda i: (0, 0))
    rows = pl.BlockSpec((block, width), lambda i: (i, 0))
    return pl.pallas_call(
        functools.partial(attend_kernel, heads, block, block),
        grid=(length // block,),
        in_specs=[rows, whole, whole, pl.BlockSpec((block, 1), lambda i: (i, 0))],
        out_specs=[rows, rows, pl.BlockSpec((heads, block), lambda i: (0, i))],
        out_shape=[
            jax.ShapeDtypeStruct((length, width), bf16),
            jax.ShapeDtypeStruct((length, width), f32),
            jax.ShapeDtypeStruct((heads, length), f32),
        ],
        scratch_shapes=[
            pltpu.VMEM((heads * block, width), f32),
            pltpu.VMEM((heads * block, 128), f32),
        ],
        cost_estimate=pl.CostEstimate(
            flops=20_000_000_000, bytes_accessed=8 * length * width, transcendentals=0
        ),
        name="attend",
    )(q, k, v, start)


def attend_back_kernel(
    heads, bq, bk, q_ref, do_ref, k_ref, v_ref, of_ref, l_ref, start_ref, dq_ref, dk_ref, dv_ref, acc
):
    i = pl.program_id(0)

    @pl.when(i == 0)
    def _():
        dk_ref[...] = jnp.zeros_like(dk_ref)
        dv_ref[...] = jnp.zeros_like(dv_ref)

    qs = head_stack(q_ref[...], heads)
    grads = do_ref[...]
    dos = head_stack(grads, heads)
    product = (grads.astype(f32) * of_ref[...]).T
    delta = jnp.concatenate(
        [
            jnp.sum(product[h * HEAD_DIM : (h + 1) * HEAD_DIM], axis=0, keepdims=True)
            for h in range(heads)
        ],
        axis=1,
    )
    log_sum = jnp.concatenate([l_ref[h : h + 1, :] for h in range(heads)], axis=1)
    start = jnp.concatenate([start_ref[...]] * heads, axis=1)
    acc[...] = jnp.zeros_like(acc)

    def step(j, diagonal):
        offset = pl.multiple_of(j * bk, bk)
        keys = k_ref[pl.ds(offset, bk), :]
        values = v_ref[pl.ds(offset, bk), :]
        scores = dot_nt(keys, qs)
        key_index = offset + lax.broadcasted_iota(jnp.int32, scores.shape, 0)
        allowed = key_index >= start
        if diagonal:
            column = lax.rem(lax.broadcasted_iota(jnp.int32, scores.shape, 1), bq)
            allowed = allowed & (key_index <= i * bq + column)
        probs = jnp.where(allowed, jnp.exp2(scores * (scale_factor * LOG2E) - log_sum), 0.0)
        prob_grad = dot_nt(values, dos)
        score_grad = (probs * (prob_grad - delta)).astype(bf16)
        dv_ref[pl.ds(offset, bk), :] += dot_nn(probs.astype(bf16), dos)
        dk_ref[pl.ds(offset, bk), :] += dot_nn(score_grad, qs)
        acc[...] += dot_tn(score_grad, keys)

    def body(j, carry):
        step(j, False)
        return carry

    lax.fori_loop(0, i, body, 0)
    step(i, True)
    dq_ref[...] = head_pick(acc[...], heads, bq)


def attend_back(q, k, v, grads, out, log_sum, start, block):
    length, width = q.shape
    heads = width // HEAD_DIM
    whole = pl.BlockSpec((length, width), lambda i: (0, 0))
    rows = pl.BlockSpec((block, width), lambda i: (i, 0))
    result = jax.ShapeDtypeStruct((length, width), f32)
    return pl.pallas_call(
        functools.partial(attend_back_kernel, heads, block, block),
        grid=(length // block,),
        in_specs=[
            rows,
            rows,
            whole,
            whole,
            rows,
            pl.BlockSpec((heads, block), lambda i: (0, i)),
            pl.BlockSpec((1, block), lambda i: (0, i)),
        ],
        out_specs=[rows, whole, whole],
        out_shape=[result, result, result],
        scratch_shapes=[pltpu.VMEM((heads * block, width), f32)],
        cost_estimate=pl.CostEstimate(
            flops=40_000_000_000, bytes_accessed=20 * length * width, transcendentals=0
        ),
        name="attend_back",
    )(q, grads, k, v, out, log_sum, start)


def feed_kernel(m_ref, w_ref, s_ref, up_ref, gate_ref, h_ref, out_ref):
    @pl.when(pl.program_id(0) == 0)
    def _():
        out_ref[...] = jnp.zeros_like(out_ref)

    tokens = m_ref[...]
    up = dot_nn(tokens, w_ref[0, 0])
    gate = dot_nn(tokens, w_ref[1, 0])
    up_ref[...] = up
    gate_ref[...] = gate
    scaled = gate * s_ref[1:2, :]
    hidden = (up * s_ref[0:1, :] * (scaled * jax.nn.sigmoid(scaled))).astype(bf16)
    h_ref[...] = hidden
    out_ref[...] += dot_nt(hidden, w_ref[2, 0])


def feed(middle, weights, scales, step):
    rows, model = middle.shape
    _, groups, _, local_width = weights.shape
    per = local_width // step
    total = groups * local_width
    columns = pl.BlockSpec((rows, step), lambda i: (0, i))
    return pl.pallas_call(
        feed_kernel,
        grid=(total // step,),
        in_specs=[
            pl.BlockSpec((rows, model), lambda i: (0, 0)),
            pl.BlockSpec((3, 1, model, step), lambda i: (0, i // per, 0, i % per)),
            pl.BlockSpec((2, step), lambda i: (0, i)),
        ],
        out_specs=[columns, columns, columns, pl.BlockSpec((rows, model), lambda i: (0, 0))],
        out_shape=[
            jax.ShapeDtypeStruct((rows, total), f32),
            jax.ShapeDtypeStruct((rows, total), f32),
            jax.ShapeDtypeStruct((rows, total), bf16),
            jax.ShapeDtypeStruct((rows, model), f32),
        ],
        cost_estimate=pl.CostEstimate(
            flops=6 * rows * model * total,
            bytes_accessed=6 * model * total + 10 * rows * total,
            transcendentals=0,
        ),
        name="feed",
    )(middle, weights, scales)


def feed_back_kernel(
    og_ref, mt_ref, w_ref, s_ref, up_ref, gate_ref, grad_ref, sg_ref, mg_ref
):
    @pl.when(pl.program_id(0) == 0)
    def _():
        mg_ref[...] = jnp.zeros_like(mg_ref)

    hidden_grad = dot_nn(og_ref[...], w_ref[2, 0])
    up = up_ref[...]
    gate = gate_ref[...]
    up_gain = s_ref[0:1, :]
    gate_gain = s_ref[1:2, :]
    scaled = gate * gate_gain
    sig = jax.nn.sigmoid(scaled)
    up_part = hidden_grad * (scaled * sig)
    gate_part = hidden_grad * (up * up_gain) * (sig * (1.0 + scaled * (1.0 - sig)))
    sg_ref[0:1, :] = jnp.sum(up_part * up, axis=0, keepdims=True)
    sg_ref[1:2, :] = jnp.sum(gate_part * gate, axis=0, keepdims=True)
    up_low = (up_part * up_gain).astype(bf16)
    gate_low = (gate_part * gate_gain).astype(bf16)
    tokens_t = mt_ref[...]
    grad_ref[0] = dot_nn(tokens_t, up_low).astype(bf16)
    grad_ref[1] = dot_nn(tokens_t, gate_low).astype(bf16)
    mg_ref[...] += dot_nt(up_low, w_ref[0, 0]) + dot_nt(gate_low, w_ref[1, 0])


def feed_back(out_grad, middle_t, weights, scales, up, gate, step):
    model, rows = middle_t.shape
    _, groups, _, local_width = weights.shape
    per = local_width // step
    total = groups * local_width
    columns = pl.BlockSpec((rows, step), lambda i: (0, i))
    return pl.pallas_call(
        feed_back_kernel,
        grid=(total // step,),
        in_specs=[
            pl.BlockSpec((rows, model), lambda i: (0, 0)),
            pl.BlockSpec((model, rows), lambda i: (0, 0)),
            pl.BlockSpec((3, 1, model, step), lambda i: (0, i // per, 0, i % per)),
            pl.BlockSpec((2, step), lambda i: (0, i)),
            columns,
            columns,
        ],
        out_specs=[
            pl.BlockSpec((2, model, step), lambda i: (0, 0, i)),
            pl.BlockSpec((2, step), lambda i: (0, i)),
            pl.BlockSpec((rows, model), lambda i: (0, 0)),
        ],
        out_shape=[
            jax.ShapeDtypeStruct((2, model, total), bf16),
            jax.ShapeDtypeStruct((2, total), f32),
            jax.ShapeDtypeStruct((rows, model), f32),
        ],
        cost_estimate=pl.CostEstimate(
            flops=10 * rows * model * total,
            bytes_accessed=10 * model * total + 8 * rows * total,
            transcendentals=0,
        ),
        name="feed_back",
    )(out_grad, middle_t, weights, scales, up, gate)


def shift(value, axis, distance, size):
    return lax.ppermute(value, axis, [(i, (i + distance) % size) for i in range(size)])


def butterfly(values, axis, size):
    step = 1
    while step < size:
        other = [lax.ppermute(v, axis, [(i, i ^ step) for i in range(size)]) for v in values]
        values = [v + o for v, o in zip(values, other)]
        step *= 2
    return values


def take_block(value, index, size, axis):
    return lax.dynamic_slice_in_dim(value, index * size, size, axis)


def put_block(whole, value, index, axis):
    return lax.dynamic_update_slice_in_dim(whole, value, index * value.shape[axis], axis)


def local(
    nd,
    nt,
    hidden_in,
    cotangent,
    segments,
    attn_weight,
    mlp_weight,
    rates,
    qk_scale,
    mlp_scales,
    attn_moment_one,
    attn_moment_two,
    mlp_moment_one,
    mlp_moment_two,
):
    rows, model = hidden_in.shape
    length = segments.shape[0]
    shard = attn_weight.shape[1]
    heads_width = attn_weight.shape[2]
    hidden_width = mlp_weight.shape[2]
    local_heads = heads_width // HEAD_DIM
    block = min(512, length)
    step = min(512, hidden_width)
    me = lax.axis_index("tensor")

    attn_low = attn_weight.astype(bf16)
    attn_shard = jnp.concatenate([attn_low[0], attn_low[1], attn_low[2], attn_low[3]], axis=1)
    attn_full = lax.all_gather(attn_shard, "dp", axis=0, tiled=True)
    mlp_low, attn_full = lax.optimization_barrier((mlp_weight.astype(bf16), attn_full))
    mlp_full = lax.all_gather(mlp_low, ("tensor", "dp"), axis=1, tiled=True)
    mlp_full = mlp_full.reshape(3, nt, model, hidden_width)
    qkv_matrix = attn_full[:, : 3 * heads_width]
    out_local = attn_full[:, 3 * heads_width :]

    hidden_row = jnp.zeros((length, model), bf16)
    hidden_row = put_block(hidden_row, hidden_in, me, 0)
    for d in range(1, nt):
        hidden_row = put_block(hidden_row, shift(hidden_in, "tensor", d, nt), (me - d) % nt, 0)
    scales_row = jnp.zeros((2, nt * hidden_width), f32)
    scales_row = put_block(scales_row, mlp_scales, me, 1)
    for d in range(1, nt):
        scales_row = put_block(scales_row, shift(mlp_scales, "tensor", d, nt), (me - d) % nt, 1)
    out_matrix = jnp.concatenate(
        [out_local] + [shift(out_local, "tensor", d, nt) for d in range(1, nt)], axis=1
    )

    projected = jnp.dot(hidden_row, qkv_matrix, preferred_element_type=f32)
    starts = starts_of(segments)
    positions = jnp.arange(length, dtype=jnp.int32) - starts

    def prepare_flat(raw, gain_flat):
        rotated = rotary(raw.reshape(length, local_heads, HEAD_DIM), positions)
        return (unit_norm(rotated) * gain_flat.reshape(local_heads, HEAD_DIM)).reshape(
            length, heads_width
        )

    query_raw = projected[:, :heads_width]
    key_raw = projected[:, heads_width : 2 * heads_width]
    query_hat = prepare_flat(query_raw, qk_scale).astype(bf16)
    key_hat = prepare_flat(key_raw, qk_scale).astype(bf16)
    value_hat = projected[:, 2 * heads_width :].astype(bf16)
    attended_row, attended_f32, log_sum = attend(
        query_hat, key_hat, value_hat, starts[:, None], block
    )
    attended = jnp.concatenate(
        [take_block(attended_row, me, rows, 0)]
        + [
            shift(take_block(attended_row, (me + d) % nt, rows, 0), "tensor", d, nt)
            for d in range(1, nt)
        ],
        axis=1,
    )
    branch = dot_nt(attended, out_matrix)
    tokens = hidden_in.astype(f32)
    middle = sphere_mix(tokens, branch, rates[0])
    middle_low = middle.astype(bf16)
    up, gate, hidden_units, mlp_out = feed(middle_low, mlp_full, scales_row, step)
    result = sphere_mix(middle, mlp_out, rates[1])
    row_segments = take_block(segments, me, rows, 0)
    upstream = cotangent.astype(f32) * (row_segments < pad_segment).astype(f32)[:, None]
    _, mlp_pull = jax.vjp(sphere_mix, middle, mlp_out, rates[1])
    middle_direct, mlp_out_grad, rate_mlp_grad = mlp_pull(upstream)
    mlp_out_low = mlp_out_grad.astype(bf16)
    down_grad = dot_tn(mlp_out_low, hidden_units).astype(bf16)
    down_part = lax.psum_scatter(down_grad, "dp", scatter_dimension=0, tiled=True)
    in_grad, scales_grad, middle_back = feed_back(
        mlp_out_low, middle_low.T, mlp_full, scales_row, up, gate, step
    )
    in_part = lax.psum_scatter(in_grad, "dp", scatter_dimension=1, tiled=True)
    _, attn_pull = jax.vjp(sphere_mix, tokens, branch, rates[0])
    token_direct, branch_grad, rate_attn_grad = attn_pull(middle_direct + middle_back)
    branch_low = branch_grad.astype(bf16)
    attended_grad = dot_nn(branch_low, out_matrix).astype(bf16)
    grad_row = jnp.zeros((length, heads_width), bf16)
    grad_row = put_block(grad_row, attended_grad[:, :heads_width], me, 0)
    for d in range(1, nt):
        piece = attended_grad[:, d * heads_width : (d + 1) * heads_width]
        grad_row = put_block(grad_row, shift(piece, "tensor", -d, nt), (me + d) % nt, 0)
    out_grad = dot_tn(branch_low, attended).astype(bf16)
    out_part = lax.psum_scatter(out_grad, "dp", scatter_dimension=0, tiled=True)

    query_hat_grad, key_hat_grad, value_grad = attend_back(
        query_hat, key_hat, value_hat, grad_row, attended_f32, log_sum, starts[None, :], block
    )
    _, query_pull = jax.vjp(prepare_flat, query_raw, qk_scale)
    query_raw_grad, gain_query = query_pull(query_hat_grad * scale_factor)
    _, key_pull = jax.vjp(prepare_flat, key_raw, qk_scale)
    key_raw_grad, gain_key = key_pull(key_hat_grad * scale_factor)
    qkv_grad = jnp.concatenate([query_raw_grad, key_raw_grad, value_grad], axis=1).astype(bf16)
    total = token_direct + dot_nt(take_block(qkv_grad, me, rows, 0), qkv_matrix)
    for d in range(1, nt):
        piece = dot_nt(take_block(qkv_grad, (me + d) % nt, rows, 0), qkv_matrix).astype(bf16)
        total = total + shift(piece, "tensor", d, nt).astype(f32)
    input_grad = total.astype(bf16)
    qkv_weight_grad = dot_tn(hidden_row, qkv_grad).astype(bf16)
    qkv_part = lax.psum_scatter(qkv_weight_grad, "dp", scatter_dimension=0, tiled=True)

    def own_sum(part, axis, width):
        total = take_block(part, me, width, axis).astype(f32)
        for d in range(1, nt):
            piece = take_block(part, (me + d) % nt, width, axis)
            total = total + shift(piece, "tensor", d, nt).astype(f32)
        return total

    out_own = out_part[:, :heads_width].astype(f32)
    for d in range(1, nt):
        piece = out_part[:, d * heads_width : (d + 1) * heads_width]
        out_own = out_own + shift(piece, "tensor", -d, nt).astype(f32)
    down_own = own_sum(down_part, 1, hidden_width)
    in_own = own_sum(in_part, 2, hidden_width)
    attn_weight_grad = jnp.stack(
        [
            qkv_part[:, :heads_width].astype(f32),
            qkv_part[:, heads_width : 2 * heads_width].astype(f32),
            qkv_part[:, 2 * heads_width :].astype(f32),
            out_own,
        ]
    )
    mlp_weight_grad = jnp.concatenate([in_own, down_own[None]], axis=0)

    rates_part = jnp.stack([rate_attn_grad, rate_mlp_grad])
    small = jnp.concatenate([rates_part, scales_grad.reshape(-1, model)], axis=0)
    (small,) = butterfly([small], "dp", nd)
    (small,) = butterfly([small], "tensor", nt)
    rates_grad = small[:2]
    mlp_scales_grad = small[2:].reshape(2, nt * hidden_width)

    attn_one, attn_two, attn_moved = adam_moved(
        attn_weight, attn_weight_grad, attn_moment_one, attn_moment_two
    )
    mlp_one, mlp_two, mlp_moved = adam_moved(
        mlp_weight, mlp_weight_grad, mlp_moment_one, mlp_moment_two
    )
    attn_square = jnp.sum(attn_moved * attn_moved, axis=1, keepdims=True)
    mlp_square = jnp.sum(mlp_moved * mlp_moved, axis=1, keepdims=True)
    gain = gain_query + gain_key
    (mlp_square,) = butterfly([mlp_square], "dp", nd)
    last = jnp.concatenate([attn_square.reshape(-1), gain])
    (last,) = butterfly([last], "dp", nd)
    attn_square = last[: 4 * heads_width].reshape(4, 1, heads_width)
    gain = last[4 * heads_width :]
    gain_row = put_block(jnp.zeros((nt * heads_width,), f32), gain, me, 0)
    for d in range(1, nt):
        gain_row = put_block(gain_row, shift(gain, "tensor", d, nt), (me - d) % nt, 0)
    attn_new = attn_moved * lax.rsqrt(attn_square + norm_eps)
    mlp_new = mlp_moved * lax.rsqrt(mlp_square + norm_eps)
    return (
        result.astype(bf16),
        input_grad,
        attn_weight_grad,
        mlp_weight_grad,
        rates_grad,
        gain_row,
        mlp_scales_grad,
        attn_one,
        attn_two,
        mlp_one,
        mlp_two,
        attn_new,
        mlp_new,
    )


def solution(mesh):
    weights = P(None, "dp", "tensor")
    tokens = P(("dp", "tensor"), None)
    return jax.shard_map(
        functools.partial(local, mesh.shape["dp"], mesh.shape["tensor"]),
        mesh=mesh,
        in_specs=(
            tokens,
            tokens,
            P("dp"),
            weights,
            weights,
            P(),
            P("tensor"),
            P(None, "tensor"),
            weights,
            weights,
            weights,
            weights,
        ),
        out_specs=(
            tokens,
            tokens,
            weights,
            weights,
            P(),
            P(),
            P(),
            weights,
            weights,
            weights,
            weights,
            weights,
            weights,
        ),
        check_vma=False,
    )
```

time: 1530 us -> 847 us (0.55)
  waiting for transfers between devices: 810 us -> 390 us
  matrix products: 336 us -> 39.7 us
  starting transfers between devices: 10.4 us -> 163 us
  Pallas kernels: 0 us -> 114 us
  other arithmetic: 141 us -> 57.6 us
  blocking collectives: 66.1 us -> 0 us
  local copies, waits for them, and re-layouts: 124 us -> 59.9 us
    all_gather x6 -> x2, waiting for transfers between devices: 365 us -> 30.7 us  [the longest x1 30.7 us: local(): attn_full = lax.all_gather(attn_shard, 'dp', axis=0, tiled=True)]
    reduce_scatter x5 -> x4, waiting for transfers between devices: 445 us -> 128 us  [the longest x1 111 us: local(): in_part = lax.psum_scatter(in_grad, 'dp', scatter_dimension=1, tiled=True)]
    dot_general x40 -> x10, matrix products: 336 us -> 39.7 us  [the longest x3 19.4 us: dot_tn(): lax.dot_general(a, b, (((0,), (0,)), ((), ())), preferred_element_type=f32)]
    ppermute x0 -> x41, waiting for transfers between devices: none -> 231 us  [the longest x30 220 us: shift(): lax.ppermute(value, axis, [(i, (i + distance) % size) for i in range(size)])]
    ppermute x0 -> x41, starting transfers between devices: none -> 163 us  [the longest x30 150 us: shift(): lax.ppermute(value, axis, [(i, (i + distance) % size) for i in range(size)])]
    pallas_call x0 -> x4, Pallas kernels: none -> 114 us  [the longest x1 40.6 us: attend_back(): pl.pallas_call(functools.partial(attend_back_kernel, heads, block, block)...]
    psum x2 -> x0, blocking collectives: 66.1 us -> none  [the longest x1 41.3 us: local(): lax.psum((rate_part, gain_part, scale_part), ('dp', 'tensor'))]
    convert_element_type x13 -> x7, other arithmetic: 59.5 us -> 10.1 us  [the longest x1 3.26 us: local(): key_hat = prepare_flat(key_raw, qk_scale).astype(bf16)]
  transfers between devices with their start and end apart: 12 -> 47, of which waited for: 10 -> 22; matrix products, arithmetic and copies ran while one was open for 27% -> 14% of each run, Pallas kernels for 0% -> 7%
where the time goes in v1:
time: 847 us; the launch traced here: 840 us
  waiting for transfers between devices  390 us (46%)
  starting transfers between devices  163 us (19%)
  Pallas kernels  114 us (13%)
  local copies, waits for them, and re-layouts  59.9 us (7%)
  other arithmetic  57.6 us (7%)
  matrix products  39.7 us (5%)
  between operations  15.8 us (2%)
    ppermute x30, waiting for transfers between devices, shift(): lax.ppermute(value, axis, [(i, (i + distance) % size) for i in range(size)])  220 us
    ppermute x30, starting transfers between devices, shift(): lax.ppermute(value, axis, [(i, (i + distance) % size) for i in range(size)])  150 us
    reduce_scatter x1, waiting for transfers between devices, local(): in_part = lax.psum_scatter(in_grad, 'dp', scatter_dimension=1, tiled=True)  111 us
    pallas_call x1, Pallas kernels, attend_back(): pl.pallas_call(functools.partial(attend_back_kernel, heads, block, block)...  40.6 us
    pallas_call x1, Pallas kernels, feed_back(): pl.pallas_call(feed_back_kernel, grid=(total // step,), in_specs=[pl.Bloc...  32.7 us
    all_gather x1, waiting for transfers between devices, local(): attn_full = lax.all_gather(attn_shard, 'dp', axis=0, tiled=True)  30.7 us
    pallas_call x1, Pallas kernels, feed(): pl.pallas_call(feed_kernel, grid=(total // step,), in_specs=[pl.BlockSpec...  20.3 us
    pallas_call x1, Pallas kernels, attend(): pl.pallas_call(functools.partial(attend_kernel, heads, block, block), gri...  20.3 us
  transfers between devices with their start and end apart: 47, of which 22 were waited for; matrix products, arithmetic and copies ran while one was open for 14% of the time, Pallas kernels for 7%

profile of v1, /device:TPU:0, one launch (start us, length us, event | category | flops | bytes accessed | tf_op | source)
XLA Modules:
  0.0 840.0 jit_solution(11789338212128699674)
XLA Ops:
  10.3 30.7 %all-gather.3.cloned.1.call-done = bf16[1024,1024]{1,0:T(8,128)(2,1)} async-done(((bf16[128,1024]{1,0:T(8,128)(2,1)}), bf16[1024,1024]{1,0:T(8,128)(2,1)}) %all-gather.3.cloned.1.call-update) | async-done | bytes 2097168 | tf_op jit(solution)/shard_map/all_gather | solution.py:399
  51.4 29.0 %collective-permute-done = bf16[512,1024]{1,0:T(8,128)(2,1)} collective-permute-done((bf16[512,1024]{1,0:T(8,128)(2,1)S(1)}, bf16[512,1024]{1,0:T(8,128)(2,1)}, u32[]{:S(2)}, u32[]{:S(2)}) %collective-permute-start) | collective-permute-done | bytes 1048608 | tf_op jit(solution)/shard_map/ppermute | solution.py:351
  81.8 59.8 %collective-permute-done.1 = bf16[512,1024]{1,0:T(8,128)(2,1)S(1)} collective-permute-done((bf16[512,1024]{1,0:T(8,128)(2,1)S(1)}, bf16[512,1024]{1,0:T(8,128)(2,1)S(1)}, u32[]{:S(2)}, u32[]{:S(2)}) %collective-permute-start.1) | collective-permute-done | bytes 1048608 | tf_op jit(solution)/shard_map/ppermute | solution.py:351
  163.9 20.3 %attend.1 = (bf16[2048,256]{1,0:T(8,128)(2,1)}, f32[2048,256]{1,0:T(8,128)}, f32[4,2048]{1,0:T(4,128)}) custom-call(bf16[2048,256]{1,0:T(8,128)(2,1)} %get-tuple-element.146.q_ref, bf16[2048,256]{1,0:T(8,128)(2,1)} %get-tuple-element.145.k_ref, bf16[2048,256]{1,0:T(8,128)(2,1)} %copy.78.v_ref, s32[2048,1]{1,0:T(8,128)} %copy.51.start_ref), custom_call_target="tpu_custom_call" | custom-call | flops 20000000000 | bytes 4194304 | tf_op jit(solution)/shard_map/attend/pallas_call | solution.py:142
  186.6 45.2 %collective-permute-start.3 = (bf16[512,256]{1,0:T(8,128)(2,1)}, bf16[512,256]{1,0:T(8,128)(2,1)}, u32[]{:S(2)}, u32[]{:S(2)}) collective-permute-start(bf16[512,256]{1,0:T(8,128)(2,1)} %get-tuple-element.120), channel_id=1, source_target_pairs={{0,1},{1,2},{2,3},{3,0},{4,5},{5,6},{6,7},{7,4},{8,9},{9,10},{10,1... | collective-permute-start | bytes 786440 | tf_op jit(solution)/shard_map/ppermute | solution.py:351
  243.1 51.1 %collective-permute-done.11 = f32[2,1024]{1,0:T(2,128)} collective-permute-done((f32[2,1024]{1,0:T(2,128)}, f32[2,1024]{1,0:T(2,128)}, u32[]{:S(2)}, u32[]{:S(2)}) %collective-permute-start.11) | collective-permute-done | bytes 8224 | tf_op jit(solution)/shard_map/ppermute | solution.py:351
  294.1 13.2 %collective-permute-start.4 = (bf16[512,256]{1,0:T(8,128)(2,1)S(1)}, bf16[512,256]{1,0:T(8,128)(2,1)S(1)}, u32[]{:S(2)}, u32[]{:S(2)}) collective-permute-start(bf16[512,256]{1,0:T(8,128)(2,1)S(1)} %copy-done.44), channel_id=1, source_target_pairs={{0,2},{1,3},{2,0},{3,1},{4,6},{5,7},{6,4},{7,5},{8,10},{9,11},{10,... | collective-permute-start | bytes 786440 | tf_op jit(solution)/shard_map/ppermute | solution.py:351
  312.3 7.9 collective-permute-done.4
  333.4 20.3 %feed.1 = (f32[512,4096]{1,0:T(8,128)}, f32[512,4096]{1,0:T(8,128)}, bf16[512,4096]{1,0:T(8,128)(2,1)}, f32[512,1024]{1,0:T(8,128)}) custom-call(bf16[512,1024]{1,0:T(8,128)(2,1)} %copy.53.m_ref, bf16[3,4,1024,1024]{3,2,1,0:T(8,128)(2,1)} %bitcast.93, f32[2,4096]{1,0:T(2,128)} %copy-done.63), custom_call_target="tpu_custom_call" | custom-call | flops 12884901888 | bytes 46137344 | tf_op jit(solution)/shard_map/feed/pallas_call | solution.py:264
  365.4 32.7 %feed_back.1 = (bf16[2,1024,4096]{2,1,0:T(8,128)(2,1)}, f32[2,4096]{1,0:T(2,128)}, f32[512,1024]{1,0:T(8,128)}) custom-call(bf16[512,1024]{1,0:T(8,128)(2,1)} %copy.58.og_ref, bf16[1024,512]{1,0:T(8,128)(2,1)} %fusion.47.mt_ref, bf16[3,4,1024,1024]{3,2,1,0:T(8,128)(2,1)} %bitcast.94, f32[2,4096]{1,0:T(2,128)} %copy-done.63, ...), custom_call_target="tpu_custom_call" | custom-call | flops 21474836480 | bytes 58720256 | tf_op jit(solution)/shard_map/feed_back/pallas_call | solution.py:320
  401.0 4.4 multiply_reduce_fusion.2
  413.8 8.6 %collective-permute-start.12 = (bf16[512,256]{1,0:T(8,128)(2,1)S(1)}, bf16[512,256]{1,0:T(8,128)(2,1)S(1)}, u32[]{:S(2)}, u32[]{:S(2)}) collective-permute-start(bf16[512,256]{1,0:T(8,128)(2,1)S(1)} %get-tuple-element.115), channel_id=1, source_target_pairs={{0,3},{1,0},{2,1},{3,2},{4,7},{5,4},{6,5},{7,6},{8,11},{9,8},{10,9... | collective-permute-start | bytes 786440 | tf_op jit(solution)/shard_map/ppermute | solution.py:351
  429.1 14.9 %collective-permute-done.13 = bf16[512,256]{1,0:T(8,128)(2,1)S(1)} collective-permute-done((bf16[512,256]{1,0:T(8,128)(2,1)S(1)}, bf16[512,256]{1,0:T(8,128)(2,1)S(1)}, u32[]{:S(2)}, u32[]{:S(2)}) %collective-permute-start.13) | collective-permute-done | bytes 262176 | tf_op jit(solution)/shard_map/ppermute | solution.py:351
  445.0 40.6 %attend_back.1 = (f32[2048,256]{1,0:T(8,128)}, f32[2048,256]{1,0:T(8,128)}, f32[2048,256]{1,0:T(8,128)}) custom-call(bf16[2048,256]{1,0:T(8,128)(2,1)} %get-tuple-element.146.q_ref, bf16[2048,256]{1,0:T(8,128)(2,1)} %copy-done.40, bf16[2048,256]{1,0:T(8,128)(2,1)} %get-tuple-element.145.k_ref, bf16[2048,256]{1,0:T(8,128)(2,1)} %copy.78.v_ref, ...), custom_call_target="tpu_custom_call" | custom-call | flops 40000000000 | bytes 10485760 | tf_op jit(solution)/shard_map/attend_back/pallas_call | solution.py:220
  508.1 6.9 convolution_convert_fusion.2
  515.1 8.9 %convolution_convert_fusion = bf16[1024,4096]{1,0:T(8,128)(2,1)} fusion(bf16[512,1024]{0,1:T(8,128)(2,1)S(1)} %copy-done.25, bf16[512,4096]{1,0:T(8,128)(2,1)} %get-tuple-element.41), kind=kOutput, calls=%fused_computation | convolution fusion | flops 4299161600 | bytes 13631488 | tf_op jit(solution)/shard_map/dot_general | solution.py:82
  555.9 12.6 %collective-permute-done.18 = bf16[128,256]{1,0:T(8,128)(2,1)S(1)} collective-permute-done((bf16[128,256]{1,0:T(8,128)(2,1)S(1)}, bf16[128,256]{1,0:T(8,128)(2,1)S(1)}, u32[]{:S(2)}, u32[]{:S(2)}) %collective-permute-start.18) | collective-permute-done | bytes 65568 | tf_op jit(solution)/shard_map/ppermute | solution.py:351
  574.7 35.1 %collective-permute-start.17 = (bf16[512,1024]{0,1:T(8,128)(2,1)}, bf16[512,1024]{0,1:T(8,128)(2,1)}, u32[]{:S(2)}, u32[]{:S(2)}) collective-permute-start(bf16[512,1024]{0,1:T(8,128)(2,1)} %convolution_convert_fusion.3), channel_id=1, source_target_pairs={{0,3},{1,0},{2,1},{3,2},{4,7},{5,4},{6,5},{7,6},{8,11},{9,8},{10,9... | collective-permute-start | bytes 3145736 | tf_op jit(solution)/shard_map/ppermute | solution.py:351
  612.1 16.8 %reduce-scatter.11.cloned.1.call-done = bf16[128,4096]{1,0:T(8,128)(2,1)} async-done(((bf16[1024,4096]{1,0:T(8,128)(2,1)}), bf16[128,4096]{1,0:T(8,128)(2,1)}) %reduce-scatter.11.cloned.1.call-update) | async-done | bytes 1048592 | tf_op jit(solution)/shard_map/reduce_scatter | solution.py:456
  637.5 111.0 %reduce-scatter.9.cloned.1.call-done = bf16[2,128,4096]{2,1,0:T(8,128)(2,1)} async-done(((bf16[2,1024,4096]{2,1,0:T(8,128)(2,1)}), bf16[2,128,4096]{2,1,0:T(8,128)(2,1)}) %reduce-scatter.9.cloned.1.call-update) | async-done | bytes 2097168 | tf_op jit(solution)/shard_map/reduce_scatter | solution.py:460
  759.5 5.0 add_convert_fusion
  768.0 9.7 %collective-permute-done.26 = bf16[128,1024]{1,0:T(8,128)(2,1)} collective-permute-done((bf16[128,1024]{1,0:T(8,128)(2,1)S(1)}, bf16[128,1024]{1,0:T(8,128)(2,1)}, u32[]{:S(2)}, u32[]{:S(2)}) %collective-permute-start.26) | collective-permute-done | bytes 262176 | tf_op jit(solution)/shard_map/ppermute | solution.py:351
  779.3 26.8 %collective-permute-done.22 = bf16[2,128,1024]{2,1,0:T(8,128)(2,1)} collective-permute-done((bf16[2,128,1024]{2,1,0:T(8,128)(2,1)}, bf16[2,128,1024]{2,1,0:T(8,128)(2,1)}, u32[]{:S(2)}, u32[]{:S(2)}) %collective-permute-start.22) | collective-permute-done | bytes 524320 | tf_op jit(solution)/shard_map/ppermute | solution.py:351
  813.4 10.8 %collective-permute-start.35 = (f32[256]{0:T(256)S(1)}, f32[256]{0:T(256)S(1)}, u32[]{:S(2)}, u32[]{:S(2)}) collective-permute-start(f32[256]{0:T(256)S(1)} %get-tuple-element.137), channel_id=1, source_target_pairs={{0,1},{1,2},{2,3},{3,0},{4,5},{5,6},{6,7},{7,4},{8,9},{9,10},{10,1... | collective-permute-start | bytes 3080 | tf_op jit(solution)/shard_map/ppermute | solution.py:351
  (372 shorter events, 202.0 us)
Async XLA Ops:
  9.2 324.2 %all-gather.5.cloned.1.call-start = ((), (), s32[]{:S(2)}) async-start(), calls=%async_computation.5 | async-start | bytes 25952256 | tf_op jit(solution)/shard_map/all_gather | solution.py:401
  41.0 508.5 %reduce-scatter.7.cloned.1.call-start = ((), (), s32[]{:S(2)}) async-start(), calls=%async_computation.7 | async-start | bytes 2359296 | tf_op jit(solution)/shard_map/reduce_scatter | solution.py:471
  41.1 39.4 %collective-permute-start = (bf16[512,1024]{1,0:T(8,128)(2,1)S(1)}, bf16[512,1024]{1,0:T(8,128)(2,1)}, u32[]{:S(2)}, u32[]{:S(2)}) collective-permute-start(bf16[512,1024]{1,0:T(8,128)(2,1)S(1)} %copy-done.23), channel_id=1, source_target_pairs={{0,1},{1,2},{2,3},{3,0},{4,5},{5,6},{6,7},{7,4},{8,9},{9,10},{10,1... | collective-permute-start | bytes 3145736 | tf_op jit(solution)/shard_map/ppermute | solution.py:351
  42.6 99.0 %collective-permute-start.1 = (bf16[512,1024]{1,0:T(8,128)(2,1)S(1)}, bf16[512,1024]{1,0:T(8,128)(2,1)S(1)}, u32[]{:S(2)}, u32[]{:S(2)}) collective-permute-start(bf16[512,1024]{1,0:T(8,128)(2,1)S(1)} %copy-done.23), channel_id=1, source_target_pairs={{0,2},{1,3},{2,0},{3,1},{4,6},{5,7},{6,4},{7,5},{8,10},{9,11},{10,... | collective-permute-start | bytes 3145736 | tf_op jit(solution)/shard_map/ppermute | solution.py:351
  45.0 96.7 %collective-permute-start.2 = (bf16[512,1024]{1,0:T(8,128)(2,1)S(1)}, bf16[512,1024]{1,0:T(8,128)(2,1)S(1)}, u32[]{:S(2)}, u32[]{:S(2)}) collective-permute-start(bf16[512,1024]{1,0:T(8,128)(2,1)S(1)} %copy-done.23), channel_id=1, source_target_pairs={{0,3},{1,0},{2,1},{3,2},{4,7},{5,4},{6,5},{7,6},{8,11},{9,8},{10,9... | collective-permute-start | bytes 3145736 | tf_op jit(solution)/shard_map/ppermute | solution.py:351
  46.5 189.1 %collective-permute-start.9 = (f32[2,1024]{1,0:T(2,128)}, f32[2,1024]{1,0:T(2,128)S(1)}, u32[]{:S(2)}, u32[]{:S(2)}) collective-permute-start(f32[2,1024]{1,0:T(2,128)} %param.19), channel_id=1, source_target_pairs={{0,1},{1,2},{2,3},{3,0},{4,5},{5,6},{6,7},{7,4},{8,9},{9,10},{10,1... | collective-permute-start | bytes 24584 | tf_op jit(solution)/shard_map/ppermute | solution.py:351
  47.0 192.0 %collective-permute-start.10 = (f32[2,1024]{1,0:T(2,128)}, f32[2,1024]{1,0:T(2,128)}, u32[]{:S(2)}, u32[]{:S(2)}) collective-permute-start(f32[2,1024]{1,0:T(2,128)} %param.19), channel_id=1, source_target_pairs={{0,2},{1,3},{2,0},{3,1},{4,6},{5,7},{6,4},{7,5},{8,10},{9,11},{10,... | collective-permute-start | bytes 24584 | tf_op jit(solution)/shard_map/ppermute | solution.py:351
  186.6 120.7 %collective-permute-start.3 = (bf16[512,256]{1,0:T(8,128)(2,1)}, bf16[512,256]{1,0:T(8,128)(2,1)}, u32[]{:S(2)}, u32[]{:S(2)}) collective-permute-start(bf16[512,256]{1,0:T(8,128)(2,1)} %get-tuple-element.120), channel_id=1, source_target_pairs={{0,1},{1,2},{2,3},{3,0},{4,5},{5,6},{6,7},{7,4},{8,9},{9,10},{10,1... | collective-permute-start | bytes 786440 | tf_op jit(solution)/shard_map/ppermute | solution.py:351
  233.7 86.4 %collective-permute-start.6 = (bf16[1024,256]{1,0:T(8,128)(2,1)}, bf16[1024,256]{1,0:T(8,128)(2,1)}, u32[]{:S(2)}, u32[]{:S(2)}) collective-permute-start(bf16[1024,256]{1,0:T(8,128)(2,1)} %slice.135), channel_id=1, source_target_pairs={{0,1},{1,2},{2,3},{3,0},{4,5},{5,6},{6,7},{7,4},{8,9},{9,10},{10,1... | collective-permute-start | bytes 1572872 | tf_op jit(solution)/shard_map/ppermute | solution.py:351
  233.8 86.3 %collective-permute-start.7 = (bf16[1024,256]{1,0:T(8,128)(2,1)}, bf16[1024,256]{1,0:T(8,128)(2,1)}, u32[]{:S(2)}, u32[]{:S(2)}) collective-permute-start(bf16[1024,256]{1,0:T(8,128)(2,1)} %slice.135), channel_id=1, source_target_pairs={{0,2},{1,3},{2,0},{3,1},{4,6},{5,7},{6,4},{7,5},{8,10},{9,11},{10,... | collective-permute-start | bytes 1572872 | tf_op jit(solution)/shard_map/ppermute | solution.py:351
  235.5 84.6 %collective-permute-start.8 = (bf16[1024,256]{1,0:T(8,128)(2,1)}, bf16[1024,256]{1,0:T(8,128)(2,1)}, u32[]{:S(2)}, u32[]{:S(2)}) collective-permute-start(bf16[1024,256]{1,0:T(8,128)(2,1)} %slice.135), channel_id=1, source_target_pairs={{0,3},{1,0},{2,1},{3,2},{4,7},{5,4},{6,5},{7,6},{8,11},{9,8},{10,9... | collective-permute-start | bytes 1572872 | tf_op jit(solution)/shard_map/ppermute | solution.py:351
  239.7 54.5 %collective-permute-start.11 = (f32[2,1024]{1,0:T(2,128)}, f32[2,1024]{1,0:T(2,128)}, u32[]{:S(2)}, u32[]{:S(2)}) collective-permute-start(f32[2,1024]{1,0:T(2,128)} %param.19), channel_id=1, source_target_pairs={{0,3},{1,0},{2,1},{3,2},{4,7},{5,4},{6,5},{7,6},{8,11},{9,8},{10,9... | collective-permute-start | bytes 24584 | tf_op jit(solution)/shard_map/ppermute | solution.py:351
  426.5 128.4 %reduce-scatter.5.cloned.1.call-start = ((), (), s32[]{:S(2)}) async-start(), calls=%async_computation.6 | async-start | bytes 1769472 | tf_op jit(solution)/shard_map/reduce_scatter | solution.py:487
  515.0 113.8 %reduce-scatter.11.cloned.1.call-start = ((), (), s32[]{:S(2)}) async-start(), calls=%async_computation.9 | async-start | bytes 9437184 | tf_op jit(solution)/shard_map/reduce_scatter | solution.py:456
  524.1 224.4 %reduce-scatter.9.cloned.1.call-start = ((), (), s32[]{:S(2)}) async-start(), calls=%async_computation.8 | async-start | bytes 18874368 | tf_op jit(solution)/shard_map/reduce_scatter | solution.py:460
  539.4 93.0 %collective-permute-start.31 = (f32[10,1024]{1,0:T(8,128)S(1)}, f32[10,1024]{1,0:T(8,128)S(1)}, u32[]{:S(2)}, u32[]{:S(2)}) collective-permute-start(f32[10,1024]{1,0:T(8,128)S(1)} %add.395), channel_id=1, source_target_pairs={{0,2},{1,3},{2,0},{3,1},{4,6},{5,7},{6,4},{7,5},{8,10},{9,11},{10,... | collective-permute-start | bytes 122888 | tf_op jit(solution)/shard_map/ppermute | solution.py:357
  545.5 205.5 %collective-permute-start.15 = (bf16[512,1024]{0,1:T(8,128)(2,1)}, bf16[512,1024]{0,1:T(8,128)(2,1)}, u32[]{:S(2)}, u32[]{:S(2)}) collective-permute-start(bf16[512,1024]{0,1:T(8,128)(2,1)} %convolution_convert_fusion.5), channel_id=1, source_target_pairs={{0,1},{1,2},{2,3},{3,0},{4,5},{5,6},{6,7},{7,4},{8,9},{9,10},{10,1... | collective-permute-start | bytes 3145736 | tf_op jit(solution)/shard_map/ppermute | solution.py:351
  554.3 55.5 %collective-permute-start.20 = (bf16[128,256]{1,0:T(8,128)(2,1)S(1)}, bf16[128,256]{1,0:T(8,128)(2,1)S(1)}, u32[]{:S(2)}, u32[]{:S(2)}) collective-permute-start(bf16[128,256]{1,0:T(8,128)(2,1)S(1)} %get-tuple-element.126), channel_id=1, source_target_pairs={{0,1},{1,2},{2,3},{3,0},{4,5},{5,6},{6,7},{7,4},{8,9},{9,10},{10,1... | collective-permute-start | bytes 196616 | tf_op jit(solution)/shard_map/ppermute | solution.py:351
  568.5 184.9 %collective-permute-start.16 = (bf16[512,1024]{0,1:T(8,128)(2,1)}, bf16[512,1024]{0,1:T(8,128)(2,1)}, u32[]{:S(2)}, u32[]{:S(2)}) collective-permute-start(bf16[512,1024]{0,1:T(8,128)(2,1)} %convolution_convert_fusion.4), channel_id=1, source_target_pairs={{0,2},{1,3},{2,0},{3,1},{4,6},{5,7},{6,4},{7,5},{8,10},{9,11},{10,... | collective-permute-start | bytes 3145736 | tf_op jit(solution)/shard_map/ppermute | solution.py:351
  574.7 180.2 %collective-permute-start.17 = (bf16[512,1024]{0,1:T(8,128)(2,1)}, bf16[512,1024]{0,1:T(8,128)(2,1)}, u32[]{:S(2)}, u32[]{:S(2)}) collective-permute-start(bf16[512,1024]{0,1:T(8,128)(2,1)} %convolution_convert_fusion.3), channel_id=1, source_target_pairs={{0,3},{1,0},{2,1},{3,2},{4,7},{5,4},{6,5},{7,6},{8,11},{9,8},{10,9... | collective-permute-start | bytes 3145736 | tf_op jit(solution)/shard_map/ppermute | solution.py:351
  630.9 125.6 %collective-permute-start.24 = (bf16[128,1024]{1,0:T(8,128)(2,1)}, bf16[128,1024]{1,0:T(8,128)(2,1)}, u32[]{:S(2)}, u32[]{:S(2)}) collective-permute-start(bf16[128,1024]{1,0:T(8,128)(2,1)} %get-tuple-element.110), channel_id=1, source_target_pairs={{0,1},{1,2},{2,3},{3,0},{4,5},{5,6},{6,7},{7,4},{8,9},{9,10},{10,1... | collective-permute-start | bytes 786440 | tf_op jit(solution)/shard_map/ppermute | solution.py:351
  636.5 119.0 %collective-permute-start.34 = (f32[1280]{0:T(1024)S(1)}, f32[1280]{0:T(1024)S(1)}, u32[]{:S(2)}, u32[]{:S(2)}) collective-permute-start(f32[1280]{0:T(1024)S(1)} %add.403), channel_id=1, source_target_pairs={{0,16},{4,20},{8,24},{12,28},{16,0},{20,4},{24,8},{28,12},{1,17},{... | collective-permute-start | bytes 15368 | tf_op jit(solution)/shard_map/ppermute | solution.py:357
  755.5 50.7 %collective-permute-start.22 = (bf16[2,128,1024]{2,1,0:T(8,128)(2,1)}, bf16[2,128,1024]{2,1,0:T(8,128)(2,1)}, u32[]{:S(2)}, u32[]{:S(2)}) collective-permute-start(bf16[2,128,1024]{2,1,0:T(8,128)(2,1)} %get-tuple-element.109), channel_id=1, source_target_pairs={{0,2},{1,3},{2,0},{3,1},{4,6},{5,7},{6,4},{7,5},{8,10},{9,11},{10,... | collective-permute-start | bytes 1572872 | tf_op jit(solution)/shard_map/ppermute | solution.py:351
  756.5 49.7 %collective-permute-start.23 = (bf16[2,128,1024]{2,1,0:T(8,128)(2,1)S(1)}, bf16[2,128,1024]{2,1,0:T(8,128)(2,1)}, u32[]{:S(2)}, u32[]{:S(2)}) collective-permute-start(bf16[2,128,1024]{2,1,0:T(8,128)(2,1)S(1)} %get-tuple-element.108), channel_id=1, source_target_pairs={{0,3},{1,0},{2,1},{3,2},{4,7},{5,4},{6,5},{7,6},{8,11},{9,8},{10,9... | collective-permute-start | bytes 1572872 | tf_op jit(solution)/shard_map/ppermute | solution.py:351
  (102 other events, 1976.5 us)
Sparse Core Ops, SparseCore 0:
  10.5 30.4 all-gather.2
  43.9 255.6 all-gather.4
  426.6 41.0 reduce-scatter.6
  515.2 38.8 reduce-scatter.4
  557.3 71.5 reduce-scatter.10
  632.3 116.1 reduce-scatter.8

commit v2 on v1

--- a/solution.py
+++ b/solution.py
@@ -24,41 +24,12 @@
 bf16 = jnp.bfloat16
 
 
-def rms_norm(vector):
-    return vector * lax.rsqrt(jnp.mean(vector * vector, axis=-1, keepdims=True) + norm_eps)
-
-
-def unit_norm(vector):
-    return vector * lax.rsqrt(jnp.sum(vector * vector, axis=-1, keepdims=True) + norm_eps)
-
-
-def sphere_mix(base, branch, rate):
-    return rms_norm(base + rate * (rms_norm(branch) - base))
-
-
 def starts_of(segment_row):
     indices = jnp.arange(segment_row.shape[0], dtype=jnp.int32)
     changed = jnp.concatenate(
         [jnp.ones((1,), dtype=jnp.bool_), segment_row[1:] != segment_row[:-1]]
     )
     return lax.cummax(jnp.where(changed, indices, jnp.zeros_like(indices)), axis=0)
-
-
-def rotary(vector, positions):
-    half_dim = vector.shape[-1] // 2
-    frequency = 10000.0 ** (-jnp.arange(half_dim, dtype=jnp.float32) / half_dim)
-    angles = positions.astype(jnp.float32)[:, None] * frequency[None, :]
-    cosine_table = jnp.cos(angles)[:, None, :]
-    sine_table = jnp.sin(angles)[:, None, :]
-    first_half = vector[..., :half_dim]
-    second_half = vector[..., half_dim:]
-    return jnp.concatenate(
-        [
-            first_half * cosine_table - second_half * sine_table,
-            second_half * cosine_table + first_half * sine_table,
-        ],
-        axis=-1,
-    )
 
 
 def adam_moved(weight, gradient, moment_one, moment_two):
@@ -239,60 +210,418 @@
     )(q, grads, k, v, out, log_sum, start)
 
 
-def feed_kernel(m_ref, w_ref, s_ref, up_ref, gate_ref, h_ref, out_ref):
+def partner(x):
+    width = x.shape[1]
+    lane = lax.broadcasted_iota(jnp.int32, x.shape, 1)
+    ahead = pltpu.roll(x, width - HEAD_DIM // 2, 1)
+    behind = pltpu.roll(x, HEAD_DIM // 2, 1)
+    return jnp.where(lax.rem(lane, HEAD_DIM) < HEAD_DIM // 2, ahead, behind)
+
+
+def head_sums(x):
+    width = x.shape[1]
+    row = lax.broadcasted_iota(jnp.int32, (width, width), 0) // HEAD_DIM
+    column = lax.broadcasted_iota(jnp.int32, (width, width), 1) // HEAD_DIM
+    same = jnp.where(row == column, 1.0, 0.0).astype(f32)
+    return lax.dot_general(
+        x,
+        same,
+        (((1,), (0,)), ((), ())),
+        precision=lax.Precision.HIGHEST,
+        preferred_element_type=f32,
+    )
+
+
+def widen(table, width):
+    return table if table.shape[1] == width else jnp.concatenate([table] * (width // 128), axis=1)
+
+
+def project_kernel(index_ref, x_ref, wq_ref, wk_ref, wv_ref, cos_ref, sin_ref, gain_ref, *refs):
+    q_ref, k_ref, v_ref, xq_ref, xk_ref = refs[-5:]
+    x = x_ref[...]
+    width = q_ref.shape[1]
+    cosine = widen(cos_ref[...], width)
+    sine = widen(sin_ref[...], width)
+    gain = gain_ref[...]
+    for w_ref, hat_ref, turned_ref in ((wq_ref, q_ref, xq_ref), (wk_ref, k_ref, xk_ref)):
+        raw = dot_nn(x, w_ref[...])
+        turned = raw * cosine + partner(raw) * sine
+        turned_ref[...] = turned
+        hat = turned * lax.rsqrt(head_sums(turned * turned) + norm_eps) * gain
+        hat_ref[...] = hat.astype(bf16)
+    v_ref[...] = dot_nn(x, wv_ref[...]).astype(bf16)
+
+
+def project(index, x, weights, cosine, sine, gain, length, previous):
+    rows, model = x.shape
+    width = gain.shape[1]
+    part = min(256, rows)
+    per = rows // part
+
+    def column(m):
+        return pl.BlockSpec((model, width), lambda i, at: (0, m))
+
+    table = pl.BlockSpec((part, 128), lambda i, at: (at[0] * per + i, 0))
+    out = pl.BlockSpec((part, width), lambda i, at: (at[0] * per + i, 0))
+    low = jax.ShapeDtypeStruct((length, width), bf16)
+    wide = jax.ShapeDtypeStruct((length, width), f32)
+    return pl.pallas_call(
+        project_kernel,
+        grid_spec=pltpu.PrefetchScalarGridSpec(
+            num_scalar_prefetch=1,
+            grid=(per,),
+            in_specs=[
+                pl.BlockSpec((part, model), lambda i, at: (i, 0)),
+                column(0),
+                column(1),
+                column(2),
+                table,
+                table,
+                pl.BlockSpec((1, width), lambda i, at: (0, 0)),
+            ]
+            + [pl.BlockSpec(memory_space=pl.ANY)] * len(previous),
+            out_specs=[out] * 5,
+        ),
+        out_shape=[low, low, low, wide, wide],
+        input_output_aliases={8 + i: i for i in range(len(previous))},
+        cost_estimate=pl.CostEstimate(
+            flops=6 * rows * model * width, bytes_accessed=8 * model * width, transcendentals=0
+        ),
+        name="project",
+    )(index, x, weights, weights, weights, cosine, sine, gain, *previous)
+
+
+def project_back_kernel(
+    index_ref,
+    dq_ref,
+    dk_ref,
+    dv_ref,
+    xq_ref,
+    xk_ref,
+    wq_ref,
+    wk_ref,
+    wv_ref,
+    cos_ref,
+    sin_ref,
+    gain_ref,
+    grad_ref,
+    piece_ref,
+    gain_grad_ref,
+):
     @pl.when(pl.program_id(0) == 0)
     def _():
-        out_ref[...] = jnp.zeros_like(out_ref)
-
+        gain_grad_ref[...] = jnp.zeros_like(gain_grad_ref)
+
+    width = dq_ref.shape[1]
+    cosine = widen(cos_ref[...], width)
+    sine = widen(sin_ref[...], width)
+    gain = gain_ref[...]
+    lows = []
+    for d_ref, x_ref in ((dq_ref, xq_ref), (dk_ref, xk_ref)):
+        turned = x_ref[...]
+        inverse = lax.rsqrt(head_sums(turned * turned) + norm_eps)
+        unit = turned * inverse
+        hat_grad = d_ref[...] * scale_factor
+        gain_grad_ref[...] += jnp.sum(hat_grad * unit, axis=0, keepdims=True)
+        unit_grad = hat_grad * gain
+        turned_grad = inverse * (unit_grad - unit * head_sums(unit * unit_grad))
+        raw_grad = turned_grad * cosine - partner(turned_grad) * sine
+        lows.append(raw_grad.astype(bf16))
+    lows.append(dv_ref[...].astype(bf16))
+    piece = jnp.zeros(piece_ref.shape, f32)
+    for m, w_ref in enumerate((wq_ref, wk_ref, wv_ref)):
+        grad_ref[:, m * width : (m + 1) * width] = lows[m]
+        piece = piece + dot_nt(lows[m], w_ref[...])
+    piece_ref[...] = piece.astype(bf16)
+
+
+def project_back(index, grads, turned, weights, cosine, sine, gain, rows):
+    length, width = grads[0].shape
+    model = weights.shape[0]
+    part = min(256, rows)
+    per = rows // part
+    blocks = length // part
+
+    def column(m):
+        return pl.BlockSpec((model, width), lambda i, at: (0, m))
+
+    def turn(i, at):
+        return (lax.rem(at[0] * per + i, blocks), 0)
+
+    tall = pl.BlockSpec((part, width), turn)
+    table = pl.BlockSpec((part, 128), turn)
+    return pl.pallas_call(
+        project_back_kernel,
+        grid_spec=pltpu.PrefetchScalarGridSpec(
+            num_scalar_prefetch=1,
+            grid=(blocks,),
+            in_specs=[tall] * 5
+            + [column(0), column(1), column(2), table, table]
+            + [pl.BlockSpec((1, width), lambda i, at: (0, 0))],
+            out_specs=[
+                pl.BlockSpec((part, 3 * width), lambda i, at: (i, 0)),
+                pl.BlockSpec((part, model), lambda i, at: (i, 0)),
+                pl.BlockSpec((1, width), lambda i, at: (0, 0)),
+            ],
+        ),
+        out_shape=[
+            jax.ShapeDtypeStruct((length, 3 * width), bf16),
+            jax.ShapeDtypeStruct((length, model), bf16),
+            jax.ShapeDtypeStruct((1, width), f32),
+        ],
+        cost_estimate=pl.CostEstimate(
+            flops=8 * length * model * width,
+            bytes_accessed=32 * length * width,
+            transcendentals=0,
+        ),
+        name="project_back",
+    )(index, *grads, *turned, weights, weights, weights, cosine, sine, gain)
+
+
+def projection_grads_kernel(count, *refs):
+    hidden, attended = refs[:count], refs[count : 2 * count]
+    grad_ref, branch_ref, out_ref = refs[2 * count :]
+    rows = branch_ref.shape[0]
+    width = attended[0].shape[1]
+    total = dot_tn(hidden[0][...], grad_ref[:rows, :])
+    for d in range(1, count):
+        total = total + dot_tn(hidden[d][...], grad_ref[d * rows : (d + 1) * rows, :])
+    out_ref[:, : 3 * width] = total.astype(bf16)
+    turned = branch_ref[...].T
+    for d in range(count):
+        out_ref[:, (3 + d) * width : (4 + d) * width] = dot_nn(turned, attended[d][...]).astype(
+            bf16
+        )
+
+
+def projection_grads(hidden, attended, qkv_grad, branch_grad):
+    count = len(hidden)
+    rows, model = branch_grad.shape
+    width = attended[0].shape[1]
+    part = 256
+    column = pl.BlockSpec((rows, part), lambda i: (0, i))
+
+    def whole(x):
+        return pl.BlockSpec(x.shape, lambda i: (0, 0))
+
+    return pl.pallas_call(
+        functools.partial(projection_grads_kernel, count),
+        grid=(model // part,),
+        in_specs=[column] * count + [whole(x) for x in attended] + [whole(qkv_grad), column],
+        out_specs=pl.BlockSpec((part, (3 + count) * width), lambda i: (i, 0)),
+        out_shape=jax.ShapeDtypeStruct((model, (3 + count) * width), bf16),
+        cost_estimate=pl.CostEstimate(
+            flops=8 * rows * count * model * width,
+            bytes_accessed=4 * rows * count * model,
+            transcendentals=0,
+        ),
+        name="projection_grads",
+    )(*hidden, *attended, qkv_grad, branch_grad)
+
+
+def rms_scale(x):
+    return lax.rsqrt(jnp.mean(x * x, axis=-1, keepdims=True) + norm_eps)
+
+
+def mix_kernel(count, *refs):
+    pieces, weights = refs[:count], refs[count : 2 * count]
+    hidden_ref, rates_ref, branch_ref, middle_ref, low_ref, turned_ref = refs[2 * count :]
+    branch = dot_nt(pieces[0][...], weights[0][...])
+    for d in range(1, count):
+        branch = branch + dot_nt(pieces[d][...], weights[d][...])
+    branch_ref[...] = branch
+    hidden = hidden_ref[...].astype(f32)
+    mixed = hidden + rates_ref[0:1, :] * (branch * rms_scale(branch) - hidden)
+    middle = mixed * rms_scale(mixed)
+    middle_ref[...] = middle
+    low_ref[...] = middle.astype(bf16)
+    turned_ref[...] = middle.T.astype(bf16)
+
+
+def mix(pieces, weights, hidden, rates):
+    count = len(pieces)
+    rows, model = hidden.shape
+    width = pieces[0].shape[1]
+    part = min(128, rows)
+
+    def column(d):
+        return pl.BlockSpec((model, width), lambda i: (0, 3 + d))
+
+    wide = pl.BlockSpec((part, model), lambda i: (i, 0))
+    return pl.pallas_call(
+        functools.partial(mix_kernel, count),
+        grid=(rows // part,),
+        in_specs=[pl.BlockSpec((part, width), lambda i: (i, 0))] * count
+        + [column(d) for d in range(count)]
+        + [wide, pl.BlockSpec((2, model), lambda i: (0, 0))],
+        out_specs=[wide, wide, wide, pl.BlockSpec((model, part), lambda i: (0, i))],
+        out_shape=[
+            jax.ShapeDtypeStruct((rows, model), f32),
+            jax.ShapeDtypeStruct((rows, model), f32),
+            jax.ShapeDtypeStruct((rows, model), bf16),
+            jax.ShapeDtypeStruct((model, rows), bf16),
+        ],
+        cost_estimate=pl.CostEstimate(
+            flops=2 * rows * model * model, bytes_accessed=14 * rows * model, transcendentals=0
+        ),
+        name="mix",
+    )(*pieces, *([weights] * count), hidden, rates)
+
+
+def block_of(w_ref):
+    value = w_ref[:, 0, 0]
+    return value.reshape(value.shape[0] * value.shape[1], value.shape[2])
+
+
+def feed_kernel(
+    m_ref,
+    wu_ref,
+    wg_ref,
+    wd_ref,
+    s_ref,
+    middle_ref,
+    cot_ref,
+    live_ref,
+    rates_ref,
+    up_ref,
+    gate_ref,
+    h_ref,
+    result_ref,
+    direct_ref,
+    low_ref,
+    turned_ref,
+    rate_ref,
+    acc,
+):
+    i = pl.program_id(0)
     tokens = m_ref[...]
-    up = dot_nn(tokens, w_ref[0, 0])
-    gate = dot_nn(tokens, w_ref[1, 0])
+    up = dot_nn(tokens, block_of(wu_ref))
+    gate = dot_nn(tokens, block_of(wg_ref))
     up_ref[...] = up
     gate_ref[...] = gate
     scaled = gate * s_ref[1:2, :]
     hidden = (up * s_ref[0:1, :] * (scaled * jax.nn.sigmoid(scaled))).astype(bf16)
     h_ref[...] = hidden
-    out_ref[...] += dot_nt(hidden, w_ref[2, 0])
-
-
-def feed(middle, weights, scales, step):
-    rows, model = middle.shape
-    _, groups, _, local_width = weights.shape
+    part_out = dot_nt(hidden, block_of(wd_ref))
+
+    @pl.when(i == 0)
+    def _():
+        acc[...] = part_out
+
+    @pl.when(i > 0)
+    def _():
+        acc[...] += part_out
+
+    @pl.when(i == pl.num_programs(0) - 1)
+    def _():
+        rate_ref[...] = jnp.zeros_like(rate_ref)
+        rate = rates_ref[1:2, :]
+        part = 32
+
+        def body(at, carry):
+            rows = pl.ds(pl.multiple_of(at * part, part), part)
+            out = acc[rows, :]
+            middle = middle_ref[rows, :]
+            out_scale = rms_scale(out)
+            unit = out * out_scale
+            mixed = middle + rate * (unit - middle)
+            scale = rms_scale(mixed)
+            final = mixed * scale
+            result_ref[rows, :] = final.astype(bf16)
+            grad = cot_ref[rows, :].astype(f32) * live_ref[rows, :]
+            mixed_grad = scale * (grad - final * jnp.mean(final * grad, axis=-1, keepdims=True))
+            direct_ref[rows, :] = mixed_grad * (1.0 - rate)
+            rate_ref[...] += jnp.sum(mixed_grad * (unit - middle), axis=0, keepdims=True)
+            unit_grad = mixed_grad * rate
+            out_grad = out_scale * (
+                unit_grad - unit * jnp.mean(unit * unit_grad, axis=-1, keepdims=True)
+            )
+            low_ref[rows, :] = out_grad.astype(bf16)
+            return carry
+
+        lax.fori_loop(0, acc.shape[0] // part, body, 0)
+        for at in range(acc.shape[0] // 128):
+            rows = slice(at * 128, (at + 1) * 128)
+            turned_ref[:, rows] = low_ref[rows, :].T
+
+
+def weight_specs(weights, step):
+    nd, _, _, shard, local_width = weights.shape
     per = local_width // step
-    total = groups * local_width
+
+    def spec(m):
+        return pl.BlockSpec((nd, 1, 1, shard, step), lambda i: (0, i // per, m, 0, i % per))
+
+    return [spec(0), spec(1), spec(2)]
+
+
+def feed(low, weights, scales, middle, cotangent, live, rates, step):
+    rows, model = low.shape
+    total = weights.shape[1] * weights.shape[4]
     columns = pl.BlockSpec((rows, step), lambda i: (0, i))
+    whole = pl.BlockSpec((rows, model), lambda i: (0, 0))
     return pl.pallas_call(
         feed_kernel,
         grid=(total // step,),
-        in_specs=[
-            pl.BlockSpec((rows, model), lambda i: (0, 0)),
-            pl.BlockSpec((3, 1, model, step), lambda i: (0, i // per, 0, i % per)),
+        in_specs=[whole]
+        + weight_specs(weights, step)
+        + [
             pl.BlockSpec((2, step), lambda i: (0, i)),
-        ],
-        out_specs=[columns, columns, columns, pl.BlockSpec((rows, model), lambda i: (0, 0))],
+            whole,
+            whole,
+            pl.BlockSpec((rows, 1), lambda i: (0, 0)),
+            pl.BlockSpec((2, model), lambda i: (0, 0)),
+        ],
+        out_specs=[columns, columns, columns, whole, whole, whole]
+        + [
+            pl.BlockSpec((model, rows), lambda i: (0, 0)),
+            pl.BlockSpec((1, model), lambda i: (0, 0)),
+        ],
         out_shape=[
             jax.ShapeDtypeStruct((rows, total), f32),
             jax.ShapeDtypeStruct((rows, total), f32),
             jax.ShapeDtypeStruct((rows, total), bf16),
+            jax.ShapeDtypeStruct((rows, model), bf16),
             jax.ShapeDtypeStruct((rows, model), f32),
-        ],
+            jax.ShapeDtypeStruct((rows, model), bf16),
+            jax.ShapeDtypeStruct((model, rows), bf16),
+            jax.ShapeDtypeStruct((1, model), f32),
+        ],
+        scratch_shapes=[pltpu.VMEM((rows, model), f32)],
         cost_estimate=pl.CostEstimate(
             flops=6 * rows * model * total,
             bytes_accessed=6 * model * total + 10 * rows * total,
             transcendentals=0,
         ),
         name="feed",
-    )(middle, weights, scales)
+    )(low, weights, weights, weights, scales, middle, cotangent, live, rates)
 
 
 def feed_back_kernel(
-    og_ref, mt_ref, w_ref, s_ref, up_ref, gate_ref, grad_ref, sg_ref, mg_ref
+    og_ref,
+    ogt_ref,
+    mt_ref,
+    wu_ref,
+    wg_ref,
+    wd_ref,
+    s_ref,
+    up_ref,
+    gate_ref,
+    h_ref,
+    direct_ref,
+    branch_ref,
+    hidden_ref,
+    rates_ref,
+    grad_ref,
+    sg_ref,
+    token_ref,
+    low_ref,
+    rate_ref,
+    acc,
 ):
-    @pl.when(pl.program_id(0) == 0)
-    def _():
-        mg_ref[...] = jnp.zeros_like(mg_ref)
-
-    hidden_grad = dot_nn(og_ref[...], w_ref[2, 0])
+    i = pl.program_id(0)
+    grad_ref[2] = dot_nn(ogt_ref[...], h_ref[...]).astype(bf16)
+    hidden_grad = dot_nn(og_ref[...], block_of(wd_ref))
     up = up_ref[...]
     gate = gate_ref[...]
     up_gain = s_ref[0:1, :]
@@ -308,43 +637,105 @@
     tokens_t = mt_ref[...]
     grad_ref[0] = dot_nn(tokens_t, up_low).astype(bf16)
     grad_ref[1] = dot_nn(tokens_t, gate_low).astype(bf16)
-    mg_ref[...] += dot_nt(up_low, w_ref[0, 0]) + dot_nt(gate_low, w_ref[1, 0])
-
-
-def feed_back(out_grad, middle_t, weights, scales, up, gate, step):
+    back = dot_nt(up_low, block_of(wu_ref)) + dot_nt(gate_low, block_of(wg_ref))
+
+    @pl.when(i == 0)
+    def _():
+        acc[...] = direct_ref[...] + back
+
+    @pl.when(i > 0)
+    def _():
+        acc[...] += back
+
+    @pl.when(i == pl.num_programs(0) - 1)
+    def _():
+        rate_ref[...] = jnp.zeros_like(rate_ref)
+        rate = rates_ref[0:1, :]
+        part = 32
+
+        def body(at, carry):
+            rows = pl.ds(pl.multiple_of(at * part, part), part)
+            grad = acc[rows, :]
+            branch = branch_ref[rows, :]
+            hidden = hidden_ref[rows, :].astype(f32)
+            branch_scale = rms_scale(branch)
+            unit = branch * branch_scale
+            mixed = hidden + rate * (unit - hidden)
+            scale = rms_scale(mixed)
+            middle = mixed * scale
+            mixed_grad = scale * (grad - middle * jnp.mean(middle * grad, axis=-1, keepdims=True))
+            token_ref[rows, :] = mixed_grad * (1.0 - rate)
+            rate_ref[...] += jnp.sum(mixed_grad * (unit - hidden), axis=0, keepdims=True)
+            unit_grad = mixed_grad * rate
+            branch_grad = branch_scale * (
+                unit_grad - unit * jnp.mean(unit * unit_grad, axis=-1, keepdims=True)
+            )
+            low_ref[rows, :] = branch_grad.astype(bf16)
+            return carry
+
+        lax.fori_loop(0, acc.shape[0] // part, body, 0)
+
+
+def feed_back(
+    out_grad, out_grad_t, middle_t, weights, scales, up, gate, hidden_units, direct, branch, hidden, rates, step
+):
     model, rows = middle_t.shape
-    _, groups, _, local_width = weights.shape
-    per = local_width // step
-    total = groups * local_width
+    total = weights.shape[1] * weights.shape[4]
     columns = pl.BlockSpec((rows, step), lambda i: (0, i))
+    whole = pl.BlockSpec((rows, model), lambda i: (0, 0))
+    turned = pl.BlockSpec((model, rows), lambda i: (0, 0))
     return pl.pallas_call(
         feed_back_kernel,
         grid=(total // step,),
-        in_specs=[
-            pl.BlockSpec((rows, model), lambda i: (0, 0)),
-            pl.BlockSpec((model, rows), lambda i: (0, 0)),
-            pl.BlockSpec((3, 1, model, step), lambda i: (0, i // per, 0, i % per)),
+        in_specs=[whole, turned, turned]
+        + weight_specs(weights, step)
+        + [
             pl.BlockSpec((2, step), lambda i: (0, i)),
             columns,
             columns,
+            columns,
+            whole,
+            whole,
+            whole,
+            pl.BlockSpec((2, model), lambda i: (0, 0)),
         ],
         out_specs=[
-            pl.BlockSpec((2, model, step), lambda i: (0, 0, i)),
+            pl.BlockSpec((3, model, step), lambda i: (0, 0, i)),
             pl.BlockSpec((2, step), lambda i: (0, i)),
-            pl.BlockSpec((rows, model), lambda i: (0, 0)),
+            whole,
+            whole,
+            pl.BlockSpec((1, model), lambda i: (0, 0)),
         ],
         out_shape=[
-            jax.ShapeDtypeStruct((2, model, total), bf16),
+            jax.ShapeDtypeStruct((3, model, total), bf16),
             jax.ShapeDtypeStruct((2, total), f32),
             jax.ShapeDtypeStruct((rows, model), f32),
-        ],
+            jax.ShapeDtypeStruct((rows, model), bf16),
+            jax.ShapeDtypeStruct((1, model), f32),
+        ],
+        scratch_shapes=[pltpu.VMEM((rows, model), f32)],
         cost_estimate=pl.CostEstimate(
-            flops=10 * rows * model * total,
-            bytes_accessed=10 * model * total + 8 * rows * total,
+            flops=12 * rows * model * total,
+            bytes_accessed=12 * model * total + 10 * rows * total,
             transcendentals=0,
         ),
         name="feed_back",
-    )(out_grad, middle_t, weights, scales, up, gate)
+    )(
+        out_grad,
+        out_grad_t,
+        middle_t,
+        weights,
+        weights,
+        weights,
+        scales,
+        up,
+        gate,
+        hidden_units,
+        direct,
+        branch,
+        hidden,
+        rates,
+    )
 
 
 def shift(value, axis, distance, size):
@@ -389,128 +780,134 @@
     shard = attn_weight.shape[1]
     heads_width = attn_weight.shape[2]
     hidden_width = mlp_weight.shape[2]
-    local_heads = heads_width // HEAD_DIM
     block = min(512, length)
     step = min(512, hidden_width)
     me = lax.axis_index("tensor")
 
+    def gather(value):
+        return [value] + [shift(value, "tensor", d, nt) for d in range(1, nt)]
+
     attn_low = attn_weight.astype(bf16)
-    attn_shard = jnp.concatenate([attn_low[0], attn_low[1], attn_low[2], attn_low[3]], axis=1)
+    attn_shard = jnp.concatenate(
+        [attn_low[0], attn_low[1], attn_low[2]] + gather(attn_low[3]), axis=1
+    )
     attn_full = lax.all_gather(attn_shard, "dp", axis=0, tiled=True)
-    mlp_low, attn_full = lax.optimization_barrier((mlp_weight.astype(bf16), attn_full))
-    mlp_full = lax.all_gather(mlp_low, ("tensor", "dp"), axis=1, tiled=True)
-    mlp_full = mlp_full.reshape(3, nt, model, hidden_width)
-    qkv_matrix = attn_full[:, : 3 * heads_width]
-    out_local = attn_full[:, 3 * heads_width :]
-
-    hidden_row = jnp.zeros((length, model), bf16)
-    hidden_row = put_block(hidden_row, hidden_in, me, 0)
-    for d in range(1, nt):
-        hidden_row = put_block(hidden_row, shift(hidden_in, "tensor", d, nt), (me - d) % nt, 0)
-    scales_row = jnp.zeros((2, nt * hidden_width), f32)
-    scales_row = put_block(scales_row, mlp_scales, me, 1)
-    for d in range(1, nt):
-        scales_row = put_block(scales_row, shift(mlp_scales, "tensor", d, nt), (me - d) % nt, 1)
-    out_matrix = jnp.concatenate(
-        [out_local] + [shift(out_local, "tensor", d, nt) for d in range(1, nt)], axis=1
-    )
-
-    projected = jnp.dot(hidden_row, qkv_matrix, preferred_element_type=f32)
+    mlp_low = mlp_weight.astype(bf16).reshape(3 * shard, hidden_width)
+    mlp_parts = gather(mlp_low)
+    scales_row = jnp.concatenate(gather(mlp_scales), axis=1)
+    hidden_in, mlp_parts = lax.optimization_barrier((hidden_in, mlp_parts))
+    mlp_full = lax.all_gather(jnp.concatenate(mlp_parts, axis=0), "dp", axis=0, tiled=True)
+    mlp_full = mlp_full.reshape(nd, nt, 3, shard, hidden_width)
+
     starts = starts_of(segments)
-    positions = jnp.arange(length, dtype=jnp.int32) - starts
-
-    def prepare_flat(raw, gain_flat):
-        rotated = rotary(raw.reshape(length, local_heads, HEAD_DIM), positions)
-        return (unit_norm(rotated) * gain_flat.reshape(local_heads, HEAD_DIM)).reshape(
-            length, heads_width
-        )
-
-    query_raw = projected[:, :heads_width]
-    key_raw = projected[:, heads_width : 2 * heads_width]
-    query_hat = prepare_flat(query_raw, qk_scale).astype(bf16)
-    key_hat = prepare_flat(key_raw, qk_scale).astype(bf16)
-    value_hat = projected[:, 2 * heads_width :].astype(bf16)
+    positions = (jnp.arange(length, dtype=jnp.int32) - starts).astype(f32)
+    lane = jnp.arange(128, dtype=jnp.int32)
+    half = HEAD_DIM // 2
+    frequency = 10000.0 ** (-(lane % half).astype(f32) / half)
+    sign = jnp.where(lane % HEAD_DIM < half, -1.0, 1.0)
+    angles = positions[:, None] * frequency[None, :]
+    cosine = jnp.cos(angles)
+    sine = jnp.sin(angles) * sign[None, :]
+    gain = qk_scale.reshape(1, heads_width)
+
+    hidden_parts = gather(hidden_in)
+    state = ()
+    for d in range(nt):
+        index = ((me + nt - d) % nt).reshape(1)
+        state = project(index, hidden_parts[d], attn_full, cosine, sine, gain, length, state)
+    query_hat, key_hat, value_hat, query_turned, key_turned = state
     attended_row, attended_f32, log_sum = attend(
         query_hat, key_hat, value_hat, starts[:, None], block
     )
-    attended = jnp.concatenate(
-        [take_block(attended_row, me, rows, 0)]
-        + [
-            shift(take_block(attended_row, (me + d) % nt, rows, 0), "tensor", d, nt)
-            for d in range(1, nt)
-        ],
-        axis=1,
-    )
-    branch = dot_nt(attended, out_matrix)
-    tokens = hidden_in.astype(f32)
-    middle = sphere_mix(tokens, branch, rates[0])
-    middle_low = middle.astype(bf16)
-    up, gate, hidden_units, mlp_out = feed(middle_low, mlp_full, scales_row, step)
-    result = sphere_mix(middle, mlp_out, rates[1])
+    attended = [take_block(attended_row, me, rows, 0)] + [
+        shift(take_block(attended_row, (me + d) % nt, rows, 0), "tensor", d, nt)
+        for d in range(1, nt)
+    ]
+    branch, middle, middle_low, middle_t = mix(attended, attn_full, hidden_in, rates)
     row_segments = take_block(segments, me, rows, 0)
-    upstream = cotangent.astype(f32) * (row_segments < pad_segment).astype(f32)[:, None]
-    _, mlp_pull = jax.vjp(sphere_mix, middle, mlp_out, rates[1])
-    middle_direct, mlp_out_grad, rate_mlp_grad = mlp_pull(upstream)
-    mlp_out_low = mlp_out_grad.astype(bf16)
-    down_grad = dot_tn(mlp_out_low, hidden_units).astype(bf16)
-    down_part = lax.psum_scatter(down_grad, "dp", scatter_dimension=0, tiled=True)
-    in_grad, scales_grad, middle_back = feed_back(
-        mlp_out_low, middle_low.T, mlp_full, scales_row, up, gate, step
-    )
-    in_part = lax.psum_scatter(in_grad, "dp", scatter_dimension=1, tiled=True)
-    _, attn_pull = jax.vjp(sphere_mix, tokens, branch, rates[0])
-    token_direct, branch_grad, rate_attn_grad = attn_pull(middle_direct + middle_back)
-    branch_low = branch_grad.astype(bf16)
-    attended_grad = dot_nn(branch_low, out_matrix).astype(bf16)
+    live = (row_segments < pad_segment).astype(f32)[:, None]
+    up, gate, hidden_units, result, middle_direct, mlp_out_low, mlp_out_t, rate_mlp_grad = feed(
+        middle_low, mlp_full, scales_row, middle, cotangent, live, rates, step
+    )
+    mlp_grad, scales_grad, token_direct, branch_low, rate_attn_grad = feed_back(
+        mlp_out_low,
+        mlp_out_t,
+        middle_t,
+        mlp_full,
+        scales_row,
+        up,
+        gate,
+        hidden_units,
+        middle_direct,
+        branch,
+        hidden_in,
+        rates,
+        step,
+    )
+    mlp_part = lax.psum_scatter(mlp_grad, "dp", scatter_dimension=1, tiled=True)
+
+    def out_block(d):
+        return attn_full[:, (3 + d) * heads_width : (4 + d) * heads_width]
+
     grad_row = jnp.zeros((length, heads_width), bf16)
-    grad_row = put_block(grad_row, attended_grad[:, :heads_width], me, 0)
-    for d in range(1, nt):
-        piece = attended_grad[:, d * heads_width : (d + 1) * heads_width]
-        grad_row = put_block(grad_row, shift(piece, "tensor", -d, nt), (me + d) % nt, 0)
-    out_grad = dot_tn(branch_low, attended).astype(bf16)
-    out_part = lax.psum_scatter(out_grad, "dp", scatter_dimension=0, tiled=True)
-
-    query_hat_grad, key_hat_grad, value_grad = attend_back(
+    for d in list(range(1, nt)) + [0]:
+        piece = dot_nn(branch_low, out_block(d)).astype(bf16)
+        piece = shift(piece, "tensor", -d, nt) if d else piece
+        grad_row = put_block(grad_row, piece, (me + d) % nt, 0)
+    head_grads = attend_back(
         query_hat, key_hat, value_hat, grad_row, attended_f32, log_sum, starts[None, :], block
     )
-    _, query_pull = jax.vjp(prepare_flat, query_raw, qk_scale)
-    query_raw_grad, gain_query = query_pull(query_hat_grad * scale_factor)
-    _, key_pull = jax.vjp(prepare_flat, key_raw, qk_scale)
-    key_raw_grad, gain_key = key_pull(key_hat_grad * scale_factor)
-    qkv_grad = jnp.concatenate([query_raw_grad, key_raw_grad, value_grad], axis=1).astype(bf16)
-    total = token_direct + dot_nt(take_block(qkv_grad, me, rows, 0), qkv_matrix)
-    for d in range(1, nt):
-        piece = dot_nt(take_block(qkv_grad, (me + d) % nt, rows, 0), qkv_matrix).astype(bf16)
-        total = total + shift(piece, "tensor", d, nt).astype(f32)
+    qkv_grad, pieces, gain_grad = project_back(
+        me.reshape(1),
+        head_grads,
+        (query_turned, key_turned),
+        attn_full,
+        cosine,
+        sine,
+        gain,
+        rows,
+    )
+    arrived = [
+        shift(pieces[d * rows : (d + 1) * rows], "tensor", d, nt) for d in range(1, nt)
+    ]
+    total = token_direct + pieces[:rows].astype(f32)
+    for piece in arrived:
+        total = total + piece.astype(f32)
     input_grad = total.astype(bf16)
-    qkv_weight_grad = dot_tn(hidden_row, qkv_grad).astype(bf16)
-    qkv_part = lax.psum_scatter(qkv_weight_grad, "dp", scatter_dimension=0, tiled=True)
+    hidden_turn = [hidden_parts[(nt - d) % nt] for d in range(nt)]
+    attn_grad = projection_grads(hidden_turn, attended, qkv_grad, branch_low)
+    attn_part = lax.psum_scatter(attn_grad, "dp", scatter_dimension=0, tiled=True)
 
     def own_sum(part, axis, width):
-        total = take_block(part, me, width, axis).astype(f32)
+        total = lax.slice_in_dim(part, 0, width, axis=axis).astype(f32)
         for d in range(1, nt):
-            piece = take_block(part, (me + d) % nt, width, axis)
-            total = total + shift(piece, "tensor", d, nt).astype(f32)
+            piece = lax.slice_in_dim(part, d * width, (d + 1) * width, axis=axis)
+            total = total + shift(piece, "tensor", -d, nt).astype(f32)
         return total
 
-    out_own = out_part[:, :heads_width].astype(f32)
-    for d in range(1, nt):
-        piece = out_part[:, d * heads_width : (d + 1) * heads_width]
-        out_own = out_own + shift(piece, "tensor", -d, nt).astype(f32)
-    down_own = own_sum(down_part, 1, hidden_width)
-    in_own = own_sum(in_part, 2, hidden_width)
+    mlp_part, arrived = lax.optimization_barrier((mlp_part, arrived))
+    mlp_weight_grad = own_sum(mlp_part, 2, hidden_width)
+    attn_part, mlp_weight_grad = lax.optimization_barrier((attn_part, mlp_weight_grad))
+    out_own = own_sum(attn_part[:, 3 * heads_width :], 1, heads_width)
     attn_weight_grad = jnp.stack(
         [
-            qkv_part[:, :heads_width].astype(f32),
-            qkv_part[:, heads_width : 2 * heads_width].astype(f32),
-            qkv_part[:, 2 * heads_width :].astype(f32),
+            attn_part[:, :heads_width].astype(f32),
+            attn_part[:, heads_width : 2 * heads_width].astype(f32),
+            attn_part[:, 2 * heads_width : 3 * heads_width].astype(f32),
             out_own,
         ]
     )
-    mlp_weight_grad = jnp.concatenate([in_own, down_own[None]], axis=0)
-
-    rates_part = jnp.stack([rate_attn_grad, rate_mlp_grad])
-    small = jnp.concatenate([rates_part, scales_grad.reshape(-1, model)], axis=0)
+
+    def spread(value):
+        width = value.shape[1] // nt
+        whole = jnp.zeros_like(value)
+        for d in range(nt):
+            piece = value[:, d * width : (d + 1) * width]
+            whole = put_block(whole, piece, (me + nt - d) % nt, 1)
+        return whole
+
+    scales_grad = spread(scales_grad).reshape(-1, model)
+    small = jnp.concatenate([rate_attn_grad, rate_mlp_grad, scales_grad], axis=0)
     (small,) = butterfly([small], "dp", nd)
     (small,) = butterfly([small], "tensor", nt)
     rates_grad = small[:2]
@@ -524,15 +921,11 @@
     )
     attn_square = jnp.sum(attn_moved * attn_moved, axis=1, keepdims=True)
     mlp_square = jnp.sum(mlp_moved * mlp_moved, axis=1, keepdims=True)
-    gain = gain_query + gain_key
     (mlp_square,) = butterfly([mlp_square], "dp", nd)
-    last = jnp.concatenate([attn_square.reshape(-1), gain])
+    last = jnp.concatenate([attn_square.reshape(1, -1), gain_grad], axis=1)
     (last,) = butterfly([last], "dp", nd)
-    attn_square = last[: 4 * heads_width].reshape(4, 1, heads_width)
-    gain = last[4 * heads_width :]
-    gain_row = put_block(jnp.zeros((nt * heads_width,), f32), gain, me, 0)
-    for d in range(1, nt):
-        gain_row = put_block(gain_row, shift(gain, "tensor", d, nt), (me - d) % nt, 0)
+    attn_square = last[:, : 4 * heads_width].reshape(4, 1, heads_width)
+    gain_row = spread(jnp.concatenate(gather(last[:, 4 * heads_width :]), axis=1)).reshape(-1)
     attn_new = attn_moved * lax.rsqrt(attn_square + norm_eps)
     mlp_new = mlp_moved * lax.rsqrt(mlp_square + norm_eps)
     return (

time: 847 us -> 656 us (0.77)
  waiting for transfers between devices: 390 us -> 258 us
  Pallas kernels: 114 us -> 203 us
  starting transfers between devices: 163 us -> 121 us
  local copies, waits for them, and re-layouts: 59.9 us -> 20.4 us
  matrix products: 39.7 us -> 6.21 us
  other arithmetic: 57.6 us -> 28.3 us
    reduce_scatter x4 -> x2, waiting for transfers between devices: 128 us -> 0.02 us  [the longest x1 0.02 us: local(): mlp_part = lax.psum_scatter(mlp_grad, 'dp', scatter_dimension=1, tiled=True)]
    pallas_call x2 -> x9, Pallas kernels: 53 us -> 141 us  [the longest x1 48.3 us: feed_back(): pl.pallas_call(feed_back_kernel, grid=(total // step,), in_specs=[whole,...]
    ppermute x30, starting transfers between devices: 150 us -> 109 us  [shift(): lax.ppermute(value, axis, [(i, (i + distance) % size) for i in range(size)])]
    ppermute x11, waiting for transfers between devices: 10.8 us -> 49.1 us  [butterfly(): lax.ppermute(v, axis, [(i, i ^ step) for i in range(size)])]
    dot_general x9 -> x0, matrix products: 36.9 us -> none  [the longest x3 19.4 us: dot_tn(): lax.dot_general(a, b, (((0,), (0,)), ((), ())), preferred_element_type=f32)]
    all_gather x1, waiting for transfers between devices: 30.7 us -> 0.01 us  [local(): attn_full = lax.all_gather(attn_shard, 'dp', axis=0, tiled=True)]
    reduce_sum x10 -> x0, other arithmetic: 24 us -> none  [the longest x2 8.41 us: sphere_mix(): return rms_norm(base + rate * (rms_norm(branch) - base))]
    mul x5 -> x0, local copies, waits for them, and re-layouts: 11.6 us -> none  [the longest x2 6.03 us: unit_norm(): vector * lax.rsqrt(jnp.sum(vector * vector, axis=-1, keepdims=True) + nor...]
  transfers between devices with their start and end apart: 47 -> 45, of which waited for: 22 -> 24; matrix products, arithmetic and copies ran while one was open for 14% -> 7% of each run, Pallas kernels for 7% -> 19%
where the time goes in v2:
time: 656 us; the launch traced here: 651 us
  waiting for transfers between devices  258 us (39%)
  Pallas kernels  203 us (31%)
  starting transfers between devices  121 us (18%)
  other arithmetic  28.3 us (4%)
  local copies, waits for them, and re-layouts  20.4 us (3%)
  between operations  14.6 us (2%)
    ppermute x30, waiting for transfers between devices, shift(): lax.ppermute(value, axis, [(i, (i + distance) % size) for i in range(size)])  209 us
    ppermute x30, starting transfers between devices, shift(): lax.ppermute(value, axis, [(i, (i + distance) % size) for i in range(size)])  109 us
    ppermute x11, waiting for transfers between devices, butterfly(): lax.ppermute(v, axis, [(i, i ^ step) for i in range(size)])  49.1 us
    pallas_call x1, Pallas kernels, feed_back(): pl.pallas_call(feed_back_kernel, grid=(total // step,), in_specs=[whole,...  48.3 us
    pallas_call x1, Pallas kernels, attend_back(): pl.pallas_call(functools.partial(attend_back_kernel, heads, block, block)...  41.4 us
    pallas_call x1, Pallas kernels, feed(): pl.pallas_call(feed_kernel, grid=(total // step,), in_specs=[whole] + wei...  33.2 us
    pallas_call x4, Pallas kernels, project(): pl.pallas_call(project_kernel, grid_spec=pltpu.PrefetchScalarGridSpec(num...  21.7 us
    pallas_call x1, Pallas kernels, project_back(): pl.pallas_call(project_back_kernel, grid_spec=pltpu.PrefetchScalarGridSpe...  20.8 us
  transfers between devices with their start and end apart: 45, of which 24 were waited for; matrix products, arithmetic and copies ran while one was open for 7% of the time, Pallas kernels for 19%

profile of v2, /device:TPU:0, one launch (start us, length us, event | category | flops | bytes accessed | tf_op | source)
XLA Modules:
  0.0 651.5 jit_solution(770134197237320255)
XLA Ops:
  23.9 18.3 %collective-permute-done = bf16[384,1024]{1,0:T(8,128)(2,1)S(1)} collective-permute-done((bf16[384,1024]{1,0:T(8,128)(2,1)S(1)}, bf16[384,1024]{1,0:T(8,128)(2,1)S(1)}, u32[]{:S(2)}, u32[]{:S(2)}) %collective-permute-start) | collective-permute-done | bytes 786464 | tf_op jit(solution)/shard_map/ppermute | solution.py:742
  42.2 32.3 %collective-permute-done.1 = bf16[384,1024]{1,0:T(8,128)(2,1)S(1)} collective-permute-done((bf16[384,1024]{1,0:T(8,128)(2,1)S(1)}, bf16[384,1024]{1,0:T(8,128)(2,1)S(1)}, u32[]{:S(2)}, u32[]{:S(2)}) %collective-permute-start.1) | collective-permute-done | bytes 786464 | tf_op jit(solution)/shard_map/ppermute | solution.py:742
  77.1 17.3 %collective-permute-start.12 = (f32[2,1024]{1,0:T(2,128)S(1)}, f32[2,1024]{1,0:T(2,128)S(1)}, u32[]{:S(2)}, u32[]{:S(2)}) collective-permute-start(f32[2,1024]{1,0:T(2,128)S(1)} %copy-done.25), channel_id=1, source_target_pairs={{0,1},{1,2},{2,3},{3,0},{4,5},{5,6},{6,7},{7,4},{8,9},{9,10},{10,1... | collective-permute-start | bytes 24584 | tf_op jit(solution)/shard_map/ppermute | solution.py:742
  103.4 5.6 fusion.2
  114.4 9.4 %collective-permute-done.8.x_ref.refs_3_ = bf16[512,1024]{1,0:T(8,128)(2,1)S(1)} collective-permute-done((bf16[512,1024]{1,0:T(8,128)(2,1)S(1)}, bf16[512,1024]{1,0:T(8,128)(2,1)S(1)}, u32[]{:S(2)}, u32[]{:S(2)}) %collective-permute-start.8) | collective-permute-done | bytes 1048608 | tf_op jit(solution)/shard_map/ppermute | solution.py:742
  130.2 36.6 %collective-permute-done.7.x_ref.refs_2_ = bf16[512,1024]{1,0:T(8,128)(2,1)S(1)} collective-permute-done((bf16[512,1024]{1,0:T(8,128)(2,1)S(1)}, bf16[512,1024]{1,0:T(8,128)(2,1)S(1)}, u32[]{:S(2)}, u32[]{:S(2)}) %collective-permute-start.7) | collective-permute-done | bytes 1048608 | tf_op jit(solution)/shard_map/ppermute | solution.py:742
  173.2 5.5 project.7
  178.7 20.3 %attend.1 = (bf16[2048,256]{1,0:T(8,128)(2,1)}, f32[2048,256]{1,0:T(8,128)}, f32[4,2048]{1,0:T(4,128)}) custom-call(bf16[2048,256]{1,0:T(8,128)(2,1)} %get-tuple-element.83.q_ref, bf16[2048,256]{1,0:T(8,128)(2,1)} %get-tuple-element.84.k_ref, bf16[2048,256]{1,0:T(8,128)(2,1)} %get-tuple-element.85.v_ref, s32[2048,1]{1,0:T(8,128)} %copy.40.start_ref), custom_call_target="tpu_custom_call" | custom-call | flops 20000000000 | bytes 4194304 | tf_op jit(solution)/shard_map/attend/pallas_call | solution.py:113
  200.9 14.9 %collective-permute-start.10 = (bf16[512,256]{1,0:T(8,128)(2,1)S(1)}, bf16[512,256]{1,0:T(8,128)(2,1)S(1)}, u32[]{:S(2)}, u32[]{:S(2)}) collective-permute-start(bf16[512,256]{1,0:T(8,128)(2,1)S(1)} %get-tuple-element.139), channel_id=1, source_target_pairs={{0,2},{1,3},{2,0},{3,1},{4,6},{5,7},{6,4},{7,5},{8,10},{9,11},{10,... | collective-permute-start | bytes 786440 | tf_op jit(solution)/shard_map/ppermute | solution.py:742
  215.8 9.5 %collective-permute-start.11 = (bf16[512,256]{1,0:T(8,128)(2,1)S(1)}, bf16[512,256]{1,0:T(8,128)(2,1)S(1)}, u32[]{:S(2)}, u32[]{:S(2)}) collective-permute-start(bf16[512,256]{1,0:T(8,128)(2,1)S(1)} %get-tuple-element.138), channel_id=1, source_target_pairs={{0,3},{1,0},{2,1},{3,2},{4,7},{5,4},{6,5},{7,6},{8,11},{9,8},{10,9... | collective-permute-start | bytes 786440 | tf_op jit(solution)/shard_map/ppermute | solution.py:742
  226.1 5.9 collective-permute-done.11.refs_3_.refs_7_
  232.0 9.5 %collective-permute-done.9.refs_1_.refs_5_ = bf16[512,256]{1,0:T(8,128)(2,1)S(1)} collective-permute-done((bf16[512,256]{1,0:T(8,128)(2,1)S(1)}, bf16[512,256]{1,0:T(8,128)(2,1)S(1)}, u32[]{:S(2)}, u32[]{:S(2)}) %collective-permute-start.9) | collective-permute-done | bytes 262176 | tf_op jit(solution)/shard_map/ppermute | solution.py:742
  242.3 7.7 %mix.1 = (f32[512,1024]{1,0:T(8,128)}, f32[512,1024]{1,0:T(8,128)}, bf16[512,1024]{1,0:T(8,128)(2,1)}, bf16[1024,512]{1,0:T(8,128)(2,1)}) custom-call(bf16[512,256]{1,0:T(8,128)(2,1)} %get-tuple-element.141.refs_0_.refs_4_, bf16[512,256]{1,0:T(8,128)(2,1)} %copy-done.18, bf16[512,256]{1,0:T(8,128)(2,1)} %copy-done.16, bf16[512,256]{1,0:T(8,128)(2,1)} %copy-done.17, ...), custom_call_target="tpu_custom_call" | custom-call | flops 1073741824 | bytes 7340032 | tf_op jit(solution)/shard_map/mix/pallas_call | solution.py:451
  250.0 33.2 %feed.1 = (f32[512,4096]{1,0:T(8,128)}, f32[512,4096]{1,0:T(8,128)}, bf16[512,4096]{1,0:T(8,128)(2,1)}, bf16[512,1024]{1,0:T(8,128)(2,1)}, f32[512,1024]{1,0:T(8...) custom-call(bf16[512,1024]{1,0:T(8,128)(2,1)} %get-tuple-element.87.m_ref, ...), custom_call_target="tpu_custom_call" | custom-call | flops 12884901888 | bytes 46137344 | tf_op jit(solution)/shard_map/feed/pallas_call | solution.py:563
  283.2 48.3 %feed_back.1 = (bf16[3,1024,4096]{2,1,0:T(8,128)(2,1)}, f32[2,4096]{1,0:T(2,128)}, f32[512,1024]{1,0:T(8,128)}, bf16[512,1024]{1,0:T(8,128)(2,1)}, f32[1,1024]{1,0:T(1,128)}) custom-call(bf16[512,1024]{1,0:T(8,128)(2,1)} %get-tuple-element.94.og_ref, bf16[1024,512]{1,0:T(8,128)(2,1)} %get-tuple-element.95.ogt_ref, ...), custom_call_target="tpu_custom_call" | custom-call | flops 25769803776 | bytes 71303168 | tf_op jit(solution)/shard_map/feed_back/pallas_call | solution.py:687
  341.6 7.6 %collective-permute-done.15 = bf16[512,256]{1,0:T(8,128)(2,1)S(1)} collective-permute-done((bf16[512,256]{1,0:T(8,128)(2,1)S(1)}, bf16[512,256]{1,0:T(8,128)(2,1)S(1)}, u32[]{:S(2)}, u32[]{:S(2)}) %collective-permute-start.15) | collective-permute-done | bytes 262176 | tf_op jit(solution)/shard_map/ppermute | solution.py:742
  357.5 41.4 %attend_back.1 = (f32[2048,256]{1,0:T(8,128)}, f32[2048,256]{1,0:T(8,128)}, f32[2048,256]{1,0:T(8,128)}) custom-call(bf16[2048,256]{1,0:T(8,128)(2,1)} %get-tuple-element.83.q_ref, bf16[2048,256]{1,0:T(8,128)(2,1)} %copy-done.12, bf16[2048,256]{1,0:T(8,128)(2,1)} %get-tuple-element.84.k_ref, bf16[2048,256]{1,0:T(8,128)(2,1)} %get-tuple-element.85.v_ref, ...), custom_call_target="tpu_custom_call" | custom-call | flops 40000000000 | bytes 10485760 | tf_op jit(solution)/shard_map/attend_back/pallas_call | solution.py:191
  398.9 20.8 %project_back.1 = (bf16[2048,768]{1,0:T(8,128)(2,1)}, bf16[2048,1024]{1,0:T(8,128)(2,1)}, f32[1,256]{1,0:T(1,128)}) custom-call(s32[1]{0:T(128)} %bitcast.15.index_ref, f32[2048,256]{1,0:T(8,128)} %get-tuple-element.106.dq_ref, f32[2048,256]{1,0:T(8,128)} %get-tuple-element.107.dk_ref, f32[2048,256]{1,0:T(8,128)} %get-tuple-element.108.dv_ref, ...), custom_call_target="tpu_custom_call" | custom-call | flops 4294967296 | bytes 16777216 | tf_op jit(solution)/shard_map/project_back/pallas_call | solution.py:353
  419.7 9.4 %projection_grads.1 = bf16[1024,1792]{1,0:T(8,128)(2,1)} custom-call(bf16[512,1024]{1,0:T(8,128)(2,1)} %refs_0_, bf16[512,1024]{1,0:T(8,128)(2,1)} %collective-permute-done.3.x_ref.refs_1_, bf16[512,1024]{1,0:T(8,128)(2,1)} %copy-done.6, bf16[512,1024]{1,0:T(8,128)(2,1)} %copy-done.5, bf16[512,256]{1,0:T(8,128)(2,1)} %get-tuple-element.141.refs_0_.refs_4_, ...), custom_call_target="tpu_custom_call" | custom-call | flops 4294967296 | bytes 8388608 | tf_op jit(solution)/shard_map/projection_grads/pallas_call | solution.py:407
  442.0 21.1 %collective-permute-done.18 = bf16[512,1024]{1,0:T(8,128)(2,1)S(1)} collective-permute-done((bf16[512,1024]{1,0:T(8,128)(2,1)}, bf16[512,1024]{1,0:T(8,128)(2,1)S(1)}, u32[]{:S(2)}, u32[]{:S(2)}) %collective-permute-start.18) | collective-permute-done | bytes 1048608 | tf_op jit(solution)/shard_map/ppermute | solution.py:742
  463.2 43.6 %collective-permute-done.19 = bf16[512,1024]{1,0:T(8,128)(2,1)S(1)} collective-permute-done((bf16[512,1024]{1,0:T(8,128)(2,1)}, bf16[512,1024]{1,0:T(8,128)(2,1)S(1)}, u32[]{:S(2)}, u32[]{:S(2)}) %collective-permute-start.19) | collective-permute-done | bytes 1048608 | tf_op jit(solution)/shard_map/ppermute | solution.py:742
  510.6 25.7 %collective-permute-start.21 = (bf16[3,128,1024]{2,1,0:T(8,128)(2,1)}, bf16[3,128,1024]{2,1,0:T(8,128)(2,1)S(1)}, u32[]{:S(2)}, u32[]{:S(2)}) collective-permute-start(bf16[3,128,1024]{2,1,0:T(8,128)(2,1)} %get-tuple-element.135), channel_id=1, source_target_pairs={{0,3},{1,0},{2,1},{3,2},{4,7},{5,4},{6,5},{7,6},{8,11},{9,8},{10,9... | collective-permute-start | bytes 2359304 | tf_op jit(solution)/shard_map/ppermute | solution.py:742
  550.2 37.4 %collective-permute-done.30 = f32[10,1024]{1,0:T(8,128)S(1)} collective-permute-done((f32[10,1024]{1,0:T(8,128)S(1)}, f32[10,1024]{1,0:T(8,128)S(1)}, u32[]{:S(2)}, u32[]{:S(2)}) %collective-permute-start.30) | collective-permute-done | bytes 40992 | tf_op jit(solution)/shard_map/ppermute | solution.py:748
  589.7 15.3 %collective-permute-done.22 = bf16[3,128,1024]{2,1,0:T(8,128)(2,1)S(1)} collective-permute-done((bf16[3,128,1024]{2,1,0:T(8,128)(2,1)}, bf16[3,128,1024]{2,1,0:T(8,128)(2,1)S(1)}, u32[]{:S(2)}, u32[]{:S(2)}) %collective-permute-start.22) | collective-permute-done | bytes 786464 | tf_op jit(solution)/shard_map/ppermute | solution.py:742
  (217 shorter events, 140.2 us)
Async XLA Ops:
  7.2 101.8 %all-gather.3.cloned.1.call-start = ((), (), s32[]{:S(2)}) async-start(), calls=%async_computation.2 | async-start | bytes 4128768 | tf_op jit(solution)/shard_map/all_gather | solution.py:794
  19.6 230.4 %all-gather.5.cloned.1.call-start = ((), (), s32[]{:S(2)}) async-start(), calls=%async_computation.3 | async-start | bytes 28311552 | tf_op jit(solution)/shard_map/all_gather | solution.py:799
  19.8 22.4 %collective-permute-start = (bf16[384,1024]{1,0:T(8,128)(2,1)S(1)}, bf16[384,1024]{1,0:T(8,128)(2,1)S(1)}, u32[]{:S(2)}, u32[]{:S(2)}) collective-permute-start(bf16[384,1024]{1,0:T(8,128)(2,1)S(1)} %bitcast.67), channel_id=1, source_target_pairs={{0,1},{1,2},{2,3},{3,0},{4,5},{5,6},{6,7},{7,4},{8,9},{9,10},{10,1... | collective-permute-start | bytes 2359304 | tf_op jit(solution)/shard_map/ppermute | solution.py:742
  21.5 53.1 %collective-permute-start.1 = (bf16[384,1024]{1,0:T(8,128)(2,1)S(1)}, bf16[384,1024]{1,0:T(8,128)(2,1)S(1)}, u32[]{:S(2)}, u32[]{:S(2)}) collective-permute-start(bf16[384,1024]{1,0:T(8,128)(2,1)S(1)} %bitcast.68), channel_id=1, source_target_pairs={{0,2},{1,3},{2,0},{3,1},{4,6},{5,7},{6,4},{7,5},{8,10},{9,11},{10,... | collective-permute-start | bytes 2359304 | tf_op jit(solution)/shard_map/ppermute | solution.py:742
  23.5 51.1 %collective-permute-start.2 = (bf16[384,1024]{1,0:T(8,128)(2,1)S(1)}, bf16[384,1024]{1,0:T(8,128)(2,1)S(1)}, u32[]{:S(2)}, u32[]{:S(2)}) collective-permute-start(bf16[384,1024]{1,0:T(8,128)(2,1)S(1)} %bitcast.69), channel_id=1, source_target_pairs={{0,3},{1,0},{2,1},{3,2},{4,7},{5,4},{6,5},{7,6},{8,11},{9,8},{10,9... | collective-permute-start | bytes 2359304 | tf_op jit(solution)/shard_map/ppermute | solution.py:742
  76.5 430.3 %reduce-scatter.5.cloned.1.call-start = ((), (), s32[]{:S(2)}) async-start(), calls=%async_computation.5 | async-start | bytes 28311552 | tf_op jit(solution)/shard_map/reduce_scatter | solution.py:847
  77.1 148.2 %collective-permute-start.12 = (f32[2,1024]{1,0:T(2,128)S(1)}, f32[2,1024]{1,0:T(2,128)S(1)}, u32[]{:S(2)}, u32[]{:S(2)}) collective-permute-start(f32[2,1024]{1,0:T(2,128)S(1)} %copy-done.25), channel_id=1, source_target_pairs={{0,1},{1,2},{2,3},{3,0},{4,5},{5,6},{6,7},{7,4},{8,9},{9,10},{10,1... | collective-permute-start | bytes 24584 | tf_op jit(solution)/shard_map/ppermute | solution.py:742
  94.4 131.6 %collective-permute-start.13 = (f32[2,1024]{1,0:T(2,128)S(1)}, f32[2,1024]{1,0:T(2,128)S(1)}, u32[]{:S(2)}, u32[]{:S(2)}) collective-permute-start(f32[2,1024]{1,0:T(2,128)S(1)} %copy-done.25), channel_id=1, source_target_pairs={{0,2},{1,3},{2,0},{3,1},{4,6},{5,7},{6,4},{7,5},{8,10},{9,11},{10,... | collective-permute-start | bytes 24584 | tf_op jit(solution)/shard_map/ppermute | solution.py:742
  95.8 28.0 %collective-permute-start.8 = (bf16[512,1024]{1,0:T(8,128)(2,1)S(1)}, bf16[512,1024]{1,0:T(8,128)(2,1)S(1)}, u32[]{:S(2)}, u32[]{:S(2)}) collective-permute-start(bf16[512,1024]{1,0:T(8,128)(2,1)S(1)} %copy-done), channel_id=1, source_target_pairs={{0,1},{1,2},{2,3},{3,0},{4,5},{5,6},{6,7},{7,4},{8,9},{9,10},{10,1... | collective-permute-start | bytes 3145736 | tf_op jit(solution)/shard_map/ppermute | solution.py:742
  95.9 70.9 %collective-permute-start.7 = (bf16[512,1024]{1,0:T(8,128)(2,1)S(1)}, bf16[512,1024]{1,0:T(8,128)(2,1)S(1)}, u32[]{:S(2)}, u32[]{:S(2)}) collective-permute-start(bf16[512,1024]{1,0:T(8,128)(2,1)S(1)} %copy-done), channel_id=1, source_target_pairs={{0,2},{1,3},{2,0},{3,1},{4,6},{5,7},{6,4},{7,5},{8,10},{9,11},{10,... | collective-permute-start | bytes 3145736 | tf_op jit(solution)/shard_map/ppermute | solution.py:742
  99.6 73.6 %collective-permute-start.3 = (bf16[512,1024]{1,0:T(8,128)(2,1)S(1)}, bf16[512,1024]{1,0:T(8,128)(2,1)}, u32[]{:S(2)}, u32[]{:S(2)}) collective-permute-start(bf16[512,1024]{1,0:T(8,128)(2,1)S(1)} %copy-done), channel_id=1, source_target_pairs={{0,3},{1,0},{2,1},{3,2},{4,7},{5,4},{6,5},{7,6},{8,11},{9,8},{10,9... | collective-permute-start | bytes 3145736 | tf_op jit(solution)/shard_map/ppermute | solution.py:742
  123.8 102.2 %collective-permute-start.14 = (f32[2,1024]{1,0:T(2,128)S(1)}, f32[2,1024]{1,0:T(2,128)S(1)}, u32[]{:S(2)}, u32[]{:S(2)}) collective-permute-start(f32[2,1024]{1,0:T(2,128)S(1)} %copy-done.25), channel_id=1, source_target_pairs={{0,3},{1,0},{2,1},{3,2},{4,7},{5,4},{6,5},{7,6},{8,11},{9,8},{10,9... | collective-permute-start | bytes 24584 | tf_op jit(solution)/shard_map/ppermute | solution.py:742
  200.9 25.2 %collective-permute-start.10 = (bf16[512,256]{1,0:T(8,128)(2,1)S(1)}, bf16[512,256]{1,0:T(8,128)(2,1)S(1)}, u32[]{:S(2)}, u32[]{:S(2)}) collective-permute-start(bf16[512,256]{1,0:T(8,128)(2,1)S(1)} %get-tuple-element.139), channel_id=1, source_target_pairs={{0,2},{1,3},{2,0},{3,1},{4,6},{5,7},{6,4},{7,5},{8,10},{9,11},{10,... | collective-permute-start | bytes 786440 | tf_op jit(solution)/shard_map/ppermute | solution.py:742
  215.8 16.2 %collective-permute-start.11 = (bf16[512,256]{1,0:T(8,128)(2,1)S(1)}, bf16[512,256]{1,0:T(8,128)(2,1)S(1)}, u32[]{:S(2)}, u32[]{:S(2)}) collective-permute-start(bf16[512,256]{1,0:T(8,128)(2,1)S(1)} %get-tuple-element.138), channel_id=1, source_target_pairs={{0,3},{1,0},{2,1},{3,2},{4,7},{5,4},{6,5},{7,6},{8,11},{9,8},{10,9... | collective-permute-start | bytes 786440 | tf_op jit(solution)/shard_map/ppermute | solution.py:742
  225.3 16.2 %collective-permute-start.9 = (bf16[512,256]{1,0:T(8,128)(2,1)S(1)}, bf16[512,256]{1,0:T(8,128)(2,1)S(1)}, u32[]{:S(2)}, u32[]{:S(2)}) collective-permute-start(bf16[512,256]{1,0:T(8,128)(2,1)S(1)} %get-tuple-element.140), channel_id=1, source_target_pairs={{0,1},{1,2},{2,3},{3,0},{4,5},{5,6},{6,7},{7,4},{8,9},{9,10},{10,1... | collective-permute-start | bytes 786440 | tf_op jit(solution)/shard_map/ppermute | solution.py:742
  331.6 276.4 %reduce-scatter.3.cloned.1.call-start = ((), (), s32[]{:S(2)}) async-start(), calls=%async_computation.4 | async-start | bytes 4128768 | tf_op jit(solution)/shard_map/reduce_scatter | solution.py:879
  432.7 30.5 %collective-permute-start.18 = (bf16[512,1024]{1,0:T(8,128)(2,1)}, bf16[512,1024]{1,0:T(8,128)(2,1)S(1)}, u32[]{:S(2)}, u32[]{:S(2)}) collective-permute-start(bf16[512,1024]{1,0:T(8,128)(2,1)} %get-tuple-element.132), channel_id=1, source_target_pairs={{0,1},{1,2},{2,3},{3,0},{4,5},{5,6},{6,7},{7,4},{8,9},{9,10},{10,1... | collective-permute-start | bytes 3145736 | tf_op jit(solution)/shard_map/ppermute | solution.py:742
  437.9 68.8 %collective-permute-start.19 = (bf16[512,1024]{1,0:T(8,128)(2,1)}, bf16[512,1024]{1,0:T(8,128)(2,1)S(1)}, u32[]{:S(2)}, u32[]{:S(2)}) collective-permute-start(bf16[512,1024]{1,0:T(8,128)(2,1)} %get-tuple-element.134), channel_id=1, source_target_pairs={{0,2},{1,3},{2,0},{3,1},{4,6},{5,7},{6,4},{7,5},{8,10},{9,11},{10,... | collective-permute-start | bytes 3145736 | tf_op jit(solution)/shard_map/ppermute | solution.py:742
  439.4 67.4 %collective-permute-start.20 = (bf16[512,1024]{1,0:T(8,128)(2,1)}, bf16[512,1024]{1,0:T(8,128)(2,1)S(1)}, u32[]{:S(2)}, u32[]{:S(2)}) collective-permute-start(bf16[512,1024]{1,0:T(8,128)(2,1)} %get-tuple-element.133), channel_id=1, source_target_pairs={{0,3},{1,0},{2,1},{3,2},{4,7},{5,4},{6,5},{7,6},{8,11},{9,8},{10,9... | collective-permute-start | bytes 3145736 | tf_op jit(solution)/shard_map/ppermute | solution.py:742
  510.6 79.1 %collective-permute-start.21 = (bf16[3,128,1024]{2,1,0:T(8,128)(2,1)}, bf16[3,128,1024]{2,1,0:T(8,128)(2,1)S(1)}, u32[]{:S(2)}, u32[]{:S(2)}) collective-permute-start(bf16[3,128,1024]{2,1,0:T(8,128)(2,1)} %get-tuple-element.135), channel_id=1, source_target_pairs={{0,3},{1,0},{2,1},{3,2},{4,7},{5,4},{6,5},{7,6},{8,11},{9,8},{10,9... | collective-permute-start | bytes 2359304 | tf_op jit(solution)/shard_map/ppermute | solution.py:742
  536.3 68.7 %collective-permute-start.22 = (bf16[3,128,1024]{2,1,0:T(8,128)(2,1)}, bf16[3,128,1024]{2,1,0:T(8,128)(2,1)S(1)}, u32[]{:S(2)}, u32[]{:S(2)}) collective-permute-start(bf16[3,128,1024]{2,1,0:T(8,128)(2,1)} %get-tuple-element.137), channel_id=1, source_target_pairs={{0,2},{1,3},{2,0},{3,1},{4,6},{5,7},{6,4},{7,5},{8,10},{9,11},{10,... | collective-permute-start | bytes 2359304 | tf_op jit(solution)/shard_map/ppermute | solution.py:742
  536.3 68.7 %collective-permute-start.23 = (bf16[3,128,1024]{2,1,0:T(8,128)(2,1)}, bf16[3,128,1024]{2,1,0:T(8,128)(2,1)}, u32[]{:S(2)}, u32[]{:S(2)}) collective-permute-start(bf16[3,128,1024]{2,1,0:T(8,128)(2,1)} %get-tuple-element.136), channel_id=1, source_target_pairs={{0,1},{1,2},{2,3},{3,0},{4,5},{5,6},{6,7},{7,4},{8,9},{9,10},{10,1... | collective-permute-start | bytes 2359304 | tf_op jit(solution)/shard_map/ppermute | solution.py:742
  547.3 40.3 %collective-permute-start.30 = (f32[10,1024]{1,0:T(8,128)S(1)}, f32[10,1024]{1,0:T(8,128)S(1)}, u32[]{:S(2)}, u32[]{:S(2)}) collective-permute-start(f32[10,1024]{1,0:T(8,128)S(1)} %add.259), channel_id=1, source_target_pairs={{0,1},{1,0},{2,3},{3,2},{4,5},{5,4},{6,7},{7,6},{8,9},{9,8},{10,11... | collective-permute-start | bytes 122888 | tf_op jit(solution)/shard_map/ppermute | solution.py:748
  588.2 31.1 %collective-permute-start.31 = (f32[10,1024]{1,0:T(8,128)}, f32[10,1024]{1,0:T(8,128)}, u32[]{:S(2)}, u32[]{:S(2)}) collective-permute-start(f32[10,1024]{1,0:T(8,128)} %add.260), channel_id=1, source_target_pairs={{0,2},{1,3},{2,0},{3,1},{4,6},{5,7},{6,4},{7,5},{8,10},{9,11},{10,... | collective-permute-start | bytes 122888 | tf_op jit(solution)/shard_map/ppermute | solution.py:748
  (50 other events, 580.9 us)
Sparse Core Ops, SparseCore 0:
  19.8 35.0 all-gather.2
  76.6 140.0 all-gather.4
  331.8 155.8 reduce-scatter.4
  490.9 48.5 reduce-scatter.2

commit v3 on v2

--- a/solution.py
+++ b/solution.py
@@ -379,44 +379,64 @@
 
 
 def projection_grads_kernel(count, *refs):
-    hidden, attended = refs[:count], refs[count : 2 * count]
-    grad_ref, branch_ref, out_ref = refs[2 * count :]
-    rows = branch_ref.shape[0]
-    width = attended[0].shape[1]
+    hidden = refs[:count]
+    grad_ref, out_ref = refs[count:]
+    rows = hidden[0].shape[0]
     total = dot_tn(hidden[0][...], grad_ref[:rows, :])
     for d in range(1, count):
         total = total + dot_tn(hidden[d][...], grad_ref[d * rows : (d + 1) * rows, :])
-    out_ref[:, : 3 * width] = total.astype(bf16)
+    out_ref[...] = total.astype(bf16)
+
+
+def projection_grads(hidden, qkv_grad):
+    count = len(hidden)
+    rows, model = hidden[0].shape
+    width = qkv_grad.shape[1]
+    part = 256
+    column = pl.BlockSpec((rows, part), lambda i: (0, i))
+    return pl.pallas_call(
+        functools.partial(projection_grads_kernel, count),
+        grid=(model // part,),
+        in_specs=[column] * count + [pl.BlockSpec(qkv_grad.shape, lambda i: (0, 0))],
+        out_specs=pl.BlockSpec((part, width), lambda i: (i, 0)),
+        out_shape=jax.ShapeDtypeStruct((model, width), bf16),
+        cost_estimate=pl.CostEstimate(
+            flops=2 * rows * count * model * width,
+            bytes_accessed=4 * rows * count * model,
+            transcendentals=0,
+        ),
+        name="projection_grads",
+    )(*hidden, qkv_grad)
+
+
+def out_grads_kernel(count, *refs):
+    attended = refs[:count]
+    branch_ref, out_ref = refs[count:]
+    width = attended[0].shape[1]
     turned = branch_ref[...].T
     for d in range(count):
-        out_ref[:, (3 + d) * width : (4 + d) * width] = dot_nn(turned, attended[d][...]).astype(
-            bf16
-        )
-
-
-def projection_grads(hidden, attended, qkv_grad, branch_grad):
-    count = len(hidden)
+        out_ref[:, d * width : (d + 1) * width] = dot_nn(turned, attended[d][...]).astype(bf16)
+
+
+def out_grads(attended, branch_grad):
+    count = len(attended)
     rows, model = branch_grad.shape
     width = attended[0].shape[1]
     part = 256
-    column = pl.BlockSpec((rows, part), lambda i: (0, i))
-
-    def whole(x):
-        return pl.BlockSpec(x.shape, lambda i: (0, 0))
-
     return pl.pallas_call(
-        functools.partial(projection_grads_kernel, count),
+        functools.partial(out_grads_kernel, count),
         grid=(model // part,),
-        in_specs=[column] * count + [whole(x) for x in attended] + [whole(qkv_grad), column],
-        out_specs=pl.BlockSpec((part, (3 + count) * width), lambda i: (i, 0)),
-        out_shape=jax.ShapeDtypeStruct((model, (3 + count) * width), bf16),
+        in_specs=[pl.BlockSpec(x.shape, lambda i: (0, 0)) for x in attended]
+        + [pl.BlockSpec((rows, part), lambda i: (0, i))],
+        out_specs=pl.BlockSpec((part, count * width), lambda i: (i, 0)),
+        out_shape=jax.ShapeDtypeStruct((model, count * width), bf16),
         cost_estimate=pl.CostEstimate(
-            flops=8 * rows * count * model * width,
+            flops=2 * rows * count * model * width,
             bytes_accessed=4 * rows * count * model,
             transcendentals=0,
         ),
-        name="projection_grads",
-    )(*hidden, *attended, qkv_grad, branch_grad)
+        name="out_grads",
+    )(*attended, branch_grad)
 
 
 def rms_scale(x):
@@ -545,12 +565,14 @@
             turned_ref[:, rows] = low_ref[rows, :].T
 
 
-def weight_specs(weights, step):
+def weight_specs(weights, step, base=0):
     nd, _, _, shard, local_width = weights.shape
     per = local_width // step
 
     def spec(m):
-        return pl.BlockSpec((nd, 1, 1, shard, step), lambda i: (0, i // per, m, 0, i % per))
+        return pl.BlockSpec(
+            (nd, 1, 1, shard, step), lambda i: (0, (i + base) // per, m, 0, (i + base) % per)
+        )
 
     return [spec(0), spec(1), spec(2)]
 
@@ -597,27 +619,8 @@
     )(low, weights, weights, weights, scales, middle, cotangent, live, rates)
 
 
-def feed_back_kernel(
-    og_ref,
-    ogt_ref,
-    mt_ref,
-    wu_ref,
-    wg_ref,
-    wd_ref,
-    s_ref,
-    up_ref,
-    gate_ref,
-    h_ref,
-    direct_ref,
-    branch_ref,
-    hidden_ref,
-    rates_ref,
-    grad_ref,
-    sg_ref,
-    token_ref,
-    low_ref,
-    rate_ref,
-    acc,
+def feed_back_step(
+    og_ref, ogt_ref, mt_ref, wu_ref, wg_ref, wd_ref, s_ref, up_ref, gate_ref, h_ref, start_ref, grad_ref, sg_ref, acc
 ):
     i = pl.program_id(0)
     grad_ref[2] = dot_nn(ogt_ref[...], h_ref[...]).astype(bf16)
@@ -641,13 +644,23 @@
 
     @pl.when(i == 0)
     def _():
-        acc[...] = direct_ref[...] + back
+        acc[...] = start_ref[...] + back
 
     @pl.when(i > 0)
     def _():
         acc[...] += back
 
-    @pl.when(i == pl.num_programs(0) - 1)
+
+def feed_back_first_kernel(*refs):
+    feed_back_step(*refs)
+
+
+def feed_back_last_kernel(*refs):
+    branch_ref, hidden_ref, rates_ref = refs[11:14]
+    grad_ref, sg_ref, token_ref, low_ref, rate_ref, acc = refs[14:]
+    feed_back_step(*refs[:11], grad_ref, sg_ref, acc)
+
+    @pl.when(pl.program_id(0) == pl.num_programs(0) - 1)
     def _():
         rate_ref[...] = jnp.zeros_like(rate_ref)
         rate = rates_ref[0:1, :]
@@ -677,49 +690,49 @@
 
 
 def feed_back(
-    out_grad, out_grad_t, middle_t, weights, scales, up, gate, hidden_units, direct, branch, hidden, rates, step
+    out_grad, out_grad_t, middle_t, weights, scales, up, gate, hidden_units, start, mixing, step, base, count
 ):
     model, rows = middle_t.shape
-    total = weights.shape[1] * weights.shape[4]
-    columns = pl.BlockSpec((rows, step), lambda i: (0, i))
+    width = count * step
+    columns = pl.BlockSpec((rows, step), lambda i: (0, i + base))
     whole = pl.BlockSpec((rows, model), lambda i: (0, 0))
     turned = pl.BlockSpec((model, rows), lambda i: (0, 0))
+    wide = jax.ShapeDtypeStruct((rows, model), f32)
+    grads_specs = [
+        pl.BlockSpec((3, model, step), lambda i: (0, 0, i)),
+        pl.BlockSpec((2, step), lambda i: (0, i)),
+    ]
+    grads_shapes = [
+        jax.ShapeDtypeStruct((3, model, width), bf16),
+        jax.ShapeDtypeStruct((2, width), f32),
+    ]
+    last = bool(mixing)
     return pl.pallas_call(
-        feed_back_kernel,
-        grid=(total // step,),
+        feed_back_last_kernel if last else feed_back_first_kernel,
+        grid=(count,),
         in_specs=[whole, turned, turned]
-        + weight_specs(weights, step)
-        + [
-            pl.BlockSpec((2, step), lambda i: (0, i)),
-            columns,
-            columns,
-            columns,
-            whole,
-            whole,
-            whole,
-            pl.BlockSpec((2, model), lambda i: (0, 0)),
-        ],
-        out_specs=[
-            pl.BlockSpec((3, model, step), lambda i: (0, 0, i)),
-            pl.BlockSpec((2, step), lambda i: (0, i)),
-            whole,
-            whole,
-            pl.BlockSpec((1, model), lambda i: (0, 0)),
-        ],
-        out_shape=[
-            jax.ShapeDtypeStruct((3, model, total), bf16),
-            jax.ShapeDtypeStruct((2, total), f32),
-            jax.ShapeDtypeStruct((rows, model), f32),
-            jax.ShapeDtypeStruct((rows, model), bf16),
-            jax.ShapeDtypeStruct((1, model), f32),
-        ],
-        scratch_shapes=[pltpu.VMEM((rows, model), f32)],
+        + weight_specs(weights, step, base)
+        + [pl.BlockSpec((2, step), lambda i: (0, i + base)), columns, columns, columns, whole]
+        + ([whole, whole, pl.BlockSpec((2, model), lambda i: (0, 0))] if last else []),
+        out_specs=grads_specs
+        + ([whole, whole, pl.BlockSpec((1, model), lambda i: (0, 0))] if last else [whole]),
+        out_shape=grads_shapes
+        + (
+            [
+                wide,
+                jax.ShapeDtypeStruct((rows, model), bf16),
+                jax.ShapeDtypeStruct((1, model), f32),
+            ]
+            if last
+            else [wide]
+        ),
+        scratch_shapes=[pltpu.VMEM((rows, model), f32)] if last else [],
         cost_estimate=pl.CostEstimate(
-            flops=12 * rows * model * total,
-            bytes_accessed=12 * model * total + 10 * rows * total,
+            flops=12 * rows * model * width,
+            bytes_accessed=12 * model * width + 10 * rows * width,
             transcendentals=0,
         ),
-        name="feed_back",
+        name="feed_back_last" if last else "feed_back_first",
     )(
         out_grad,
         out_grad_t,
@@ -731,15 +744,34 @@
         up,
         gate,
         hidden_units,
-        direct,
-        branch,
-        hidden,
-        rates,
+        start,
+        *mixing,
     )
 
 
 def shift(value, axis, distance, size):
     return lax.ppermute(value, axis, [(i, (i + distance) % size) for i in range(size)])
+
+
+def carry_on(up, down, hop, axis, size):
+    up = lax.ppermute(up, axis, [(i, i + 1) for i in range(hop - 1, size - 1)])
+    down = lax.ppermute(down, axis, [(i, i - 1) for i in range(1, size - hop + 1)])
+    return up, down
+
+
+def line_sum(pieces, axis, size, second, other):
+    up = down = None
+    for hop in range(1, size):
+        if hop == 2:
+            up, down, second = lax.optimization_barrier((up, down, second))
+        if hop == size - 1 and hop > 2:
+            up, down, other = lax.optimization_barrier((up, down, other))
+        ahead, behind = pieces[size - hop], pieces[hop]
+        ahead = ahead if up is None else ahead + up
+        behind = behind if down is None else behind + down
+        up = lax.ppermute(ahead, axis, [(i, i + 1) for i in range(hop)])
+        down = lax.ppermute(behind, axis, [(i, i - 1) for i in range(size - hop, size)])
+    return up, down, second, other
 
 
 def butterfly(values, axis, size):
@@ -787,16 +819,31 @@
     def gather(value):
         return [value] + [shift(value, "tensor", d, nt) for d in range(1, nt)]
 
+    def line(value):
+        ups, downs = [value], [value]
+        for hop in range(1, nt):
+            up, down = carry_on(ups[-1], downs[-1], hop, "tensor", nt)
+            ups.append(up)
+            downs.append(down)
+        return ups, downs
+
+    def join(ups, downs, d):
+        return ups[0] if d == 0 else jnp.where(me >= d, ups[d], downs[nt - d])
+
     attn_low = attn_weight.astype(bf16)
     attn_shard = jnp.concatenate(
         [attn_low[0], attn_low[1], attn_low[2]] + gather(attn_low[3]), axis=1
     )
     attn_full = lax.all_gather(attn_shard, "dp", axis=0, tiled=True)
-    mlp_low = mlp_weight.astype(bf16).reshape(3 * shard, hidden_width)
-    mlp_parts = gather(mlp_low)
     scales_row = jnp.concatenate(gather(mlp_scales), axis=1)
-    hidden_in, mlp_parts = lax.optimization_barrier((hidden_in, mlp_parts))
-    mlp_full = lax.all_gather(jnp.concatenate(mlp_parts, axis=0), "dp", axis=0, tiled=True)
+    ups, downs = line(mlp_weight.astype(bf16).reshape(3 * shard, hidden_width))
+    before = max(1, nt - 2)
+    hidden_in, ups[before], downs[before] = lax.optimization_barrier(
+        (hidden_in, ups[before], downs[before])
+    )
+    mlp_full = lax.all_gather(
+        jnp.concatenate([join(ups, downs, d) for d in range(nt)], axis=0), "dp", axis=0, tiled=True
+    )
     mlp_full = mlp_full.reshape(nd, nt, 3, shard, hidden_width)
 
     starts = starts_of(segments)
@@ -810,9 +857,10 @@
     sine = jnp.sin(angles) * sign[None, :]
     gain = qk_scale.reshape(1, heads_width)
 
-    hidden_parts = gather(hidden_in)
+    ups, downs = line(hidden_in)
+    hidden_parts = [join(ups, downs, d) for d in range(nt)]
     state = ()
-    for d in range(nt):
+    for d in sorted(range(nt), key=lambda d: max(d, nt - d) if d else 0):
         index = ((me + nt - d) % nt).reshape(1)
         state = project(index, hidden_parts[d], attn_full, cosine, sine, gain, length, state)
     query_hat, key_hat, value_hat, query_turned, key_turned = state
@@ -829,22 +877,18 @@
     up, gate, hidden_units, result, middle_direct, mlp_out_low, mlp_out_t, rate_mlp_grad = feed(
         middle_low, mlp_full, scales_row, middle, cotangent, live, rates, step
     )
-    mlp_grad, scales_grad, token_direct, branch_low, rate_attn_grad = feed_back(
-        mlp_out_low,
-        mlp_out_t,
-        middle_t,
-        mlp_full,
-        scales_row,
-        up,
-        gate,
-        hidden_units,
-        middle_direct,
-        branch,
-        hidden_in,
-        rates,
-        step,
-    )
-    mlp_part = lax.psum_scatter(mlp_grad, "dp", scatter_dimension=1, tiled=True)
+    blocks = nt * hidden_width // step
+    half = blocks // 2
+    feed_args = (mlp_out_low, mlp_out_t, middle_t, mlp_full, scales_row, up, gate, hidden_units)
+    far_grad, far_scales, partial = feed_back(
+        *feed_args, middle_direct, (), step, half, blocks - half
+    )
+    far_part = lax.psum_scatter(far_grad, "dp", scatter_dimension=1, tiled=True)
+    near_grad, near_scales, token_direct, branch_low, rate_attn_grad = feed_back(
+        *feed_args, partial, (branch, hidden_in, rates), step, 0, half
+    )
+    near_part = lax.psum_scatter(near_grad, "dp", scatter_dimension=1, tiled=True)
+    scales_grad = jnp.concatenate([near_scales, far_scales], axis=1)
 
     def out_block(d):
         return attn_full[:, (3 + d) * heads_width : (4 + d) * heads_width]
@@ -854,9 +898,14 @@
         piece = dot_nn(branch_low, out_block(d)).astype(bf16)
         piece = shift(piece, "tensor", -d, nt) if d else piece
         grad_row = put_block(grad_row, piece, (me + d) % nt, 0)
+    out_grad = out_grads(attended, branch_low)
+    small = jnp.concatenate([rate_attn_grad, rate_mlp_grad], axis=0)
+    small, grad_row = lax.optimization_barrier((small, grad_row))
     head_grads = attend_back(
         query_hat, key_hat, value_hat, grad_row, attended_f32, log_sum, starts[None, :], block
     )
+    head_grads, far_part, out_grad = lax.optimization_barrier((head_grads, far_part, out_grad))
+    out_part = lax.psum_scatter(out_grad, "dp", scatter_dimension=0, tiled=True)
     qkv_grad, pieces, gain_grad = project_back(
         me.reshape(1),
         head_grads,
@@ -867,36 +916,28 @@
         gain,
         rows,
     )
-    arrived = [
-        shift(pieces[d * rows : (d + 1) * rows], "tensor", d, nt) for d in range(1, nt)
-    ]
-    total = token_direct + pieces[:rows].astype(f32)
-    for piece in arrived:
-        total = total + piece.astype(f32)
+    pieces = [pieces[d * rows : (d + 1) * rows] for d in range(nt)]
+    hidden_turn = [hidden_parts[(nt - d) % nt] for d in range(nt)]
+    qkv_grad = projection_grads(hidden_turn, qkv_grad)
+    total = token_direct + pieces[0].astype(f32)
+    from_below, from_above, qkv_grad, near_part = line_sum(
+        pieces, "tensor", nt, qkv_grad, near_part
+    )
+    qkv_part = lax.psum_scatter(qkv_grad, "dp", scatter_dimension=0, tiled=True)
+    total = total + from_below.astype(f32) + from_above.astype(f32)
     input_grad = total.astype(bf16)
-    hidden_turn = [hidden_parts[(nt - d) % nt] for d in range(nt)]
-    attn_grad = projection_grads(hidden_turn, attended, qkv_grad, branch_low)
-    attn_part = lax.psum_scatter(attn_grad, "dp", scatter_dimension=0, tiled=True)
-
-    def own_sum(part, axis, width):
-        total = lax.slice_in_dim(part, 0, width, axis=axis).astype(f32)
-        for d in range(1, nt):
-            piece = lax.slice_in_dim(part, d * width, (d + 1) * width, axis=axis)
-            total = total + shift(piece, "tensor", -d, nt).astype(f32)
-        return total
-
-    mlp_part, arrived = lax.optimization_barrier((mlp_part, arrived))
-    mlp_weight_grad = own_sum(mlp_part, 2, hidden_width)
-    attn_part, mlp_weight_grad = lax.optimization_barrier((attn_part, mlp_weight_grad))
-    out_own = own_sum(attn_part[:, 3 * heads_width :], 1, heads_width)
-    attn_weight_grad = jnp.stack(
-        [
-            attn_part[:, :heads_width].astype(f32),
-            attn_part[:, heads_width : 2 * heads_width].astype(f32),
-            attn_part[:, 2 * heads_width : 3 * heads_width].astype(f32),
-            out_own,
+
+    def sent(part, axis, width, first):
+        count = part.shape[axis] // width
+        pieces = [lax.slice_in_dim(part, d * width, (d + 1) * width, axis=axis) for d in range(count)]
+        return [
+            (shift(piece, "tensor", -(d + first), nt) if d + first else piece).astype(f32)
+            for d, piece in enumerate(pieces)
         ]
-    )
+
+    out_own = sum(sent(out_part, 1, heads_width, 0))
+    split = half * step // hidden_width
+    mlp_weight_grad = sum(sent(near_part, 2, hidden_width, 0) + sent(far_part, 2, hidden_width, split))
 
     def spread(value):
         width = value.shape[1] // nt
@@ -907,25 +948,44 @@
         return whole
 
     scales_grad = spread(scales_grad).reshape(-1, model)
-    small = jnp.concatenate([rate_attn_grad, rate_mlp_grad, scales_grad], axis=0)
+    small = jnp.concatenate([small, scales_grad], axis=0)
     (small,) = butterfly([small], "dp", nd)
     (small,) = butterfly([small], "tensor", nt)
     rates_grad = small[:2]
     mlp_scales_grad = small[2:].reshape(2, nt * hidden_width)
 
-    attn_one, attn_two, attn_moved = adam_moved(
-        attn_weight, attn_weight_grad, attn_moment_one, attn_moment_two
-    )
-    mlp_one, mlp_two, mlp_moved = adam_moved(
+    def adam(weight, gradient, one, two):
+        one, two, moved = adam_moved(weight, gradient, one, two)
+        return one, two, moved, jnp.sum(moved * moved, axis=1, keepdims=True)
+
+    mlp_one, mlp_two, mlp_moved, mlp_square = adam(
         mlp_weight, mlp_weight_grad, mlp_moment_one, mlp_moment_two
     )
-    attn_square = jnp.sum(attn_moved * attn_moved, axis=1, keepdims=True)
-    mlp_square = jnp.sum(mlp_moved * mlp_moved, axis=1, keepdims=True)
-    (mlp_square,) = butterfly([mlp_square], "dp", nd)
-    last = jnp.concatenate([attn_square.reshape(1, -1), gain_grad], axis=1)
-    (last,) = butterfly([last], "dp", nd)
-    attn_square = last[:, : 4 * heads_width].reshape(4, 1, heads_width)
-    gain_row = spread(jnp.concatenate(gather(last[:, 4 * heads_width :]), axis=1)).reshape(-1)
+    out_one, out_two, out_moved, out_square = adam(
+        attn_weight[3:], out_own[None], attn_moment_one[3:], attn_moment_two[3:]
+    )
+    early = jnp.concatenate(
+        [mlp_square.reshape(1, -1), out_square.reshape(1, -1), gain_grad], axis=1
+    )
+    (early,) = butterfly([early], "dp", nd)
+    qkv_part, early = lax.optimization_barrier((qkv_part, early))
+    qkv_own = jnp.stack(
+        [qkv_part[:, m * heads_width : (m + 1) * heads_width].astype(f32) for m in range(3)]
+    )
+    qkv_one, qkv_two, qkv_moved, qkv_square = adam(
+        attn_weight[:3], qkv_own, attn_moment_one[:3], attn_moment_two[:3]
+    )
+    (qkv_square,) = butterfly([qkv_square], "dp", nd)
+    mlp_square = early[:, : 3 * hidden_width].reshape(3, 1, hidden_width)
+    out_square = early[:, 3 * hidden_width : 3 * hidden_width + heads_width].reshape(1, 1, heads_width)
+    gain_row = spread(
+        jnp.concatenate(gather(early[:, 3 * hidden_width + heads_width :]), axis=1)
+    ).reshape(-1)
+    attn_weight_grad = jnp.concatenate([qkv_own, out_own[None]], axis=0)
+    attn_one = jnp.concatenate([qkv_one, out_one], axis=0)
+    attn_two = jnp.concatenate([qkv_two, out_two], axis=0)
+    attn_moved = jnp.concatenate([qkv_moved, out_moved], axis=0)
+    attn_square = jnp.concatenate([qkv_square, out_square], axis=0)
     attn_new = attn_moved * lax.rsqrt(attn_square + norm_eps)
     mlp_new = mlp_moved * lax.rsqrt(mlp_square + norm_eps)
     return (

time: 656 us -> 624 us (0.951)
  waiting for transfers between devices: 258 us -> 201 us
  other arithmetic: 28.3 us -> 44.5 us
  Pallas kernels: 203 us -> 215 us
  starting transfers between devices: 121 us -> 114 us
    ppermute x30 -> x21, waiting for transfers between devices: 209 us -> 40 us  [shift(): lax.ppermute(value, axis, [(i, (i + distance) % size) for i in range(size)])]
    ppermute x0 -> x18, waiting for transfers between devices: none -> 113 us  [the longest x6 65.7 us: carry_on(): lax.ppermute(down, axis, [(i, i - 1) for i in range(1, size - hop + 1)])]
    ppermute x30 -> x21, starting transfers between devices: 109 us -> 44.1 us  [shift(): lax.ppermute(value, axis, [(i, (i + distance) % size) for i in range(size)])]
    ppermute x0 -> x18, starting transfers between devices: none -> 30.2 us  [the longest x6 10.4 us: carry_on(): up = lax.ppermute(up, axis, [(i, i + 1) for i in range(hop - 1, size - 1)])]
    ppermute x11, starting transfers between devices: 11.8 us -> 39.3 us  [butterfly(): lax.ppermute(v, axis, [(i, i ^ step) for i in range(size)])]
    ppermute x11, waiting for transfers between devices: 49.1 us -> 29.8 us  [butterfly(): lax.ppermute(v, axis, [(i, i ^ step) for i in range(size)])]
    reduce_scatter x2 -> x4, waiting for transfers between devices: 0.02 us -> 18.4 us  [the longest x1 18.4 us: local(): lax.psum_scatter(near_grad, 'dp', scatter_dimension=1, tiled=True)]
    pallas_call x1 -> x3, Pallas kernels: 48.3 us -> 60.9 us  [the longest x2 56 us: feed_back(): pl.pallas_call(feed_back_last_kernel if last else feed_back_first_kernel,...]
  transfers between devices with their start and end apart: 45 -> 56, of which waited for: 24 -> 24; matrix products, arithmetic and copies ran while one was open for 7% -> 10% of each run, Pallas kernels for 19% -> 26%
where the time goes in v3:
time: 624 us; the launch traced here: 619 us
  Pallas kernels  215 us (34%)
  waiting for transfers between devices  201 us (32%)
  starting transfers between devices  114 us (18%)
  other arithmetic  44.5 us (7%)
  local copies, waits for them, and re-layouts  23.3 us (4%)
  between operations  15.2 us (2%)
    ppermute x6, waiting for transfers between devices, carry_on(): lax.ppermute(down, axis, [(i, i - 1) for i in range(1, size - hop + 1)])  65.7 us
    pallas_call x2, Pallas kernels, feed_back(): pl.pallas_call(feed_back_last_kernel if last else feed_back_first_kernel,...  56 us
    ppermute x21, starting transfers between devices, shift(): lax.ppermute(value, axis, [(i, (i + distance) % size) for i in range(size)])  44.1 us
    pallas_call x1, Pallas kernels, attend_back(): pl.pallas_call(functools.partial(attend_back_kernel, heads, block, block)...  41.2 us
    ppermute x21, waiting for transfers between devices, shift(): lax.ppermute(value, axis, [(i, (i + distance) % size) for i in range(size)])  40 us
    ppermute x11, starting transfers between devices, butterfly(): lax.ppermute(v, axis, [(i, i ^ step) for i in range(size)])  39.3 us
    ppermute x6, waiting for transfers between devices, carry_on(): up = lax.ppermute(up, axis, [(i, i + 1) for i in range(hop - 1, size - 1)])  34.2 us
    pallas_call x1, Pallas kernels, feed(): pl.pallas_call(feed_kernel, grid=(total // step,), in_specs=[whole] + wei...  33.3 us
  transfers between devices with their start and end apart: 56, of which 24 were waited for; matrix products, arithmetic and copies ran while one was open for 10% of the time, Pallas kernels for 26%

profile of v3, /device:TPU:0, one launch (start us, length us, event | category | flops | bytes accessed | tf_op | source)
XLA Modules:
  0.0 619.3 jit_solution(3856273214497051812)
XLA Ops:
  24.7 15.6 %collective-permute-done = bf16[384,1024]{1,0:T(8,128)(2,1)S(1)} collective-permute-done((bf16[384,1024]{1,0:T(8,128)(2,1)S(1)}, bf16[384,1024]{1,0:T(8,128)(2,1)S(1)}, u32[]{:S(2)}, u32[]{:S(2)}) %collective-permute-start) | collective-permute-done | bytes 786464 | tf_op jit(solution)/shard_map/ppermute | solution.py:757
  47.2 17.4 %collective-permute-done.3 = bf16[384,1024]{1,0:T(8,128)(2,1)} collective-permute-done((bf16[384,1024]{1,0:T(8,128)(2,1)S(1)}, bf16[384,1024]{1,0:T(8,128)(2,1)}, u32[]{:S(2)}, u32[]{:S(2)}) %collective-permute-start.3) | collective-permute-done | bytes 786464 | tf_op jit(solution)/shard_map/ppermute | solution.py:758
  67.3 17.0 %collective-permute-done.16 = bf16[384,1024]{1,0:T(8,128)(2,1)} collective-permute-done((bf16[384,1024]{1,0:T(8,128)(2,1)}, bf16[384,1024]{1,0:T(8,128)(2,1)}, u32[]{:S(2)}, u32[]{:S(2)}) %collective-permute-start.16) | collective-permute-done | bytes 786464 | tf_op jit(solution)/shard_map/ppermute | solution.py:758
  91.3 18.6 %collective-permute-done.4 = bf16[512,1024]{1,0:T(8,128)(2,1)S(1)} collective-permute-done((bf16[512,1024]{1,0:T(8,128)(2,1)S(1)}, bf16[512,1024]{1,0:T(8,128)(2,1)S(1)}, u32[]{:S(2)}, u32[]{:S(2)}) %collective-permute-start.4) | collective-permute-done | bytes 1048608 | tf_op jit(solution)/shard_map/ppermute | solution.py:757
  125.8 12.0 %collective-permute-done.11 = bf16[512,1024]{1,0:T(8,128)(2,1)S(1)} collective-permute-done((bf16[512,1024]{1,0:T(8,128)(2,1)S(1)}, bf16[512,1024]{1,0:T(8,128)(2,1)S(1)}, u32[]{:S(2)}, u32[]{:S(2)}) %collective-permute-start.11) | collective-permute-done | bytes 1048608 | tf_op jit(solution)/shard_map/ppermute | solution.py:758
  139.3 5.6 fusion.2
  147.0 13.4 %collective-permute-done.12 = bf16[512,1024]{1,0:T(8,128)(2,1)S(1)} collective-permute-done((bf16[512,1024]{1,0:T(8,128)(2,1)S(1)}, bf16[512,1024]{1,0:T(8,128)(2,1)S(1)}, u32[]{:S(2)}, u32[]{:S(2)}) %collective-permute-start.12) | collective-permute-done | bytes 1048608 | tf_op jit(solution)/shard_map/ppermute | solution.py:758
  166.9 5.5 project.5
  183.5 20.3 %attend.1 = (bf16[2048,256]{1,0:T(8,128)(2,1)}, f32[2048,256]{1,0:T(8,128)}, f32[4,2048]{1,0:T(4,128)}) custom-call(bf16[2048,256]{1,0:T(8,128)(2,1)} %get-tuple-element.96.q_ref, bf16[2048,256]{1,0:T(8,128)(2,1)} %get-tuple-element.97.k_ref, bf16[2048,256]{1,0:T(8,128)(2,1)} %get-tuple-element.98.v_ref, s32[2048,1]{1,0:T(8,128)} %copy.40.start_ref), custom_call_target="tpu_custom_call" | custom-call | flops 20000000000 | bytes 4194304 | tf_op jit(solution)/shard_map/attend/pallas_call | solution.py:113
  209.8 7.0 %collective-permute-done.13.refs_1_ = bf16[512,256]{1,0:T(8,128)(2,1)S(1)} collective-permute-done((bf16[512,256]{1,0:T(8,128)(2,1)S(1)}, bf16[512,256]{1,0:T(8,128)(2,1)S(1)}, u32[]{:S(2)}, u32[]{:S(2)}) %collective-permute-start.13) | collective-permute-done | bytes 262176 | tf_op jit(solution)/shard_map/ppermute | solution.py:753
  216.7 6.0 collective-permute-done.14.refs_2_
  223.6 7.7 %mix.1 = (f32[512,1024]{1,0:T(8,128)}, f32[512,1024]{1,0:T(8,128)}, bf16[512,1024]{1,0:T(8,128)(2,1)}, bf16[1024,512]{1,0:T(8,128)(2,1)}) custom-call(bf16[512,256]{1,0:T(8,128)(2,1)} %get-tuple-element.173.refs_0_, bf16[512,256]{1,0:T(8,128)(2,1)} %copy-done.12, bf16[512,256]{1,0:T(8,128)(2,1)} %copy-done.13, bf16[512,256]{1,0:T(8,128)(2,1)} %copy-done.14, ...), custom_call_target="tpu_custom_call" | custom-call | flops 1073741824 | bytes 7340032 | tf_op jit(solution)/shard_map/mix/pallas_call | solution.py:471
  231.3 33.3 %feed.1 = (f32[512,4096]{1,0:T(8,128)}, f32[512,4096]{1,0:T(8,128)}, bf16[512,4096]{1,0:T(8,128)(2,1)}, bf16[512,1024]{1,0:T(8,128)(2,1)}, f32[512,1024]{1,0:T(8...) custom-call(bf16[512,1024]{1,0:T(8,128)(2,1)} %get-tuple-element.100.m_ref, ...), custom_call_target="tpu_custom_call" | custom-call | flops 12884901888 | bytes 46137344 | tf_op jit(solution)/shard_map/feed/pallas_call | solution.py:585
  264.6 23.5 %feed_back_first.1 = (bf16[3,1024,2048]{2,1,0:T(8,128)(2,1)}, f32[2,2048]{1,0:T(2,128)}, f32[512,1024]{1,0:T(8,128)}) custom-call(bf16[512,1024]{1,0:T(8,128)(2,1)} %get-tuple-element.105.refs_0_, bf16[1024,512]{1,0:T(8,128)(2,1)} %get-tuple-element.106.refs_1_, bf16[1024,512]{1,0:T(8,128)(2,1)} %get-tuple-element.107.refs_2_, ...), custom_call_target="tpu_custom_call" | custom-call | flops 12884901888 | bytes 35651584 | tf_op jit(solution)/shard_map/feed_back_first/pallas_call | solution.py:710
  288.2 32.5 %feed_back_last.1 = (bf16[3,1024,2048]{2,1,0:T(8,128)(2,1)}, f32[2,2048]{1,0:T(2,128)}, f32[512,1024]{1,0:T(8,128)}, bf16[512,1024]{1,0:T(8,128)(2,1)}, f32[1,1024]{1,0:T(1,128)}) custom-call(bf16[512,1024]{1,0:T(8,128)(2,1)} %get-tuple-element.105.refs_0_, bf16[1024,512]{1,0:T(8,128)(2,1)} %get-tuple-element.106.refs_1_, ...), custom_call_target="tpu_custom_call" | custom-call | flops 12884901888 | bytes 35651584 | tf_op jit(solution)/shard_map/feed_back_last/pallas_call | solution.py:710
  339.8 13.3 %collective-permute-done.22 = bf16[512,256]{1,0:T(8,128)(2,1)S(1)} collective-permute-done((bf16[512,256]{1,0:T(8,128)(2,1)S(1)}, bf16[512,256]{1,0:T(8,128)(2,1)S(1)}, u32[]{:S(2)}, u32[]{:S(2)}) %collective-permute-start.22) | collective-permute-done | bytes 262176 | tf_op jit(solution)/shard_map/ppermute | solution.py:753
  355.7 41.2 %attend_back.1 = (f32[2048,256]{1,0:T(8,128)}, f32[2048,256]{1,0:T(8,128)}, f32[2048,256]{1,0:T(8,128)}) custom-call(bf16[2048,256]{1,0:T(8,128)(2,1)} %get-tuple-element.96.q_ref, bf16[2048,256]{1,0:T(8,128)(2,1)} %copy-done.7, bf16[2048,256]{1,0:T(8,128)(2,1)} %get-tuple-element.97.k_ref, bf16[2048,256]{1,0:T(8,128)(2,1)} %get-tuple-element.98.v_ref, ...), custom_call_target="tpu_custom_call" | custom-call | flops 40000000000 | bytes 10485760 | tf_op jit(solution)/shard_map/attend_back/pallas_call | solution.py:191
  396.9 21.6 %project_back.1 = (bf16[2048,768]{1,0:T(8,128)(2,1)}, bf16[2048,1024]{1,0:T(8,128)(2,1)}, f32[1,256]{1,0:T(1,128)}) custom-call(s32[1]{0:T(128)} %bitcast.15.index_ref, f32[2048,256]{1,0:T(8,128)} %get-tuple-element.125.dq_ref, f32[2048,256]{1,0:T(8,128)} %get-tuple-element.126.dk_ref, f32[2048,256]{1,0:T(8,128)} %get-tuple-element.127.dv_ref, ...), custom_call_target="tpu_custom_call" | custom-call | flops 4294967296 | bytes 16777216 | tf_op jit(solution)/shard_map/project_back/pallas_call | solution.py:353
  424.7 8.1 %projection_grads.1 = bf16[1024,768]{1,0:T(8,128)(2,1)} custom-call(bf16[512,1024]{1,0:T(8,128)(2,1)} %refs_0_, bf16[512,1024]{1,0:T(8,128)(2,1)} %broadcast_select_fusion.2.x_ref.refs_1_, bf16[512,1024]{1,0:T(8,128)(2,1)} %broadcast_select_fusion.x_ref.refs_2_, bf16[512,1024]{1,0:T(8,128)(2,1)} %broadcast_select_fusion.1.x_ref.refs_3_, ...), custom_call_target="tpu_custom_call" | custom-call | flops 3221225472 | bytes 8388608 | tf_op jit(solution)/shard_map/projection_grads/pallas_call | solution.py:397
  432.9 10.8 %collective-permute-done.24 = bf16[512,1024]{1,0:T(8,128)(2,1)S(1)} collective-permute-done((bf16[512,1024]{1,0:T(8,128)(2,1)}, bf16[512,1024]{1,0:T(8,128)(2,1)S(1)}, u32[]{:S(2)}, u32[]{:S(2)}) %collective-permute-start.24) | collective-permute-done | bytes 1048608 | tf_op jit(solution)/shard_map/ppermute | solution.py:772
  458.5 18.4 %reduce-scatter.7.cloned.1.call-done = bf16[3,128,2048]{2,1,0:T(8,128)(2,1)} async-done(((bf16[3,1024,2048]{2,1,0:T(8,128)(2,1)}), bf16[3,128,2048]{2,1,0:T(8,128)(2,1)}) %reduce-scatter.7.cloned.1.call-update) | async-done | bytes 1572880 | tf_op jit(solution)/shard_map/reduce_scatter | solution.py:890
  490.5 35.8 %collective-permute-start.42 = (f32[10,1024]{1,0:T(8,128)S(1)}, f32[10,1024]{1,0:T(8,128)S(1)}, u32[]{:S(2)}, u32[]{:S(2)}) collective-permute-start(f32[10,1024]{1,0:T(8,128)S(1)} %add.303), channel_id=1, source_target_pairs={{0,1},{1,0},{2,3},{3,2},{4,5},{5,4},{6,7},{7,6},{8,9},{9,8},{10,11... | collective-permute-start | bytes 122888 | tf_op jit(solution)/shard_map/ppermute | solution.py:780
  526.4 18.4 %collective-permute-done.42 = f32[10,1024]{1,0:T(8,128)S(1)} collective-permute-done((f32[10,1024]{1,0:T(8,128)S(1)}, f32[10,1024]{1,0:T(8,128)S(1)}, u32[]{:S(2)}, u32[]{:S(2)}) %collective-permute-start.42) | collective-permute-done | bytes 40992 | tf_op jit(solution)/shard_map/ppermute | solution.py:780
  557.9 5.8 multiply_reduce_fusion
  (271 shorter events, 195.5 us)
Async XLA Ops:
  7.2 154.3 %all-gather.3.cloned.1.call-start = ((), (), s32[]{:S(2)}) async-start(), calls=%async_computation.4 | async-start | bytes 4128768 | tf_op jit(solution)/shard_map/all_gather | solution.py:837
  19.6 211.7 %all-gather.5.cloned.1.call-start = ((), (), s32[]{:S(2)}) async-start(), calls=%async_computation.5 | async-start | bytes 28311552 | tf_op jit(solution)/shard_map/all_gather | solution.py:844
  87.5 309.4 %reduce-scatter.5.cloned.1.call-start = ((), (), s32[]{:S(2)}) async-start(), calls=%async_computation.6 | async-start | bytes 14155776 | tf_op jit(solution)/shard_map/reduce_scatter | solution.py:886
  90.0 24.1 %collective-permute-start.7 = (bf16[512,1024]{1,0:T(8,128)(2,1)S(1)}, bf16[512,1024]{1,0:T(8,128)(2,1)S(1)}, u32[]{:S(2)}, u32[]{:S(2)}) collective-permute-start(bf16[512,1024]{1,0:T(8,128)(2,1)S(1)} %copy-done), channel_id=1, source_target_pairs={{1,0},{2,1},{3,2},{5,4},{6,5},{7,6},{9,8},{10,9},{11,10},{13,12},{... | collective-permute-start | bytes 3145736 | tf_op jit(solution)/shard_map/ppermute | solution.py:758
  114.1 23.8 %collective-permute-start.11 = (bf16[512,1024]{1,0:T(8,128)(2,1)S(1)}, bf16[512,1024]{1,0:T(8,128)(2,1)S(1)}, u32[]{:S(2)}, u32[]{:S(2)}) collective-permute-start(bf16[512,1024]{1,0:T(8,128)(2,1)S(1)} %collective-permute-done.7), channel_id=1, source_target_pairs={{1,0},{2,1},{5,4},{6,5},{9,8},{10,9},{13,12},{14,13},{17,16},{18,1... | collective-permute-start | bytes 3145736 | tf_op jit(solution)/shard_map/ppermute | solution.py:758
  115.4 91.7 %collective-permute-start.18 = (f32[2,1024]{1,0:T(2,128)S(1)}, f32[2,1024]{1,0:T(2,128)S(1)}, u32[]{:S(2)}, u32[]{:S(2)}) collective-permute-start(f32[2,1024]{1,0:T(2,128)S(1)} %copy-done.30), channel_id=1, source_target_pairs={{0,1},{1,2},{2,3},{3,0},{4,5},{5,6},{6,7},{7,4},{8,9},{9,10},{10,1... | collective-permute-start | bytes 24584 | tf_op jit(solution)/shard_map/ppermute | solution.py:753
  118.1 91.7 %collective-permute-start.19 = (f32[2,1024]{1,0:T(2,128)S(1)}, f32[2,1024]{1,0:T(2,128)S(1)}, u32[]{:S(2)}, u32[]{:S(2)}) collective-permute-start(f32[2,1024]{1,0:T(2,128)S(1)} %copy-done.30), channel_id=1, source_target_pairs={{0,2},{1,3},{2,0},{3,1},{4,6},{5,7},{6,4},{7,5},{8,10},{9,11},{10,... | collective-permute-start | bytes 24584 | tf_op jit(solution)/shard_map/ppermute | solution.py:753
  118.2 91.5 %collective-permute-start.20 = (f32[2,1024]{1,0:T(2,128)S(1)}, f32[2,1024]{1,0:T(2,128)S(1)}, u32[]{:S(2)}, u32[]{:S(2)}) collective-permute-start(f32[2,1024]{1,0:T(2,128)S(1)} %copy-done.30), channel_id=1, source_target_pairs={{0,3},{1,0},{2,1},{3,2},{4,7},{5,4},{6,5},{7,6},{8,11},{9,8},{10,9... | collective-permute-start | bytes 24584 | tf_op jit(solution)/shard_map/ppermute | solution.py:753
  121.8 24.1 %collective-permute-start.6 = (bf16[512,1024]{1,0:T(8,128)(2,1)}, bf16[512,1024]{1,0:T(8,128)(2,1)}, u32[]{:S(2)}, u32[]{:S(2)}) collective-permute-start(bf16[512,1024]{1,0:T(8,128)(2,1)} %collective-permute-done.5), channel_id=1, source_target_pairs={{2,3},{6,7},{10,11},{14,15},{18,19},{22,23},{26,27},{30,31}} | collective-permute-start | bytes 3145736 | tf_op jit(solution)/shard_map/ppermute | solution.py:757
  137.8 22.5 %collective-permute-start.12 = (bf16[512,1024]{1,0:T(8,128)(2,1)S(1)}, bf16[512,1024]{1,0:T(8,128)(2,1)S(1)}, u32[]{:S(2)}, u32[]{:S(2)}) collective-permute-start(bf16[512,1024]{1,0:T(8,128)(2,1)S(1)} %collective-permute-done.11), channel_id=1, source_target_pairs={{1,0},{5,4},{9,8},{13,12},{17,16},{21,20},{25,24},{29,28}} | collective-permute-start | bytes 3145736 | tf_op jit(solution)/shard_map/ppermute | solution.py:758
  288.1 188.7 %reduce-scatter.7.cloned.1.call-start = ((), (), s32[]{:S(2)}) async-start(), calls=%async_computation.7 | async-start | bytes 14155776 | tf_op jit(solution)/shard_map/reduce_scatter | solution.py:890
  320.7 229.3 %reduce-scatter.11.cloned.1.call-start = ((), (), s32[]{:S(2)}) async-start(), calls=%async_computation.9 | async-start | bytes 2359296 | tf_op jit(solution)/shard_map/reduce_scatter | solution.py:908
  330.4 22.7 %collective-permute-start.22 = (bf16[512,256]{1,0:T(8,128)(2,1)S(1)}, bf16[512,256]{1,0:T(8,128)(2,1)S(1)}, u32[]{:S(2)}, u32[]{:S(2)}) collective-permute-start(bf16[512,256]{1,0:T(8,128)(2,1)S(1)} %convolution_convert_fusion.2), channel_id=1, source_target_pairs={{0,2},{1,3},{2,0},{3,1},{4,6},{5,7},{6,4},{7,5},{8,10},{9,11},{10,... | collective-permute-start | bytes 786440 | tf_op jit(solution)/shard_map/ppermute | solution.py:753
  396.9 194.9 %reduce-scatter.9.cloned.1.call-start = ((), (), s32[]{:S(2)}) async-start(), calls=%async_computation.8 | async-start | bytes 1769472 | tf_op jit(solution)/shard_map/reduce_scatter | solution.py:926
  421.6 22.0 %collective-permute-start.24 = (bf16[512,1024]{1,0:T(8,128)(2,1)}, bf16[512,1024]{1,0:T(8,128)(2,1)S(1)}, u32[]{:S(2)}, u32[]{:S(2)}) collective-permute-start(bf16[512,1024]{1,0:T(8,128)(2,1)} %get-tuple-element.167), channel_id=1, source_target_pairs={{0,1},{4,5},{8,9},{12,13},{16,17},{20,21},{24,25},{28,29}} | collective-permute-start | bytes 3145736 | tf_op jit(solution)/shard_map/ppermute | solution.py:772
  446.7 30.2 %collective-permute-start.26 = (bf16[512,1024]{1,0:T(8,128)(2,1)}, bf16[512,1024]{1,0:T(8,128)(2,1)S(1)}, u32[]{:S(2)}, u32[]{:S(2)}) collective-permute-start(bf16[512,1024]{1,0:T(8,128)(2,1)} %get-tuple-element.165), channel_id=1, source_target_pairs={{0,1},{1,2},{4,5},{5,6},{8,9},{9,10},{12,13},{13,14},{16,17},{17,1... | collective-permute-start | bytes 3145736 | tf_op jit(solution)/shard_map/ppermute | solution.py:772
  451.0 25.8 %collective-permute-start.27 = (bf16[512,1024]{1,0:T(8,128)(2,1)}, bf16[512,1024]{1,0:T(8,128)(2,1)}, u32[]{:S(2)}, u32[]{:S(2)}) collective-permute-start(bf16[512,1024]{1,0:T(8,128)(2,1)} %get-tuple-element.164), channel_id=1, source_target_pairs={{2,1},{3,2},{6,5},{7,6},{10,9},{11,10},{14,13},{15,14},{18,17},{19... | collective-permute-start | bytes 3145736 | tf_op jit(solution)/shard_map/ppermute | solution.py:773
  453.0 28.9 %collective-permute-start.39 = (f32[10,1024]{1,0:T(8,128)S(1)}, f32[10,1024]{1,0:T(8,128)S(1)}, u32[]{:S(2)}, u32[]{:S(2)}) collective-permute-start(f32[10,1024]{1,0:T(8,128)S(1)} %pad_maximum_fusion.5), channel_id=1, source_target_pairs={{0,4},{4,0},{8,12},{12,8},{16,20},{20,16},{24,28},{28,24},{1,5},{5... | collective-permute-start | bytes 122888 | tf_op jit(solution)/shard_map/ppermute | solution.py:780
  454.3 96.7 %collective-permute-start.32 = (bf16[3,128,1024]{2,1,0:T(8,128)(2,1)}, bf16[3,128,1024]{2,1,0:T(8,128)(2,1)S(1)}, u32[]{:S(2)}, u32[]{:S(2)}) collective-permute-start(bf16[3,128,1024]{2,1,0:T(8,128)(2,1)} %get-tuple-element.169), channel_id=1, source_target_pairs={{0,1},{1,2},{2,3},{3,0},{4,5},{5,6},{6,7},{7,4},{8,9},{9,10},{10,1... | collective-permute-start | bytes 2359304 | tf_op jit(solution)/shard_map/ppermute | solution.py:753
  456.0 97.7 %collective-permute-start.31 = (bf16[3,128,1024]{2,1,0:T(8,128)(2,1)}, bf16[3,128,1024]{2,1,0:T(8,128)(2,1)}, u32[]{:S(2)}, u32[]{:S(2)}) collective-permute-start(bf16[3,128,1024]{2,1,0:T(8,128)(2,1)} %get-tuple-element.168), channel_id=1, source_target_pairs={{0,2},{1,3},{2,0},{3,1},{4,6},{5,7},{6,4},{7,5},{8,10},{9,11},{10,... | collective-permute-start | bytes 2359304 | tf_op jit(solution)/shard_map/ppermute | solution.py:753
  478.4 79.2 %collective-permute-start.30 = (bf16[3,128,1024]{2,1,0:T(8,128)(2,1)S(1)}, bf16[3,128,1024]{2,1,0:T(8,128)(2,1)}, u32[]{:S(2)}, u32[]{:S(2)}) collective-permute-start(bf16[3,128,1024]{2,1,0:T(8,128)(2,1)S(1)} %slice.144), channel_id=1, source_target_pairs={{0,3},{1,0},{2,1},{3,2},{4,7},{5,4},{6,5},{7,6},{8,11},{9,8},{10,9... | collective-permute-start | bytes 2359304 | tf_op jit(solution)/shard_map/ppermute | solution.py:753
  490.5 54.2 %collective-permute-start.42 = (f32[10,1024]{1,0:T(8,128)S(1)}, f32[10,1024]{1,0:T(8,128)S(1)}, u32[]{:S(2)}, u32[]{:S(2)}) collective-permute-start(f32[10,1024]{1,0:T(8,128)S(1)} %add.303), channel_id=1, source_target_pairs={{0,1},{1,0},{2,3},{3,2},{4,5},{5,4},{6,7},{7,6},{8,9},{9,8},{10,11... | collective-permute-start | bytes 122888 | tf_op jit(solution)/shard_map/ppermute | solution.py:780
  544.7 33.4 %collective-permute-start.43 = (f32[10,1024]{1,0:T(8,128)S(1)}, f32[10,1024]{1,0:T(8,128)}, u32[]{:S(2)}, u32[]{:S(2)}) collective-permute-start(f32[10,1024]{1,0:T(8,128)S(1)} %add.304), channel_id=1, source_target_pairs={{0,2},{1,3},{2,0},{3,1},{4,6},{5,7},{6,4},{7,5},{8,10},{9,11},{10,... | collective-permute-start | bytes 122888 | tf_op jit(solution)/shard_map/ppermute | solution.py:780
  548.8 31.6 %collective-permute-start.29 = (bf16[512,1024]{1,0:T(8,128)(2,1)}, bf16[512,1024]{1,0:T(8,128)(2,1)}, u32[]{:S(2)}, u32[]{:S(2)}) collective-permute-start(bf16[512,1024]{1,0:T(8,128)(2,1)} %get-tuple-element.163), channel_id=1, source_target_pairs={{1,0},{2,1},{3,2},{5,4},{6,5},{7,6},{9,8},{10,9},{11,10},{13,12},{... | collective-permute-start | bytes 3145736 | tf_op jit(solution)/shard_map/ppermute | solution.py:773
  (68 other events, 814.1 us)
Sparse Core Ops, SparseCore 0:
  19.8 35.0 all-gather.2
  87.6 122.7 all-gather.4
  288.3 93.0 reduce-scatter.4
  384.7 92.0 reduce-scatter.6
  480.0 41.0 reduce-scatter.10
  545.0 36.9 reduce-scatter.8

commit v4 on v3

--- a/solution.py
+++ b/solution.py
@@ -465,7 +465,7 @@
     part = min(128, rows)
 
     def column(d):
-        return pl.BlockSpec((model, width), lambda i: (0, 3 + d))
+        return pl.BlockSpec((model, width), lambda i: (0, d))
 
     wide = pl.BlockSpec((part, model), lambda i: (i, 0))
     return pl.pallas_call(
@@ -759,28 +759,44 @@
     return up, down
 
 
-def line_sum(pieces, axis, size, second, other):
-    up = down = None
-    for hop in range(1, size):
-        if hop == 2:
-            up, down, second = lax.optimization_barrier((up, down, second))
-        if hop == size - 1 and hop > 2:
-            up, down, other = lax.optimization_barrier((up, down, other))
-        ahead, behind = pieces[size - hop], pieces[hop]
-        ahead = ahead if up is None else ahead + up
-        behind = behind if down is None else behind + down
-        up = lax.ppermute(ahead, axis, [(i, i + 1) for i in range(hop)])
-        down = lax.ppermute(behind, axis, [(i, i - 1) for i in range(size - hop, size)])
-    return up, down, second, other
-
-
-def butterfly(values, axis, size):
+def line_sum(pieces, hop, up, down, axis, size):
+    ahead, behind = pieces[size - hop], pieces[hop]
+    ahead = ahead if up is None else ahead + up
+    behind = behind if down is None else behind + down
+    up = lax.ppermute(ahead, axis, [(i, i + 1) for i in range(hop)])
+    down = lax.ppermute(behind, axis, [(i, i - 1) for i in range(size - hop, size)])
+    return up, down
+
+
+def halving(value, axis, size):
+    rows, width = value.shape[0] // size, value.shape[1]
+    index = lax.axis_index(axis)
+    value = value.reshape(size, rows, width)
     step = 1
     while step < size:
-        other = [lax.ppermute(v, axis, [(i, i ^ step) for i in range(size)]) for v in values]
-        values = [v + o for v, o in zip(values, other)]
+        bit = (index // step) % 2
+        pairs = value.reshape(-1, 2, rows, width)
+        sent = lax.dynamic_index_in_dim(pairs, 1 - bit, 1, False)
+        kept = lax.dynamic_index_in_dim(pairs, bit, 1, False)
+        other = lax.ppermute(sent, axis, [(i, i ^ step) for i in range(size)])
+        value = kept.astype(f32) + other.astype(f32)
         step *= 2
-    return values
+        value = value if step == size else value.astype(bf16)
+    return value.reshape(rows, width).astype(f32)
+
+
+def exchange_add(value, axis, size, step):
+    return value + lax.ppermute(value, axis, [(i, i ^ step) for i in range(size)])
+
+
+def doublings(size):
+    return [1 << k for k in range(size.bit_length() - 1)]
+
+
+def butterfly(value, axis, size):
+    for step in doublings(size):
+        value = exchange_add(value, axis, size, step)
+    return value
 
 
 def take_block(value, index, size, axis):
@@ -830,21 +846,26 @@
     def join(ups, downs, d):
         return ups[0] if d == 0 else jnp.where(me >= d, ups[d], downs[nt - d])
 
+    middle_hop = nt // 2
+    order = [d for d in range(nt) if d != middle_hop] + [middle_hop]
     attn_low = attn_weight.astype(bf16)
-    attn_shard = jnp.concatenate(
-        [attn_low[0], attn_low[1], attn_low[2]] + gather(attn_low[3]), axis=1
-    )
-    attn_full = lax.all_gather(attn_shard, "dp", axis=0, tiled=True)
-    scales_row = jnp.concatenate(gather(mlp_scales), axis=1)
+    qkv_full = lax.all_gather(
+        jnp.concatenate([attn_low[0], attn_low[1], attn_low[2]], axis=1), "dp", axis=0, tiled=True
+    )
     ups, downs = line(mlp_weight.astype(bf16).reshape(3 * shard, hidden_width))
+    out_full = lax.all_gather(
+        jnp.concatenate(gather(attn_low[3]), axis=1), "dp", axis=0, tiled=True
+    )
     before = max(1, nt - 2)
     hidden_in, ups[before], downs[before] = lax.optimization_barrier(
         (hidden_in, ups[before], downs[before])
     )
     mlp_full = lax.all_gather(
-        jnp.concatenate([join(ups, downs, d) for d in range(nt)], axis=0), "dp", axis=0, tiled=True
+        jnp.concatenate([join(ups, downs, d) for d in order], axis=0), "dp", axis=0, tiled=True
     )
     mlp_full = mlp_full.reshape(nd, nt, 3, shard, hidden_width)
+    scales_parts = gather(mlp_scales)
+    scales_row = jnp.concatenate([scales_parts[d] for d in order], axis=1)
 
     starts = starts_of(segments)
     positions = (jnp.arange(length, dtype=jnp.int32) - starts).astype(f32)
@@ -857,12 +878,25 @@
     sine = jnp.sin(angles) * sign[None, :]
     gain = qk_scale.reshape(1, heads_width)
 
-    ups, downs = line(hidden_in)
-    hidden_parts = [join(ups, downs, d) for d in range(nt)]
-    state = ()
-    for d in sorted(range(nt), key=lambda d: max(d, nt - d) if d else 0):
-        index = ((me + nt - d) % nt).reshape(1)
-        state = project(index, hidden_parts[d], attn_full, cosine, sine, gain, length, state)
+    ups, downs, state = [hidden_in], [hidden_in], ()
+    hidden_parts = [None] * nt
+
+    def projected(hop, state):
+        for d in range(nt):
+            if (max(d, nt - d) if d else 0) == hop:
+                hidden_parts[d] = join(ups, downs, d)
+                index = ((me + nt - d) % nt).reshape(1)
+                state = project(index, hidden_parts[d], qkv_full, cosine, sine, gain, length, state)
+        return state
+
+    for hop in range(1, nt):
+        ups[-1], downs[-1], state = lax.optimization_barrier((ups[-1], downs[-1], state))
+        up, down = carry_on(ups[-1], downs[-1], hop, "tensor", nt)
+        ups.append(up)
+        downs.append(down)
+        state = projected(hop - 1, state)
+    ups[-1], downs[-1], state = lax.optimization_barrier((ups[-1], downs[-1], state))
+    state = projected(nt - 1, state)
     query_hat, key_hat, value_hat, query_turned, key_turned = state
     attended_row, attended_f32, log_sum = attend(
         query_hat, key_hat, value_hat, starts[:, None], block
@@ -871,122 +905,126 @@
         shift(take_block(attended_row, (me + d) % nt, rows, 0), "tensor", d, nt)
         for d in range(1, nt)
     ]
-    branch, middle, middle_low, middle_t = mix(attended, attn_full, hidden_in, rates)
+    branch, middle, middle_low, middle_t = mix(attended, out_full, hidden_in, rates)
     row_segments = take_block(segments, me, rows, 0)
     live = (row_segments < pad_segment).astype(f32)[:, None]
     up, gate, hidden_units, result, middle_direct, mlp_out_low, mlp_out_t, rate_mlp_grad = feed(
         middle_low, mlp_full, scales_row, middle, cotangent, live, rates, step
     )
-    blocks = nt * hidden_width // step
-    half = blocks // 2
+    def spread(value, places):
+        width = value.shape[1] // nt
+        whole = jnp.zeros_like(value)
+        for p, d in enumerate(places):
+            piece = value[:, p * width : (p + 1) * width]
+            whole = put_block(whole, piece, (me + nt - d) % nt, 1)
+        return whole
+
+    per = hidden_width // step
+    near = (nt - 1) * per
     feed_args = (mlp_out_low, mlp_out_t, middle_t, mlp_full, scales_row, up, gate, hidden_units)
-    far_grad, far_scales, partial = feed_back(
-        *feed_args, middle_direct, (), step, half, blocks - half
-    )
+    far_grad, far_scales, partial = feed_back(*feed_args, middle_direct, (), step, near, per)
     far_part = lax.psum_scatter(far_grad, "dp", scatter_dimension=1, tiled=True)
     near_grad, near_scales, token_direct, branch_low, rate_attn_grad = feed_back(
-        *feed_args, partial, (branch, hidden_in, rates), step, 0, half
+        *feed_args, partial, (branch, hidden_in, rates), step, 0, near
     )
     near_part = lax.psum_scatter(near_grad, "dp", scatter_dimension=1, tiled=True)
-    scales_grad = jnp.concatenate([near_scales, far_scales], axis=1)
-
-    def out_block(d):
-        return attn_full[:, (3 + d) * heads_width : (4 + d) * heads_width]
 
     grad_row = jnp.zeros((length, heads_width), bf16)
     for d in list(range(1, nt)) + [0]:
-        piece = dot_nn(branch_low, out_block(d)).astype(bf16)
+        piece = dot_nn(branch_low, out_full[:, d * heads_width : (d + 1) * heads_width])
+        piece = piece.astype(bf16)
         piece = shift(piece, "tensor", -d, nt) if d else piece
         grad_row = put_block(grad_row, piece, (me + d) % nt, 0)
     out_grad = out_grads(attended, branch_low)
-    small = jnp.concatenate([rate_attn_grad, rate_mlp_grad], axis=0)
-    small, grad_row = lax.optimization_barrier((small, grad_row))
+
+    scales_grad = spread(jnp.concatenate([near_scales, far_scales], axis=1), order)
+    small = jnp.concatenate(
+        [rate_attn_grad, rate_mlp_grad, scales_grad.reshape(-1, model)], axis=0
+    )
+    steps = [("tensor", nt, k) for k in doublings(nt)] + [("dp", nd, k) for k in doublings(nd)]
+
+    def advance(small):
+        return exchange_add(small, *steps.pop(0)) if steps else small
+
+    far_part, grad_row, out_grad, small = lax.optimization_barrier(
+        (far_part, grad_row, out_grad, small)
+    )
+    far_part = shift(far_part, "tensor", -middle_hop, nt)
+    small = advance(small)
     head_grads = attend_back(
         query_hat, key_hat, value_hat, grad_row, attended_f32, log_sum, starts[None, :], block
     )
-    head_grads, far_part, out_grad = lax.optimization_barrier((head_grads, far_part, out_grad))
-    out_part = lax.psum_scatter(out_grad, "dp", scatter_dimension=0, tiled=True)
+    head_grads, far_part, small = lax.optimization_barrier((head_grads, far_part, small))
+    small = advance(small)
+    out_sum = halving(out_grad, "dp", nd)
     qkv_grad, pieces, gain_grad = project_back(
         me.reshape(1),
         head_grads,
         (query_turned, key_turned),
-        attn_full,
+        qkv_full,
         cosine,
         sine,
         gain,
         rows,
     )
+    qkv_grad, pieces, small = lax.optimization_barrier((qkv_grad, pieces, small))
     pieces = [pieces[d * rows : (d + 1) * rows] for d in range(nt)]
     hidden_turn = [hidden_parts[(nt - d) % nt] for d in range(nt)]
     qkv_grad = projection_grads(hidden_turn, qkv_grad)
+    gain_row = spread(jnp.concatenate(gather(gain_grad), axis=1), range(nt))
+
+    def own_pieces(part, axis, width, places):
+        pieces = [
+            lax.slice_in_dim(part, p * width, (p + 1) * width, axis=axis)
+            for p in range(len(places))
+        ]
+        return [shift(piece, "tensor", -d, nt) if d else piece for d, piece in zip(places, pieces)]
+
+    ahead = behind = None
+    for hop in range(1, nt):
+        if hop == 2:
+            small = advance(small)
+            ahead, behind, qkv_grad, small = lax.optimization_barrier(
+                (ahead, behind, qkv_grad, small)
+            )
+            small = advance(small)
+            qkv_sum = halving(qkv_grad, "dp", nd)
+            near_part, qkv_sum = lax.optimization_barrier((near_part, qkv_sum))
+        if hop == max(2, nt - 1):
+            ahead, behind, near_part, small = lax.optimization_barrier(
+                (ahead, behind, near_part, small)
+            )
+        ahead, behind = line_sum(pieces, hop, ahead, behind, "tensor", nt)
+    while steps:
+        small = advance(small)
     total = token_direct + pieces[0].astype(f32)
-    from_below, from_above, qkv_grad, near_part = line_sum(
-        pieces, "tensor", nt, qkv_grad, near_part
-    )
-    qkv_part = lax.psum_scatter(qkv_grad, "dp", scatter_dimension=0, tiled=True)
-    total = total + from_below.astype(f32) + from_above.astype(f32)
-    input_grad = total.astype(bf16)
-
-    def sent(part, axis, width, first):
-        count = part.shape[axis] // width
-        pieces = [lax.slice_in_dim(part, d * width, (d + 1) * width, axis=axis) for d in range(count)]
-        return [
-            (shift(piece, "tensor", -(d + first), nt) if d + first else piece).astype(f32)
-            for d, piece in enumerate(pieces)
-        ]
-
-    out_own = sum(sent(out_part, 1, heads_width, 0))
-    split = half * step // hidden_width
-    mlp_weight_grad = sum(sent(near_part, 2, hidden_width, 0) + sent(far_part, 2, hidden_width, split))
-
-    def spread(value):
-        width = value.shape[1] // nt
-        whole = jnp.zeros_like(value)
-        for d in range(nt):
-            piece = value[:, d * width : (d + 1) * width]
-            whole = put_block(whole, piece, (me + nt - d) % nt, 1)
-        return whole
-
-    scales_grad = spread(scales_grad).reshape(-1, model)
-    small = jnp.concatenate([small, scales_grad], axis=0)
-    (small,) = butterfly([small], "dp", nd)
-    (small,) = butterfly([small], "tensor", nt)
+    input_grad = (total + ahead.astype(f32) + behind.astype(f32)).astype(bf16)
     rates_grad = small[:2]
     mlp_scales_grad = small[2:].reshape(2, nt * hidden_width)
 
-    def adam(weight, gradient, one, two):
-        one, two, moved = adam_moved(weight, gradient, one, two)
-        return one, two, moved, jnp.sum(moved * moved, axis=1, keepdims=True)
-
-    mlp_one, mlp_two, mlp_moved, mlp_square = adam(
+    out_own = sum(
+        piece.astype(f32) for piece in own_pieces(out_sum.astype(bf16), 1, heads_width, range(nt))
+    )
+    attn_weight_grad = jnp.stack(
+        [qkv_sum[:, m * heads_width : (m + 1) * heads_width] for m in range(3)] + [out_own]
+    )
+    attn_one, attn_two, attn_moved = adam_moved(
+        attn_weight, attn_weight_grad, attn_moment_one, attn_moment_two
+    )
+    attn_square = jnp.sum(attn_moved * attn_moved, axis=1, keepdims=True)
+    last = jnp.concatenate([attn_square.reshape(1, -1), gain_row], axis=1)
+    last = butterfly(last, "dp", nd)
+    attn_square = last[:, : 4 * heads_width].reshape(4, 1, heads_width)
+    gain_row = last[:, 4 * heads_width :].reshape(-1)
+    attn_new = attn_moved * lax.rsqrt(attn_square + norm_eps)
+
+    mlp_pieces = own_pieces(near_part, 2, hidden_width, order[:-1]) + [far_part]
+    mlp_weight_grad = sum(piece.astype(f32) for piece in mlp_pieces)
+    mlp_one, mlp_two, mlp_moved = adam_moved(
         mlp_weight, mlp_weight_grad, mlp_moment_one, mlp_moment_two
     )
-    out_one, out_two, out_moved, out_square = adam(
-        attn_weight[3:], out_own[None], attn_moment_one[3:], attn_moment_two[3:]
-    )
-    early = jnp.concatenate(
-        [mlp_square.reshape(1, -1), out_square.reshape(1, -1), gain_grad], axis=1
-    )
-    (early,) = butterfly([early], "dp", nd)
-    qkv_part, early = lax.optimization_barrier((qkv_part, early))
-    qkv_own = jnp.stack(
-        [qkv_part[:, m * heads_width : (m + 1) * heads_width].astype(f32) for m in range(3)]
-    )
-    qkv_one, qkv_two, qkv_moved, qkv_square = adam(
-        attn_weight[:3], qkv_own, attn_moment_one[:3], attn_moment_two[:3]
-    )
-    (qkv_square,) = butterfly([qkv_square], "dp", nd)
-    mlp_square = early[:, : 3 * hidden_width].reshape(3, 1, hidden_width)
-    out_square = early[:, 3 * hidden_width : 3 * hidden_width + heads_width].reshape(1, 1, heads_width)
-    gain_row = spread(
-        jnp.concatenate(gather(early[:, 3 * hidden_width + heads_width :]), axis=1)
-    ).reshape(-1)
-    attn_weight_grad = jnp.concatenate([qkv_own, out_own[None]], axis=0)
-    attn_one = jnp.concatenate([qkv_one, out_one], axis=0)
-    attn_two = jnp.concatenate([qkv_two, out_two], axis=0)
-    attn_moved = jnp.concatenate([qkv_moved, out_moved], axis=0)
-    attn_square = jnp.concatenate([qkv_square, out_square], axis=0)
-    attn_new = attn_moved * lax.rsqrt(attn_square + norm_eps)
+    mlp_square = jnp.sum(mlp_moved * mlp_moved, axis=1, keepdims=True)
+    mlp_square = butterfly(mlp_square.reshape(1, -1), "dp", nd).reshape(mlp_square.shape)
     mlp_new = mlp_moved * lax.rsqrt(mlp_square + norm_eps)
     return (
         result.astype(bf16),

time: 624 us -> 589 us (0.944)
  starting transfers between devices: 114 us -> 82.1 us
    ppermute x21, waiting for transfers between devices: 40 us -> 78.8 us  [shift(): lax.ppermute(value, axis, [(i, (i + distance) % size) for i in range(size)])]
    ppermute x11 -> x17, starting transfers between devices: 39.3 us -> 15.4 us  [the longest x11 10.6 us: exchange_add(): lax.ppermute(value, axis, [(i, i ^ step) for i in range(size)])]
    reduce_scatter x1, waiting for transfers between devices: 18.4 us -> 0.02 us  [local(): lax.psum_scatter(near_grad, 'dp', scatter_dimension=1, tiled=True)]
    ppermute x6, waiting for transfers between devices: 34.2 us -> 21 us  [carry_on(): up = lax.ppermute(up, axis, [(i, i + 1) for i in range(hop - 1, size - 1)])]
    ppermute x21, starting transfers between devices: 44.1 us -> 33.1 us  [shift(): lax.ppermute(value, axis, [(i, (i + distance) % size) for i in range(size)])]
    ppermute x11 -> x17, waiting for transfers between devices: 29.8 us -> 22.6 us  [the longest x6 18.7 us: halving(): other = lax.ppermute(sent, axis, [(i, i ^ step) for i in range(size)])]
  transfers between devices with their start and end apart: 56 -> 61, of which waited for: 24 -> 25; matrix products, arithmetic and copies ran while one was open for 10% -> 10% of each run, Pallas kernels for 26% -> 28%
where the time goes in v4:
time: 589 us; the launch traced here: 583 us
  Pallas kernels  213 us (36%)
  waiting for transfers between devices  205 us (35%)
  starting transfers between devices  82.1 us (14%)
  other arithmetic  40.1 us (7%)
  local copies, waits for them, and re-layouts  22.9 us (4%)
  between operations  15 us (3%)
    ppermute x21, waiting for transfers between devices, shift(): lax.ppermute(value, axis, [(i, (i + distance) % size) for i in range(size)])  78.8 us
    ppermute x6, waiting for transfers between devices, carry_on(): lax.ppermute(down, axis, [(i, i - 1) for i in range(1, size - hop + 1)])  70.5 us
    pallas_call x2, Pallas kernels, feed_back(): pl.pallas_call(feed_back_last_kernel if last else feed_back_first_kernel,...  55.1 us
    pallas_call x1, Pallas kernels, attend_back(): pl.pallas_call(functools.partial(attend_back_kernel, heads, block, block)...  41.2 us
    pallas_call x1, Pallas kernels, feed(): pl.pallas_call(feed_kernel, grid=(total // step,), in_specs=[whole] + wei...  33.2 us
    ppermute x21, starting transfers between devices, shift(): lax.ppermute(value, axis, [(i, (i + distance) % size) for i in range(size)])  33.1 us
    pallas_call x4, Pallas kernels, project(): pl.pallas_call(project_kernel, grid_spec=pltpu.PrefetchScalarGridSpec(num...  22.4 us
    ppermute x6, waiting for transfers between devices, carry_on(): up = lax.ppermute(up, axis, [(i, i + 1) for i in range(hop - 1, size - 1)])  21 us
  transfers between devices with their start and end apart: 61, of which 25 were waited for; matrix products, arithmetic and copies ran while one was open for 10% of the time, Pallas kernels for 28%

profile of v4, /device:TPU:0, one launch (start us, length us, event | category | flops | bytes accessed | tf_op | source)
XLA Modules:
  0.0 583.3 jit_solution(8874550877718697844)
XLA Ops:
  25.2 14.9 %collective-permute-done = bf16[384,1024]{1,0:T(8,128)(2,1)S(1)} collective-permute-done((bf16[384,1024]{1,0:T(8,128)(2,1)S(1)}, bf16[384,1024]{1,0:T(8,128)(2,1)S(1)}, u32[]{:S(2)}, u32[]{:S(2)}) %collective-permute-start) | collective-permute-done | bytes 786464 | tf_op jit(solution)/shard_map/ppermute | solution.py:757
  47.7 17.3 %collective-permute-done.3 = bf16[384,1024]{1,0:T(8,128)(2,1)} collective-permute-done((bf16[384,1024]{1,0:T(8,128)(2,1)S(1)}, bf16[384,1024]{1,0:T(8,128)(2,1)}, u32[]{:S(2)}, u32[]{:S(2)}) %collective-permute-start.3) | collective-permute-done | bytes 786464 | tf_op jit(solution)/shard_map/ppermute | solution.py:758
  67.6 16.8 %collective-permute-done.16 = bf16[384,1024]{1,0:T(8,128)(2,1)} collective-permute-done((bf16[384,1024]{1,0:T(8,128)(2,1)}, bf16[384,1024]{1,0:T(8,128)(2,1)}, u32[]{:S(2)}, u32[]{:S(2)}) %collective-permute-start.16) | collective-permute-done | bytes 786464 | tf_op jit(solution)/shard_map/ppermute | solution.py:758
  97.6 6.1 %project.4 = (bf16[2048,256]{1,0:T(8,128)(2,1)}, bf16[2048,256]{1,0:T(8,128)(2,1)}, bf16[2048,256]{1,0:T(8,128)(2,1)}, f32[2048,256]{1,0:T(8,128)}, f32[2048,256]{1,0:T(8,128)}) custom-call(s32[1]{0:T(128)} %bitcast.2.index_ref, bf16[512,1024]{1,0:T(8,128)(2,1)} %refs_0_, bf16[1024,768]{1,0:T(8,128)(2,1)} %all-gather.4.cloned.1.call-done.wq_ref.wk_ref.wv_ref, ...), custom_call_target="tpu_custom_call" | custom-call | flops 805306368 | bytes 2097152 | tf_op jit(solution)/shard_map/project/pallas_call | solution.py:268
  103.7 6.0 %collective-permute-done.4 = bf16[512,1024]{1,0:T(8,128)(2,1)S(1)} collective-permute-done((bf16[512,1024]{1,0:T(8,128)(2,1)S(1)}, bf16[512,1024]{1,0:T(8,128)(2,1)S(1)}, u32[]{:S(2)}, u32[]{:S(2)}) %collective-permute-start.4) | collective-permute-done | bytes 1048608 | tf_op jit(solution)/shard_map/ppermute | solution.py:757
  116.9 21.9 %collective-permute-done.7 = bf16[512,1024]{1,0:T(8,128)(2,1)} collective-permute-done((bf16[512,1024]{1,0:T(8,128)(2,1)S(1)}, bf16[512,1024]{1,0:T(8,128)(2,1)}, u32[]{:S(2)}, u32[]{:S(2)}) %collective-permute-start.7) | collective-permute-done | bytes 1048608 | tf_op jit(solution)/shard_map/ppermute | solution.py:758
  156.2 6.4 %collective-permute-done.9 = bf16[512,1024]{1,0:T(8,128)(2,1)} collective-permute-done((bf16[512,1024]{1,0:T(8,128)(2,1)}, bf16[512,1024]{1,0:T(8,128)(2,1)}, u32[]{:S(2)}, u32[]{:S(2)}) %collective-permute-start.9) | collective-permute-done | bytes 1048608 | tf_op jit(solution)/shard_map/ppermute | solution.py:758
  176.8 20.3 %attend.1 = (bf16[2048,256]{1,0:T(8,128)(2,1)}, f32[2048,256]{1,0:T(8,128)}, f32[4,2048]{1,0:T(4,128)}) custom-call(bf16[2048,256]{1,0:T(8,128)(2,1)} %get-tuple-element.149.q_ref, bf16[2048,256]{1,0:T(8,128)(2,1)} %get-tuple-element.150.k_ref, bf16[2048,256]{1,0:T(8,128)(2,1)} %get-tuple-element.151.v_ref, s32[2048,1]{1,0:T(8,128)} %copy.40.start_ref), custom_call_target="tpu_custom_call" | custom-call | flops 20000000000 | bytes 4194304 | tf_op jit(solution)/shard_map/attend/pallas_call | solution.py:113
  203.4 6.1 %collective-permute-done.10.refs_1_ = bf16[512,256]{1,0:T(8,128)(2,1)S(1)} collective-permute-done((bf16[512,256]{1,0:T(8,128)(2,1)S(1)}, bf16[512,256]{1,0:T(8,128)(2,1)S(1)}, u32[]{:S(2)}, u32[]{:S(2)}) %collective-permute-start.10) | collective-permute-done | bytes 262176 | tf_op jit(solution)/shard_map/ppermute | solution.py:753
  209.5 5.7 collective-permute-done.11.refs_2_
  216.0 7.9 %mix.1 = (f32[512,1024]{1,0:T(8,128)}, f32[512,1024]{1,0:T(8,128)}, bf16[512,1024]{1,0:T(8,128)(2,1)}, bf16[1024,512]{1,0:T(8,128)(2,1)}) custom-call(bf16[512,256]{1,0:T(8,128)(2,1)} %get-tuple-element.230.refs_0_, bf16[512,256]{1,0:T(8,128)(2,1)} %copy-done.11, bf16[512,256]{1,0:T(8,128)(2,1)} %copy-done.12, bf16[512,256]{1,0:T(8,128)(2,1)} %copy-done.13, ...), custom_call_target="tpu_custom_call" | custom-call | flops 1073741824 | bytes 7340032 | tf_op jit(solution)/shard_map/mix/pallas_call | solution.py:471
  223.9 33.2 %feed.1 = (f32[512,4096]{1,0:T(8,128)}, f32[512,4096]{1,0:T(8,128)}, bf16[512,4096]{1,0:T(8,128)(2,1)}, bf16[512,1024]{1,0:T(8,128)(2,1)}, f32[512,1024]{1,0:T(8...) custom-call(bf16[512,1024]{1,0:T(8,128)(2,1)} %get-tuple-element.153.m_ref, ...), custom_call_target="tpu_custom_call" | custom-call | flops 12884901888 | bytes 46137344 | tf_op jit(solution)/shard_map/feed/pallas_call | solution.py:585
  257.1 15.0 %feed_back_first.1 = (bf16[3,1024,1024]{2,1,0:T(8,128)(2,1)}, f32[2,1024]{1,0:T(2,128)}, f32[512,1024]{1,0:T(8,128)}) custom-call(bf16[512,1024]{1,0:T(8,128)(2,1)} %get-tuple-element.158.refs_0_, bf16[1024,512]{1,0:T(8,128)(2,1)} %get-tuple-element.159.refs_1_, bf16[1024,512]{1,0:T(8,128)(2,1)} %get-tuple-element.160.refs_2_, ...), custom_call_target="tpu_custom_call" | custom-call | flops 6442450944 | bytes 17825792 | tf_op jit(solution)/shard_map/feed_back_first/pallas_call | solution.py:710
  272.2 40.2 %feed_back_last.1 = (bf16[3,1024,3072]{2,1,0:T(8,128)(2,1)}, f32[2,3072]{1,0:T(2,128)}, f32[512,1024]{1,0:T(8,128)}, bf16[512,1024]{1,0:T(8,128)(2,1)}, f32[1,1024]{1,0:T(1,128)}) custom-call(bf16[512,1024]{1,0:T(8,128)(2,1)} %get-tuple-element.158.refs_0_, bf16[1024,512]{1,0:T(8,128)(2,1)} %get-tuple-element.159.refs_1_, ...), custom_call_target="tpu_custom_call" | custom-call | flops 19327352832 | bytes 53477376 | tf_op jit(solution)/shard_map/feed_back_last/pallas_call | solution.py:710
  315.3 5.9 %collective-permute-start.21 = (bf16[512,256]{1,0:T(8,128)(2,1)}, bf16[512,256]{1,0:T(8,128)(2,1)}, u32[]{:S(2)}, u32[]{:S(2)}) collective-permute-start(bf16[512,256]{1,0:T(8,128)(2,1)} %convolution_convert_fusion.3), channel_id=1, source_target_pairs={{0,3},{1,0},{2,1},{3,2},{4,7},{5,4},{6,5},{7,6},{8,11},{9,8},{10,9... | collective-permute-start | bytes 786440 | tf_op jit(solution)/shard_map/ppermute | solution.py:753
  332.2 23.2 %collective-permute-done.22 = bf16[512,256]{1,0:T(8,128)(2,1)S(1)} collective-permute-done((bf16[512,256]{1,0:T(8,128)(2,1)}, bf16[512,256]{1,0:T(8,128)(2,1)S(1)}, u32[]{:S(2)}, u32[]{:S(2)}) %collective-permute-start.22) | collective-permute-done | bytes 262176 | tf_op jit(solution)/shard_map/ppermute | solution.py:753
  359.6 41.2 %attend_back.1 = (f32[2048,256]{1,0:T(8,128)}, f32[2048,256]{1,0:T(8,128)}, f32[2048,256]{1,0:T(8,128)}) custom-call(bf16[2048,256]{1,0:T(8,128)(2,1)} %get-tuple-element.149.q_ref, bf16[2048,256]{1,0:T(8,128)(2,1)} %fusion.3.do_ref, bf16[2048,256]{1,0:T(8,128)(2,1)} %get-tuple-element.150.k_ref, bf16[2048,256]{1,0:T(8,128)(2,1)} %get-tuple-element.151.v_ref, ...), custom_call_target="tpu_custom_call" | custom-call | flops 40000000000 | bytes 10485760 | tf_op jit(solution)/shard_map/attend_back/pallas_call | solution.py:191
  403.8 20.9 %project_back.1 = (bf16[2048,768]{1,0:T(8,128)(2,1)}, bf16[2048,1024]{1,0:T(8,128)(2,1)}, f32[1,256]{1,0:T(1,128)}) custom-call(s32[1]{0:T(128)} %bitcast.15.index_ref, f32[2048,256]{1,0:T(8,128)} %get-tuple-element.182.dq_ref, f32[2048,256]{1,0:T(8,128)} %get-tuple-element.183.dk_ref, f32[2048,256]{1,0:T(8,128)} %get-tuple-element.184.dv_ref, ...), custom_call_target="tpu_custom_call" | custom-call | flops 4294967296 | bytes 16777216 | tf_op jit(solution)/shard_map/project_back/pallas_call | solution.py:353
  437.9 7.6 %projection_grads.1 = bf16[1024,768]{1,0:T(8,128)(2,1)} custom-call(bf16[512,1024]{1,0:T(8,128)(2,1)} %refs_0_, bf16[512,1024]{1,0:T(8,128)(2,1)} %broadcast_select_fusion.2.x_ref.refs_1_, bf16[512,1024]{1,0:T(8,128)(2,1)} %broadcast_select_fusion.1.x_ref.refs_2_, bf16[512,1024]{1,0:T(8,128)(2,1)} %broadcast_select_fusion.x_ref.refs_3_, ...), custom_call_target="tpu_custom_call" | custom-call | flops 3221225472 | bytes 8388608 | tf_op jit(solution)/shard_map/projection_grads/pallas_call | solution.py:397
  445.6 9.3 %collective-permute-done.27 = bf16[512,1024]{1,0:T(8,128)(2,1)} collective-permute-done((bf16[512,1024]{1,0:T(8,128)(2,1)}, bf16[512,1024]{1,0:T(8,128)(2,1)}, u32[]{:S(2)}, u32[]{:S(2)}) %collective-permute-start.27) | collective-permute-done | bytes 1048608 | tf_op jit(solution)/shard_map/ppermute | solution.py:766
  463.3 10.2 %collective-permute-done.40 = bf16[1,128,1024]{2,1,0:T(8,128)(2,1)S(1)} collective-permute-done((bf16[1,128,1024]{2,1,0:T(8,128)(2,1)S(1)}, bf16[1,128,1024]{2,1,0:T(8,128)(2,1)S(1)}, u32[]{:S(2)}, u32[]{:S(2)}) %collective-permute-start.40) | collective-permute-done | bytes 262176 | tf_op jit(solution)/shard_map/ppermute | solution.py:781
  487.4 20.7 %collective-permute-done.43 = bf16[128,256]{1,0:T(8,128)(2,1)S(1)} collective-permute-done((bf16[128,256]{1,0:T(8,128)(2,1)S(1)}, bf16[128,256]{1,0:T(8,128)(2,1)S(1)}, u32[]{:S(2)}, u32[]{:S(2)}) %collective-permute-start.43) | collective-permute-done | bytes 65568 | tf_op jit(solution)/shard_map/ppermute | solution.py:753
  530.2 5.6 collective-permute-start.36
  540.8 12.6 %collective-permute-done.44 = bf16[3,128,1024]{2,1,0:T(8,128)(2,1)S(1)} collective-permute-done((bf16[3,128,1024]{2,1,0:T(8,128)(2,1)S(1)}, bf16[3,128,1024]{2,1,0:T(8,128)(2,1)S(1)}, u32[]{:S(2)}, u32[]{:S(2)}) %collective-permute-start.44) | collective-permute-done | bytes 786464 | tf_op jit(solution)/shard_map/ppermute | solution.py:753
  (271 shorter events, 193.5 us)
Async XLA Ops:
  7.2 90.5 %all-gather.4.cloned.1.call-start = ((), (), s32[]{:S(2)}) async-start(), calls=%async_computation.2 | async-start | bytes 1769472 | tf_op jit(solution)/shard_map/all_gather | solution.py:852
  9.2 194.2 %all-gather.6.cloned.1.call-start = ((), (), s32[]{:S(2)}) async-start(), calls=%async_computation.3 | async-start | bytes 2359296 | tf_op jit(solution)/shard_map/all_gather | solution.py:856
  21.6 202.3 %all-gather.8.cloned.1.call-start = ((), (), s32[]{:S(2)}) async-start(), calls=%async_computation.4 | async-start | bytes 28311552 | tf_op jit(solution)/shard_map/all_gather | solution.py:863
  87.5 270.5 %reduce-scatter.3.cloned.1.call-start = ((), (), s32[]{:S(2)}) async-start(), calls=%async_computation.5 | async-start | bytes 7077888 | tf_op jit(solution)/shard_map/reduce_scatter | solution.py:926
  140.9 58.2 %collective-permute-start.18 = (f32[2,1024]{1,0:T(2,128)S(1)}, f32[2,1024]{1,0:T(2,128)S(1)}, u32[]{:S(2)}, u32[]{:S(2)}) collective-permute-start(f32[2,1024]{1,0:T(2,128)S(1)} %copy-done.26), channel_id=1, source_target_pairs={{0,1},{1,2},{2,3},{3,0},{4,5},{5,6},{6,7},{7,4},{8,9},{9,10},{10,1... | collective-permute-start | bytes 24584 | tf_op jit(solution)/shard_map/ppermute | solution.py:753
  144.5 58.8 %collective-permute-start.19 = (f32[2,1024]{1,0:T(2,128)S(1)}, f32[2,1024]{1,0:T(2,128)S(1)}, u32[]{:S(2)}, u32[]{:S(2)}) collective-permute-start(f32[2,1024]{1,0:T(2,128)S(1)} %copy-done.26), channel_id=1, source_target_pairs={{0,3},{1,0},{2,1},{3,2},{4,7},{5,4},{6,5},{7,6},{8,11},{9,8},{10,9... | collective-permute-start | bytes 24584 | tf_op jit(solution)/shard_map/ppermute | solution.py:753
  145.0 58.4 %collective-permute-start.20 = (f32[2,1024]{1,0:T(2,128)S(1)}, f32[2,1024]{1,0:T(2,128)S(1)}, u32[]{:S(2)}, u32[]{:S(2)}) collective-permute-start(f32[2,1024]{1,0:T(2,128)S(1)} %copy-done.26), channel_id=1, source_target_pairs={{0,2},{1,3},{2,0},{3,1},{4,6},{5,7},{6,4},{7,5},{8,10},{9,11},{10,... | collective-permute-start | bytes 24584 | tf_op jit(solution)/shard_map/ppermute | solution.py:753
  272.1 244.7 %reduce-scatter.5.cloned.1.call-start = ((), (), s32[]{:S(2)}) async-start(), calls=%async_computation.6 | async-start | bytes 21233664 | tf_op jit(solution)/shard_map/reduce_scatter | solution.py:930
  322.4 33.0 %collective-permute-start.22 = (bf16[512,256]{1,0:T(8,128)(2,1)}, bf16[512,256]{1,0:T(8,128)(2,1)S(1)}, u32[]{:S(2)}, u32[]{:S(2)}) collective-permute-start(bf16[512,256]{1,0:T(8,128)(2,1)} %convolution_convert_fusion.2), channel_id=1, source_target_pairs={{0,2},{1,3},{2,0},{3,1},{4,6},{5,7},{6,4},{7,5},{8,10},{9,11},{10,... | collective-permute-start | bytes 786440 | tf_op jit(solution)/shard_map/ppermute | solution.py:753
  324.3 31.8 %collective-permute-start.23 = (bf16[512,256]{1,0:T(8,128)(2,1)}, bf16[512,256]{1,0:T(8,128)(2,1)S(1)}, u32[]{:S(2)}, u32[]{:S(2)}) collective-permute-start(bf16[512,256]{1,0:T(8,128)(2,1)} %convolution_convert_fusion.1), channel_id=1, source_target_pairs={{0,1},{1,2},{2,3},{3,0},{4,5},{5,6},{6,7},{7,4},{8,9},{9,10},{10,1... | collective-permute-start | bytes 786440 | tf_op jit(solution)/shard_map/ppermute | solution.py:753
  358.0 42.8 %collective-permute-start.24 = (bf16[3,128,1024]{2,1,0:T(8,128)(2,1)}, bf16[3,128,1024]{2,1,0:T(8,128)(2,1)S(1)}, u32[]{:S(2)}, u32[]{:S(2)}) collective-permute-start(bf16[3,128,1024]{2,1,0:T(8,128)(2,1)} %reduce-scatter.3.cloned.1.call-done), channel_id=1, source_target_pairs={{0,2},{1,3},{2,0},{3,1},{4,6},{5,7},{6,4},{7,5},{8,10},{9,11},{10,... | collective-permute-start | bytes 2359304 | tf_op jit(solution)/shard_map/ppermute | solution.py:753
  358.0 42.8 %collective-permute-start.25 = (f32[10,1024]{1,0:T(8,128)S(1)}, f32[10,1024]{1,0:T(8,128)S(1)}, u32[]{:S(2)}, u32[]{:S(2)}) collective-permute-start(f32[10,1024]{1,0:T(8,128)S(1)} %pad_maximum_fusion.4), channel_id=1, source_target_pairs={{0,1},{1,0},{2,3},{3,2},{4,5},{5,4},{6,7},{7,6},{8,9},{9,8},{10,11... | collective-permute-start | bytes 122888 | tf_op jit(solution)/shard_map/ppermute | solution.py:789
  359.6 75.2 %collective-permute-start.38 = (bf16[4,128,1024]{2,1,0:T(8,128)(2,1)S(1)}, bf16[4,128,1024]{2,1,0:T(8,128)(2,1)}, u32[]{:S(2)}, u32[]{:S(2)}) collective-permute-start(bf16[4,128,1024]{2,1,0:T(8,128)(2,1)S(1)} %dynamic-slice_bitcast_fusion), channel_id=1, source_target_pairs={{0,4},{4,0},{8,12},{12,8},{16,20},{20,16},{24,28},{28,24},{1,5},{5... | collective-permute-start | bytes 3145736 | tf_op jit(solution)/shard_map/ppermute | solution.py:781
  427.9 27.0 %collective-permute-start.27 = (bf16[512,1024]{1,0:T(8,128)(2,1)}, bf16[512,1024]{1,0:T(8,128)(2,1)}, u32[]{:S(2)}, u32[]{:S(2)}) collective-permute-start(bf16[512,1024]{1,0:T(8,128)(2,1)} %get-tuple-element.224), channel_id=1, source_target_pairs={{0,1},{4,5},{8,9},{12,13},{16,17},{20,21},{24,25},{28,29}} | collective-permute-start | bytes 3145736 | tf_op jit(solution)/shard_map/ppermute | solution.py:766
  434.5 28.7 %collective-permute-start.47 = (f32[1,256]{1,0:T(1,128)S(1)}, f32[1,256]{1,0:T(1,128)S(1)}, u32[]{:S(2)}, u32[]{:S(2)}) collective-permute-start(f32[1,256]{1,0:T(1,128)S(1)} %copy-done.30), channel_id=1, source_target_pairs={{0,1},{1,2},{2,3},{3,0},{4,5},{5,6},{6,7},{7,4},{8,9},{9,10},{10,1... | collective-permute-start | bytes 3080 | tf_op jit(solution)/shard_map/ppermute | solution.py:753
  436.4 25.0 %collective-permute-start.39 = (bf16[2,128,1024]{2,1,0:T(8,128)(2,1)S(1)}, bf16[2,128,1024]{2,1,0:T(8,128)(2,1)S(1)}, u32[]{:S(2)}, u32[]{:S(2)}) collective-permute-start(bf16[2,128,1024]{2,1,0:T(8,128)(2,1)S(1)} %dynamic-slice_bitcast_fusion.2), channel_id=1, source_target_pairs={{0,8},{4,12},{8,0},{12,4},{16,24},{20,28},{24,16},{28,20},{1,9},{5... | collective-permute-start | bytes 1572872 | tf_op jit(solution)/shard_map/ppermute | solution.py:781
  476.5 40.3 %collective-permute-start.30 = (bf16[512,1024]{1,0:T(8,128)(2,1)S(1)}, bf16[512,1024]{1,0:T(8,128)(2,1)}, u32[]{:S(2)}, u32[]{:S(2)}) collective-permute-start(bf16[512,1024]{1,0:T(8,128)(2,1)S(1)} %get-tuple-element.222), channel_id=1, source_target_pairs={{0,1},{1,2},{4,5},{5,6},{8,9},{9,10},{12,13},{13,14},{16,17},{17,1... | collective-permute-start | bytes 3145736 | tf_op jit(solution)/shard_map/ppermute | solution.py:766
  479.0 37.8 %collective-permute-start.31 = (bf16[512,1024]{1,0:T(8,128)(2,1)S(1)}, bf16[512,1024]{1,0:T(8,128)(2,1)}, u32[]{:S(2)}, u32[]{:S(2)}) collective-permute-start(bf16[512,1024]{1,0:T(8,128)(2,1)S(1)} %get-tuple-element.221), channel_id=1, source_target_pairs={{2,1},{3,2},{6,5},{7,6},{10,9},{11,10},{14,13},{15,14},{18,17},{19... | collective-permute-start | bytes 3145736 | tf_op jit(solution)/shard_map/ppermute | solution.py:767
  480.7 27.4 %collective-permute-start.43 = (bf16[128,256]{1,0:T(8,128)(2,1)S(1)}, bf16[128,256]{1,0:T(8,128)(2,1)S(1)}, u32[]{:S(2)}, u32[]{:S(2)}) collective-permute-start(bf16[128,256]{1,0:T(8,128)(2,1)S(1)} %get-tuple-element.235), channel_id=1, source_target_pairs={{0,1},{1,2},{2,3},{3,0},{4,5},{5,6},{6,7},{7,4},{8,9},{9,10},{10,1... | collective-permute-start | bytes 196616 | tf_op jit(solution)/shard_map/ppermute | solution.py:753
  481.7 29.3 %collective-permute-start.42 = (bf16[128,256]{1,0:T(8,128)(2,1)S(1)}, bf16[128,256]{1,0:T(8,128)(2,1)S(1)}, u32[]{:S(2)}, u32[]{:S(2)}) collective-permute-start(bf16[128,256]{1,0:T(8,128)(2,1)S(1)} %get-tuple-element.236), channel_id=1, source_target_pairs={{0,2},{1,3},{2,0},{3,1},{4,6},{5,7},{6,4},{7,5},{8,10},{9,11},{10,... | collective-permute-start | bytes 196616 | tf_op jit(solution)/shard_map/ppermute | solution.py:753
  484.4 27.6 %collective-permute-start.41 = (bf16[128,256]{1,0:T(8,128)(2,1)S(1)}, bf16[128,256]{1,0:T(8,128)(2,1)S(1)}, u32[]{:S(2)}, u32[]{:S(2)}) collective-permute-start(bf16[128,256]{1,0:T(8,128)(2,1)S(1)} %get-tuple-element.234), channel_id=1, source_target_pairs={{0,3},{1,0},{2,1},{3,2},{4,7},{5,4},{6,5},{7,6},{8,11},{9,8},{10,9... | collective-permute-start | bytes 196616 | tf_op jit(solution)/shard_map/ppermute | solution.py:753
  518.6 34.8 %collective-permute-start.44 = (bf16[3,128,1024]{2,1,0:T(8,128)(2,1)S(1)}, bf16[3,128,1024]{2,1,0:T(8,128)(2,1)S(1)}, u32[]{:S(2)}, u32[]{:S(2)}) collective-permute-start(bf16[3,128,1024]{2,1,0:T(8,128)(2,1)S(1)} %get-tuple-element.225), channel_id=1, source_target_pairs={{0,3},{1,0},{2,1},{3,2},{4,7},{5,4},{6,5},{7,6},{8,11},{9,8},{10,9... | collective-permute-start | bytes 2359304 | tf_op jit(solution)/shard_map/ppermute | solution.py:753
  528.9 44.3 %collective-permute-start.37 = (bf16[512,1024]{1,0:T(8,128)(2,1)}, bf16[512,1024]{1,0:T(8,128)(2,1)S(1)}, u32[]{:S(2)}, u32[]{:S(2)}) collective-permute-start(bf16[512,1024]{1,0:T(8,128)(2,1)} %get-tuple-element.220), channel_id=1, source_target_pairs={{1,0},{2,1},{3,2},{5,4},{6,5},{7,6},{9,8},{10,9},{11,10},{13,12},{... | collective-permute-start | bytes 3145736 | tf_op jit(solution)/shard_map/ppermute | solution.py:767
  530.2 43.0 %collective-permute-start.36 = (bf16[512,1024]{1,0:T(8,128)(2,1)}, bf16[512,1024]{1,0:T(8,128)(2,1)}, u32[]{:S(2)}, u32[]{:S(2)}) collective-permute-start(bf16[512,1024]{1,0:T(8,128)(2,1)} %get-tuple-element.219), channel_id=1, source_target_pairs={{0,1},{1,2},{2,3},{4,5},{5,6},{6,7},{8,9},{9,10},{10,11},{12,13},{... | collective-permute-start | bytes 3145736 | tf_op jit(solution)/shard_map/ppermute | solution.py:766
  (68 other events, 946.3 us)
Sparse Core Ops, SparseCore 0:
  10.5 28.2 all-gather.3
  41.2 27.7 all-gather.5
  87.6 123.3 all-gather.7
  272.2 64.4 reduce-scatter.2
  340.1 136.8 reduce-scatter.4

commit v5 on v4

--- a/solution.py
+++ b/solution.py
@@ -236,9 +236,17 @@
     return table if table.shape[1] == width else jnp.concatenate([table] * (width // 128), axis=1)
 
 
-def project_kernel(index_ref, x_ref, wq_ref, wk_ref, wv_ref, cos_ref, sin_ref, gain_ref, *refs):
+def added(refs):
+    total = refs[0][...]
+    for ref in refs[1:]:
+        total = total + ref[...]
+    return total
+
+
+def project_kernel(count, index_ref, *refs):
+    wq_ref, wk_ref, wv_ref, cos_ref, sin_ref, gain_ref = refs[count : count + 6]
     q_ref, k_ref, v_ref, xq_ref, xk_ref = refs[-5:]
-    x = x_ref[...]
+    x = added(refs[:count])
     width = q_ref.shape[1]
     cosine = widen(cos_ref[...], width)
     sine = widen(sin_ref[...], width)
@@ -252,8 +260,9 @@
     v_ref[...] = dot_nn(x, wv_ref[...]).astype(bf16)
 
 
-def project(index, x, weights, cosine, sine, gain, length, previous):
-    rows, model = x.shape
+def project(index, parts, weights, cosine, sine, gain, length, previous):
+    rows, model = parts[0].shape
+    count = len(parts)
     width = gain.shape[1]
     part = min(256, rows)
     per = rows // part
@@ -266,12 +275,12 @@
     low = jax.ShapeDtypeStruct((length, width), bf16)
     wide = jax.ShapeDtypeStruct((length, width), f32)
     return pl.pallas_call(
-        project_kernel,
+        functools.partial(project_kernel, count),
         grid_spec=pltpu.PrefetchScalarGridSpec(
             num_scalar_prefetch=1,
             grid=(per,),
-            in_specs=[
-                pl.BlockSpec((part, model), lambda i, at: (i, 0)),
+            in_specs=[pl.BlockSpec((part, model), lambda i, at: (i, 0))] * count
+            + [
                 column(0),
                 column(1),
                 column(2),
@@ -283,12 +292,12 @@
             out_specs=[out] * 5,
         ),
         out_shape=[low, low, low, wide, wide],
-        input_output_aliases={8 + i: i for i in range(len(previous))},
+        input_output_aliases={7 + count + i: i for i in range(len(previous))},
         cost_estimate=pl.CostEstimate(
             flops=6 * rows * model * width, bytes_accessed=8 * model * width, transcendentals=0
         ),
         name="project",
-    )(index, x, weights, weights, weights, cosine, sine, gain, *previous)
+    )(index, *parts, weights, weights, weights, cosine, sine, gain, *previous)
 
 
 def project_back_kernel(
@@ -305,8 +314,8 @@
     sin_ref,
     gain_ref,
     grad_ref,
-    piece_ref,
     gain_grad_ref,
+    *piece_refs,
 ):
     @pl.when(pl.program_id(0) == 0)
     def _():
@@ -328,11 +337,17 @@
         raw_grad = turned_grad * cosine - partner(turned_grad) * sine
         lows.append(raw_grad.astype(bf16))
     lows.append(dv_ref[...].astype(bf16))
-    piece = jnp.zeros(piece_ref.shape, f32)
+    piece = jnp.zeros(piece_refs[0].shape, f32)
     for m, w_ref in enumerate((wq_ref, wk_ref, wv_ref)):
         grad_ref[:, m * width : (m + 1) * width] = lows[m]
         piece = piece + dot_nt(lows[m], w_ref[...])
-    piece_ref[...] = piece.astype(bf16)
+    low = piece.astype(bf16)
+    block = pl.program_id(0) // (pl.num_programs(0) // len(piece_refs))
+    for d, piece_ref in enumerate(piece_refs):
+
+        @pl.when(block == d)
+        def _(piece_ref=piece_ref):
+            piece_ref[...] = low
 
 
 def project_back(index, grads, turned, weights, cosine, sine, gain, rows):
@@ -347,6 +362,9 @@
 
     def turn(i, at):
         return (lax.rem(at[0] * per + i, blocks), 0)
+
+    def piece_block(d):
+        return pl.BlockSpec((part, model), lambda i, at: (jnp.clip(i - d * per, 0, per - 1), 0))
 
     tall = pl.BlockSpec((part, width), turn)
     table = pl.BlockSpec((part, 128), turn)
@@ -360,15 +378,15 @@
             + [pl.BlockSpec((1, width), lambda i, at: (0, 0))],
             out_specs=[
                 pl.BlockSpec((part, 3 * width), lambda i, at: (i, 0)),
-                pl.BlockSpec((part, model), lambda i, at: (i, 0)),
                 pl.BlockSpec((1, width), lambda i, at: (0, 0)),
-            ],
+            ]
+            + [piece_block(d) for d in range(length // rows)],
         ),
         out_shape=[
             jax.ShapeDtypeStruct((length, 3 * width), bf16),
-            jax.ShapeDtypeStruct((length, model), bf16),
             jax.ShapeDtypeStruct((1, width), f32),
-        ],
+        ]
+        + [jax.ShapeDtypeStruct((rows, model), bf16)] * (length // rows),
         cost_estimate=pl.CostEstimate(
             flops=8 * length * model * width,
             bytes_accessed=32 * length * width,
@@ -378,35 +396,37 @@
     )(index, *grads, *turned, weights, weights, weights, cosine, sine, gain)
 
 
-def projection_grads_kernel(count, *refs):
-    hidden = refs[:count]
-    grad_ref, out_ref = refs[count:]
-    rows = hidden[0].shape[0]
-    total = dot_tn(hidden[0][...], grad_ref[:rows, :])
-    for d in range(1, count):
-        total = total + dot_tn(hidden[d][...], grad_ref[d * rows : (d + 1) * rows, :])
+def projection_grads_kernel(counts, *refs):
+    grad_ref, out_ref = refs[-2:]
+    total = None
+    for d, count in enumerate(counts):
+        hidden = added(refs[:count])
+        refs = refs[count:]
+        rows = hidden.shape[0]
+        part = dot_tn(hidden, grad_ref[d * rows : (d + 1) * rows, :])
+        total = part if total is None else total + part
     out_ref[...] = total.astype(bf16)
 
 
 def projection_grads(hidden, qkv_grad):
-    count = len(hidden)
-    rows, model = hidden[0].shape
-    width = qkv_grad.shape[1]
+    rows, model = hidden[0][0].shape
+    length, width = qkv_grad.shape
+    counts = tuple(len(parts) for parts in hidden)
     part = 256
-    column = pl.BlockSpec((rows, part), lambda i: (0, i))
     return pl.pallas_call(
-        functools.partial(projection_grads_kernel, count),
+        functools.partial(projection_grads_kernel, counts),
         grid=(model // part,),
-        in_specs=[column] * count + [pl.BlockSpec(qkv_grad.shape, lambda i: (0, 0))],
+        in_specs=[pl.BlockSpec((rows, part), lambda i: (0, i))] * sum(counts)
+        + [pl.BlockSpec(qkv_grad.shape, lambda i: (0, 0))],
         out_specs=pl.BlockSpec((part, width), lambda i: (i, 0)),
         out_shape=jax.ShapeDtypeStruct((model, width), bf16),
         cost_estimate=pl.CostEstimate(
-            flops=2 * rows * count * model * width,
-            bytes_accessed=4 * rows * count * model,
+            flops=2 * length * model * width,
+            bytes_accessed=8 * length * model,
             transcendentals=0,
         ),
         name="projection_grads",
-    )(*hidden, qkv_grad)
+    )(*[x for parts in hidden for x in parts], qkv_grad)
 
 
 def out_grads_kernel(count, *refs):
@@ -768,21 +788,15 @@
     return up, down
 
 
-def halving(value, axis, size):
-    rows, width = value.shape[0] // size, value.shape[1]
-    index = lax.axis_index(axis)
-    value = value.reshape(size, rows, width)
-    step = 1
-    while step < size:
-        bit = (index // step) % 2
-        pairs = value.reshape(-1, 2, rows, width)
-        sent = lax.dynamic_index_in_dim(pairs, 1 - bit, 1, False)
-        kept = lax.dynamic_index_in_dim(pairs, bit, 1, False)
-        other = lax.ppermute(sent, axis, [(i, i ^ step) for i in range(size)])
-        value = kept.astype(f32) + other.astype(f32)
-        step *= 2
-        value = value if step == size else value.astype(bf16)
-    return value.reshape(rows, width).astype(f32)
+def halving(value, axis, size, step):
+    count, rows, width = value.shape
+    bit = (lax.axis_index(axis) // step) % 2
+    pairs = value.reshape(count // 2, 2, rows, width)
+    sent = lax.dynamic_index_in_dim(pairs, 1 - bit, 1, False)
+    kept = lax.dynamic_index_in_dim(pairs, bit, 1, False)
+    other = lax.ppermute(sent, axis, [(i, i ^ step) for i in range(size)])
+    value = kept.astype(f32) + other.astype(f32)
+    return value[0] if 2 * step == size else value.astype(bf16)
 
 
 def exchange_add(value, axis, size, step):
@@ -835,16 +849,8 @@
     def gather(value):
         return [value] + [shift(value, "tensor", d, nt) for d in range(1, nt)]
 
-    def line(value):
-        ups, downs = [value], [value]
-        for hop in range(1, nt):
-            up, down = carry_on(ups[-1], downs[-1], hop, "tensor", nt)
-            ups.append(up)
-            downs.append(down)
-        return ups, downs
-
-    def join(ups, downs, d):
-        return ups[0] if d == 0 else jnp.where(me >= d, ups[d], downs[nt - d])
+    def both(ups, downs, d):
+        return (ups[0],) if d == 0 else (ups[d], downs[nt - d])
 
     middle_hop = nt // 2
     order = [d for d in range(nt) if d != middle_hop] + [middle_hop]
@@ -852,16 +858,20 @@
     qkv_full = lax.all_gather(
         jnp.concatenate([attn_low[0], attn_low[1], attn_low[2]], axis=1), "dp", axis=0, tiled=True
     )
-    ups, downs = line(mlp_weight.astype(bf16).reshape(3 * shard, hidden_width))
-    out_full = lax.all_gather(
-        jnp.concatenate(gather(attn_low[3]), axis=1), "dp", axis=0, tiled=True
-    )
-    before = max(1, nt - 2)
-    hidden_in, ups[before], downs[before] = lax.optimization_barrier(
-        (hidden_in, ups[before], downs[before])
-    )
+    mlp_low = mlp_weight.astype(bf16).reshape(3 * shard, hidden_width)
+    out_low = attn_low[3]
+    ups, downs = [mlp_low], [mlp_low]
+    for hop in range(1, nt):
+        if hop == 2:
+            ups[1], downs[1], out_low = lax.optimization_barrier((ups[1], downs[1], out_low))
+        if hop == nt - 1:
+            ups[-1], downs[-1], hidden_in = lax.optimization_barrier((ups[-1], downs[-1], hidden_in))
+        up, down = carry_on(ups[-1], downs[-1], hop, "tensor", nt)
+        ups.append(up)
+        downs.append(down)
+    out_full = lax.all_gather(jnp.concatenate(gather(out_low), axis=1), "dp", axis=0, tiled=True)
     mlp_full = lax.all_gather(
-        jnp.concatenate([join(ups, downs, d) for d in order], axis=0), "dp", axis=0, tiled=True
+        jnp.concatenate([sum(both(ups, downs, d)) for d in order], axis=0), "dp", axis=0, tiled=True
     )
     mlp_full = mlp_full.reshape(nd, nt, 3, shard, hidden_width)
     scales_parts = gather(mlp_scales)
@@ -884,7 +894,7 @@
     def projected(hop, state):
         for d in range(nt):
             if (max(d, nt - d) if d else 0) == hop:
-                hidden_parts[d] = join(ups, downs, d)
+                hidden_parts[d] = both(ups, downs, d)
                 index = ((me + nt - d) % nt).reshape(1)
                 state = project(index, hidden_parts[d], qkv_full, cosine, sine, gain, length, state)
         return state
@@ -949,15 +959,19 @@
     far_part, grad_row, out_grad, small = lax.optimization_barrier(
         (far_part, grad_row, out_grad, small)
     )
+    small = advance(small)
+    halvings = doublings(nd)
+    out_sum = halving(out_grad.reshape(nd, shard, -1), "dp", nd, halvings[0])
+    head_grads = attend_back(
+        query_hat, key_hat, value_hat, grad_row, attended_f32, log_sum, starts[None, :], block
+    )
+    head_grads, far_part, small, out_sum = lax.optimization_barrier(
+        (head_grads, far_part, small, out_sum)
+    )
     far_part = shift(far_part, "tensor", -middle_hop, nt)
     small = advance(small)
-    head_grads = attend_back(
-        query_hat, key_hat, value_hat, grad_row, attended_f32, log_sum, starts[None, :], block
-    )
-    head_grads, far_part, small = lax.optimization_barrier((head_grads, far_part, small))
-    small = advance(small)
-    out_sum = halving(out_grad, "dp", nd)
-    qkv_grad, pieces, gain_grad = project_back(
+    out_sum = halving(out_sum, "dp", nd, halvings[1])
+    qkv_grad, gain_grad, *pieces = project_back(
         me.reshape(1),
         head_grads,
         (query_turned, key_turned),
@@ -967,11 +981,14 @@
         gain,
         rows,
     )
-    qkv_grad, pieces, small = lax.optimization_barrier((qkv_grad, pieces, small))
-    pieces = [pieces[d * rows : (d + 1) * rows] for d in range(nt)]
+    qkv_grad, pieces, small, out_sum, far_part = lax.optimization_barrier(
+        (qkv_grad, pieces, small, out_sum, far_part)
+    )
+    for k in halvings[2:]:
+        out_sum = halving(out_sum, "dp", nd, k)
     hidden_turn = [hidden_parts[(nt - d) % nt] for d in range(nt)]
-    qkv_grad = projection_grads(hidden_turn, qkv_grad)
-    gain_row = spread(jnp.concatenate(gather(gain_grad), axis=1), range(nt))
+    qkv_sum = projection_grads(hidden_turn, qkv_grad)
+    qkv_sum = qkv_sum.reshape(nd, shard, -1)
 
     def own_pieces(part, axis, width, places):
         pieces = [
@@ -983,18 +1000,26 @@
     ahead = behind = None
     for hop in range(1, nt):
         if hop == 2:
-            small = advance(small)
-            ahead, behind, qkv_grad, small = lax.optimization_barrier(
-                (ahead, behind, qkv_grad, small)
+            ahead, behind, qkv_sum, out_sum = lax.optimization_barrier(
+                (ahead, behind, qkv_sum, out_sum)
             )
-            small = advance(small)
-            qkv_sum = halving(qkv_grad, "dp", nd)
-            near_part, qkv_sum = lax.optimization_barrier((near_part, qkv_sum))
+            out_pieces = own_pieces(out_sum.astype(bf16), 1, heads_width, range(nt))
+            gain_parts = gather(gain_grad)
         if hop == max(2, nt - 1):
-            ahead, behind, near_part, small = lax.optimization_barrier(
-                (ahead, behind, near_part, small)
+            ahead, behind, near_part, qkv_sum, out_pieces, gain_parts, small = (
+                lax.optimization_barrier(
+                    (ahead, behind, near_part, qkv_sum, out_pieces, gain_parts, small)
+                )
             )
+            near_pieces = own_pieces(near_part, 2, hidden_width, order[:-1])
+            for k in halvings[:2]:
+                qkv_sum = halving(qkv_sum, "dp", nd, k)
+            ahead, behind, qkv_sum = lax.optimization_barrier((ahead, behind, qkv_sum))
         ahead, behind = line_sum(pieces, hop, ahead, behind, "tensor", nt)
+    for k in halvings[2:]:
+        qkv_sum = halving(qkv_sum, "dp", nd, k)
+    near_pieces, qkv_sum = lax.optimization_barrier((near_pieces, qkv_sum))
+    gain_row = spread(jnp.concatenate(gain_parts, axis=1), range(nt))
     while steps:
         small = advance(small)
     total = token_direct + pieces[0].astype(f32)
@@ -1002,9 +1027,7 @@
     rates_grad = small[:2]
     mlp_scales_grad = small[2:].reshape(2, nt * hidden_width)
 
-    out_own = sum(
-        piece.astype(f32) for piece in own_pieces(out_sum.astype(bf16), 1, heads_width, range(nt))
-    )
+    out_own = sum(piece.astype(f32) for piece in out_pieces)
     attn_weight_grad = jnp.stack(
         [qkv_sum[:, m * heads_width : (m + 1) * heads_width] for m in range(3)] + [out_own]
     )
@@ -1018,8 +1041,7 @@
     gain_row = last[:, 4 * heads_width :].reshape(-1)
     attn_new = attn_moved * lax.rsqrt(attn_square + norm_eps)
 
-    mlp_pieces = own_pieces(near_part, 2, hidden_width, order[:-1]) + [far_part]
-    mlp_weight_grad = sum(piece.astype(f32) for piece in mlp_pieces)
+    mlp_weight_grad = sum(piece.astype(f32) for piece in near_pieces + [far_part])
     mlp_one, mlp_two, mlp_moved = adam_moved(
         mlp_weight, mlp_weight_grad, mlp_moment_one, mlp_moment_two
     )

time: 589 us -> 589 us (level)
  waiting for transfers between devices: 205 us -> 214 us
  other arithmetic: 40.1 us -> 31.6 us
    ppermute x11, waiting for transfers between devices: 3.88 us -> 17.7 us  [exchange_add(): lax.ppermute(value, axis, [(i, i ^ step) for i in range(size)])]
    ppermute x21, waiting for transfers between devices: 78.8 us -> 69.4 us  [shift(): lax.ppermute(value, axis, [(i, (i + distance) % size) for i in range(size)])]
    select_n x6 -> x0, other arithmetic: 8.23 us -> none  [join(): return ups[0] if d == 0 else jnp.where(me >= d, ups[d], downs[nt - d])]
  transfers between devices with their start and end apart: 61 -> 61, of which waited for: 25 -> 28; matrix products, arithmetic and copies ran while one was open for 10% -> 8% of each run, Pallas kernels for 28% -> 29%
where the time goes in v5:
time: 589 us; the launch traced here: 583 us
  Pallas kernels  217 us (37%)
  waiting for transfers between devices  214 us (36%)
  starting transfers between devices  82.4 us (14%)
  other arithmetic  31.6 us (5%)
  local copies, waits for them, and re-layouts  18.2 us (3%)
  between operations  15 us (3%)
    ppermute x6, waiting for transfers between devices, carry_on(): lax.ppermute(down, axis, [(i, i - 1) for i in range(1, size - hop + 1)])  75.3 us
    ppermute x21, waiting for transfers between devices, shift(): lax.ppermute(value, axis, [(i, (i + distance) % size) for i in range(size)])  69.4 us
    pallas_call x2, Pallas kernels, feed_back(): pl.pallas_call(feed_back_last_kernel if last else feed_back_first_kernel,...  55.2 us
    pallas_call x1, Pallas kernels, attend_back(): pl.pallas_call(functools.partial(attend_back_kernel, heads, block, block)...  41.3 us
    pallas_call x1, Pallas kernels, feed(): pl.pallas_call(feed_kernel, grid=(total // step,), in_specs=[whole] + wei...  33.3 us
    ppermute x21, starting transfers between devices, shift(): lax.ppermute(value, axis, [(i, (i + distance) % size) for i in range(size)])  30.6 us
    pallas_call x4, Pallas kernels, project(): pl.pallas_call(functools.partial(project_kernel, count), grid_spec=pltpu....  23.3 us
    pallas_call x1, Pallas kernels, project_back(): pl.pallas_call(project_back_kernel, grid_spec=pltpu.PrefetchScalarGridSpe...  22.6 us
  transfers between devices with their start and end apart: 61, of which 28 were waited for; matrix products, arithmetic and copies ran while one was open for 8% of the time, Pallas kernels for 29%

profile of v5, /device:TPU:0, one launch (start us, length us, event | category | flops | bytes accessed | tf_op | source)
XLA Modules:
  0.0 583.3 jit_solution(13278582131533182894)
XLA Ops:
  15.7 15.4 %collective-permute-done = bf16[384,1024]{1,0:T(8,128)(2,1)S(1)} collective-permute-done((bf16[384,1024]{1,0:T(8,128)(2,1)S(1)}, bf16[384,1024]{1,0:T(8,128)(2,1)S(1)}, u32[]{:S(2)}, u32[]{:S(2)}) %collective-permute-start) | collective-permute-done | bytes 786464 | tf_op jit(solution)/shard_map/ppermute | solution.py:777
  47.1 19.5 %collective-permute-done.3 = bf16[384,1024]{1,0:T(8,128)(2,1)S(1)} collective-permute-done((bf16[384,1024]{1,0:T(8,128)(2,1)S(1)}, bf16[384,1024]{1,0:T(8,128)(2,1)S(1)}, u32[]{:S(2)}, u32[]{:S(2)}) %collective-permute-start.3) | collective-permute-done | bytes 786464 | tf_op jit(solution)/shard_map/ppermute | solution.py:778
  69.3 17.3 %collective-permute-done.16 = bf16[384,1024]{1,0:T(8,128)(2,1)S(1)} collective-permute-done((bf16[384,1024]{1,0:T(8,128)(2,1)S(1)}, bf16[384,1024]{1,0:T(8,128)(2,1)S(1)}, u32[]{:S(2)}, u32[]{:S(2)}) %collective-permute-start.16) | collective-permute-done | bytes 786464 | tf_op jit(solution)/shard_map/ppermute | solution.py:778
  99.1 6.1 %project.4 = (bf16[2048,256]{1,0:T(8,128)(2,1)}, bf16[2048,256]{1,0:T(8,128)(2,1)}, bf16[2048,256]{1,0:T(8,128)(2,1)}, f32[2048,256]{1,0:T(8,128)}, f32[2048,256]{1,0:T(8,128)}) custom-call(s32[1]{0:T(128)} %bitcast.3.index_ref, bf16[512,1024]{1,0:T(8,128)(2,1)} %refs_0_.1, ...), custom_call_target="tpu_custom_call" | custom-call | flops 805306368 | bytes 2097152 | tf_op jit(solution)/shard_map/project/pallas_call | solution.py:277
  105.2 6.0 %collective-permute-done.4.refs_0_.refs_5_ = bf16[512,1024]{1,0:T(8,128)(2,1)S(1)} collective-permute-done((bf16[512,1024]{1,0:T(8,128)(2,1)S(1)}, bf16[512,1024]{1,0:T(8,128)(2,1)S(1)}, u32[]{:S(2)}, u32[]{:S(2)}) %collective-permute-start.4) | collective-permute-done | bytes 1048608 | tf_op jit(solution)/shard_map/ppermute | solution.py:777
  117.5 21.9 %collective-permute-done.7.refs_1_.refs_4_ = bf16[512,1024]{1,0:T(8,128)(2,1)} collective-permute-done((bf16[512,1024]{1,0:T(8,128)(2,1)S(1)}, bf16[512,1024]{1,0:T(8,128)(2,1)}, u32[]{:S(2)}, u32[]{:S(2)}) %collective-permute-start.7) | collective-permute-done | bytes 1048608 | tf_op jit(solution)/shard_map/ppermute | solution.py:778
  155.8 8.3 %collective-permute-done.9.refs_1_.refs_6_ = bf16[512,1024]{1,0:T(8,128)(2,1)} collective-permute-done((bf16[512,1024]{1,0:T(8,128)(2,1)}, bf16[512,1024]{1,0:T(8,128)(2,1)}, u32[]{:S(2)}, u32[]{:S(2)}) %collective-permute-start.9) | collective-permute-done | bytes 1048608 | tf_op jit(solution)/shard_map/ppermute | solution.py:778
  169.8 5.7 project.7
  175.5 20.3 %attend.1 = (bf16[2048,256]{1,0:T(8,128)(2,1)}, f32[2048,256]{1,0:T(8,128)}, f32[4,2048]{1,0:T(4,128)}) custom-call(bf16[2048,256]{1,0:T(8,128)(2,1)} %get-tuple-element.177.q_ref, bf16[2048,256]{1,0:T(8,128)(2,1)} %get-tuple-element.178.k_ref, bf16[2048,256]{1,0:T(8,128)(2,1)} %get-tuple-element.179.v_ref, s32[2048,1]{1,0:T(8,128)} %copy.44.start_ref), custom_call_target="tpu_custom_call" | custom-call | flops 20000000000 | bytes 4194304 | tf_op jit(solution)/shard_map/attend/pallas_call | solution.py:113
  202.2 6.3 %collective-permute-done.10.refs_1_ = bf16[512,256]{1,0:T(8,128)(2,1)S(1)} collective-permute-done((bf16[512,256]{1,0:T(8,128)(2,1)S(1)}, bf16[512,256]{1,0:T(8,128)(2,1)S(1)}, u32[]{:S(2)}, u32[]{:S(2)}) %collective-permute-start.10) | collective-permute-done | bytes 262176 | tf_op jit(solution)/shard_map/ppermute | solution.py:773
  214.9 7.8 %mix.1 = (f32[512,1024]{1,0:T(8,128)}, f32[512,1024]{1,0:T(8,128)}, bf16[512,1024]{1,0:T(8,128)(2,1)}, bf16[1024,512]{1,0:T(8,128)(2,1)}) custom-call(bf16[512,256]{1,0:T(8,128)(2,1)} %get-tuple-element.279.refs_0_, bf16[512,256]{1,0:T(8,128)(2,1)} %copy-done.16, bf16[512,256]{1,0:T(8,128)(2,1)} %copy-done.17, bf16[512,256]{1,0:T(8,128)(2,1)} %copy-done.18, ...), custom_call_target="tpu_custom_call" | custom-call | flops 1073741824 | bytes 7340032 | tf_op jit(solution)/shard_map/mix/pallas_call | solution.py:491
  222.8 33.3 %feed.1 = (f32[512,4096]{1,0:T(8,128)}, f32[512,4096]{1,0:T(8,128)}, bf16[512,4096]{1,0:T(8,128)(2,1)}, bf16[512,1024]{1,0:T(8,128)(2,1)}, f32[512,1024]{1,0:T(8...) custom-call(bf16[512,1024]{1,0:T(8,128)(2,1)} %get-tuple-element.182.m_ref, ...), custom_call_target="tpu_custom_call" | custom-call | flops 12884901888 | bytes 46137344 | tf_op jit(solution)/shard_map/feed/pallas_call | solution.py:605
  256.1 15.0 %feed_back_first.1 = (bf16[3,1024,1024]{2,1,0:T(8,128)(2,1)}, f32[2,1024]{1,0:T(2,128)}, f32[512,1024]{1,0:T(8,128)}) custom-call(bf16[512,1024]{1,0:T(8,128)(2,1)} %get-tuple-element.187.refs_0_, bf16[1024,512]{1,0:T(8,128)(2,1)} %get-tuple-element.188.refs_1_, bf16[1024,512]{1,0:T(8,128)(2,1)} %get-tuple-element.189.refs_2_, ...), custom_call_target="tpu_custom_call" | custom-call | flops 6442450944 | bytes 17825792 | tf_op jit(solution)/shard_map/feed_back_first/pallas_call | solution.py:730
  271.2 40.2 %feed_back_last.1 = (bf16[3,1024,3072]{2,1,0:T(8,128)(2,1)}, f32[2,3072]{1,0:T(2,128)}, f32[512,1024]{1,0:T(8,128)}, bf16[512,1024]{1,0:T(8,128)(2,1)}, f32[1,1024]{1,0:T(1,128)}) custom-call(bf16[512,1024]{1,0:T(8,128)(2,1)} %get-tuple-element.187.refs_0_, bf16[1024,512]{1,0:T(8,128)(2,1)} %get-tuple-element.188.refs_1_, ...), custom_call_target="tpu_custom_call" | custom-call | flops 19327352832 | bytes 53477376 | tf_op jit(solution)/shard_map/feed_back_last/pallas_call | solution.py:730
  314.4 5.8 collective-permute-start.21
  331.4 12.5 %collective-permute-done.22 = bf16[512,256]{1,0:T(8,128)(2,1)S(1)} collective-permute-done((bf16[512,256]{1,0:T(8,128)(2,1)}, bf16[512,256]{1,0:T(8,128)(2,1)S(1)}, u32[]{:S(2)}, u32[]{:S(2)}) %collective-permute-start.22) | collective-permute-done | bytes 262176 | tf_op jit(solution)/shard_map/ppermute | solution.py:773
  348.1 41.3 %attend_back.1 = (f32[2048,256]{1,0:T(8,128)}, f32[2048,256]{1,0:T(8,128)}, f32[2048,256]{1,0:T(8,128)}) custom-call(bf16[2048,256]{1,0:T(8,128)(2,1)} %get-tuple-element.177.q_ref, bf16[2048,256]{1,0:T(8,128)(2,1)} %fusion.3.do_ref, bf16[2048,256]{1,0:T(8,128)(2,1)} %get-tuple-element.178.k_ref, bf16[2048,256]{1,0:T(8,128)(2,1)} %get-tuple-element.179.v_ref, ...), custom_call_target="tpu_custom_call" | custom-call | flops 40000000000 | bytes 10485760 | tf_op jit(solution)/shard_map/attend_back/pallas_call | solution.py:191
  395.6 22.6 %project_back.1 = (bf16[2048,768]{1,0:T(8,128)(2,1)}, f32[1,256]{1,0:T(1,128)}, bf16[512,1024]{1,0:T(8,128)(2,1)}, bf16[512,1024]{1,0:T(8,128)(2,1)}, bf16[512,1...) custom-call(s32[1]{0:T(128)} %bitcast.15.index_ref, f32[2048,256]{1,0:T(8,128)} %get-tuple-element.212.dq_ref, ...), custom_call_target="tpu_custom_call" | custom-call | flops 4294967296 | bytes 16777216 | tf_op jit(solution)/shard_map/project_back/pallas_call | solution.py:371
  418.2 13.7 %collective-permute-done.26 = f32[10,1024]{1,0:T(8,128)S(1)} collective-permute-done((f32[10,1024]{1,0:T(8,128)S(1)}, f32[10,1024]{1,0:T(8,128)S(1)}, u32[]{:S(2)}, u32[]{:S(2)}) %collective-permute-start.26) | collective-permute-done | bytes 40992 | tf_op jit(solution)/shard_map/ppermute | solution.py:803
  437.8 8.4 %projection_grads.1 = bf16[1024,768]{1,0:T(8,128)(2,1)} custom-call(bf16[512,1024]{1,0:T(8,128)(2,1)} %refs_0_.1, bf16[512,1024]{1,0:T(8,128)(2,1)} %collective-permute-done.8.refs_0_.refs_1_, bf16[512,1024]{1,0:T(8,128)(2,1)} %copy-done.7, bf16[512,1024]{1,0:T(8,128)(2,1)} %copy-done.8, bf16[512,1024]{1,0:T(8,128)(2,1)} %collective-permute-done.7.refs_1_.refs_4_, ...), custom_call_target="tpu_custom_call" | custom-call | flops 3221225472 | bytes 16777216 | tf_op jit(solution)/shard_map/projection_grads/pallas_call | solution.py:416
  446.3 10.1 %collective-permute-done.29 = bf16[512,1024]{1,0:T(8,128)(2,1)} collective-permute-done((bf16[512,1024]{1,0:T(8,128)(2,1)}, bf16[512,1024]{1,0:T(8,128)(2,1)}, u32[]{:S(2)}, u32[]{:S(2)}) %collective-permute-start.29) | collective-permute-done | bytes 1048608 | tf_op jit(solution)/shard_map/ppermute | solution.py:786
  471.3 18.3 %collective-permute-done.37 = f32[1,256]{1,0:T(1,128)S(1)} collective-permute-done((f32[1,256]{1,0:T(1,128)S(1)}, f32[1,256]{1,0:T(1,128)S(1)}, u32[]{:S(2)}, u32[]{:S(2)}) %collective-permute-start.37) | collective-permute-done | bytes 1056 | tf_op jit(solution)/shard_map/ppermute | solution.py:773
  505.3 10.1 %collective-permute-done.41 = bf16[2,128,768]{2,1,0:T(8,128)(2,1)S(1)} collective-permute-done((bf16[2,128,768]{2,1,0:T(8,128)(2,1)S(1)}, bf16[2,128,768]{2,1,0:T(8,128)(2,1)S(1)}, u32[]{:S(2)}, u32[]{:S(2)}) %collective-permute-start.41) | collective-permute-done | bytes 393248 | tf_op jit(solution)/shard_map/ppermute | solution.py:797
  522.1 15.1 %collective-permute-done.45 = bf16[3,128,1024]{2,1,0:T(8,128)(2,1)S(1)} collective-permute-done((bf16[3,128,1024]{2,1,0:T(8,128)(2,1)S(1)}, bf16[3,128,1024]{2,1,0:T(8,128)(2,1)S(1)}, u32[]{:S(2)}, u32[]{:S(2)}) %collective-permute-start.45) | collective-permute-done | bytes 786464 | tf_op jit(solution)/shard_map/ppermute | solution.py:773
  (276 shorter events, 187.3 us)
Async XLA Ops:
  7.2 91.9 %all-gather.4.cloned.1.call-start = ((), (), s32[]{:S(2)}) async-start(), calls=%async_computation.2 | async-start | bytes 1769472 | tf_op jit(solution)/shard_map/all_gather | solution.py:858
  9.2 193.0 %all-gather.6.cloned.1.call-start = ((), (), s32[]{:S(2)}) async-start(), calls=%async_computation.3 | async-start | bytes 2359296 | tf_op jit(solution)/shard_map/all_gather | solution.py:872
  45.1 177.7 %all-gather.8.cloned.1.call-start = ((), (), s32[]{:S(2)}) async-start(), calls=%async_computation.4 | async-start | bytes 28311552 | tf_op jit(solution)/shard_map/all_gather | solution.py:873
  88.8 257.6 %reduce-scatter.3.cloned.1.call-start = ((), (), s32[]{:S(2)}) async-start(), calls=%async_computation.5 | async-start | bytes 7077888 | tf_op jit(solution)/shard_map/reduce_scatter | solution.py:936
  91.6 23.9 %collective-permute-start.5 = (bf16[512,1024]{1,0:T(8,128)(2,1)S(1)}, bf16[512,1024]{1,0:T(8,128)(2,1)S(1)}, u32[]{:S(2)}, u32[]{:S(2)}) collective-permute-start(bf16[512,1024]{1,0:T(8,128)(2,1)S(1)} %copy-done.1), channel_id=1, source_target_pairs={{1,0},{2,1},{3,2},{5,4},{6,5},{7,6},{9,8},{10,9},{11,10},{13,12},{... | collective-permute-start | bytes 3145736 | tf_op jit(solution)/shard_map/ppermute | solution.py:778
  116.2 23.2 %collective-permute-start.7 = (bf16[512,1024]{1,0:T(8,128)(2,1)S(1)}, bf16[512,1024]{1,0:T(8,128)(2,1)}, u32[]{:S(2)}, u32[]{:S(2)}) collective-permute-start(bf16[512,1024]{1,0:T(8,128)(2,1)S(1)} %collective-permute-done.5.refs_1_.refs_2_), channel_id=1, source_target_pairs={{1,0},{2,1},{5,4},{6,5},{9,8},{10,9},{13,12},{14,13},{17,16},{18,1... | collective-permute-start | bytes 3145736 | tf_op jit(solution)/shard_map/ppermute | solution.py:778
  141.1 23.0 %collective-permute-start.9 = (bf16[512,1024]{1,0:T(8,128)(2,1)}, bf16[512,1024]{1,0:T(8,128)(2,1)}, u32[]{:S(2)}, u32[]{:S(2)}) collective-permute-start(bf16[512,1024]{1,0:T(8,128)(2,1)} %collective-permute-done.7.refs_1_.refs_4_), channel_id=1, source_target_pairs={{1,0},{5,4},{9,8},{13,12},{17,16},{21,20},{25,24},{29,28}} | collective-permute-start | bytes 3145736 | tf_op jit(solution)/shard_map/ppermute | solution.py:778
  142.4 55.5 %collective-permute-start.18 = (f32[2,1024]{1,0:T(2,128)S(1)}, f32[2,1024]{1,0:T(2,128)S(1)}, u32[]{:S(2)}, u32[]{:S(2)}) collective-permute-start(f32[2,1024]{1,0:T(2,128)S(1)} %copy-done.30), channel_id=1, source_target_pairs={{0,1},{1,2},{2,3},{3,0},{4,5},{5,6},{6,7},{7,4},{8,9},{9,10},{10,1... | collective-permute-start | bytes 24584 | tf_op jit(solution)/shard_map/ppermute | solution.py:773
  146.0 56.1 %collective-permute-start.19 = (f32[2,1024]{1,0:T(2,128)S(1)}, f32[2,1024]{1,0:T(2,128)S(1)}, u32[]{:S(2)}, u32[]{:S(2)}) collective-permute-start(f32[2,1024]{1,0:T(2,128)S(1)} %copy-done.30), channel_id=1, source_target_pairs={{0,3},{1,0},{2,1},{3,2},{4,7},{5,4},{6,5},{7,6},{8,11},{9,8},{10,9... | collective-permute-start | bytes 24584 | tf_op jit(solution)/shard_map/ppermute | solution.py:773
  146.5 55.7 %collective-permute-start.20 = (f32[2,1024]{1,0:T(2,128)S(1)}, f32[2,1024]{1,0:T(2,128)S(1)}, u32[]{:S(2)}, u32[]{:S(2)}) collective-permute-start(f32[2,1024]{1,0:T(2,128)S(1)} %copy-done.30), channel_id=1, source_target_pairs={{0,2},{1,3},{2,0},{3,1},{4,6},{5,7},{6,4},{7,5},{8,10},{9,11},{10,... | collective-permute-start | bytes 24584 | tf_op jit(solution)/shard_map/ppermute | solution.py:773
  271.1 226.4 %reduce-scatter.5.cloned.1.call-start = ((), (), s32[]{:S(2)}) async-start(), calls=%async_computation.6 | async-start | bytes 21233664 | tf_op jit(solution)/shard_map/reduce_scatter | solution.py:940
  346.5 42.9 %collective-permute-start.24 = (f32[10,1024]{1,0:T(8,128)S(1)}, f32[10,1024]{1,0:T(8,128)S(1)}, u32[]{:S(2)}, u32[]{:S(2)}) collective-permute-start(f32[10,1024]{1,0:T(8,128)S(1)} %pad_maximum_fusion.4), channel_id=1, source_target_pairs={{0,1},{1,0},{2,3},{3,2},{4,5},{5,4},{6,7},{7,6},{8,9},{9,8},{10,11... | collective-permute-start | bytes 122888 | tf_op jit(solution)/shard_map/ppermute | solution.py:803
  348.0 41.4 %collective-permute-start.25 = (bf16[4,128,1024]{2,1,0:T(8,128)(2,1)S(1)}, bf16[4,128,1024]{2,1,0:T(8,128)(2,1)}, u32[]{:S(2)}, u32[]{:S(2)}) collective-permute-start(bf16[4,128,1024]{2,1,0:T(8,128)(2,1)S(1)} %dynamic-slice_bitcast_fusion), channel_id=1, source_target_pairs={{0,4},{4,0},{8,12},{12,8},{16,20},{20,16},{24,28},{28,24},{1,5},{5... | collective-permute-start | bytes 3145736 | tf_op jit(solution)/shard_map/ppermute | solution.py:797
  391.0 41.1 %collective-permute-start.28 = (bf16[3,128,1024]{2,1,0:T(8,128)(2,1)}, bf16[3,128,1024]{2,1,0:T(8,128)(2,1)S(1)}, u32[]{:S(2)}, u32[]{:S(2)}) collective-permute-start(bf16[3,128,1024]{2,1,0:T(8,128)(2,1)} %reduce-scatter.3.cloned.1.call-done), channel_id=1, source_target_pairs={{0,2},{1,3},{2,0},{3,1},{4,6},{5,7},{6,4},{7,5},{8,10},{9,11},{10,... | collective-permute-start | bytes 2359304 | tf_op jit(solution)/shard_map/ppermute | solution.py:773
  391.2 40.8 %collective-permute-start.27 = (bf16[2,128,1024]{2,1,0:T(8,128)(2,1)S(1)}, bf16[2,128,1024]{2,1,0:T(8,128)(2,1)S(1)}, u32[]{:S(2)}, u32[]{:S(2)}) collective-permute-start(bf16[2,128,1024]{2,1,0:T(8,128)(2,1)S(1)} %dynamic-slice_bitcast_fusion.2), channel_id=1, source_target_pairs={{0,8},{4,12},{8,0},{12,4},{16,24},{20,28},{24,16},{28,20},{1,9},{5... | collective-permute-start | bytes 1572872 | tf_op jit(solution)/shard_map/ppermute | solution.py:797
  392.7 39.2 %collective-permute-start.26 = (f32[10,1024]{1,0:T(8,128)S(1)}, f32[10,1024]{1,0:T(8,128)S(1)}, u32[]{:S(2)}, u32[]{:S(2)}) collective-permute-start(f32[10,1024]{1,0:T(8,128)S(1)} %add.340), channel_id=1, source_target_pairs={{0,2},{1,3},{2,0},{3,1},{4,6},{5,7},{6,4},{7,5},{8,10},{9,11},{10,... | collective-permute-start | bytes 122888 | tf_op jit(solution)/shard_map/ppermute | solution.py:803
  432.2 24.2 %collective-permute-start.29 = (bf16[512,1024]{1,0:T(8,128)(2,1)}, bf16[512,1024]{1,0:T(8,128)(2,1)}, u32[]{:S(2)}, u32[]{:S(2)}) collective-permute-start(bf16[512,1024]{1,0:T(8,128)(2,1)} %get-tuple-element.228), channel_id=1, source_target_pairs={{0,1},{4,5},{8,9},{12,13},{16,17},{20,21},{24,25},{28,29}} | collective-permute-start | bytes 3145736 | tf_op jit(solution)/shard_map/ppermute | solution.py:786
  458.2 39.3 %collective-permute-start.32 = (bf16[512,1024]{1,0:T(8,128)(2,1)S(1)}, bf16[512,1024]{1,0:T(8,128)(2,1)S(1)}, u32[]{:S(2)}, u32[]{:S(2)}) collective-permute-start(bf16[512,1024]{1,0:T(8,128)(2,1)S(1)} %get-tuple-element.275), channel_id=1, source_target_pairs={{0,1},{1,2},{4,5},{5,6},{8,9},{9,10},{12,13},{13,14},{16,17},{17,1... | collective-permute-start | bytes 3145736 | tf_op jit(solution)/shard_map/ppermute | solution.py:786
  463.0 34.6 %collective-permute-start.33 = (bf16[512,1024]{1,0:T(8,128)(2,1)S(1)}, bf16[512,1024]{1,0:T(8,128)(2,1)}, u32[]{:S(2)}, u32[]{:S(2)}) collective-permute-start(bf16[512,1024]{1,0:T(8,128)(2,1)S(1)} %get-tuple-element.274), channel_id=1, source_target_pairs={{2,1},{3,2},{6,5},{7,6},{10,9},{11,10},{14,13},{15,14},{18,17},{19... | collective-permute-start | bytes 3145736 | tf_op jit(solution)/shard_map/ppermute | solution.py:787
  464.6 25.0 %collective-permute-start.37 = (f32[1,256]{1,0:T(1,128)S(1)}, f32[1,256]{1,0:T(1,128)S(1)}, u32[]{:S(2)}, u32[]{:S(2)}) collective-permute-start(f32[1,256]{1,0:T(1,128)S(1)} %copy-done.34), channel_id=1, source_target_pairs={{0,1},{1,2},{2,3},{3,0},{4,5},{5,6},{6,7},{7,4},{8,9},{9,10},{10,1... | collective-permute-start | bytes 3080 | tf_op jit(solution)/shard_map/ppermute | solution.py:773
  466.3 24.7 %collective-permute-start.38 = (f32[1,256]{1,0:T(1,128)S(1)}, f32[1,256]{1,0:T(1,128)S(1)}, u32[]{:S(2)}, u32[]{:S(2)}) collective-permute-start(f32[1,256]{1,0:T(1,128)S(1)} %copy-done.34), channel_id=1, source_target_pairs={{0,2},{1,3},{2,0},{3,1},{4,6},{5,7},{6,4},{7,5},{8,10},{9,11},{10,... | collective-permute-start | bytes 3080 | tf_op jit(solution)/shard_map/ppermute | solution.py:773
  501.1 36.1 %collective-permute-start.45 = (bf16[3,128,1024]{2,1,0:T(8,128)(2,1)S(1)}, bf16[3,128,1024]{2,1,0:T(8,128)(2,1)S(1)}, u32[]{:S(2)}, u32[]{:S(2)}) collective-permute-start(bf16[3,128,1024]{2,1,0:T(8,128)(2,1)S(1)} %get-tuple-element.271), channel_id=1, source_target_pairs={{0,1},{1,2},{2,3},{3,0},{4,5},{5,6},{6,7},{7,4},{8,9},{9,10},{10,1... | collective-permute-start | bytes 2359304 | tf_op jit(solution)/shard_map/ppermute | solution.py:773
  542.9 27.7 %collective-permute-start.43 = (bf16[512,1024]{1,0:T(8,128)(2,1)}, bf16[512,1024]{1,0:T(8,128)(2,1)}, u32[]{:S(2)}, u32[]{:S(2)}) collective-permute-start(bf16[512,1024]{1,0:T(8,128)(2,1)} %add.361), channel_id=1, source_target_pairs={{1,0},{2,1},{3,2},{5,4},{6,5},{7,6},{9,8},{10,9},{11,10},{13,12},{... | collective-permute-start | bytes 3145736 | tf_op jit(solution)/shard_map/ppermute | solution.py:787
  545.9 27.3 %collective-permute-start.42 = (bf16[512,1024]{1,0:T(8,128)(2,1)}, bf16[512,1024]{1,0:T(8,128)(2,1)}, u32[]{:S(2)}, u32[]{:S(2)}) collective-permute-start(bf16[512,1024]{1,0:T(8,128)(2,1)} %add.359), channel_id=1, source_target_pairs={{0,1},{1,2},{2,3},{4,5},{5,6},{6,7},{8,9},{9,10},{10,11},{12,13},{... | collective-permute-start | bytes 3145736 | tf_op jit(solution)/shard_map/ppermute | solution.py:786
  (72 other events, 1039.2 us)
Sparse Core Ops, SparseCore 0:
  10.5 28.2 all-gather.3
  45.2 26.4 all-gather.5
  89.0 123.5 all-gather.7
  271.2 64.6 reduce-scatter.2
  339.4 137.5 reduce-scatter.4

commit v6 on v5

--- a/solution.py
+++ b/solution.py
@@ -132,7 +132,7 @@
 
 
 def attend_back_kernel(
-    heads, bq, bk, q_ref, do_ref, k_ref, v_ref, of_ref, l_ref, start_ref, dq_ref, dk_ref, dv_ref, acc
+    first, heads, bq, bk, q_ref, do_ref, k_ref, v_ref, of_ref, l_ref, start_ref, dq_ref, dk_ref, dv_ref, acc
 ):
     i = pl.program_id(0)
 
@@ -152,7 +152,7 @@
         ],
         axis=1,
     )
-    log_sum = jnp.concatenate([l_ref[h : h + 1, :] for h in range(heads)], axis=1)
+    log_sum = jnp.concatenate([l_ref[first + h : first + h + 1, :] for h in range(heads)], axis=1)
     start = jnp.concatenate([start_ref[...]] * heads, axis=1)
     acc[...] = jnp.zeros_like(acc)
 
@@ -182,22 +182,24 @@
     dq_ref[...] = head_pick(acc[...], heads, bq)
 
 
-def attend_back(q, k, v, grads, out, log_sum, start, block):
-    length, width = q.shape
+def attend_back(q, k, v, grads, out, log_sum, start, block, group, width):
+    length = q.shape[0]
     heads = width // HEAD_DIM
+    taken = pl.BlockSpec((length, width), lambda i: (0, group))
+    taken_rows = pl.BlockSpec((block, width), lambda i: (i, group))
     whole = pl.BlockSpec((length, width), lambda i: (0, 0))
     rows = pl.BlockSpec((block, width), lambda i: (i, 0))
     result = jax.ShapeDtypeStruct((length, width), f32)
     return pl.pallas_call(
-        functools.partial(attend_back_kernel, heads, block, block),
+        functools.partial(attend_back_kernel, group * heads, heads, block, block),
         grid=(length // block,),
         in_specs=[
-            rows,
-            rows,
-            whole,
-            whole,
-            rows,
-            pl.BlockSpec((heads, block), lambda i: (0, i)),
+            taken_rows,
+            taken_rows,
+            taken,
+            taken,
+            taken_rows,
+            pl.BlockSpec((log_sum.shape[0], block), lambda i: (0, i)),
             pl.BlockSpec((1, block), lambda i: (0, i)),
         ],
         out_specs=[rows, whole, whole],
@@ -300,43 +302,45 @@
     )(index, *parts, weights, weights, weights, cosine, sine, gain, *previous)
 
 
-def project_back_kernel(
-    index_ref,
-    dq_ref,
-    dk_ref,
-    dv_ref,
-    xq_ref,
-    xk_ref,
-    wq_ref,
-    wk_ref,
-    wv_ref,
-    cos_ref,
-    sin_ref,
-    gain_ref,
-    grad_ref,
-    gain_grad_ref,
-    *piece_refs,
-):
+def project_back_kernel(groups, index_ref, *refs):
+    dq_refs, dk_refs, dv_refs = (refs[m * groups : (m + 1) * groups] for m in range(3))
+    (
+        xq_ref,
+        xk_ref,
+        wq_ref,
+        wk_ref,
+        wv_ref,
+        cos_ref,
+        sin_ref,
+        gain_ref,
+        grad_ref,
+        gain_grad_ref,
+        *piece_refs,
+    ) = refs[3 * groups :]
+
     @pl.when(pl.program_id(0) == 0)
     def _():
         gain_grad_ref[...] = jnp.zeros_like(gain_grad_ref)
 
-    width = dq_ref.shape[1]
+    def joined(refs):
+        return jnp.concatenate([ref[...] for ref in refs], axis=1) if groups > 1 else refs[0][...]
+
+    width = xq_ref.shape[1]
     cosine = widen(cos_ref[...], width)
     sine = widen(sin_ref[...], width)
     gain = gain_ref[...]
     lows = []
-    for d_ref, x_ref in ((dq_ref, xq_ref), (dk_ref, xk_ref)):
+    for d_refs, x_ref in ((dq_refs, xq_ref), (dk_refs, xk_ref)):
         turned = x_ref[...]
         inverse = lax.rsqrt(head_sums(turned * turned) + norm_eps)
         unit = turned * inverse
-        hat_grad = d_ref[...] * scale_factor
+        hat_grad = joined(d_refs) * scale_factor
         gain_grad_ref[...] += jnp.sum(hat_grad * unit, axis=0, keepdims=True)
         unit_grad = hat_grad * gain
         turned_grad = inverse * (unit_grad - unit * head_sums(unit * unit_grad))
         raw_grad = turned_grad * cosine - partner(turned_grad) * sine
         lows.append(raw_grad.astype(bf16))
-    lows.append(dv_ref[...].astype(bf16))
+    lows.append(joined(dv_refs).astype(bf16))
     piece = jnp.zeros(piece_refs[0].shape, f32)
     for m, w_ref in enumerate((wq_ref, wk_ref, wv_ref)):
         grad_ref[:, m * width : (m + 1) * width] = lows[m]
@@ -351,7 +355,8 @@
 
 
 def project_back(index, grads, turned, weights, cosine, sine, gain, rows):
-    length, width = grads[0].shape
+    length, width = turned[0].shape
+    groups = len(grads)
     model = weights.shape[0]
     part = min(256, rows)
     per = rows // part
@@ -369,11 +374,12 @@
     tall = pl.BlockSpec((part, width), turn)
     table = pl.BlockSpec((part, 128), turn)
     return pl.pallas_call(
-        project_back_kernel,
+        functools.partial(project_back_kernel, groups),
         grid_spec=pltpu.PrefetchScalarGridSpec(
             num_scalar_prefetch=1,
             grid=(blocks,),
-            in_specs=[tall] * 5
+            in_specs=[pl.BlockSpec((part, width // groups), turn)] * (3 * groups)
+            + [tall] * 2
             + [column(0), column(1), column(2), table, table]
             + [pl.BlockSpec((1, width), lambda i, at: (0, 0))],
             out_specs=[
@@ -388,12 +394,10 @@
         ]
         + [jax.ShapeDtypeStruct((rows, model), bf16)] * (length // rows),
         cost_estimate=pl.CostEstimate(
-            flops=8 * length * model * width,
-            bytes_accessed=32 * length * width,
-            transcendentals=0,
+            flops=length * width, bytes_accessed=length * width, transcendentals=0
         ),
         name="project_back",
-    )(index, *grads, *turned, weights, weights, weights, cosine, sine, gain)
+    )(index, *[g[m] for m in range(3) for g in grads], *turned, weights, weights, weights, cosine, sine, gain)
 
 
 def projection_grads_kernel(counts, *refs):
@@ -789,14 +793,14 @@
 
 
 def halving(value, axis, size, step):
-    count, rows, width = value.shape
+    lead, (count, rows, width) = value.shape[:-3], value.shape[-3:]
     bit = (lax.axis_index(axis) // step) % 2
-    pairs = value.reshape(count // 2, 2, rows, width)
-    sent = lax.dynamic_index_in_dim(pairs, 1 - bit, 1, False)
-    kept = lax.dynamic_index_in_dim(pairs, bit, 1, False)
+    pairs = value.reshape(lead + (count // 2, 2, rows, width))
+    sent = lax.dynamic_index_in_dim(pairs, 1 - bit, len(lead) + 1, False)
+    kept = lax.dynamic_index_in_dim(pairs, bit, len(lead) + 1, False)
     other = lax.ppermute(sent, axis, [(i, i ^ step) for i in range(size)])
     value = kept.astype(f32) + other.astype(f32)
-    return value[0] if 2 * step == size else value.astype(bf16)
+    return value.reshape(lead + (rows, width)) if 2 * step == size else value.astype(bf16)
 
 
 def exchange_add(value, axis, size, step):
@@ -933,6 +937,7 @@
     near = (nt - 1) * per
     feed_args = (mlp_out_low, mlp_out_t, middle_t, mlp_full, scales_row, up, gate, hidden_units)
     far_grad, far_scales, partial = feed_back(*feed_args, middle_direct, (), step, near, per)
+    halvings = doublings(nd)
     far_part = lax.psum_scatter(far_grad, "dp", scatter_dimension=1, tiled=True)
     near_grad, near_scales, token_direct, branch_low, rate_attn_grad = feed_back(
         *feed_args, partial, (branch, hidden_in, rates), step, 0, near
@@ -960,17 +965,39 @@
         (far_part, grad_row, out_grad, small)
     )
     small = advance(small)
-    halvings = doublings(nd)
     out_sum = halving(out_grad.reshape(nd, shard, -1), "dp", nd, halvings[0])
-    head_grads = attend_back(
-        query_hat, key_hat, value_hat, grad_row, attended_f32, log_sum, starts[None, :], block
-    )
-    head_grads, far_part, small, out_sum = lax.optimization_barrier(
-        (head_grads, far_part, small, out_sum)
-    )
-    far_part = shift(far_part, "tensor", -middle_hop, nt)
+    head_group = max(128, heads_width // 2)
+    head_grads = []
+    for group in range(heads_width // head_group):
+        if group == 1:
+            head_grads, grad_row, far_part, small, out_sum = lax.optimization_barrier(
+                (head_grads, grad_row, far_part, small, out_sum)
+            )
+            small = advance(small)
+            out_sum = halving(out_sum, "dp", nd, halvings[1])
+        head_grads.append(
+            attend_back(
+                query_hat,
+                key_hat,
+                value_hat,
+                grad_row,
+                attended_f32,
+                log_sum,
+                starts[None, :],
+                block,
+                group,
+                head_group,
+            )
+        )
+    far_first = shift(far_part[:2], "tensor", -middle_hop, nt)
+    far_last = far_part[2:]
+    head_grads, small, out_sum, far_first, far_last = lax.optimization_barrier(
+        (head_grads, small, out_sum, far_first, far_last)
+    )
+    far_last = shift(far_last, "tensor", -middle_hop, nt)
     small = advance(small)
-    out_sum = halving(out_sum, "dp", nd, halvings[1])
+    for k in halvings[1 if len(head_grads) == 1 else 2 :]:
+        out_sum = halving(out_sum, "dp", nd, k)
     qkv_grad, gain_grad, *pieces = project_back(
         me.reshape(1),
         head_grads,
@@ -981,11 +1008,11 @@
         gain,
         rows,
     )
-    qkv_grad, pieces, small, out_sum, far_part = lax.optimization_barrier(
-        (qkv_grad, pieces, small, out_sum, far_part)
-    )
-    for k in halvings[2:]:
-        out_sum = halving(out_sum, "dp", nd, k)
+    qkv_grad, pieces, small, out_sum, far_last = lax.optimization_barrier(
+        (qkv_grad, pieces, small, out_sum, far_last)
+    )
+    far_part = jnp.concatenate([far_first, far_last], axis=0)
+    small = advance(small)
     hidden_turn = [hidden_parts[(nt - d) % nt] for d in range(nt)]
     qkv_sum = projection_grads(hidden_turn, qkv_grad)
     qkv_sum = qkv_sum.reshape(nd, shard, -1)
@@ -1000,9 +1027,7 @@
     ahead = behind = None
     for hop in range(1, nt):
         if hop == 2:
-            ahead, behind, qkv_sum, out_sum = lax.optimization_barrier(
-                (ahead, behind, qkv_sum, out_sum)
-            )
+            ahead, behind, qkv_sum = lax.optimization_barrier((ahead, behind, qkv_sum))
             out_pieces = own_pieces(out_sum.astype(bf16), 1, heads_width, range(nt))
             gain_parts = gather(gain_grad)
         if hop == max(2, nt - 1):
@@ -1012,18 +1037,14 @@
                 )
             )
             near_pieces = own_pieces(near_part, 2, hidden_width, order[:-1])
-            for k in halvings[:2]:
-                qkv_sum = halving(qkv_sum, "dp", nd, k)
-            ahead, behind, qkv_sum = lax.optimization_barrier((ahead, behind, qkv_sum))
         ahead, behind = line_sum(pieces, hop, ahead, behind, "tensor", nt)
-    for k in halvings[2:]:
+        if hop == 2:
+            qkv_sum = halving(qkv_sum, "dp", nd, halvings[0])
+    for k in halvings[1:]:
         qkv_sum = halving(qkv_sum, "dp", nd, k)
-    near_pieces, qkv_sum = lax.optimization_barrier((near_pieces, qkv_sum))
     gain_row = spread(jnp.concatenate(gain_parts, axis=1), range(nt))
     while steps:
         small = advance(small)
-    total = token_direct + pieces[0].astype(f32)
-    input_grad = (total + ahead.astype(f32) + behind.astype(f32)).astype(bf16)
     rates_grad = small[:2]
     mlp_scales_grad = small[2:].reshape(2, nt * hidden_width)
 
@@ -1037,6 +1058,7 @@
     attn_square = jnp.sum(attn_moved * attn_moved, axis=1, keepdims=True)
     last = jnp.concatenate([attn_square.reshape(1, -1), gain_row], axis=1)
     last = butterfly(last, "dp", nd)
+    near_pieces, last = lax.optimization_barrier((near_pieces, last))
     attn_square = last[:, : 4 * heads_width].reshape(4, 1, heads_width)
     gain_row = last[:, 4 * heads_width :].reshape(-1)
     attn_new = attn_moved * lax.rsqrt(attn_square + norm_eps)
@@ -1047,6 +1069,9 @@
     )
     mlp_square = jnp.sum(mlp_moved * mlp_moved, axis=1, keepdims=True)
     mlp_square = butterfly(mlp_square.reshape(1, -1), "dp", nd).reshape(mlp_square.shape)
+    mlp_square, ahead, behind = lax.optimization_barrier((mlp_square, ahead, behind))
+    total = token_direct + pieces[0].astype(f32)
+    input_grad = (total + ahead.astype(f32) + behind.astype(f32)).astype(bf16)
     mlp_new = mlp_moved * lax.rsqrt(mlp_square + norm_eps)
     return (
         result.astype(bf16),

time: 589 us -> 581 us (0.986)
  waiting for transfers between devices: 214 us -> 199 us
    ppermute x11, waiting for transfers between devices: 17.7 us -> 6.25 us  [exchange_add(): lax.ppermute(value, axis, [(i, i ^ step) for i in range(size)])]
    ppermute x21 -> x22, waiting for transfers between devices: 69.4 us -> 61.8 us  [shift(): lax.ppermute(value, axis, [(i, (i + distance) % size) for i in range(size)])]
    ppermute x3, waiting for transfers between devices: 12.6 us -> 19.6 us  [line_sum(): up = lax.ppermute(ahead, axis, [(i, i + 1) for i in range(hop)])]
    pallas_call x2 -> x3, Pallas kernels: 63.9 us -> 65.7 us  [the longest x2 42.3 us: attend_back(): pl.pallas_call(functools.partial(attend_back_kernel, group * heads, heads...]
    ppermute x21 -> x22, starting transfers between devices: 30.6 us -> 30.9 us  [shift(): lax.ppermute(value, axis, [(i, (i + distance) % size) for i in range(size)])]
  transfers between devices with their start and end apart: 61 -> 62, of which waited for: 28 -> 30; matrix products, arithmetic and copies ran while one was open for 8% -> 8% of each run, Pallas kernels for 29% -> 30%
where the time goes in v6:
time: 581 us; the launch traced here: 576 us
  Pallas kernels  219 us (38%)
  waiting for transfers between devices  199 us (34%)
  starting transfers between devices  80.9 us (14%)
  other arithmetic  33.5 us (6%)
  local copies, waits for them, and re-layouts  23.2 us (4%)
  between operations  15.2 us (3%)
    ppermute x6, waiting for transfers between devices, carry_on(): lax.ppermute(down, axis, [(i, i - 1) for i in range(1, size - hop + 1)])  75.1 us
    ppermute x22, waiting for transfers between devices, shift(): lax.ppermute(value, axis, [(i, (i + distance) % size) for i in range(size)])  61.8 us
    pallas_call x2, Pallas kernels, feed_back(): pl.pallas_call(feed_back_last_kernel if last else feed_back_first_kernel,...  55 us
    pallas_call x2, Pallas kernels, attend_back(): pl.pallas_call(functools.partial(attend_back_kernel, group * heads, heads...  42.3 us
    pallas_call x1, Pallas kernels, feed(): pl.pallas_call(feed_kernel, grid=(total // step,), in_specs=[whole] + wei...  33.2 us
    ppermute x22, starting transfers between devices, shift(): lax.ppermute(value, axis, [(i, (i + distance) % size) for i in range(size)])  30.9 us
    pallas_call x1, Pallas kernels, project_back(): pl.pallas_call(functools.partial(project_back_kernel, groups), grid_spec=...  23.5 us
    pallas_call x4, Pallas kernels, project(): pl.pallas_call(functools.partial(project_kernel, count), grid_spec=pltpu....  23.3 us
  transfers between devices with their start and end apart: 62, of which 30 were waited for; matrix products, arithmetic and copies ran while one was open for 8% of the time, Pallas kernels for 30%

profile of v6, /device:TPU:0, one launch (start us, length us, event | category | flops | bytes accessed | tf_op | source)
XLA Modules:
  0.0 575.6 jit_solution(16259246082686890025)
XLA Ops:
  15.7 15.4 %collective-permute-done = bf16[384,1024]{1,0:T(8,128)(2,1)S(1)} collective-permute-done((bf16[384,1024]{1,0:T(8,128)(2,1)S(1)}, bf16[384,1024]{1,0:T(8,128)(2,1)S(1)}, u32[]{:S(2)}, u32[]{:S(2)}) %collective-permute-start) | collective-permute-done | bytes 786464 | tf_op jit(solution)/shard_map/ppermute | solution.py:781
  47.1 19.5 %collective-permute-done.3 = bf16[384,1024]{1,0:T(8,128)(2,1)S(1)} collective-permute-done((bf16[384,1024]{1,0:T(8,128)(2,1)S(1)}, bf16[384,1024]{1,0:T(8,128)(2,1)S(1)}, u32[]{:S(2)}, u32[]{:S(2)}) %collective-permute-start.3) | collective-permute-done | bytes 786464 | tf_op jit(solution)/shard_map/ppermute | solution.py:782
  69.3 17.3 %collective-permute-done.16 = bf16[384,1024]{1,0:T(8,128)(2,1)S(1)} collective-permute-done((bf16[384,1024]{1,0:T(8,128)(2,1)S(1)}, bf16[384,1024]{1,0:T(8,128)(2,1)S(1)}, u32[]{:S(2)}, u32[]{:S(2)}) %collective-permute-start.16) | collective-permute-done | bytes 786464 | tf_op jit(solution)/shard_map/ppermute | solution.py:782
  99.2 6.1 %project.4 = (bf16[2048,256]{1,0:T(8,128)(2,1)}, bf16[2048,256]{1,0:T(8,128)(2,1)}, bf16[2048,256]{1,0:T(8,128)(2,1)}, f32[2048,256]{1,0:T(8,128)}, f32[2048,256]{1,0:T(8,128)}) custom-call(s32[1]{0:T(128)} %bitcast.3.index_ref, bf16[512,1024]{1,0:T(8,128)(2,1)} %refs_0_.1, ...), custom_call_target="tpu_custom_call" | custom-call | flops 805306368 | bytes 2097152 | tf_op jit(solution)/shard_map/project/pallas_call | solution.py:279
  105.3 6.0 %collective-permute-done.4.refs_0_.refs_5_ = bf16[512,1024]{1,0:T(8,128)(2,1)S(1)} collective-permute-done((bf16[512,1024]{1,0:T(8,128)(2,1)S(1)}, bf16[512,1024]{1,0:T(8,128)(2,1)S(1)}, u32[]{:S(2)}, u32[]{:S(2)}) %collective-permute-start.4) | collective-permute-done | bytes 1048608 | tf_op jit(solution)/shard_map/ppermute | solution.py:781
  117.5 21.9 %collective-permute-done.7.refs_1_.refs_4_ = bf16[512,1024]{1,0:T(8,128)(2,1)} collective-permute-done((bf16[512,1024]{1,0:T(8,128)(2,1)S(1)}, bf16[512,1024]{1,0:T(8,128)(2,1)}, u32[]{:S(2)}, u32[]{:S(2)}) %collective-permute-start.7) | collective-permute-done | bytes 1048608 | tf_op jit(solution)/shard_map/ppermute | solution.py:782
  150.2 5.8 %project.5 = (bf16[2048,256]{1,0:T(8,128)(2,1)}, bf16[2048,256]{1,0:T(8,128)(2,1)}, bf16[2048,256]{1,0:T(8,128)(2,1)}, f32[2048,256]{1,0:T(8,128)}, f32[2048,256]{1,0:T(8,128)}) custom-call(s32[1]{0:T(128)} %bitcast.10.index_ref, bf16[512,1024]{1,0:T(8,128)(2,1)} %copy-done.8, ...), custom_call_target="tpu_custom_call", output_to_operand_aliasing={{0}: (9, {}), {1}: (10, {}), {2}: (11, {}), {3}: (12, {}), ... | custom-call | flops 805306368 | bytes 2097152 | tf_op jit(solution)/shard_map/project/pallas_call | solution.py:279
  156.0 8.0 %collective-permute-done.9.refs_1_.refs_6_ = bf16[512,1024]{1,0:T(8,128)(2,1)} collective-permute-done((bf16[512,1024]{1,0:T(8,128)(2,1)}, bf16[512,1024]{1,0:T(8,128)(2,1)}, u32[]{:S(2)}, u32[]{:S(2)}) %collective-permute-start.9) | collective-permute-done | bytes 1048608 | tf_op jit(solution)/shard_map/ppermute | solution.py:782
  175.5 20.3 %attend.1 = (bf16[2048,256]{1,0:T(8,128)(2,1)}, f32[2048,256]{1,0:T(8,128)}, f32[4,2048]{1,0:T(4,128)}) custom-call(bf16[2048,256]{1,0:T(8,128)(2,1)} %get-tuple-element.190.q_ref, bf16[2048,256]{1,0:T(8,128)(2,1)} %get-tuple-element.191.k_ref, bf16[2048,256]{1,0:T(8,128)(2,1)} %get-tuple-element.192.v_ref, s32[2048,1]{1,0:T(8,128)} %copy.44.start_ref), custom_call_target="tpu_custom_call" | custom-call | flops 20000000000 | bytes 4194304 | tf_op jit(solution)/shard_map/attend/pallas_call | solution.py:113
  201.9 6.6 %collective-permute-done.10.refs_1_ = bf16[512,256]{1,0:T(8,128)(2,1)S(1)} collective-permute-done((bf16[512,256]{1,0:T(8,128)(2,1)S(1)}, bf16[512,256]{1,0:T(8,128)(2,1)S(1)}, u32[]{:S(2)}, u32[]{:S(2)}) %collective-permute-start.10) | collective-permute-done | bytes 262176 | tf_op jit(solution)/shard_map/ppermute | solution.py:777
  215.0 7.9 %mix.1 = (f32[512,1024]{1,0:T(8,128)}, f32[512,1024]{1,0:T(8,128)}, bf16[512,1024]{1,0:T(8,128)(2,1)}, bf16[1024,512]{1,0:T(8,128)(2,1)}) custom-call(bf16[512,256]{1,0:T(8,128)(2,1)} %get-tuple-element.305.refs_0_, bf16[512,256]{1,0:T(8,128)(2,1)} %copy-done.16, bf16[512,256]{1,0:T(8,128)(2,1)} %copy-done.17, bf16[512,256]{1,0:T(8,128)(2,1)} %copy-done.18, ...), custom_call_target="tpu_custom_call" | custom-call | flops 1073741824 | bytes 7340032 | tf_op jit(solution)/shard_map/mix/pallas_call | solution.py:495
  222.8 33.2 %feed.1 = (f32[512,4096]{1,0:T(8,128)}, f32[512,4096]{1,0:T(8,128)}, bf16[512,4096]{1,0:T(8,128)(2,1)}, bf16[512,1024]{1,0:T(8,128)(2,1)}, f32[512,1024]{1,0:T(8...) custom-call(bf16[512,1024]{1,0:T(8,128)(2,1)} %get-tuple-element.195.m_ref, ...), custom_call_target="tpu_custom_call" | custom-call | flops 12884901888 | bytes 46137344 | tf_op jit(solution)/shard_map/feed/pallas_call | solution.py:609
  256.0 15.0 %feed_back_first.1 = (bf16[3,1024,1024]{2,1,0:T(8,128)(2,1)}, f32[2,1024]{1,0:T(2,128)}, f32[512,1024]{1,0:T(8,128)}) custom-call(bf16[512,1024]{1,0:T(8,128)(2,1)} %get-tuple-element.200.refs_0_, bf16[1024,512]{1,0:T(8,128)(2,1)} %get-tuple-element.201.refs_1_, bf16[1024,512]{1,0:T(8,128)(2,1)} %get-tuple-element.202.refs_2_, ...), custom_call_target="tpu_custom_call" | custom-call | flops 6442450944 | bytes 17825792 | tf_op jit(solution)/shard_map/feed_back_first/pallas_call | solution.py:734
  271.1 40.1 %feed_back_last.1 = (bf16[3,1024,3072]{2,1,0:T(8,128)(2,1)}, f32[2,3072]{1,0:T(2,128)}, f32[512,1024]{1,0:T(8,128)}, bf16[512,1024]{1,0:T(8,128)(2,1)}, f32[1,1024]{1,0:T(1,128)}) custom-call(bf16[512,1024]{1,0:T(8,128)(2,1)} %get-tuple-element.200.refs_0_, bf16[1024,512]{1,0:T(8,128)(2,1)} %get-tuple-element.201.refs_1_, ...), custom_call_target="tpu_custom_call" | custom-call | flops 19327352832 | bytes 53477376 | tf_op jit(solution)/shard_map/feed_back_last/pallas_call | solution.py:734
  314.2 5.8 %collective-permute-start.21 = (bf16[512,256]{1,0:T(8,128)(2,1)}, bf16[512,256]{1,0:T(8,128)(2,1)}, u32[]{:S(2)}, u32[]{:S(2)}) collective-permute-start(bf16[512,256]{1,0:T(8,128)(2,1)} %convolution_convert_fusion.3), channel_id=1, source_target_pairs={{0,3},{1,0},{2,1},{3,2},{4,7},{5,4},{6,5},{7,6},{8,11},{9,8},{10,9... | collective-permute-start | bytes 786440 | tf_op jit(solution)/shard_map/ppermute | solution.py:777
  331.3 12.3 %collective-permute-done.22 = bf16[512,256]{1,0:T(8,128)(2,1)S(1)} collective-permute-done((bf16[512,256]{1,0:T(8,128)(2,1)}, bf16[512,256]{1,0:T(8,128)(2,1)S(1)}, u32[]{:S(2)}, u32[]{:S(2)}) %collective-permute-start.22) | collective-permute-done | bytes 262176 | tf_op jit(solution)/shard_map/ppermute | solution.py:777
  347.7 21.5 %attend_back.2 = (f32[2048,128]{1,0:T(8,128)}, f32[2048,128]{1,0:T(8,128)}, f32[2048,128]{1,0:T(8,128)}) custom-call(bf16[2048,256]{1,0:T(8,128)(2,1)} %get-tuple-element.190.q_ref, bf16[2048,256]{1,0:T(8,128)(2,1)} %fusion.3.do_ref, bf16[2048,256]{1,0:T(8,128)(2,1)} %get-tuple-element.191.k_ref, bf16[2048,256]{1,0:T(8,128)(2,1)} %get-tuple-element.192.v_ref, ...), custom_call_target="tpu_custom_call" | custom-call | flops 40000000000 | bytes 5242880 | tf_op jit(solution)/shard_map/attend_back/pallas_call | solution.py:193
  375.8 20.8 %attend_back.3 = (f32[2048,128]{1,0:T(8,128)}, f32[2048,128]{1,0:T(8,128)}, f32[2048,128]{1,0:T(8,128)}) custom-call(bf16[2048,256]{1,0:T(8,128)(2,1)} %get-tuple-element.190.q_ref, bf16[2048,256]{1,0:T(8,128)(2,1)} %fusion.3.do_ref, bf16[2048,256]{1,0:T(8,128)(2,1)} %get-tuple-element.191.k_ref, bf16[2048,256]{1,0:T(8,128)(2,1)} %get-tuple-element.192.v_ref, ...), custom_call_target="tpu_custom_call" | custom-call | flops 40000000000 | bytes 5242880 | tf_op jit(solution)/shard_map/attend_back/pallas_call | solution.py:193
  401.9 23.5 %project_back.1 = (bf16[2048,768]{1,0:T(8,128)(2,1)}, f32[1,256]{1,0:T(1,128)}, bf16[512,1024]{1,0:T(8,128)(2,1)}, bf16[512,1024]{1,0:T(8,128)(2,1)}, bf16[512,1...) custom-call(s32[1]{0:T(128)} %bitcast.15.index_ref, f32[2048,128]{1,0:T(8,128)} %get-tuple-element.235.refs_0_, ...), custom_call_target="tpu_custom_call" | custom-call | flops 524288 | bytes 524288 | tf_op jit(solution)/shard_map/project_back/pallas_call | solution.py:376
  432.3 8.4 %projection_grads.1 = bf16[1024,768]{1,0:T(8,128)(2,1)} custom-call(bf16[512,1024]{1,0:T(8,128)(2,1)} %refs_0_.1, bf16[512,1024]{1,0:T(8,128)(2,1)} %collective-permute-done.8.refs_0_.refs_1_, bf16[512,1024]{1,0:T(8,128)(2,1)} %copy-done.7, bf16[512,1024]{1,0:T(8,128)(2,1)} %copy-done.8, bf16[512,1024]{1,0:T(8,128)(2,1)} %collective-permute-done.7.refs_1_.refs_4_, ...), custom_call_target="tpu_custom_call" | custom-call | flops 3221225472 | bytes 16777216 | tf_op jit(solution)/shard_map/projection_grads/pallas_call | solution.py:420
  440.8 12.9 %collective-permute-done.32 = bf16[512,1024]{1,0:T(8,128)(2,1)S(1)} collective-permute-done((bf16[512,1024]{1,0:T(8,128)(2,1)}, bf16[512,1024]{1,0:T(8,128)(2,1)S(1)}, u32[]{:S(2)}, u32[]{:S(2)}) %collective-permute-start.32) | collective-permute-done | bytes 1048608 | tf_op jit(solution)/shard_map/ppermute | solution.py:790
  467.5 23.0 %collective-permute-done.40 = f32[1,256]{1,0:T(1,128)S(1)} collective-permute-done((f32[1,256]{1,0:T(1,128)S(1)}, f32[1,256]{1,0:T(1,128)S(1)}, u32[]{:S(2)}, u32[]{:S(2)}) %collective-permute-start.40) | collective-permute-done | bytes 1056 | tf_op jit(solution)/shard_map/ppermute | solution.py:777
  509.3 6.3 %collective-permute-done.46 = bf16[2,128,768]{2,1,0:T(8,128)(2,1)S(1)} collective-permute-done((bf16[2,128,768]{2,1,0:T(8,128)(2,1)S(1)}, bf16[2,128,768]{2,1,0:T(8,128)(2,1)S(1)}, u32[]{:S(2)}, u32[]{:S(2)}) %collective-permute-start.46) | collective-permute-done | bytes 393248 | tf_op jit(solution)/shard_map/ppermute | solution.py:801
  553.1 6.7 %collective-permute-done.54 = bf16[512,1024]{1,0:T(8,128)(2,1)} collective-permute-done((bf16[512,1024]{1,0:T(8,128)(2,1)}, bf16[512,1024]{1,0:T(8,128)(2,1)}, u32[]{:S(2)}, u32[]{:S(2)}) %collective-permute-start.54) | collective-permute-done | bytes 1048608 | tf_op jit(solution)/shard_map/ppermute | solution.py:790
  (298 shorter events, 196.3 us)
Async XLA Ops:
  7.2 92.0 %all-gather.4.cloned.1.call-start = ((), (), s32[]{:S(2)}) async-start(), calls=%async_computation.2 | async-start | bytes 1769472 | tf_op jit(solution)/shard_map/all_gather | solution.py:862
  9.2 192.7 %all-gather.6.cloned.1.call-start = ((), (), s32[]{:S(2)}) async-start(), calls=%async_computation.3 | async-start | bytes 2359296 | tf_op jit(solution)/shard_map/all_gather | solution.py:876
  45.1 177.8 %all-gather.8.cloned.1.call-start = ((), (), s32[]{:S(2)}) async-start(), calls=%async_computation.4 | async-start | bytes 28311552 | tf_op jit(solution)/shard_map/all_gather | solution.py:877
  88.9 257.3 %reduce-scatter.3.cloned.1.call-start = ((), (), s32[]{:S(2)}) async-start(), calls=%async_computation.5 | async-start | bytes 7077888 | tf_op jit(solution)/shard_map/reduce_scatter | solution.py:941
  91.6 23.9 %collective-permute-start.5 = (bf16[512,1024]{1,0:T(8,128)(2,1)S(1)}, bf16[512,1024]{1,0:T(8,128)(2,1)S(1)}, u32[]{:S(2)}, u32[]{:S(2)}) collective-permute-start(bf16[512,1024]{1,0:T(8,128)(2,1)S(1)} %copy-done.1), channel_id=1, source_target_pairs={{1,0},{2,1},{3,2},{5,4},{6,5},{7,6},{9,8},{10,9},{11,10},{13,12},{... | collective-permute-start | bytes 3145736 | tf_op jit(solution)/shard_map/ppermute | solution.py:782
  142.4 55.5 %collective-permute-start.18 = (f32[2,1024]{1,0:T(2,128)S(1)}, f32[2,1024]{1,0:T(2,128)S(1)}, u32[]{:S(2)}, u32[]{:S(2)}) collective-permute-start(f32[2,1024]{1,0:T(2,128)S(1)} %copy-done.38), channel_id=1, source_target_pairs={{0,1},{1,2},{2,3},{3,0},{4,5},{5,6},{6,7},{7,4},{8,9},{9,10},{10,1... | collective-permute-start | bytes 24584 | tf_op jit(solution)/shard_map/ppermute | solution.py:777
  146.0 55.8 %collective-permute-start.19 = (f32[2,1024]{1,0:T(2,128)S(1)}, f32[2,1024]{1,0:T(2,128)S(1)}, u32[]{:S(2)}, u32[]{:S(2)}) collective-permute-start(f32[2,1024]{1,0:T(2,128)S(1)} %copy-done.38), channel_id=1, source_target_pairs={{0,3},{1,0},{2,1},{3,2},{4,7},{5,4},{6,5},{7,6},{8,11},{9,8},{10,9... | collective-permute-start | bytes 24584 | tf_op jit(solution)/shard_map/ppermute | solution.py:777
  146.7 55.1 %collective-permute-start.20 = (f32[2,1024]{1,0:T(2,128)S(1)}, f32[2,1024]{1,0:T(2,128)S(1)}, u32[]{:S(2)}, u32[]{:S(2)}) collective-permute-start(f32[2,1024]{1,0:T(2,128)S(1)} %copy-done.38), channel_id=1, source_target_pairs={{0,2},{1,3},{2,0},{3,1},{4,6},{5,7},{6,4},{7,5},{8,10},{9,11},{10,... | collective-permute-start | bytes 24584 | tf_op jit(solution)/shard_map/ppermute | solution.py:777
  271.0 232.7 %reduce-scatter.5.cloned.1.call-start = ((), (), s32[]{:S(2)}) async-start(), calls=%async_computation.6 | async-start | bytes 21233664 | tf_op jit(solution)/shard_map/reduce_scatter | solution.py:945
  371.0 27.3 %collective-permute-start.26 = (f32[10,1024]{1,0:T(8,128)S(1)}, f32[10,1024]{1,0:T(8,128)S(1)}, u32[]{:S(2)}, u32[]{:S(2)}) collective-permute-start(f32[10,1024]{1,0:T(8,128)S(1)} %add.334), channel_id=1, source_target_pairs={{0,2},{1,3},{2,0},{3,1},{4,6},{5,7},{6,4},{7,5},{8,10},{9,11},{10,... | collective-permute-start | bytes 122888 | tf_op jit(solution)/shard_map/ppermute | solution.py:807
  371.1 27.1 %collective-permute-start.27 = (bf16[2,128,1024]{2,1,0:T(8,128)(2,1)S(1)}, bf16[2,128,1024]{2,1,0:T(8,128)(2,1)S(1)}, u32[]{:S(2)}, u32[]{:S(2)}) collective-permute-start(bf16[2,128,1024]{2,1,0:T(8,128)(2,1)S(1)} %dynamic-slice_bitcast_fusion.2), channel_id=1, source_target_pairs={{0,8},{4,12},{8,0},{12,4},{16,24},{20,28},{24,16},{28,20},{1,9},{5... | collective-permute-start | bytes 1572872 | tf_op jit(solution)/shard_map/ppermute | solution.py:801
  372.8 27.6 %collective-permute-start.28 = (bf16[2,128,1024]{2,1,0:T(8,128)(2,1)S(1)}, bf16[2,128,1024]{2,1,0:T(8,128)(2,1)S(1)}, u32[]{:S(2)}, u32[]{:S(2)}) collective-permute-start(bf16[2,128,1024]{2,1,0:T(8,128)(2,1)S(1)} %slice.109), channel_id=1, source_target_pairs={{0,2},{1,3},{2,0},{3,1},{4,6},{5,7},{6,4},{7,5},{8,10},{9,11},{10,... | collective-permute-start | bytes 1572872 | tf_op jit(solution)/shard_map/ppermute | solution.py:777
  400.4 25.0 %collective-permute-start.30 = (bf16[1,128,1024]{2,1,0:T(8,128)(2,1)S(1)}, bf16[1,128,1024]{2,1,0:T(8,128)(2,1)S(1)}, u32[]{:S(2)}, u32[]{:S(2)}) collective-permute-start(bf16[1,128,1024]{2,1,0:T(8,128)(2,1)S(1)} %constant_dynamic-slice_fusion.1), channel_id=1, source_target_pairs={{0,16},{4,20},{8,24},{12,28},{16,0},{20,4},{24,8},{28,12},{1,17},{... | collective-permute-start | bytes 786440 | tf_op jit(solution)/shard_map/ppermute | solution.py:801
  401.9 24.3 %collective-permute-start.31 = (bf16[1,128,1024]{2,1,0:T(8,128)(2,1)}, bf16[1,128,1024]{2,1,0:T(8,128)(2,1)S(1)}, u32[]{:S(2)}, u32[]{:S(2)}) collective-permute-start(bf16[1,128,1024]{2,1,0:T(8,128)(2,1)} %slice.110), channel_id=1, source_target_pairs={{0,2},{1,3},{2,0},{3,1},{4,6},{5,7},{6,4},{7,5},{8,10},{9,11},{10,... | collective-permute-start | bytes 786440 | tf_op jit(solution)/shard_map/ppermute | solution.py:777
  426.2 27.5 %collective-permute-start.32 = (bf16[512,1024]{1,0:T(8,128)(2,1)}, bf16[512,1024]{1,0:T(8,128)(2,1)S(1)}, u32[]{:S(2)}, u32[]{:S(2)}) collective-permute-start(bf16[512,1024]{1,0:T(8,128)(2,1)} %get-tuple-element.253), channel_id=1, source_target_pairs={{0,1},{4,5},{8,9},{12,13},{16,17},{20,21},{24,25},{28,29}} | collective-permute-start | bytes 3145736 | tf_op jit(solution)/shard_map/ppermute | solution.py:790
  455.7 41.3 %collective-permute-start.36 = (bf16[4,128,768]{2,1,0:T(8,128)(2,1)}, bf16[4,128,768]{2,1,0:T(8,128)(2,1)}, u32[]{:S(2)}, u32[]{:S(2)}) collective-permute-start(bf16[4,128,768]{2,1,0:T(8,128)(2,1)} %dynamic-slice_bitcast_fusion.1), channel_id=1, source_target_pairs={{0,4},{4,0},{8,12},{12,8},{16,20},{20,16},{24,28},{28,24},{1,5},{5... | collective-permute-start | bytes 2359304 | tf_op jit(solution)/shard_map/ppermute | solution.py:801
  458.6 44.5 %collective-permute-start.34 = (bf16[512,1024]{1,0:T(8,128)(2,1)}, bf16[512,1024]{1,0:T(8,128)(2,1)}, u32[]{:S(2)}, u32[]{:S(2)}) collective-permute-start(bf16[512,1024]{1,0:T(8,128)(2,1)} %get-tuple-element.301), channel_id=1, source_target_pairs={{0,1},{1,2},{4,5},{5,6},{8,9},{9,10},{12,13},{13,14},{16,17},{17,1... | collective-permute-start | bytes 3145736 | tf_op jit(solution)/shard_map/ppermute | solution.py:790
  464.0 39.7 %collective-permute-start.35 = (bf16[512,1024]{1,0:T(8,128)(2,1)}, bf16[512,1024]{1,0:T(8,128)(2,1)S(1)}, u32[]{:S(2)}, u32[]{:S(2)}) collective-permute-start(bf16[512,1024]{1,0:T(8,128)(2,1)} %get-tuple-element.300), channel_id=1, source_target_pairs={{2,1},{3,2},{6,5},{7,6},{10,9},{11,10},{14,13},{15,14},{18,17},{19... | collective-permute-start | bytes 3145736 | tf_op jit(solution)/shard_map/ppermute | solution.py:791
  464.7 25.8 %collective-permute-start.43 = (f32[10,1024]{1,0:T(8,128)S(1)}, f32[10,1024]{1,0:T(8,128)S(1)}, u32[]{:S(2)}, u32[]{:S(2)}) collective-permute-start(f32[10,1024]{1,0:T(8,128)S(1)} %add.344), channel_id=1, source_target_pairs={{0,8},{4,12},{8,0},{12,4},{16,24},{20,28},{24,16},{28,20},{1,9},{5... | collective-permute-start | bytes 122888 | tf_op jit(solution)/shard_map/ppermute | solution.py:807
  465.5 25.0 %collective-permute-start.40 = (f32[1,256]{1,0:T(1,128)S(1)}, f32[1,256]{1,0:T(1,128)S(1)}, u32[]{:S(2)}, u32[]{:S(2)}) collective-permute-start(f32[1,256]{1,0:T(1,128)S(1)} %copy-done.42), channel_id=1, source_target_pairs={{0,1},{1,2},{2,3},{3,0},{4,5},{5,6},{6,7},{7,4},{8,9},{9,10},{10,1... | collective-permute-start | bytes 3080 | tf_op jit(solution)/shard_map/ppermute | solution.py:777
  505.6 34.3 %collective-permute-start.44 = (bf16[3,128,1024]{2,1,0:T(8,128)(2,1)S(1)}, bf16[3,128,1024]{2,1,0:T(8,128)(2,1)S(1)}, u32[]{:S(2)}, u32[]{:S(2)}) collective-permute-start(bf16[3,128,1024]{2,1,0:T(8,128)(2,1)S(1)} %get-tuple-element.298), channel_id=1, source_target_pairs={{0,3},{1,0},{2,1},{3,2},{4,7},{5,4},{6,5},{7,6},{8,11},{9,8},{10,9... | collective-permute-start | bytes 2359304 | tf_op jit(solution)/shard_map/ppermute | solution.py:777
  507.1 34.0 %collective-permute-start.45 = (bf16[3,128,1024]{2,1,0:T(8,128)(2,1)S(1)}, bf16[3,128,1024]{2,1,0:T(8,128)(2,1)S(1)}, u32[]{:S(2)}, u32[]{:S(2)}) collective-permute-start(bf16[3,128,1024]{2,1,0:T(8,128)(2,1)S(1)} %get-tuple-element.297), channel_id=1, source_target_pairs={{0,1},{1,2},{2,3},{3,0},{4,5},{5,6},{6,7},{7,4},{8,9},{9,10},{10,1... | collective-permute-start | bytes 2359304 | tf_op jit(solution)/shard_map/ppermute | solution.py:777
  531.7 28.2 %collective-permute-start.54 = (bf16[512,1024]{1,0:T(8,128)(2,1)}, bf16[512,1024]{1,0:T(8,128)(2,1)}, u32[]{:S(2)}, u32[]{:S(2)}) collective-permute-start(bf16[512,1024]{1,0:T(8,128)(2,1)} %add.380), channel_id=1, source_target_pairs={{0,1},{1,2},{2,3},{4,5},{5,6},{6,7},{8,9},{9,10},{10,11},{12,13},{... | collective-permute-start | bytes 3145736 | tf_op jit(solution)/shard_map/ppermute | solution.py:790
  538.0 26.0 %collective-permute-start.55 = (bf16[512,1024]{1,0:T(8,128)(2,1)}, bf16[512,1024]{1,0:T(8,128)(2,1)}, u32[]{:S(2)}, u32[]{:S(2)}) collective-permute-start(bf16[512,1024]{1,0:T(8,128)(2,1)} %add.381), channel_id=1, source_target_pairs={{1,0},{2,1},{3,2},{5,4},{6,5},{7,6},{9,8},{10,9},{11,10},{13,12},{... | collective-permute-start | bytes 3145736 | tf_op jit(solution)/shard_map/ppermute | solution.py:791
  (81 other events, 1077.4 us)
Sparse Core Ops, SparseCore 0:
  10.5 28.2 all-gather.3
  45.2 26.4 all-gather.5
  89.0 123.5 all-gather.7
  271.1 64.6 reduce-scatter.2
  339.3 135.6 reduce-scatter.4

commit v7 on v6

--- a/solution.py
+++ b/solution.py
@@ -224,14 +224,10 @@
     width = x.shape[1]
     row = lax.broadcasted_iota(jnp.int32, (width, width), 0) // HEAD_DIM
     column = lax.broadcasted_iota(jnp.int32, (width, width), 1) // HEAD_DIM
-    same = jnp.where(row == column, 1.0, 0.0).astype(f32)
-    return lax.dot_general(
-        x,
-        same,
-        (((1,), (0,)), ((), ())),
-        precision=lax.Precision.HIGHEST,
-        preferred_element_type=f32,
-    )
+    same = jnp.where(row == column, 1.0, 0.0).astype(bf16)
+    high = x.astype(bf16)
+    low = (x - high.astype(f32)).astype(bf16)
+    return dot_nn(high, same) + dot_nn(low, same)
 
 
 def widen(table, width):
@@ -469,10 +465,17 @@
 
 def mix_kernel(count, *refs):
     pieces, weights = refs[:count], refs[count : 2 * count]
-    hidden_ref, rates_ref, branch_ref, middle_ref, low_ref, turned_ref = refs[2 * count :]
-    branch = dot_nt(pieces[0][...], weights[0][...])
+    hidden_ref, rates_ref, branch_ref, middle_ref, low_ref, turned_ref, out_ref = refs[2 * count :]
+    branch = dot_nt(pieces[0][...], block_of(weights[0]))
     for d in range(1, count):
-        branch = branch + dot_nt(pieces[d][...], weights[d][...])
+        branch = branch + dot_nt(pieces[d][...], block_of(weights[d]))
+
+    @pl.when(pl.program_id(0) == 0)
+    def _():
+        width = pieces[0].shape[1]
+        for d in range(count):
+            out_ref[:, d * width : (d + 1) * width] = block_of(weights[d])
+
     branch_ref[...] = branch
     hidden = hidden_ref[...].astype(f32)
     mixed = hidden + rates_ref[0:1, :] * (branch * rms_scale(branch) - hidden)
@@ -488,8 +491,12 @@
     width = pieces[0].shape[1]
     part = min(128, rows)
 
+    nd, blocks, shard, local_width = weights.shape
+    per = local_width // width
+    first = blocks - count // per
+
     def column(d):
-        return pl.BlockSpec((model, width), lambda i: (0, d))
+        return pl.BlockSpec((nd, 1, shard, width), lambda i: (0, first + d // per, 0, d % per))
 
     wide = pl.BlockSpec((part, model), lambda i: (i, 0))
     return pl.pallas_call(
@@ -498,12 +505,14 @@
         in_specs=[pl.BlockSpec((part, width), lambda i: (i, 0))] * count
         + [column(d) for d in range(count)]
         + [wide, pl.BlockSpec((2, model), lambda i: (0, 0))],
-        out_specs=[wide, wide, wide, pl.BlockSpec((model, part), lambda i: (0, i))],
+        out_specs=[wide, wide, wide, pl.BlockSpec((model, part), lambda i: (0, i))]
+        + [pl.BlockSpec((model, count * width), lambda i: (0, 0))],
         out_shape=[
             jax.ShapeDtypeStruct((rows, model), f32),
             jax.ShapeDtypeStruct((rows, model), f32),
             jax.ShapeDtypeStruct((rows, model), bf16),
             jax.ShapeDtypeStruct((model, rows), bf16),
+            jax.ShapeDtypeStruct((model, count * width), bf16),
         ],
         cost_estimate=pl.CostEstimate(
             flops=2 * rows * model * model, bytes_accessed=14 * rows * model, transcendentals=0
@@ -513,7 +522,7 @@
 
 
 def block_of(w_ref):
-    value = w_ref[:, 0, 0]
+    value = w_ref[:, 0]
     return value.reshape(value.shape[0] * value.shape[1], value.shape[2])
 
 
@@ -560,7 +569,7 @@
     def _():
         rate_ref[...] = jnp.zeros_like(rate_ref)
         rate = rates_ref[1:2, :]
-        part = 32
+        part = min(64, acc.shape[0])
 
         def body(at, carry):
             rows = pl.ds(pl.multiple_of(at * part, part), part)
@@ -590,12 +599,12 @@
 
 
 def weight_specs(weights, step, base=0):
-    nd, _, _, shard, local_width = weights.shape
+    nd, _, shard, local_width = weights.shape
     per = local_width // step
 
     def spec(m):
         return pl.BlockSpec(
-            (nd, 1, 1, shard, step), lambda i: (0, (i + base) // per, m, 0, (i + base) % per)
+            (nd, 1, shard, step), lambda i: (0, 3 * ((i + base) // per) + m, 0, (i + base) % per)
         )
 
     return [spec(0), spec(1), spec(2)]
@@ -603,7 +612,7 @@
 
 def feed(low, weights, scales, middle, cotangent, live, rates, step):
     rows, model = low.shape
-    total = weights.shape[1] * weights.shape[4]
+    total = scales.shape[1]
     columns = pl.BlockSpec((rows, step), lambda i: (0, i))
     whole = pl.BlockSpec((rows, model), lambda i: (0, 0))
     return pl.pallas_call(
@@ -688,7 +697,7 @@
     def _():
         rate_ref[...] = jnp.zeros_like(rate_ref)
         rate = rates_ref[0:1, :]
-        part = 32
+        part = min(64, acc.shape[0])
 
         def body(at, carry):
             rows = pl.ds(pl.multiple_of(at * part, part), part)
@@ -862,22 +871,38 @@
     qkv_full = lax.all_gather(
         jnp.concatenate([attn_low[0], attn_low[1], attn_low[2]], axis=1), "dp", axis=0, tiled=True
     )
-    mlp_low = mlp_weight.astype(bf16).reshape(3 * shard, hidden_width)
-    out_low = attn_low[3]
-    ups, downs = [mlp_low], [mlp_low]
+    low_block = jnp.concatenate(
+        [
+            mlp_weight.astype(bf16).reshape(3 * shard, hidden_width),
+            attn_low[3].reshape(-1, hidden_width),
+        ],
+        axis=0,
+    )
+    ups, downs = [low_block], [low_block]
     for hop in range(1, nt):
-        if hop == 2:
-            ups[1], downs[1], out_low = lax.optimization_barrier((ups[1], downs[1], out_low))
         if hop == nt - 1:
             ups[-1], downs[-1], hidden_in = lax.optimization_barrier((ups[-1], downs[-1], hidden_in))
         up, down = carry_on(ups[-1], downs[-1], hop, "tensor", nt)
         ups.append(up)
         downs.append(down)
-    out_full = lax.all_gather(jnp.concatenate(gather(out_low), axis=1), "dp", axis=0, tiled=True)
+    low_blocks = [sum(both(ups, downs, d)) for d in range(nt)]
+    out_low = jnp.concatenate(
+        [low[3 * shard :].reshape(shard, heads_width) for low in low_blocks], axis=1
+    )
     mlp_full = lax.all_gather(
-        jnp.concatenate([sum(both(ups, downs, d)) for d in order], axis=0), "dp", axis=0, tiled=True
-    )
-    mlp_full = mlp_full.reshape(nd, nt, 3, shard, hidden_width)
+        jnp.concatenate(
+            [low_blocks[d][: 3 * shard] for d in order]
+            + [
+                out_low[:, at : at + hidden_width]
+                for at in range(0, nt * heads_width, hidden_width)
+            ],
+            axis=0,
+        ),
+        "dp",
+        axis=0,
+        tiled=True,
+    )
+    mlp_full = mlp_full.reshape(nd, -1, shard, hidden_width)
     scales_parts = gather(mlp_scales)
     scales_row = jnp.concatenate([scales_parts[d] for d in order], axis=1)
 
@@ -919,7 +944,7 @@
         shift(take_block(attended_row, (me + d) % nt, rows, 0), "tensor", d, nt)
         for d in range(1, nt)
     ]
-    branch, middle, middle_low, middle_t = mix(attended, out_full, hidden_in, rates)
+    branch, middle, middle_low, middle_t, out_full = mix(attended, mlp_full, hidden_in, rates)
     row_segments = take_block(segments, me, rows, 0)
     live = (row_segments < pad_segment).astype(f32)[:, None]
     up, gate, hidden_units, result, middle_direct, mlp_out_low, mlp_out_t, rate_mlp_grad = feed(
@@ -1012,42 +1037,44 @@
         (qkv_grad, pieces, small, out_sum, far_last)
     )
     far_part = jnp.concatenate([far_first, far_last], axis=0)
-    small = advance(small)
     hidden_turn = [hidden_parts[(nt - d) % nt] for d in range(nt)]
     qkv_sum = projection_grads(hidden_turn, qkv_grad)
     qkv_sum = qkv_sum.reshape(nd, shard, -1)
 
-    def own_pieces(part, axis, width, places):
-        pieces = [
-            lax.slice_in_dim(part, p * width, (p + 1) * width, axis=axis)
-            for p in range(len(places))
+    def blocks_of(part, axis, width):
+        return [
+            lax.slice_in_dim(part, at, at + width, axis=axis)
+            for at in range(0, part.shape[axis], width)
         ]
+
+    def to_owners(pieces, places):
         return [shift(piece, "tensor", -d, nt) if d else piece for d, piece in zip(places, pieces)]
 
+    out_sum, gain_grad, qkv_sum = lax.optimization_barrier((out_sum, gain_grad, qkv_sum))
+    out_pieces = to_owners(blocks_of(out_sum.astype(bf16), 1, heads_width), range(nt))
+    gain_parts = gather(gain_grad)
     ahead = behind = None
     for hop in range(1, nt):
         if hop == 2:
-            ahead, behind, qkv_sum = lax.optimization_barrier((ahead, behind, qkv_sum))
-            out_pieces = own_pieces(out_sum.astype(bf16), 1, heads_width, range(nt))
-            gain_parts = gather(gain_grad)
+            ahead, behind, qkv_sum, out_pieces, gain_parts = lax.optimization_barrier(
+                (ahead, behind, qkv_sum, out_pieces, gain_parts)
+            )
         if hop == max(2, nt - 1):
-            ahead, behind, near_part, qkv_sum, out_pieces, gain_parts, small = (
-                lax.optimization_barrier(
-                    (ahead, behind, near_part, qkv_sum, out_pieces, gain_parts, small)
-                )
+            ahead, behind, near_part, qkv_sum = lax.optimization_barrier(
+                (ahead, behind, near_part, qkv_sum)
             )
-            near_pieces = own_pieces(near_part, 2, hidden_width, order[:-1])
+            near_pieces = blocks_of(near_part, 2, hidden_width)
+            near_pieces, qkv_sum, small = lax.optimization_barrier((near_pieces, qkv_sum, small))
+            near_pieces = to_owners(near_pieces, order[:-1])
         ahead, behind = line_sum(pieces, hop, ahead, behind, "tensor", nt)
         if hop == 2:
-            qkv_sum = halving(qkv_sum, "dp", nd, halvings[0])
-    for k in halvings[1:]:
+            for k in halvings[:2]:
+                qkv_sum = halving(qkv_sum, "dp", nd, k)
+    for k in halvings[2:]:
         qkv_sum = halving(qkv_sum, "dp", nd, k)
     gain_row = spread(jnp.concatenate(gain_parts, axis=1), range(nt))
     while steps:
         small = advance(small)
-    rates_grad = small[:2]
-    mlp_scales_grad = small[2:].reshape(2, nt * hidden_width)
-
     out_own = sum(piece.astype(f32) for piece in out_pieces)
     attn_weight_grad = jnp.stack(
         [qkv_sum[:, m * heads_width : (m + 1) * heads_width] for m in range(3)] + [out_own]
@@ -1058,7 +1085,10 @@
     attn_square = jnp.sum(attn_moved * attn_moved, axis=1, keepdims=True)
     last = jnp.concatenate([attn_square.reshape(1, -1), gain_row], axis=1)
     last = butterfly(last, "dp", nd)
-    near_pieces, last = lax.optimization_barrier((near_pieces, last))
+    near_pieces, last, small = lax.optimization_barrier((near_pieces, last, small))
+    rates_grad = small[:2]
+    mlp_scales_grad = small[2:].reshape(2, nt * hidden_width)
+
     attn_square = last[:, : 4 * heads_width].reshape(4, 1, heads_width)
     gain_row = last[:, 4 * heads_width :].reshape(-1)
     attn_new = attn_moved * lax.rsqrt(attn_square + norm_eps)

time: 581 us -> 566 us (0.974)
  Pallas kernels: 219 us -> 207 us
    ppermute x3, waiting for transfers between devices: 19.6 us -> 9.69 us  [line_sum(): up = lax.ppermute(ahead, axis, [(i, i + 1) for i in range(hop)])]
    pallas_call x1, Pallas kernels: 23.5 us -> 16.2 us  [project_back(): pl.pallas_call(functools.partial(project_back_kernel, groups), grid_spec=...]
    all_gather x2 -> x1, waiting for transfers between devices: 0.03 us -> 6.58 us  [local(): lax.all_gather(jnp.concatenate([low_blocks[d][:3 * shard] for d in order]...]
    ppermute x22 -> x19, waiting for transfers between devices: 61.8 us -> 57.3 us  [shift(): lax.ppermute(value, axis, [(i, (i + distance) % size) for i in range(size)])]
    ppermute x22 -> x19, starting transfers between devices: 30.9 us -> 27.1 us  [shift(): lax.ppermute(value, axis, [(i, (i + distance) % size) for i in range(size)])]
  transfers between devices with their start and end apart: 62 -> 58, of which waited for: 30 -> 27; matrix products, arithmetic and copies ran while one was open for 8% -> 9% of each run, Pallas kernels for 30% -> 27%
where the time goes in v7:
time: 566 us; the launch traced here: 560 us
  Pallas kernels  207 us (37%)
  waiting for transfers between devices  197 us (35%)
  starting transfers between devices  77 us (14%)
  other arithmetic  31.7 us (6%)
  local copies, waits for them, and re-layouts  23.1 us (4%)
  between operations  15.1 us (3%)
  matrix products  8.06 us (1%)
    ppermute x6, waiting for transfers between devices, carry_on(): lax.ppermute(down, axis, [(i, i - 1) for i in range(1, size - hop + 1)])  74.4 us
    ppermute x19, waiting for transfers between devices, shift(): lax.ppermute(value, axis, [(i, (i + distance) % size) for i in range(size)])  57.3 us
    pallas_call x2, Pallas kernels, feed_back(): pl.pallas_call(feed_back_last_kernel if last else feed_back_first_kernel,...  52.6 us
    pallas_call x2, Pallas kernels, attend_back(): pl.pallas_call(functools.partial(attend_back_kernel, group * heads, heads...  41.6 us
    pallas_call x1, Pallas kernels, feed(): pl.pallas_call(feed_kernel, grid=(total // step,), in_specs=[whole] + wei...  30.4 us
    ppermute x19, starting transfers between devices, shift(): lax.ppermute(value, axis, [(i, (i + distance) % size) for i in range(size)])  27.1 us
    pallas_call x4, Pallas kernels, project(): pl.pallas_call(functools.partial(project_kernel, count), grid_spec=pltpu....  23.5 us
    ppermute x6, waiting for transfers between devices, carry_on(): up = lax.ppermute(up, axis, [(i, i + 1) for i in range(hop - 1, size - 1)])  22.7 us
  transfers between devices with their start and end apart: 58, of which 27 were waited for; matrix products, arithmetic and copies ran while one was open for 9% of the time, Pallas kernels for 27%

profile of v7, /device:TPU:0, one launch (start us, length us, event | category | flops | bytes accessed | tf_op | source)
XLA Modules:
  0.0 559.5 jit_solution(9697506952289811433)
XLA Ops:
  17.9 16.4 %collective-permute-done = bf16[416,1024]{1,0:T(8,128)(2,1)S(1)} collective-permute-done((bf16[416,1024]{1,0:T(8,128)(2,1)}, bf16[416,1024]{1,0:T(8,128)(2,1)S(1)}, u32[]{:S(2)}, u32[]{:S(2)}) %collective-permute-start) | collective-permute-done | bytes 852000 | tf_op jit(solution)/shard_map/ppermute | solution.py:790
  39.7 20.4 %collective-permute-done.3 = bf16[416,1024]{1,0:T(8,128)(2,1)} collective-permute-done((bf16[416,1024]{1,0:T(8,128)(2,1)S(1)}, bf16[416,1024]{1,0:T(8,128)(2,1)}, u32[]{:S(2)}, u32[]{:S(2)}) %collective-permute-start.3) | collective-permute-done | bytes 852000 | tf_op jit(solution)/shard_map/ppermute | solution.py:791
  67.6 15.1 %collective-permute-done.13 = bf16[416,1024]{1,0:T(8,128)(2,1)} collective-permute-done((bf16[416,1024]{1,0:T(8,128)(2,1)}, bf16[416,1024]{1,0:T(8,128)(2,1)}, u32[]{:S(2)}, u32[]{:S(2)}) %collective-permute-start.13) | collective-permute-done | bytes 852000 | tf_op jit(solution)/shard_map/ppermute | solution.py:791
  97.5 5.9 %project.4 = (bf16[2048,256]{1,0:T(8,128)(2,1)}, bf16[2048,256]{1,0:T(8,128)(2,1)}, bf16[2048,256]{1,0:T(8,128)(2,1)}, f32[2048,256]{1,0:T(8,128)}, f32[2048,256]{1,0:T(8,128)}) custom-call(s32[1]{0:T(128)} %bitcast.2.index_ref, bf16[512,1024]{1,0:T(8,128)(2,1)} %refs_0_.1, ...), custom_call_target="tpu_custom_call" | custom-call | flops 805306368 | bytes 2097152 | tf_op jit(solution)/shard_map/project/pallas_call | solution.py:275
  103.4 6.3 %collective-permute-done.4.refs_0_.refs_5_ = bf16[512,1024]{1,0:T(8,128)(2,1)S(1)} collective-permute-done((bf16[512,1024]{1,0:T(8,128)(2,1)S(1)}, bf16[512,1024]{1,0:T(8,128)(2,1)S(1)}, u32[]{:S(2)}, u32[]{:S(2)}) %collective-permute-start.4) | collective-permute-done | bytes 1048608 | tf_op jit(solution)/shard_map/ppermute | solution.py:790
  115.9 23.1 %collective-permute-done.7.refs_1_.refs_4_ = bf16[512,1024]{1,0:T(8,128)(2,1)} collective-permute-done((bf16[512,1024]{1,0:T(8,128)(2,1)S(1)}, bf16[512,1024]{1,0:T(8,128)(2,1)}, u32[]{:S(2)}, u32[]{:S(2)}) %collective-permute-start.7) | collective-permute-done | bytes 1048608 | tf_op jit(solution)/shard_map/ppermute | solution.py:791
  149.5 5.9 %project.5 = (bf16[2048,256]{1,0:T(8,128)(2,1)}, bf16[2048,256]{1,0:T(8,128)(2,1)}, bf16[2048,256]{1,0:T(8,128)(2,1)}, f32[2048,256]{1,0:T(8,128)}, f32[2048,256]{1,0:T(8,128)}) custom-call(s32[1]{0:T(128)} %bitcast.9.index_ref, bf16[512,1024]{1,0:T(8,128)(2,1)} %copy-done.6, ...), custom_call_target="tpu_custom_call", output_to_operand_aliasing={{0}: (9, {}), {1}: (10, {}), {2}: (11, {}), {3}: (12, {}), ... | custom-call | flops 805306368 | bytes 2097152 | tf_op jit(solution)/shard_map/project/pallas_call | solution.py:275
  155.4 8.3 %collective-permute-done.9.refs_1_.refs_6_ = bf16[512,1024]{1,0:T(8,128)(2,1)} collective-permute-done((bf16[512,1024]{1,0:T(8,128)(2,1)}, bf16[512,1024]{1,0:T(8,128)(2,1)}, u32[]{:S(2)}, u32[]{:S(2)}) %collective-permute-start.9) | collective-permute-done | bytes 1048608 | tf_op jit(solution)/shard_map/ppermute | solution.py:791
  175.5 20.3 %attend.1 = (bf16[2048,256]{1,0:T(8,128)(2,1)}, f32[2048,256]{1,0:T(8,128)}, f32[4,2048]{1,0:T(4,128)}) custom-call(bf16[2048,256]{1,0:T(8,128)(2,1)} %get-tuple-element.194.q_ref, bf16[2048,256]{1,0:T(8,128)(2,1)} %get-tuple-element.195.k_ref, bf16[2048,256]{1,0:T(8,128)(2,1)} %get-tuple-element.196.v_ref, s32[2048,1]{1,0:T(8,128)} %copy.44.start_ref), custom_call_target="tpu_custom_call" | custom-call | flops 20000000000 | bytes 4194304 | tf_op jit(solution)/shard_map/attend/pallas_call | solution.py:113
  202.0 6.1 %collective-permute-done.10.refs_1_ = bf16[512,256]{1,0:T(8,128)(2,1)S(1)} collective-permute-done((bf16[512,256]{1,0:T(8,128)(2,1)S(1)}, bf16[512,256]{1,0:T(8,128)(2,1)S(1)}, u32[]{:S(2)}, u32[]{:S(2)}) %collective-permute-start.10) | collective-permute-done | bytes 262176 | tf_op jit(solution)/shard_map/ppermute | solution.py:786
  213.8 6.6 %all-gather.5.cloned.1.call-done = bf16[13312,1024]{1,0:T(8,128)(2,1)} async-done(((bf16[1664,1024]{1,0:T(8,128)(2,1)}), bf16[13312,1024]{1,0:T(8,128)(2,1)}) %all-gather.5.cloned.1.call-update) | async-done | bytes 27262992 | tf_op jit(solution)/shard_map/all_gather | solution.py:892
  220.4 9.1 %mix.1 = (f32[512,1024]{1,0:T(8,128)}, f32[512,1024]{1,0:T(8,128)}, bf16[512,1024]{1,0:T(8,128)(2,1)}, bf16[1024,512]{1,0:T(8,128)(2,1)}, bf16[1024,1024]{1,0:T(8,128)(2,1)}) custom-call(bf16[512,256]{1,0:T(8,128)(2,1)} %get-tuple-element.317.refs_0_, bf16[512,256]{1,0:T(8,128)(2,1)} %copy-done.11, bf16[512,256]{1,0:T(8,128)(2,1)} %copy-done.12, ...), custom_call_target="tpu_custom_call" | custom-call | flops 1073741824 | bytes 7340032 | tf_op jit(solution)/shard_map/mix/pallas_call | solution.py:502
  229.5 30.4 %feed.1 = (f32[512,4096]{1,0:T(8,128)}, f32[512,4096]{1,0:T(8,128)}, bf16[512,4096]{1,0:T(8,128)(2,1)}, bf16[512,1024]{1,0:T(8,128)(2,1)}, f32[512,1024]{1,0:T(8...) custom-call(bf16[512,1024]{1,0:T(8,128)(2,1)} %get-tuple-element.200.m_ref, ...), custom_call_target="tpu_custom_call" | custom-call | flops 12884901888 | bytes 46137344 | tf_op jit(solution)/shard_map/feed/pallas_call | solution.py:618
  259.8 15.1 %feed_back_first.1 = (bf16[3,1024,1024]{2,1,0:T(8,128)(2,1)}, f32[2,1024]{1,0:T(2,128)}, f32[512,1024]{1,0:T(8,128)}) custom-call(bf16[512,1024]{1,0:T(8,128)(2,1)} %get-tuple-element.203.refs_0_, bf16[1024,512]{1,0:T(8,128)(2,1)} %get-tuple-element.204.refs_1_, bf16[1024,512]{1,0:T(8,128)(2,1)} %get-tuple-element.205.refs_2_, ...), custom_call_target="tpu_custom_call" | custom-call | flops 6442450944 | bytes 17825792 | tf_op jit(solution)/shard_map/feed_back_first/pallas_call | solution.py:743
  275.1 37.4 %feed_back_last.1 = (bf16[3,1024,3072]{2,1,0:T(8,128)(2,1)}, f32[2,3072]{1,0:T(2,128)}, f32[512,1024]{1,0:T(8,128)}, bf16[512,1024]{1,0:T(8,128)(2,1)}, f32[1,1024]{1,0:T(1,128)}) custom-call(bf16[512,1024]{1,0:T(8,128)(2,1)} %get-tuple-element.203.refs_0_, bf16[1024,512]{1,0:T(8,128)(2,1)} %get-tuple-element.204.refs_1_, ...), custom_call_target="tpu_custom_call" | custom-call | flops 19327352832 | bytes 53477376 | tf_op jit(solution)/shard_map/feed_back_last/pallas_call | solution.py:743
  332.5 9.2 %collective-permute-done.19 = bf16[512,256]{1,0:T(8,128)(2,1)S(1)} collective-permute-done((bf16[512,256]{1,0:T(8,128)(2,1)}, bf16[512,256]{1,0:T(8,128)(2,1)S(1)}, u32[]{:S(2)}, u32[]{:S(2)}) %collective-permute-start.19) | collective-permute-done | bytes 262176 | tf_op jit(solution)/shard_map/ppermute | solution.py:786
  346.3 20.8 %attend_back.2 = (f32[2048,128]{1,0:T(8,128)}, f32[2048,128]{1,0:T(8,128)}, f32[2048,128]{1,0:T(8,128)}) custom-call(bf16[2048,256]{1,0:T(8,128)(2,1)} %get-tuple-element.194.q_ref, bf16[2048,256]{1,0:T(8,128)(2,1)} %fusion.3.do_ref, bf16[2048,256]{1,0:T(8,128)(2,1)} %get-tuple-element.195.k_ref, bf16[2048,256]{1,0:T(8,128)(2,1)} %get-tuple-element.196.v_ref, ...), custom_call_target="tpu_custom_call" | custom-call | flops 40000000000 | bytes 5242880 | tf_op jit(solution)/shard_map/attend_back/pallas_call | solution.py:193
  373.7 20.8 %attend_back.3 = (f32[2048,128]{1,0:T(8,128)}, f32[2048,128]{1,0:T(8,128)}, f32[2048,128]{1,0:T(8,128)}) custom-call(bf16[2048,256]{1,0:T(8,128)(2,1)} %get-tuple-element.194.q_ref, bf16[2048,256]{1,0:T(8,128)(2,1)} %fusion.3.do_ref, bf16[2048,256]{1,0:T(8,128)(2,1)} %get-tuple-element.195.k_ref, bf16[2048,256]{1,0:T(8,128)(2,1)} %get-tuple-element.196.v_ref, ...), custom_call_target="tpu_custom_call" | custom-call | flops 40000000000 | bytes 5242880 | tf_op jit(solution)/shard_map/attend_back/pallas_call | solution.py:193
  399.9 16.2 %project_back.1 = (bf16[2048,768]{1,0:T(8,128)(2,1)}, f32[1,256]{1,0:T(1,128)}, bf16[512,1024]{1,0:T(8,128)(2,1)}, bf16[512,1024]{1,0:T(8,128)(2,1)}, bf16[512,1...) custom-call(s32[1]{0:T(128)} %bitcast.15.index_ref, f32[2048,128]{1,0:T(8,128)} %get-tuple-element.239.refs_0_, ...), custom_call_target="tpu_custom_call" | custom-call | flops 524288 | bytes 524288 | tf_op jit(solution)/shard_map/project_back/pallas_call | solution.py:372
  423.6 8.6 %projection_grads.1 = bf16[1024,768]{1,0:T(8,128)(2,1)} custom-call(bf16[512,1024]{1,0:T(8,128)(2,1)} %refs_0_.1, bf16[512,1024]{1,0:T(8,128)(2,1)} %collective-permute-done.8.refs_0_.refs_1_, bf16[512,1024]{1,0:T(8,128)(2,1)} %copy-done.5, bf16[512,1024]{1,0:T(8,128)(2,1)} %copy-done.6, bf16[512,1024]{1,0:T(8,128)(2,1)} %collective-permute-done.7.refs_1_.refs_4_, ...), custom_call_target="tpu_custom_call" | custom-call | flops 3221225472 | bytes 16777216 | tf_op jit(solution)/shard_map/projection_grads/pallas_call | solution.py:416
  436.2 11.8 %collective-permute-done.34 = f32[1,256]{1,0:T(1,128)S(1)} collective-permute-done((f32[1,256]{1,0:T(1,128)S(1)}, f32[1,256]{1,0:T(1,128)S(1)}, u32[]{:S(2)}, u32[]{:S(2)}) %collective-permute-start.34) | collective-permute-done | bytes 1056 | tf_op jit(solution)/shard_map/ppermute | solution.py:786
  463.3 15.7 %collective-permute-done.40 = bf16[2,128,768]{2,1,0:T(8,128)(2,1)S(1)} collective-permute-done((bf16[2,128,768]{2,1,0:T(8,128)(2,1)S(1)}, bf16[2,128,768]{2,1,0:T(8,128)(2,1)S(1)}, u32[]{:S(2)}, u32[]{:S(2)}) %collective-permute-start.40) | collective-permute-done | bytes 393248 | tf_op jit(solution)/shard_map/ppermute | solution.py:810
  510.1 17.0 %collective-permute-done.42 = bf16[3,128,1024]{2,1,0:T(8,128)(2,1)S(1)} collective-permute-done((bf16[3,128,1024]{2,1,0:T(8,128)(2,1)S(1)}, bf16[3,128,1024]{2,1,0:T(8,128)(2,1)S(1)}, u32[]{:S(2)}, u32[]{:S(2)}) %collective-permute-start.42) | collective-permute-done | bytes 786464 | tf_op jit(solution)/shard_map/ppermute | solution.py:786
  539.1 6.1 %collective-permute-done.52 = bf16[512,1024]{1,0:T(8,128)(2,1)} collective-permute-done((bf16[512,1024]{1,0:T(8,128)(2,1)}, bf16[512,1024]{1,0:T(8,128)(2,1)}, u32[]{:S(2)}, u32[]{:S(2)}) %collective-permute-start.52) | collective-permute-done | bytes 1048608 | tf_op jit(solution)/shard_map/ppermute | solution.py:799
  (300 shorter events, 191.9 us)
Async XLA Ops:
  7.2 90.3 %all-gather.3.cloned.1.call-start = ((), (), s32[]{:S(2)}) async-start(), calls=%async_computation.2 | async-start | bytes 1769472 | tf_op jit(solution)/shard_map/all_gather | solution.py:871
  10.9 23.5 %collective-permute-start = (bf16[416,1024]{1,0:T(8,128)(2,1)}, bf16[416,1024]{1,0:T(8,128)(2,1)S(1)}, u32[]{:S(2)}, u32[]{:S(2)}) collective-permute-start(bf16[416,1024]{1,0:T(8,128)(2,1)} %pad_maximum_fusion), channel_id=1, source_target_pairs={{0,1},{1,2},{2,3},{4,5},{5,6},{6,7},{8,9},{9,10},{10,11},{12,13},{... | collective-permute-start | bytes 2555912 | tf_op jit(solution)/shard_map/ppermute | solution.py:790
  15.9 22.5 %collective-permute-start.2 = (bf16[416,1024]{1,0:T(8,128)(2,1)}, bf16[416,1024]{1,0:T(8,128)(2,1)S(1)}, u32[]{:S(2)}, u32[]{:S(2)}) collective-permute-start(bf16[416,1024]{1,0:T(8,128)(2,1)} %pad_maximum_fusion), channel_id=1, source_target_pairs={{1,0},{2,1},{3,2},{5,4},{6,5},{7,6},{9,8},{10,9},{11,10},{13,12},{... | collective-permute-start | bytes 2555912 | tf_op jit(solution)/shard_map/ppermute | solution.py:791
  17.9 202.5 %all-gather.5.cloned.1.call-start = ((), (), s32[]{:S(2)}) async-start(), calls=%async_computation.3 | async-start | bytes 30670848 | tf_op jit(solution)/shard_map/all_gather | solution.py:892
  87.9 257.4 %reduce-scatter.3.cloned.1.call-start = ((), (), s32[]{:S(2)}) async-start(), calls=%async_computation.4 | async-start | bytes 7077888 | tf_op jit(solution)/shard_map/reduce_scatter | solution.py:966
  90.0 23.9 %collective-permute-start.5 = (bf16[512,1024]{1,0:T(8,128)(2,1)S(1)}, bf16[512,1024]{1,0:T(8,128)(2,1)S(1)}, u32[]{:S(2)}, u32[]{:S(2)}) collective-permute-start(bf16[512,1024]{1,0:T(8,128)(2,1)S(1)} %copy-done), channel_id=1, source_target_pairs={{1,0},{2,1},{3,2},{5,4},{6,5},{7,6},{9,8},{10,9},{11,10},{13,12},{... | collective-permute-start | bytes 3145736 | tf_op jit(solution)/shard_map/ppermute | solution.py:791
  114.6 24.4 %collective-permute-start.7 = (bf16[512,1024]{1,0:T(8,128)(2,1)S(1)}, bf16[512,1024]{1,0:T(8,128)(2,1)}, u32[]{:S(2)}, u32[]{:S(2)}) collective-permute-start(bf16[512,1024]{1,0:T(8,128)(2,1)S(1)} %collective-permute-done.5.refs_1_.refs_2_), channel_id=1, source_target_pairs={{1,0},{2,1},{5,4},{6,5},{9,8},{10,9},{13,12},{14,13},{17,16},{18,1... | collective-permute-start | bytes 3145736 | tf_op jit(solution)/shard_map/ppermute | solution.py:791
  140.7 23.1 %collective-permute-start.9 = (bf16[512,1024]{1,0:T(8,128)(2,1)}, bf16[512,1024]{1,0:T(8,128)(2,1)}, u32[]{:S(2)}, u32[]{:S(2)}) collective-permute-start(bf16[512,1024]{1,0:T(8,128)(2,1)} %collective-permute-done.7.refs_1_.refs_4_), channel_id=1, source_target_pairs={{1,0},{5,4},{9,8},{13,12},{17,16},{21,20},{25,24},{29,28}} | collective-permute-start | bytes 3145736 | tf_op jit(solution)/shard_map/ppermute | solution.py:791
  142.0 55.8 %collective-permute-start.15 = (f32[2,1024]{1,0:T(2,128)S(1)}, f32[2,1024]{1,0:T(2,128)S(1)}, u32[]{:S(2)}, u32[]{:S(2)}) collective-permute-start(f32[2,1024]{1,0:T(2,128)S(1)} %copy-done.36), channel_id=1, source_target_pairs={{0,1},{1,2},{2,3},{3,0},{4,5},{5,6},{6,7},{7,4},{8,9},{9,10},{10,1... | collective-permute-start | bytes 24584 | tf_op jit(solution)/shard_map/ppermute | solution.py:786
  145.6 56.4 %collective-permute-start.16 = (f32[2,1024]{1,0:T(2,128)S(1)}, f32[2,1024]{1,0:T(2,128)S(1)}, u32[]{:S(2)}, u32[]{:S(2)}) collective-permute-start(f32[2,1024]{1,0:T(2,128)S(1)} %copy-done.36), channel_id=1, source_target_pairs={{0,3},{1,0},{2,1},{3,2},{4,7},{5,4},{6,5},{7,6},{8,11},{9,8},{10,9... | collective-permute-start | bytes 24584 | tf_op jit(solution)/shard_map/ppermute | solution.py:786
  146.0 55.9 %collective-permute-start.17 = (f32[2,1024]{1,0:T(2,128)S(1)}, f32[2,1024]{1,0:T(2,128)S(1)}, u32[]{:S(2)}, u32[]{:S(2)}) collective-permute-start(f32[2,1024]{1,0:T(2,128)S(1)} %copy-done.36), channel_id=1, source_target_pairs={{0,2},{1,3},{2,0},{3,1},{4,6},{5,7},{6,4},{7,5},{8,10},{9,11},{10,... | collective-permute-start | bytes 24584 | tf_op jit(solution)/shard_map/ppermute | solution.py:786
  275.0 207.7 %reduce-scatter.5.cloned.1.call-start = ((), (), s32[]{:S(2)}) async-start(), calls=%async_computation.5 | async-start | bytes 21233664 | tf_op jit(solution)/shard_map/reduce_scatter | solution.py:970
  345.3 21.7 %collective-permute-start.21 = (f32[10,1024]{1,0:T(8,128)S(1)}, f32[10,1024]{1,0:T(8,128)S(1)}, u32[]{:S(2)}, u32[]{:S(2)}) collective-permute-start(f32[10,1024]{1,0:T(8,128)S(1)} %pad_maximum_fusion.3), channel_id=1, source_target_pairs={{0,1},{1,0},{2,3},{3,2},{4,5},{5,4},{6,7},{7,6},{8,9},{9,8},{10,11... | collective-permute-start | bytes 122888 | tf_op jit(solution)/shard_map/ppermute | solution.py:816
  368.9 27.3 %collective-permute-start.23 = (f32[10,1024]{1,0:T(8,128)S(1)}, f32[10,1024]{1,0:T(8,128)S(1)}, u32[]{:S(2)}, u32[]{:S(2)}) collective-permute-start(f32[10,1024]{1,0:T(8,128)S(1)} %add.334), channel_id=1, source_target_pairs={{0,2},{1,3},{2,0},{3,1},{4,6},{5,7},{6,4},{7,5},{8,10},{9,11},{10,... | collective-permute-start | bytes 122888 | tf_op jit(solution)/shard_map/ppermute | solution.py:816
  371.1 25.1 %collective-permute-start.24 = (bf16[2,128,1024]{2,1,0:T(8,128)(2,1)S(1)}, bf16[2,128,1024]{2,1,0:T(8,128)(2,1)S(1)}, u32[]{:S(2)}, u32[]{:S(2)}) collective-permute-start(bf16[2,128,1024]{2,1,0:T(8,128)(2,1)S(1)} %dynamic-slice_bitcast_fusion.2), channel_id=1, source_target_pairs={{0,8},{4,12},{8,0},{12,4},{16,24},{20,28},{24,16},{28,20},{1,9},{5... | collective-permute-start | bytes 1572872 | tf_op jit(solution)/shard_map/ppermute | solution.py:810
  372.7 25.8 %collective-permute-start.25 = (bf16[2,128,1024]{2,1,0:T(8,128)(2,1)S(1)}, bf16[2,128,1024]{2,1,0:T(8,128)(2,1)S(1)}, u32[]{:S(2)}, u32[]{:S(2)}) collective-permute-start(bf16[2,128,1024]{2,1,0:T(8,128)(2,1)S(1)} %slice.133), channel_id=1, source_target_pairs={{0,2},{1,3},{2,0},{3,1},{4,6},{5,7},{6,4},{7,5},{8,10},{9,11},{10,... | collective-permute-start | bytes 1572872 | tf_op jit(solution)/shard_map/ppermute | solution.py:786
  417.0 38.6 %collective-permute-start.29 = (bf16[512,1024]{1,0:T(8,128)(2,1)}, bf16[512,1024]{1,0:T(8,128)(2,1)S(1)}, u32[]{:S(2)}, u32[]{:S(2)}) collective-permute-start(bf16[512,1024]{1,0:T(8,128)(2,1)} %get-tuple-element.257), channel_id=1, source_target_pairs={{0,1},{4,5},{8,9},{12,13},{16,17},{20,21},{24,25},{28,29}} | collective-permute-start | bytes 3145736 | tf_op jit(solution)/shard_map/ppermute | solution.py:799
  422.7 32.9 %collective-permute-start.30 = (bf16[512,1024]{1,0:T(8,128)(2,1)}, bf16[512,1024]{1,0:T(8,128)(2,1)S(1)}, u32[]{:S(2)}, u32[]{:S(2)}) collective-permute-start(bf16[512,1024]{1,0:T(8,128)(2,1)} %get-tuple-element.258), channel_id=1, source_target_pairs={{3,2},{7,6},{11,10},{15,14},{19,18},{23,22},{27,26},{31,30}} | collective-permute-start | bytes 3145736 | tf_op jit(solution)/shard_map/ppermute | solution.py:800
  458.0 24.8 %collective-permute-start.37 = (bf16[512,1024]{1,0:T(8,128)(2,1)S(1)}, bf16[512,1024]{1,0:T(8,128)(2,1)S(1)}, u32[]{:S(2)}, u32[]{:S(2)}) collective-permute-start(bf16[512,1024]{1,0:T(8,128)(2,1)S(1)} %get-tuple-element.313), channel_id=1, source_target_pairs={{0,1},{1,2},{4,5},{5,6},{8,9},{9,10},{12,13},{13,14},{16,17},{17,1... | collective-permute-start | bytes 3145736 | tf_op jit(solution)/shard_map/ppermute | solution.py:799
  459.7 23.0 %collective-permute-start.38 = (bf16[512,1024]{1,0:T(8,128)(2,1)S(1)}, bf16[512,1024]{1,0:T(8,128)(2,1)S(1)}, u32[]{:S(2)}, u32[]{:S(2)}) collective-permute-start(bf16[512,1024]{1,0:T(8,128)(2,1)S(1)} %get-tuple-element.312), channel_id=1, source_target_pairs={{2,1},{3,2},{6,5},{7,6},{10,9},{11,10},{14,13},{15,14},{18,17},{19... | collective-permute-start | bytes 3145736 | tf_op jit(solution)/shard_map/ppermute | solution.py:800
  485.5 24.6 %collective-permute-start.41 = (bf16[3,128,1024]{2,1,0:T(8,128)(2,1)S(1)}, bf16[3,128,1024]{2,1,0:T(8,128)(2,1)S(1)}, u32[]{:S(2)}, u32[]{:S(2)}) collective-permute-start(bf16[3,128,1024]{2,1,0:T(8,128)(2,1)S(1)} %get-tuple-element.273), channel_id=1, source_target_pairs={{0,3},{1,0},{2,1},{3,2},{4,7},{5,4},{6,5},{7,6},{8,11},{9,8},{10,9... | collective-permute-start | bytes 2359304 | tf_op jit(solution)/shard_map/ppermute | solution.py:786
  489.4 37.8 %collective-permute-start.42 = (bf16[3,128,1024]{2,1,0:T(8,128)(2,1)S(1)}, bf16[3,128,1024]{2,1,0:T(8,128)(2,1)S(1)}, u32[]{:S(2)}, u32[]{:S(2)}) collective-permute-start(bf16[3,128,1024]{2,1,0:T(8,128)(2,1)S(1)} %get-tuple-element.274), channel_id=1, source_target_pairs={{0,1},{1,2},{2,3},{3,0},{4,5},{5,6},{6,7},{7,4},{8,9},{9,10},{10,1... | collective-permute-start | bytes 2359304 | tf_op jit(solution)/shard_map/ppermute | solution.py:786
  502.9 42.2 %collective-permute-start.52 = (bf16[512,1024]{1,0:T(8,128)(2,1)}, bf16[512,1024]{1,0:T(8,128)(2,1)}, u32[]{:S(2)}, u32[]{:S(2)}) collective-permute-start(bf16[512,1024]{1,0:T(8,128)(2,1)} %add.381), channel_id=1, source_target_pairs={{0,1},{1,2},{2,3},{4,5},{5,6},{6,7},{8,9},{9,10},{10,11},{12,13},{... | collective-permute-start | bytes 3145736 | tf_op jit(solution)/shard_map/ppermute | solution.py:799
  508.8 39.4 %collective-permute-start.53 = (bf16[512,1024]{1,0:T(8,128)(2,1)S(1)}, bf16[512,1024]{1,0:T(8,128)(2,1)}, u32[]{:S(2)}, u32[]{:S(2)}) collective-permute-start(bf16[512,1024]{1,0:T(8,128)(2,1)S(1)} %add.382), channel_id=1, source_target_pairs={{1,0},{2,1},{3,2},{5,4},{6,5},{7,6},{9,8},{10,9},{11,10},{13,12},{... | collective-permute-start | bytes 3145736 | tf_op jit(solution)/shard_map/ppermute | solution.py:800
  (77 other events, 1034.8 us)
Sparse Core Ops, SparseCore 0:
  18.0 27.8 all-gather.2
  88.0 132.2 all-gather.4
  275.1 61.6 reduce-scatter.2
  340.3 137.6 reduce-scatter.4

commit v8 on v7

--- a/solution.py
+++ b/solution.py
@@ -68,36 +68,40 @@
     return picked
 
 
-def attend_kernel(heads, bq, bk, q_ref, k_ref, v_ref, start_ref, o_ref, of_ref, l_ref, acc, lsum):
+def attend_kernel(heads, bq, bk, bounds_ref, q_ref, k_ref, v_ref, start_ref, o_ref, of_ref, l_ref, acc, lsum):
     i = pl.program_id(0)
     qs = head_stack(q_ref[...], heads)
     acc[...] = jnp.zeros_like(acc)
     lsum[...] = jnp.zeros_like(lsum)
     start = jnp.concatenate([start_ref[...]] * heads, axis=0)
 
-    def step(j, diagonal):
+    def step(j, masked, diagonal):
         offset = pl.multiple_of(j * bk, bk)
         keys = k_ref[pl.ds(offset, bk), :]
         values = v_ref[pl.ds(offset, bk), :]
         scores = dot_nt(qs, keys)
-        key_index = offset + lax.broadcasted_iota(jnp.int32, scores.shape, 1)
-        allowed = key_index >= start
-        if diagonal:
-            row = lax.rem(lax.broadcasted_iota(jnp.int32, scores.shape, 0), bq)
-            allowed = allowed & (key_index <= i * bq + row)
-        weights = jnp.where(allowed, jnp.exp2(scores * (scale_factor * LOG2E)), 0.0)
+        weights = jnp.exp2(scores * (scale_factor * LOG2E))
+        if masked:
+            key_index = offset + lax.broadcasted_iota(jnp.int32, scores.shape, 1)
+            allowed = key_index >= start
+            if diagonal:
+                row = lax.rem(lax.broadcasted_iota(jnp.int32, scores.shape, 0), bq)
+                allowed = allowed & (key_index <= i * bq + row)
+            weights = jnp.where(allowed, weights, 0.0)
         total = weights[:, :128]
         for part in range(1, bk // 128):
             total = total + weights[:, part * 128 : (part + 1) * 128]
         lsum[...] += total
         acc[...] += dot_nn(weights.astype(bf16), values)
 
-    def body(j, carry):
-        step(j, False)
+    def body(masked, j, carry):
+        step(j, masked, False)
         return carry
 
-    lax.fori_loop(0, i, body, 0)
-    step(i, True)
+    inside = bounds_ref[1, i]
+    lax.fori_loop(bounds_ref[0, i], inside, functools.partial(body, True), 0)
+    lax.fori_loop(inside, i, functools.partial(body, False), 0)
+    step(i, True, True)
     summed = jnp.sum(lsum[...], axis=1, keepdims=True)
     out = head_pick(acc[...] * (1.0 / summed), heads, bq)
     of_ref[...] = out
@@ -105,7 +109,14 @@
     l_ref[...] = jnp.log2(summed).reshape(heads, bq)
 
 
-def attend(q, k, v, start, block):
+def key_bounds(starts, block):
+    blocks = jnp.arange(starts.shape[0] // block, dtype=jnp.int32)
+    first = starts[::block] // block
+    inside = (starts[block - 1 :: block] + (block - 1)) // block
+    return jnp.stack([first, jnp.clip(inside, first, blocks)])
+
+
+def attend(bounds, q, k, v, start, block):
     length, width = q.shape
     heads = width // HEAD_DIM
     whole = pl.BlockSpec((length, width), lambda i: (0, 0))
@@ -113,7 +124,8 @@
     return pl.pallas_call(
         functools.partial(attend_kernel, heads, block, block),
         grid=(length // block,),
-        in_specs=[rows, whole, whole, pl.BlockSpec((block, 1), lambda i: (i, 0))],
+        in_specs=[pl.BlockSpec(memory_space=pltpu.SMEM), rows, whole, whole]
+        + [pl.BlockSpec((block, 1), lambda i: (i, 0))],
         out_specs=[rows, rows, pl.BlockSpec((heads, block), lambda i: (0, i))],
         out_shape=[
             jax.ShapeDtypeStruct((length, width), bf16),
@@ -128,11 +140,11 @@
             flops=20_000_000_000, bytes_accessed=8 * length * width, transcendentals=0
         ),
         name="attend",
-    )(q, k, v, start)
+    )(bounds, q, k, v, start)
 
 
 def attend_back_kernel(
-    first, heads, bq, bk, q_ref, do_ref, k_ref, v_ref, of_ref, l_ref, start_ref, dq_ref, dk_ref, dv_ref, acc
+    first, heads, bq, bk, bounds_ref, q_ref, do_ref, k_ref, v_ref, of_ref, l_ref, start_ref, dq_ref, dk_ref, dv_ref, acc
 ):
     i = pl.program_id(0)
 
@@ -156,33 +168,37 @@
     start = jnp.concatenate([start_ref[...]] * heads, axis=1)
     acc[...] = jnp.zeros_like(acc)
 
-    def step(j, diagonal):
+    def step(j, masked, diagonal):
         offset = pl.multiple_of(j * bk, bk)
         keys = k_ref[pl.ds(offset, bk), :]
         values = v_ref[pl.ds(offset, bk), :]
         scores = dot_nt(keys, qs)
-        key_index = offset + lax.broadcasted_iota(jnp.int32, scores.shape, 0)
-        allowed = key_index >= start
-        if diagonal:
-            column = lax.rem(lax.broadcasted_iota(jnp.int32, scores.shape, 1), bq)
-            allowed = allowed & (key_index <= i * bq + column)
-        probs = jnp.where(allowed, jnp.exp2(scores * (scale_factor * LOG2E) - log_sum), 0.0)
+        probs = jnp.exp2(scores * (scale_factor * LOG2E) - log_sum)
+        if masked:
+            key_index = offset + lax.broadcasted_iota(jnp.int32, scores.shape, 0)
+            allowed = key_index >= start
+            if diagonal:
+                column = lax.rem(lax.broadcasted_iota(jnp.int32, scores.shape, 1), bq)
+                allowed = allowed & (key_index <= i * bq + column)
+            probs = jnp.where(allowed, probs, 0.0)
         prob_grad = dot_nt(values, dos)
         score_grad = (probs * (prob_grad - delta)).astype(bf16)
         dv_ref[pl.ds(offset, bk), :] += dot_nn(probs.astype(bf16), dos)
         dk_ref[pl.ds(offset, bk), :] += dot_nn(score_grad, qs)
         acc[...] += dot_tn(score_grad, keys)
 
-    def body(j, carry):
-        step(j, False)
+    def body(masked, j, carry):
+        step(j, masked, False)
         return carry
 
-    lax.fori_loop(0, i, body, 0)
-    step(i, True)
+    inside = bounds_ref[1, i]
+    lax.fori_loop(bounds_ref[0, i], inside, functools.partial(body, True), 0)
+    lax.fori_loop(inside, i, functools.partial(body, False), 0)
+    step(i, True, True)
     dq_ref[...] = head_pick(acc[...], heads, bq)
 
 
-def attend_back(q, k, v, grads, out, log_sum, start, block, group, width):
+def attend_back(bounds, q, k, v, grads, out, log_sum, start, block, group, width):
     length = q.shape[0]
     heads = width // HEAD_DIM
     taken = pl.BlockSpec((length, width), lambda i: (0, group))
@@ -194,6 +210,7 @@
         functools.partial(attend_back_kernel, group * heads, heads, block, block),
         grid=(length // block,),
         in_specs=[
+            pl.BlockSpec(memory_space=pltpu.SMEM),
             taken_rows,
             taken_rows,
             taken,
@@ -209,7 +226,7 @@
             flops=40_000_000_000, bytes_accessed=20 * length * width, transcendentals=0
         ),
         name="attend_back",
-    )(q, grads, k, v, out, log_sum, start)
+    )(bounds, q, grads, k, v, out, log_sum, start)
 
 
 def partner(x):
@@ -569,7 +586,7 @@
     def _():
         rate_ref[...] = jnp.zeros_like(rate_ref)
         rate = rates_ref[1:2, :]
-        part = min(64, acc.shape[0])
+        part = min(128, acc.shape[0])
 
         def body(at, carry):
             rows = pl.ds(pl.multiple_of(at * part, part), part)
@@ -697,7 +714,7 @@
     def _():
         rate_ref[...] = jnp.zeros_like(rate_ref)
         rate = rates_ref[0:1, :]
-        part = min(64, acc.shape[0])
+        part = min(128, acc.shape[0])
 
         def body(at, carry):
             rows = pl.ds(pl.multiple_of(at * part, part), part)
@@ -937,8 +954,9 @@
     ups[-1], downs[-1], state = lax.optimization_barrier((ups[-1], downs[-1], state))
     state = projected(nt - 1, state)
     query_hat, key_hat, value_hat, query_turned, key_turned = state
+    bounds = key_bounds(starts, block)
     attended_row, attended_f32, log_sum = attend(
-        query_hat, key_hat, value_hat, starts[:, None], block
+        bounds, query_hat, key_hat, value_hat, starts[:, None], block
     )
     attended = [take_block(attended_row, me, rows, 0)] + [
         shift(take_block(attended_row, (me + d) % nt, rows, 0), "tensor", d, nt)
@@ -958,6 +976,15 @@
             whole = put_block(whole, piece, (me + nt - d) % nt, 1)
         return whole
 
+    def blocks_of(part, axis, width):
+        return [
+            lax.slice_in_dim(part, at, at + width, axis=axis)
+            for at in range(0, part.shape[axis], width)
+        ]
+
+    def to_owners(pieces, places):
+        return [shift(piece, "tensor", -d, nt) if d else piece for d, piece in zip(places, pieces)]
+
     per = hidden_width // step
     near = (nt - 1) * per
     feed_args = (mlp_out_low, mlp_out_t, middle_t, mlp_full, scales_row, up, gate, hidden_units)
@@ -969,13 +996,16 @@
     )
     near_part = lax.psum_scatter(near_grad, "dp", scatter_dimension=1, tiled=True)
 
-    grad_row = jnp.zeros((length, heads_width), bf16)
+    grad_pieces = []
     for d in list(range(1, nt)) + [0]:
         piece = dot_nn(branch_low, out_full[:, d * heads_width : (d + 1) * heads_width])
         piece = piece.astype(bf16)
-        piece = shift(piece, "tensor", -d, nt) if d else piece
+        grad_pieces.append((d, shift(piece, "tensor", -d, nt) if d else piece))
+    grad_row = jnp.zeros((length, heads_width), bf16)
+    for d, piece in grad_pieces[-1:] + grad_pieces[:-1]:
         grad_row = put_block(grad_row, piece, (me + d) % nt, 0)
-    out_grad = out_grads(attended, branch_low)
+    out_sum = out_grads(attended, branch_low).reshape(nd, shard, -1)
+    out_sum = halving(out_sum, "dp", nd, halvings[0])
 
     scales_grad = spread(jnp.concatenate([near_scales, far_scales], axis=1), order)
     small = jnp.concatenate(
@@ -986,11 +1016,11 @@
     def advance(small):
         return exchange_add(small, *steps.pop(0)) if steps else small
 
-    far_part, grad_row, out_grad, small = lax.optimization_barrier(
-        (far_part, grad_row, out_grad, small)
+    far_part, grad_row, out_sum, small = lax.optimization_barrier(
+        (far_part, grad_row, out_sum, small)
     )
     small = advance(small)
-    out_sum = halving(out_grad.reshape(nd, shard, -1), "dp", nd, halvings[0])
+    out_sum = halving(out_sum, "dp", nd, halvings[1])
     head_group = max(128, heads_width // 2)
     head_grads = []
     for group in range(heads_width // head_group):
@@ -999,9 +1029,10 @@
                 (head_grads, grad_row, far_part, small, out_sum)
             )
             small = advance(small)
-            out_sum = halving(out_sum, "dp", nd, halvings[1])
+            out_sum = halving(out_sum, "dp", nd, halvings[2])
         head_grads.append(
             attend_back(
+                bounds,
                 query_hat,
                 key_hat,
                 value_hat,
@@ -1021,8 +1052,9 @@
     )
     far_last = shift(far_last, "tensor", -middle_hop, nt)
     small = advance(small)
-    for k in halvings[1 if len(head_grads) == 1 else 2 :]:
+    for k in halvings[2 if len(head_grads) == 1 else 3 :]:
         out_sum = halving(out_sum, "dp", nd, k)
+    out_pieces = to_owners(blocks_of(out_sum.astype(bf16), 1, heads_width), range(nt))
     qkv_grad, gain_grad, *pieces = project_back(
         me.reshape(1),
         head_grads,
@@ -1033,35 +1065,24 @@
         gain,
         rows,
     )
-    qkv_grad, pieces, small, out_sum, far_last = lax.optimization_barrier(
-        (qkv_grad, pieces, small, out_sum, far_last)
+    qkv_grad, pieces, small, out_pieces, far_last = lax.optimization_barrier(
+        (qkv_grad, pieces, small, out_pieces, far_last)
     )
     far_part = jnp.concatenate([far_first, far_last], axis=0)
     hidden_turn = [hidden_parts[(nt - d) % nt] for d in range(nt)]
     qkv_sum = projection_grads(hidden_turn, qkv_grad)
     qkv_sum = qkv_sum.reshape(nd, shard, -1)
 
-    def blocks_of(part, axis, width):
-        return [
-            lax.slice_in_dim(part, at, at + width, axis=axis)
-            for at in range(0, part.shape[axis], width)
-        ]
-
-    def to_owners(pieces, places):
-        return [shift(piece, "tensor", -d, nt) if d else piece for d, piece in zip(places, pieces)]
-
-    out_sum, gain_grad, qkv_sum = lax.optimization_barrier((out_sum, gain_grad, qkv_sum))
-    out_pieces = to_owners(blocks_of(out_sum.astype(bf16), 1, heads_width), range(nt))
-    gain_parts = gather(gain_grad)
     ahead = behind = None
     for hop in range(1, nt):
         if hop == 2:
-            ahead, behind, qkv_sum, out_pieces, gain_parts = lax.optimization_barrier(
-                (ahead, behind, qkv_sum, out_pieces, gain_parts)
+            ahead, behind, qkv_sum, gain_grad = lax.optimization_barrier(
+                (ahead, behind, qkv_sum, gain_grad)
             )
+            gain_parts = gather(gain_grad)
         if hop == max(2, nt - 1):
-            ahead, behind, near_part, qkv_sum = lax.optimization_barrier(
-                (ahead, behind, near_part, qkv_sum)
+            ahead, behind, near_part, qkv_sum, gain_parts = lax.optimization_barrier(
+                (ahead, behind, near_part, qkv_sum, gain_parts)
             )
             near_pieces = blocks_of(near_part, 2, hidden_width)
             near_pieces, qkv_sum, small = lax.optimization_barrier((near_pieces, qkv_sum, small))

time: 566 us -> 556 us (0.982)
  starting transfers between devices: 77 us -> 69.1 us
    ppermute x19, waiting for transfers between devices: 57.3 us -> 38.4 us  [shift(): lax.ppermute(value, axis, [(i, (i + distance) % size) for i in range(size)])]
    ppermute x3, waiting for transfers between devices: 9.69 us -> 21.4 us  [line_sum(): up = lax.ppermute(ahead, axis, [(i, i + 1) for i in range(hop)])]
    ppermute x6, waiting for transfers between devices: 15.7 us -> 21.9 us  [halving(): other = lax.ppermute(sent, axis, [(i, i ^ step) for i in range(size)])]
where the time goes in v8:
time: 556 us; the launch traced here: 549 us
  Pallas kernels  203 us (37%)
  waiting for transfers between devices  199 us (36%)
  starting transfers between devices  69.1 us (12%)
  other arithmetic  34.6 us (6%)
  local copies, waits for them, and re-layouts  22.8 us (4%)
  between operations  15.3 us (3%)
  matrix products  5.8 us (1%)
    ppermute x6, waiting for transfers between devices, carry_on(): lax.ppermute(down, axis, [(i, i - 1) for i in range(1, size - hop + 1)])  73.5 us
    pallas_call x2, Pallas kernels, feed_back(): pl.pallas_call(feed_back_last_kernel if last else feed_back_first_kernel,...  51.2 us
    pallas_call x2, Pallas kernels, attend_back(): pl.pallas_call(functools.partial(attend_back_kernel, group * heads, heads...  40.4 us
    ppermute x19, waiting for transfers between devices, shift(): lax.ppermute(value, axis, [(i, (i + distance) % size) for i in range(size)])  38.4 us
    ppermute x19, starting transfers between devices, shift(): lax.ppermute(value, axis, [(i, (i + distance) % size) for i in range(size)])  29 us
    pallas_call x1, Pallas kernels, feed(): pl.pallas_call(feed_kernel, grid=(total // step,), in_specs=[whole] + wei...  28.8 us
    pallas_call x4, Pallas kernels, project(): pl.pallas_call(functools.partial(project_kernel, count), grid_spec=pltpu....  23.5 us
    ppermute x6, waiting for transfers between devices, carry_on(): up = lax.ppermute(up, axis, [(i, i + 1) for i in range(hop - 1, size - 1)])  22.7 us
  transfers between devices with their start and end apart: 58, of which 27 were waited for; matrix products, arithmetic and copies ran while one was open for 9% of the time, Pallas kernels for 27%

profile of v8, /device:TPU:0, one launch (start us, length us, event | category | flops | bytes accessed | tf_op | source)
XLA Modules:
  0.0 549.2 jit_solution(7674363243096722941)
XLA Ops:
  17.9 16.4 %collective-permute-done = bf16[416,1024]{1,0:T(8,128)(2,1)S(1)} collective-permute-done((bf16[416,1024]{1,0:T(8,128)(2,1)}, bf16[416,1024]{1,0:T(8,128)(2,1)S(1)}, u32[]{:S(2)}, u32[]{:S(2)}) %collective-permute-start) | collective-permute-done | bytes 852000 | tf_op jit(solution)/shard_map/ppermute | solution.py:807
  39.7 20.4 %collective-permute-done.3 = bf16[416,1024]{1,0:T(8,128)(2,1)} collective-permute-done((bf16[416,1024]{1,0:T(8,128)(2,1)S(1)}, bf16[416,1024]{1,0:T(8,128)(2,1)}, u32[]{:S(2)}, u32[]{:S(2)}) %collective-permute-start.3) | collective-permute-done | bytes 852000 | tf_op jit(solution)/shard_map/ppermute | solution.py:808
  67.6 15.1 %collective-permute-done.13 = bf16[416,1024]{1,0:T(8,128)(2,1)} collective-permute-done((bf16[416,1024]{1,0:T(8,128)(2,1)}, bf16[416,1024]{1,0:T(8,128)(2,1)}, u32[]{:S(2)}, u32[]{:S(2)}) %collective-permute-start.13) | collective-permute-done | bytes 852000 | tf_op jit(solution)/shard_map/ppermute | solution.py:808
  97.5 5.9 %project.4 = (bf16[2048,256]{1,0:T(8,128)(2,1)}, bf16[2048,256]{1,0:T(8,128)(2,1)}, bf16[2048,256]{1,0:T(8,128)(2,1)}, f32[2048,256]{1,0:T(8,128)}, f32[2048,256]{1,0:T(8,128)}) custom-call(s32[1]{0:T(128)} %bitcast.6.index_ref, bf16[512,1024]{1,0:T(8,128)(2,1)} %refs_0_.1, ...), custom_call_target="tpu_custom_call" | custom-call | flops 805306368 | bytes 2097152 | tf_op jit(solution)/shard_map/project/pallas_call | solution.py:292
  103.5 6.3 %collective-permute-done.4.refs_0_.refs_5_ = bf16[512,1024]{1,0:T(8,128)(2,1)S(1)} collective-permute-done((bf16[512,1024]{1,0:T(8,128)(2,1)S(1)}, bf16[512,1024]{1,0:T(8,128)(2,1)S(1)}, u32[]{:S(2)}, u32[]{:S(2)}) %collective-permute-start.4) | collective-permute-done | bytes 1048608 | tf_op jit(solution)/shard_map/ppermute | solution.py:807
  115.9 23.1 %collective-permute-done.7.refs_1_.refs_4_ = bf16[512,1024]{1,0:T(8,128)(2,1)} collective-permute-done((bf16[512,1024]{1,0:T(8,128)(2,1)S(1)}, bf16[512,1024]{1,0:T(8,128)(2,1)}, u32[]{:S(2)}, u32[]{:S(2)}) %collective-permute-start.7) | collective-permute-done | bytes 1048608 | tf_op jit(solution)/shard_map/ppermute | solution.py:808
  150.4 5.9 %project.5 = (bf16[2048,256]{1,0:T(8,128)(2,1)}, bf16[2048,256]{1,0:T(8,128)(2,1)}, bf16[2048,256]{1,0:T(8,128)(2,1)}, f32[2048,256]{1,0:T(8,128)}, f32[2048,256]{1,0:T(8,128)}) custom-call(s32[1]{0:T(128)} %bitcast.11.index_ref, bf16[512,1024]{1,0:T(8,128)(2,1)} %copy-done.6, ...), custom_call_target="tpu_custom_call", output_to_operand_aliasing={{0}: (9, {}), {1}: (10, {}), {2}: (11, {}), {3}: (12, {}), ... | custom-call | flops 805306368 | bytes 2097152 | tf_op jit(solution)/shard_map/project/pallas_call | solution.py:292
  156.3 7.5 %collective-permute-done.9.refs_1_.refs_6_ = bf16[512,1024]{1,0:T(8,128)(2,1)} collective-permute-done((bf16[512,1024]{1,0:T(8,128)(2,1)}, bf16[512,1024]{1,0:T(8,128)(2,1)}, u32[]{:S(2)}, u32[]{:S(2)}) %collective-permute-start.9) | collective-permute-done | bytes 1048608 | tf_op jit(solution)/shard_map/ppermute | solution.py:808
  169.6 5.9 %project.7 = (bf16[2048,256]{1,0:T(8,128)(2,1)}, bf16[2048,256]{1,0:T(8,128)(2,1)}, bf16[2048,256]{1,0:T(8,128)(2,1)}, f32[2048,256]{1,0:T(8,128)}, f32[2048,256]{1,0:T(8,128)}) custom-call(s32[1]{0:T(128)} %bitcast.4.index_ref, ...), custom_call_target="tpu_custom_call", output_to_operand_aliasing={{0}: (9, {}), {1}: (10, {}), {2}: (11, {}), {3}: (12, {}), ... | custom-call | flops 805306368 | bytes 2097152 | tf_op jit(solution)/shard_map/project/pallas_call | solution.py:292
  175.5 20.1 %attend.1 = (bf16[2048,256]{1,0:T(8,128)(2,1)}, f32[2048,256]{1,0:T(8,128)}, f32[4,2048]{1,0:T(4,128)}) custom-call(s32[2,4]{1,0:T(2,128)} %pad_add_fusion.bounds_ref, bf16[2048,256]{1,0:T(8,128)(2,1)} %get-tuple-element.191.q_ref, bf16[2048,256]{1,0:T(8,128)(2,1)} %get-tuple-element.192.k_ref, bf16[2048,256]{1,0:T(8,128)(2,1)} %get-tuple-element.193.v_ref, ...), custom_call_target="tpu_custom_call" | custom-call | flops 20000000000 | bytes 4194304 | tf_op jit(solution)/shard_map/attend/pallas_call | solution.py:124
  210.5 9.8 %all-gather.5.cloned.1.call-done = bf16[13312,1024]{1,0:T(8,128)(2,1)} async-done(((bf16[1664,1024]{1,0:T(8,128)(2,1)}), bf16[13312,1024]{1,0:T(8,128)(2,1)}) %all-gather.5.cloned.1.call-update) | async-done | bytes 27262992 | tf_op jit(solution)/shard_map/all_gather | solution.py:909
  220.4 9.1 %mix.1 = (f32[512,1024]{1,0:T(8,128)}, f32[512,1024]{1,0:T(8,128)}, bf16[512,1024]{1,0:T(8,128)(2,1)}, bf16[1024,512]{1,0:T(8,128)(2,1)}, bf16[1024,1024]{1,0:T(8,128)(2,1)}) custom-call(bf16[512,256]{1,0:T(8,128)(2,1)} %get-tuple-element.313.refs_0_, bf16[512,256]{1,0:T(8,128)(2,1)} %copy-done.11, bf16[512,256]{1,0:T(8,128)(2,1)} %copy-done.12, ...), custom_call_target="tpu_custom_call" | custom-call | flops 1073741824 | bytes 7340032 | tf_op jit(solution)/shard_map/mix/pallas_call | solution.py:519
  229.5 28.8 %feed.1 = (f32[512,4096]{1,0:T(8,128)}, f32[512,4096]{1,0:T(8,128)}, bf16[512,4096]{1,0:T(8,128)(2,1)}, bf16[512,1024]{1,0:T(8,128)(2,1)}, f32[512,1024]{1,0:T(8...) custom-call(bf16[512,1024]{1,0:T(8,128)(2,1)} %get-tuple-element.197.m_ref, ...), custom_call_target="tpu_custom_call" | custom-call | flops 12884901888 | bytes 46137344 | tf_op jit(solution)/shard_map/feed/pallas_call | solution.py:635
  258.2 15.1 %feed_back_first.1 = (bf16[3,1024,1024]{2,1,0:T(8,128)(2,1)}, f32[2,1024]{1,0:T(2,128)}, f32[512,1024]{1,0:T(8,128)}) custom-call(bf16[512,1024]{1,0:T(8,128)(2,1)} %get-tuple-element.200.refs_0_, bf16[1024,512]{1,0:T(8,128)(2,1)} %get-tuple-element.201.refs_1_, bf16[1024,512]{1,0:T(8,128)(2,1)} %get-tuple-element.202.refs_2_, ...), custom_call_target="tpu_custom_call" | custom-call | flops 6442450944 | bytes 17825792 | tf_op jit(solution)/shard_map/feed_back_first/pallas_call | solution.py:760
  273.4 36.1 %feed_back_last.1 = (bf16[3,1024,3072]{2,1,0:T(8,128)(2,1)}, f32[2,3072]{1,0:T(2,128)}, f32[512,1024]{1,0:T(8,128)}, bf16[512,1024]{1,0:T(8,128)(2,1)}, f32[1,1024]{1,0:T(1,128)}) custom-call(bf16[512,1024]{1,0:T(8,128)(2,1)} %get-tuple-element.200.refs_0_, bf16[1024,512]{1,0:T(8,128)(2,1)} %get-tuple-element.201.refs_1_, ...), custom_call_target="tpu_custom_call" | custom-call | flops 19327352832 | bytes 53477376 | tf_op jit(solution)/shard_map/feed_back_last/pallas_call | solution.py:760
  331.3 8.2 %collective-permute-done.19 = bf16[512,256]{1,0:T(8,128)(2,1)} collective-permute-done((bf16[512,256]{1,0:T(8,128)(2,1)}, bf16[512,256]{1,0:T(8,128)(2,1)}, u32[]{:S(2)}, u32[]{:S(2)}) %collective-permute-start.19) | collective-permute-done | bytes 262176 | tf_op jit(solution)/shard_map/ppermute | solution.py:803
  345.2 20.2 %attend_back.2 = (f32[2048,128]{1,0:T(8,128)}, f32[2048,128]{1,0:T(8,128)}, f32[2048,128]{1,0:T(8,128)}) custom-call(s32[2,4]{1,0:T(2,128)} %pad_add_fusion.bounds_ref, bf16[2048,256]{1,0:T(8,128)(2,1)} %get-tuple-element.191.q_ref, bf16[2048,256]{1,0:T(8,128)(2,1)} %constant_dynamic-update-slice_fusion.10.do_ref, ...), custom_call_target="tpu_custom_call" | custom-call | flops 40000000000 | bytes 5242880 | tf_op jit(solution)/shard_map/attend_back/pallas_call | solution.py:209
  368.8 20.2 %attend_back.3 = (f32[2048,128]{1,0:T(8,128)}, f32[2048,128]{1,0:T(8,128)}, f32[2048,128]{1,0:T(8,128)}) custom-call(s32[2,4]{1,0:T(2,128)} %pad_add_fusion.bounds_ref, bf16[2048,256]{1,0:T(8,128)(2,1)} %get-tuple-element.191.q_ref, bf16[2048,256]{1,0:T(8,128)(2,1)} %constant_dynamic-update-slice_fusion.10.do_ref, ...), custom_call_target="tpu_custom_call" | custom-call | flops 40000000000 | bytes 5242880 | tf_op jit(solution)/shard_map/attend_back/pallas_call | solution.py:209
  399.9 16.2 %project_back.1 = (bf16[2048,768]{1,0:T(8,128)(2,1)}, f32[1,256]{1,0:T(1,128)}, bf16[512,1024]{1,0:T(8,128)(2,1)}, bf16[512,1024]{1,0:T(8,128)(2,1)}, bf16[512,1...) custom-call(s32[1]{0:T(128)} %bitcast.17.index_ref, f32[2048,128]{1,0:T(8,128)} %get-tuple-element.236.refs_0_, ...), custom_call_target="tpu_custom_call" | custom-call | flops 524288 | bytes 524288 | tf_op jit(solution)/shard_map/project_back/pallas_call | solution.py:389
  419.4 8.4 %projection_grads.1 = bf16[1024,768]{1,0:T(8,128)(2,1)} custom-call(bf16[512,1024]{1,0:T(8,128)(2,1)} %refs_0_.1, bf16[512,1024]{1,0:T(8,128)(2,1)} %collective-permute-done.8.refs_0_.refs_1_, bf16[512,1024]{1,0:T(8,128)(2,1)} %copy-done.5, bf16[512,1024]{1,0:T(8,128)(2,1)} %copy-done.6, bf16[512,1024]{1,0:T(8,128)(2,1)} %collective-permute-done.7.refs_1_.refs_4_, ...), custom_call_target="tpu_custom_call" | custom-call | flops 3221225472 | bytes 16777216 | tf_op jit(solution)/shard_map/projection_grads/pallas_call | solution.py:433
  427.9 13.9 %collective-permute-done.32 = bf16[512,1024]{1,0:T(8,128)(2,1)S(1)} collective-permute-done((bf16[512,1024]{1,0:T(8,128)(2,1)}, bf16[512,1024]{1,0:T(8,128)(2,1)S(1)}, u32[]{:S(2)}, u32[]{:S(2)}) %collective-permute-start.32) | collective-permute-done | bytes 1048608 | tf_op jit(solution)/shard_map/ppermute | solution.py:816
  454.9 16.5 %collective-permute-done.37 = bf16[2,128,768]{2,1,0:T(8,128)(2,1)S(1)} collective-permute-done((bf16[2,128,768]{2,1,0:T(8,128)(2,1)S(1)}, bf16[2,128,768]{2,1,0:T(8,128)(2,1)S(1)}, u32[]{:S(2)}, u32[]{:S(2)}) %collective-permute-start.37) | collective-permute-done | bytes 393248 | tf_op jit(solution)/shard_map/ppermute | solution.py:827
  504.4 10.3 %collective-permute-done.41 = bf16[3,128,1024]{2,1,0:T(8,128)(2,1)S(1)} collective-permute-done((bf16[3,128,1024]{2,1,0:T(8,128)(2,1)S(1)}, bf16[3,128,1024]{2,1,0:T(8,128)(2,1)S(1)}, u32[]{:S(2)}, u32[]{:S(2)}) %collective-permute-start.41) | collective-permute-done | bytes 786464 | tf_op jit(solution)/shard_map/ppermute | solution.py:803
  528.3 7.5 %collective-permute-done.52 = bf16[512,1024]{1,0:T(8,128)(2,1)} collective-permute-done((bf16[512,1024]{1,0:T(8,128)(2,1)}, bf16[512,1024]{1,0:T(8,128)(2,1)}, u32[]{:S(2)}, u32[]{:S(2)}) %collective-permute-start.52) | collective-permute-done | bytes 1048608 | tf_op jit(solution)/shard_map/ppermute | solution.py:816
  (302 shorter events, 187.1 us)
Async XLA Ops:
  7.2 90.3 %all-gather.3.cloned.1.call-start = ((), (), s32[]{:S(2)}) async-start(), calls=%async_computation.2 | async-start | bytes 1769472 | tf_op jit(solution)/shard_map/all_gather | solution.py:888
  10.9 23.5 %collective-permute-start = (bf16[416,1024]{1,0:T(8,128)(2,1)}, bf16[416,1024]{1,0:T(8,128)(2,1)S(1)}, u32[]{:S(2)}, u32[]{:S(2)}) collective-permute-start(bf16[416,1024]{1,0:T(8,128)(2,1)} %pad_maximum_fusion), channel_id=1, source_target_pairs={{0,1},{1,2},{2,3},{4,5},{5,6},{6,7},{8,9},{9,10},{10,11},{12,13},{... | collective-permute-start | bytes 2555912 | tf_op jit(solution)/shard_map/ppermute | solution.py:807
  17.9 202.5 %all-gather.5.cloned.1.call-start = ((), (), s32[]{:S(2)}) async-start(), calls=%async_computation.3 | async-start | bytes 30670848 | tf_op jit(solution)/shard_map/all_gather | solution.py:909
  87.9 255.6 %reduce-scatter.3.cloned.1.call-start = ((), (), s32[]{:S(2)}) async-start(), calls=%async_computation.4 | async-start | bytes 7077888 | tf_op jit(solution)/shard_map/reduce_scatter | solution.py:993
  90.0 23.9 %collective-permute-start.5 = (bf16[512,1024]{1,0:T(8,128)(2,1)S(1)}, bf16[512,1024]{1,0:T(8,128)(2,1)S(1)}, u32[]{:S(2)}, u32[]{:S(2)}) collective-permute-start(bf16[512,1024]{1,0:T(8,128)(2,1)S(1)} %copy-done), channel_id=1, source_target_pairs={{1,0},{2,1},{3,2},{5,4},{6,5},{7,6},{9,8},{10,9},{11,10},{13,12},{... | collective-permute-start | bytes 3145736 | tf_op jit(solution)/shard_map/ppermute | solution.py:808
  114.6 24.4 %collective-permute-start.7 = (bf16[512,1024]{1,0:T(8,128)(2,1)S(1)}, bf16[512,1024]{1,0:T(8,128)(2,1)}, u32[]{:S(2)}, u32[]{:S(2)}) collective-permute-start(bf16[512,1024]{1,0:T(8,128)(2,1)S(1)} %collective-permute-done.5.refs_1_.refs_2_), channel_id=1, source_target_pairs={{1,0},{2,1},{5,4},{6,5},{9,8},{10,9},{13,12},{14,13},{17,16},{18,1... | collective-permute-start | bytes 3145736 | tf_op jit(solution)/shard_map/ppermute | solution.py:808
  140.7 23.1 %collective-permute-start.9 = (bf16[512,1024]{1,0:T(8,128)(2,1)}, bf16[512,1024]{1,0:T(8,128)(2,1)}, u32[]{:S(2)}, u32[]{:S(2)}) collective-permute-start(bf16[512,1024]{1,0:T(8,128)(2,1)} %collective-permute-done.7.refs_1_.refs_4_), channel_id=1, source_target_pairs={{1,0},{5,4},{9,8},{13,12},{17,16},{21,20},{25,24},{29,28}} | collective-permute-start | bytes 3145736 | tf_op jit(solution)/shard_map/ppermute | solution.py:808
  142.0 55.6 %collective-permute-start.15 = (f32[2,1024]{1,0:T(2,128)S(1)}, f32[2,1024]{1,0:T(2,128)S(1)}, u32[]{:S(2)}, u32[]{:S(2)}) collective-permute-start(f32[2,1024]{1,0:T(2,128)S(1)} %copy-done.36), channel_id=1, source_target_pairs={{0,1},{1,2},{2,3},{3,0},{4,5},{5,6},{6,7},{7,4},{8,9},{9,10},{10,1... | collective-permute-start | bytes 24584 | tf_op jit(solution)/shard_map/ppermute | solution.py:803
  145.6 56.3 %collective-permute-start.16 = (f32[2,1024]{1,0:T(2,128)S(1)}, f32[2,1024]{1,0:T(2,128)S(1)}, u32[]{:S(2)}, u32[]{:S(2)}) collective-permute-start(f32[2,1024]{1,0:T(2,128)S(1)} %copy-done.36), channel_id=1, source_target_pairs={{0,3},{1,0},{2,1},{3,2},{4,7},{5,4},{6,5},{7,6},{8,11},{9,8},{10,9... | collective-permute-start | bytes 24584 | tf_op jit(solution)/shard_map/ppermute | solution.py:803
  146.1 55.8 %collective-permute-start.17 = (f32[2,1024]{1,0:T(2,128)S(1)}, f32[2,1024]{1,0:T(2,128)S(1)}, u32[]{:S(2)}, u32[]{:S(2)}) collective-permute-start(f32[2,1024]{1,0:T(2,128)S(1)} %copy-done.36), channel_id=1, source_target_pairs={{0,2},{1,3},{2,0},{3,1},{4,6},{5,7},{6,4},{7,5},{8,10},{9,11},{10,... | collective-permute-start | bytes 24584 | tf_op jit(solution)/shard_map/ppermute | solution.py:803
  273.4 204.4 %reduce-scatter.5.cloned.1.call-start = ((), (), s32[]{:S(2)}) async-start(), calls=%async_computation.5 | async-start | bytes 21233664 | tf_op jit(solution)/shard_map/reduce_scatter | solution.py:997
  318.6 22.5 %collective-permute-start.20 = (bf16[512,256]{1,0:T(8,128)(2,1)}, bf16[512,256]{1,0:T(8,128)(2,1)S(1)}, u32[]{:S(2)}, u32[]{:S(2)}) collective-permute-start(bf16[512,256]{1,0:T(8,128)(2,1)} %convolution_convert_fusion), channel_id=1, source_target_pairs={{0,1},{1,2},{2,3},{3,0},{4,5},{5,6},{6,7},{7,4},{8,9},{9,10},{10,1... | collective-permute-start | bytes 786440 | tf_op jit(solution)/shard_map/ppermute | solution.py:803
  365.6 23.5 %collective-permute-start.24 = (f32[10,1024]{1,0:T(8,128)S(1)}, f32[10,1024]{1,0:T(8,128)S(1)}, u32[]{:S(2)}, u32[]{:S(2)}) collective-permute-start(f32[10,1024]{1,0:T(8,128)S(1)} %add.344), channel_id=1, source_target_pairs={{0,2},{1,3},{2,0},{3,1},{4,6},{5,7},{6,4},{7,5},{8,10},{9,11},{10,... | collective-permute-start | bytes 122888 | tf_op jit(solution)/shard_map/ppermute | solution.py:833
  367.4 27.4 %collective-permute-start.26 = (bf16[2,128,1024]{2,1,0:T(8,128)(2,1)S(1)}, bf16[2,128,1024]{2,1,0:T(8,128)(2,1)S(1)}, u32[]{:S(2)}, u32[]{:S(2)}) collective-permute-start(bf16[2,128,1024]{2,1,0:T(8,128)(2,1)S(1)} %slice.141), channel_id=1, source_target_pairs={{0,2},{1,3},{2,0},{3,1},{4,6},{5,7},{6,4},{7,5},{8,10},{9,11},{10,... | collective-permute-start | bytes 1572872 | tf_op jit(solution)/shard_map/ppermute | solution.py:803
  416.3 25.5 %collective-permute-start.32 = (bf16[512,1024]{1,0:T(8,128)(2,1)}, bf16[512,1024]{1,0:T(8,128)(2,1)S(1)}, u32[]{:S(2)}, u32[]{:S(2)}) collective-permute-start(bf16[512,1024]{1,0:T(8,128)(2,1)} %get-tuple-element.254), channel_id=1, source_target_pairs={{0,1},{4,5},{8,9},{12,13},{16,17},{20,21},{24,25},{28,29}} | collective-permute-start | bytes 3145736 | tf_op jit(solution)/shard_map/ppermute | solution.py:816
  418.7 23.1 %collective-permute-start.33 = (bf16[512,1024]{1,0:T(8,128)(2,1)}, bf16[512,1024]{1,0:T(8,128)(2,1)S(1)}, u32[]{:S(2)}, u32[]{:S(2)}) collective-permute-start(bf16[512,1024]{1,0:T(8,128)(2,1)} %get-tuple-element.255), channel_id=1, source_target_pairs={{3,2},{7,6},{11,10},{15,14},{19,18},{23,22},{27,26},{31,30}} | collective-permute-start | bytes 3145736 | tf_op jit(solution)/shard_map/ppermute | solution.py:817
  444.6 33.2 %collective-permute-start.34 = (bf16[512,1024]{1,0:T(8,128)(2,1)}, bf16[512,1024]{1,0:T(8,128)(2,1)}, u32[]{:S(2)}, u32[]{:S(2)}) collective-permute-start(bf16[512,1024]{1,0:T(8,128)(2,1)} %get-tuple-element.309), channel_id=1, source_target_pairs={{0,1},{1,2},{4,5},{5,6},{8,9},{9,10},{12,13},{13,14},{16,17},{17,1... | collective-permute-start | bytes 3145736 | tf_op jit(solution)/shard_map/ppermute | solution.py:816
  450.1 27.7 %collective-permute-start.35 = (bf16[512,1024]{1,0:T(8,128)(2,1)}, bf16[512,1024]{1,0:T(8,128)(2,1)S(1)}, u32[]{:S(2)}, u32[]{:S(2)}) collective-permute-start(bf16[512,1024]{1,0:T(8,128)(2,1)} %get-tuple-element.308), channel_id=1, source_target_pairs={{2,1},{3,2},{6,5},{7,6},{10,9},{11,10},{14,13},{15,14},{18,17},{19... | collective-permute-start | bytes 3145736 | tf_op jit(solution)/shard_map/ppermute | solution.py:817
  451.3 25.6 %collective-permute-start.38 = (f32[1,256]{1,0:T(1,128)S(1)}, f32[1,256]{1,0:T(1,128)S(1)}, u32[]{:S(2)}, u32[]{:S(2)}) collective-permute-start(f32[1,256]{1,0:T(1,128)S(1)} %copy-done.40), channel_id=1, source_target_pairs={{0,1},{1,2},{2,3},{3,0},{4,5},{5,6},{6,7},{7,4},{8,9},{9,10},{10,1... | collective-permute-start | bytes 3080 | tf_op jit(solution)/shard_map/ppermute | solution.py:803
  452.7 25.1 %collective-permute-start.39 = (f32[1,256]{1,0:T(1,128)S(1)}, f32[1,256]{1,0:T(1,128)S(1)}, u32[]{:S(2)}, u32[]{:S(2)}) collective-permute-start(f32[1,256]{1,0:T(1,128)S(1)} %copy-done.40), channel_id=1, source_target_pairs={{0,2},{1,3},{2,0},{3,1},{4,6},{5,7},{6,4},{7,5},{8,10},{9,11},{10,... | collective-permute-start | bytes 3080 | tf_op jit(solution)/shard_map/ppermute | solution.py:803
  479.7 35.0 %collective-permute-start.41 = (bf16[3,128,1024]{2,1,0:T(8,128)(2,1)S(1)}, bf16[3,128,1024]{2,1,0:T(8,128)(2,1)S(1)}, u32[]{:S(2)}, u32[]{:S(2)}) collective-permute-start(bf16[3,128,1024]{2,1,0:T(8,128)(2,1)S(1)} %get-tuple-element.267), channel_id=1, source_target_pairs={{0,3},{1,0},{2,1},{3,2},{4,7},{5,4},{6,5},{7,6},{8,11},{9,8},{10,9... | collective-permute-start | bytes 2359304 | tf_op jit(solution)/shard_map/ppermute | solution.py:803
  481.0 35.4 %collective-permute-start.42 = (bf16[3,128,1024]{2,1,0:T(8,128)(2,1)S(1)}, bf16[3,128,1024]{2,1,0:T(8,128)(2,1)S(1)}, u32[]{:S(2)}, u32[]{:S(2)}) collective-permute-start(bf16[3,128,1024]{2,1,0:T(8,128)(2,1)S(1)} %get-tuple-element.268), channel_id=1, source_target_pairs={{0,1},{1,2},{2,3},{3,0},{4,5},{5,6},{6,7},{7,4},{8,9},{9,10},{10,1... | collective-permute-start | bytes 2359304 | tf_op jit(solution)/shard_map/ppermute | solution.py:803
  498.0 37.9 %collective-permute-start.52 = (bf16[512,1024]{1,0:T(8,128)(2,1)}, bf16[512,1024]{1,0:T(8,128)(2,1)}, u32[]{:S(2)}, u32[]{:S(2)}) collective-permute-start(bf16[512,1024]{1,0:T(8,128)(2,1)} %add.387), channel_id=1, source_target_pairs={{0,1},{1,2},{2,3},{4,5},{5,6},{6,7},{8,9},{9,10},{10,11},{12,13},{... | collective-permute-start | bytes 3145736 | tf_op jit(solution)/shard_map/ppermute | solution.py:816
  503.1 34.7 %collective-permute-start.53 = (bf16[512,1024]{1,0:T(8,128)(2,1)}, bf16[512,1024]{1,0:T(8,128)(2,1)}, u32[]{:S(2)}, u32[]{:S(2)}) collective-permute-start(bf16[512,1024]{1,0:T(8,128)(2,1)} %add.388), channel_id=1, source_target_pairs={{1,0},{2,1},{3,2},{5,4},{6,5},{7,6},{9,8},{10,9},{11,10},{13,12},{... | collective-permute-start | bytes 3145736 | tf_op jit(solution)/shard_map/ppermute | solution.py:817
  (76 other events, 1034.6 us)
Sparse Core Ops, SparseCore 0:
  18.0 27.8 all-gather.2
  88.0 132.2 all-gather.4
  273.5 61.6 reduce-scatter.2
  338.6 134.6 reduce-scatter.4

commit v9 on v8

--- a/solution.py
+++ b/solution.py
@@ -368,18 +368,18 @@
 
 
 def project_back(index, grads, turned, weights, cosine, sine, gain, rows):
-    length, width = turned[0].shape
+    width = turned[0].shape[1]
+    count = index.shape[0]
     groups = len(grads)
     model = weights.shape[0]
     part = min(256, rows)
     per = rows // part
-    blocks = length // part
 
     def column(m):
         return pl.BlockSpec((model, width), lambda i, at: (0, m))
 
     def turn(i, at):
-        return (lax.rem(at[0] * per + i, blocks), 0)
+        return (at[i // per] * per + i % per, 0)
 
     def piece_block(d):
         return pl.BlockSpec((part, model), lambda i, at: (jnp.clip(i - d * per, 0, per - 1), 0))
@@ -390,7 +390,7 @@
         functools.partial(project_back_kernel, groups),
         grid_spec=pltpu.PrefetchScalarGridSpec(
             num_scalar_prefetch=1,
-            grid=(blocks,),
+            grid=(count * per,),
             in_specs=[pl.BlockSpec((part, width // groups), turn)] * (3 * groups)
             + [tall] * 2
             + [column(0), column(1), column(2), table, table]
@@ -399,42 +399,45 @@
                 pl.BlockSpec((part, 3 * width), lambda i, at: (i, 0)),
                 pl.BlockSpec((1, width), lambda i, at: (0, 0)),
             ]
-            + [piece_block(d) for d in range(length // rows)],
+            + [piece_block(d) for d in range(count)],
         ),
         out_shape=[
-            jax.ShapeDtypeStruct((length, 3 * width), bf16),
+            jax.ShapeDtypeStruct((count * rows, 3 * width), bf16),
             jax.ShapeDtypeStruct((1, width), f32),
         ]
-        + [jax.ShapeDtypeStruct((rows, model), bf16)] * (length // rows),
+        + [jax.ShapeDtypeStruct((rows, model), bf16)] * count,
         cost_estimate=pl.CostEstimate(
-            flops=length * width, bytes_accessed=length * width, transcendentals=0
+            flops=rows * width, bytes_accessed=rows * width, transcendentals=0
         ),
         name="project_back",
     )(index, *[g[m] for m in range(3) for g in grads], *turned, weights, weights, weights, cosine, sine, gain)
 
 
 def projection_grads_kernel(counts, *refs):
-    grad_ref, out_ref = refs[-2:]
+    calls = sum(1 for _ in counts)
+    grads, out_ref = refs[-calls - 1 : -1], refs[-1]
     total = None
-    for d, count in enumerate(counts):
-        hidden = added(refs[:count])
-        refs = refs[count:]
-        rows = hidden.shape[0]
-        part = dot_tn(hidden, grad_ref[d * rows : (d + 1) * rows, :])
-        total = part if total is None else total + part
+    for call, grad_ref in zip(counts, grads):
+        for d, count in enumerate(call):
+            hidden = added(refs[:count])
+            refs = refs[count:]
+            rows = hidden.shape[0]
+            part = dot_tn(hidden, grad_ref[d * rows : (d + 1) * rows, :])
+            total = part if total is None else total + part
     out_ref[...] = total.astype(bf16)
 
 
-def projection_grads(hidden, qkv_grad):
-    rows, model = hidden[0][0].shape
-    length, width = qkv_grad.shape
-    counts = tuple(len(parts) for parts in hidden)
+def projection_grads(hidden, grads):
+    rows, model = hidden[0][0][0].shape
+    width = grads[0].shape[1]
+    length = sum(g.shape[0] for g in grads)
+    counts = tuple(tuple(len(parts) for parts in call) for call in hidden)
     part = 256
     return pl.pallas_call(
         functools.partial(projection_grads_kernel, counts),
         grid=(model // part,),
-        in_specs=[pl.BlockSpec((rows, part), lambda i: (0, i))] * sum(counts)
-        + [pl.BlockSpec(qkv_grad.shape, lambda i: (0, 0))],
+        in_specs=[pl.BlockSpec((rows, part), lambda i: (0, i))] * sum(sum(c) for c in counts)
+        + [pl.BlockSpec(g.shape, lambda i: (0, 0)) for g in grads],
         out_specs=pl.BlockSpec((part, width), lambda i: (i, 0)),
         out_shape=jax.ShapeDtypeStruct((model, width), bf16),
         cost_estimate=pl.CostEstimate(
@@ -443,7 +446,7 @@
             transcendentals=0,
         ),
         name="projection_grads",
-    )(*[x for parts in hidden for x in parts], qkv_grad)
+    )(*[x for call in hidden for parts in call for x in parts], *grads)
 
 
 def out_grads_kernel(count, *refs):
@@ -615,14 +618,16 @@
             turned_ref[:, rows] = low_ref[rows, :].T
 
 
-def weight_specs(weights, step, base=0):
+def weight_specs(weights, step, total, base=0):
     nd, _, shard, local_width = weights.shape
     per = local_width // step
 
     def spec(m):
-        return pl.BlockSpec(
-            (nd, 1, shard, step), lambda i: (0, 3 * ((i + base) // per) + m, 0, (i + base) % per)
-        )
+        def place(i):
+            p = (i + base) // per
+            return (0, 2 * p + m if m < 2 else 2 * (total // local_width) + p, 0, (i + base) % per)
+
+        return pl.BlockSpec((nd, 1, shard, step), place)
 
     return [spec(0), spec(1), spec(2)]
 
@@ -636,7 +641,7 @@
         feed_kernel,
         grid=(total // step,),
         in_specs=[whole]
-        + weight_specs(weights, step)
+        + weight_specs(weights, step, total)
         + [
             pl.BlockSpec((2, step), lambda i: (0, i)),
             whole,
@@ -761,7 +766,7 @@
         feed_back_last_kernel if last else feed_back_first_kernel,
         grid=(count,),
         in_specs=[whole, turned, turned]
-        + weight_specs(weights, step, base)
+        + weight_specs(weights, step, scales.shape[1], base)
         + [pl.BlockSpec((2, step), lambda i: (0, i + base)), columns, columns, columns, whole]
         + ([whole, whole, pl.BlockSpec((2, model), lambda i: (0, 0))] if last else []),
         out_specs=grads_specs
@@ -888,27 +893,31 @@
     qkv_full = lax.all_gather(
         jnp.concatenate([attn_low[0], attn_low[1], attn_low[2]], axis=1), "dp", axis=0, tiled=True
     )
-    low_block = jnp.concatenate(
-        [
-            mlp_weight.astype(bf16).reshape(3 * shard, hidden_width),
-            attn_low[3].reshape(-1, hidden_width),
-        ],
-        axis=0,
-    )
-    ups, downs = [low_block], [low_block]
+    mlp_low = mlp_weight.astype(bf16)
+    chunks = [
+        mlp_low[:2].reshape(2 * shard, hidden_width),
+        jnp.concatenate([mlp_low[2], attn_low[3].reshape(-1, hidden_width)], axis=0),
+    ]
+    lines = [([chunk], [chunk]) for chunk in chunks]
     for hop in range(1, nt):
-        if hop == nt - 1:
-            ups[-1], downs[-1], hidden_in = lax.optimization_barrier((ups[-1], downs[-1], hidden_in))
-        up, down = carry_on(ups[-1], downs[-1], hop, "tensor", nt)
-        ups.append(up)
-        downs.append(down)
-    low_blocks = [sum(both(ups, downs, d)) for d in range(nt)]
+        for c, (ups, downs) in enumerate(lines):
+            if hop == nt - 1 and c == 1:
+                ups[-1], downs[-1], hidden_in = lax.optimization_barrier(
+                    (ups[-1], downs[-1], hidden_in)
+                )
+            up, down = carry_on(ups[-1], downs[-1], hop, "tensor", nt)
+            ups.append(up)
+            downs.append(down)
+    wide_blocks, low_blocks = [
+        [sum(both(ups, downs, d)) for d in range(nt)] for ups, downs in lines
+    ]
     out_low = jnp.concatenate(
-        [low[3 * shard :].reshape(shard, heads_width) for low in low_blocks], axis=1
+        [low[shard:].reshape(shard, heads_width) for low in low_blocks], axis=1
     )
     mlp_full = lax.all_gather(
         jnp.concatenate(
-            [low_blocks[d][: 3 * shard] for d in order]
+            [wide_blocks[d] for d in order]
+            + [low_blocks[d][:shard] for d in order]
             + [
                 out_low[:, at : at + hidden_width]
                 for at in range(0, nt * heads_width, hidden_width)
@@ -1055,26 +1064,36 @@
     for k in halvings[2 if len(head_grads) == 1 else 3 :]:
         out_sum = halving(out_sum, "dp", nd, k)
     out_pieces = to_owners(blocks_of(out_sum.astype(bf16), 1, heads_width), range(nt))
-    qkv_grad, gain_grad, *pieces = project_back(
-        me.reshape(1),
-        head_grads,
-        (query_turned, key_turned),
-        qkv_full,
-        cosine,
-        sine,
-        gain,
-        rows,
-    )
-    qkv_grad, pieces, small, out_pieces, far_last = lax.optimization_barrier(
-        (qkv_grad, pieces, small, out_pieces, far_last)
+    places = [[nt - 1, 1], [d for d in range(nt) if d not in (nt - 1, 1)]]
+    pieces, qkv_grads, gain_grads = [None] * nt, [], []
+
+    def back(call):
+        grad, gain_grad, *results = project_back(
+            jnp.stack([(me + d) % nt for d in call]),
+            head_grads,
+            (query_turned, key_turned),
+            qkv_full,
+            cosine,
+            sine,
+            gain,
+            rows,
+        )
+        qkv_grads.append(grad)
+        gain_grads.append(gain_grad)
+        for d, piece in zip(call, results):
+            pieces[d] = piece
+
+    back(places[0])
+    pieces[1], pieces[nt - 1], small, out_pieces, far_last, head_grads = lax.optimization_barrier(
+        (pieces[1], pieces[nt - 1], small, out_pieces, far_last, head_grads)
     )
     far_part = jnp.concatenate([far_first, far_last], axis=0)
-    hidden_turn = [hidden_parts[(nt - d) % nt] for d in range(nt)]
-    qkv_sum = projection_grads(hidden_turn, qkv_grad)
-    qkv_sum = qkv_sum.reshape(nd, shard, -1)
-
-    ahead = behind = None
-    for hop in range(1, nt):
+    ahead, behind = line_sum(pieces, 1, None, None, "tensor", nt)
+    back(places[1])
+    gain_grad = sum(gain_grads)
+    hidden_turn = [[hidden_parts[(nt - d) % nt] for d in call] for call in places]
+    qkv_sum = projection_grads(hidden_turn, qkv_grads).reshape(nd, shard, -1)
+    for hop in range(2, nt):
         if hop == 2:
             ahead, behind, qkv_sum, gain_grad = lax.optimization_barrier(
                 (ahead, behind, qkv_sum, gain_grad)

time: 556 us -> 554 us (level)
  waiting for transfers between devices: 199 us -> 169 us
  starting transfers between devices: 69.1 us -> 87.6 us
    ppermute x6 -> x9, waiting for transfers between devices: 22.7 us -> 8.99 us  [carry_on(): up = lax.ppermute(up, axis, [(i, i + 1) for i in range(hop - 1, size - 1)])]
    ppermute x3, waiting for transfers between devices: 21.4 us -> 11.6 us  [line_sum(): up = lax.ppermute(ahead, axis, [(i, i + 1) for i in range(hop)])]
    ppermute x6 -> x9, starting transfers between devices: 11.2 us -> 20.5 us  [carry_on(): up = lax.ppermute(up, axis, [(i, i + 1) for i in range(hop - 1, size - 1)])]
    unnamed x0 -> x3, other arithmetic: none -> 6.21 us
    pallas_call x1 -> x2, Pallas kernels: 16.2 us -> 20.3 us  [project_back(): pl.pallas_call(functools.partial(project_back_kernel, groups), grid_spec=...]
    ppermute x6 -> x9, starting transfers between devices: 7.72 us -> 11.6 us  [carry_on(): lax.ppermute(down, axis, [(i, i - 1) for i in range(1, size - hop + 1)])]
    ppermute x6 -> x9, waiting for transfers between devices: 73.5 us -> 69.7 us  [carry_on(): lax.ppermute(down, axis, [(i, i - 1) for i in range(1, size - hop + 1)])]
  transfers between devices with their start and end apart: 58 -> 64, of which waited for: 27 -> 27; matrix products, arithmetic and copies ran while one was open for 9% -> 11% of each run, Pallas kernels for 27% -> 28%
where the time goes in v9:
time: 554 us; the launch traced here: 547 us
  Pallas kernels  206 us (37%)
  waiting for transfers between devices  169 us (31%)
  starting transfers between devices  87.6 us (16%)
  other arithmetic  40 us (7%)
  local copies, waits for them, and re-layouts  23.5 us (4%)
  between operations  15.4 us (3%)
  matrix products  5.79 us (1%)
    ppermute x9, waiting for transfers between devices, carry_on(): lax.ppermute(down, axis, [(i, i - 1) for i in range(1, size - hop + 1)])  69.7 us
    pallas_call x2, Pallas kernels, feed_back(): pl.pallas_call(feed_back_last_kernel if last else feed_back_first_kernel,...  51.1 us
    ppermute x19, waiting for transfers between devices, shift(): lax.ppermute(value, axis, [(i, (i + distance) % size) for i in range(size)])  43.3 us
    pallas_call x2, Pallas kernels, attend_back(): pl.pallas_call(functools.partial(attend_back_kernel, group * heads, heads...  40.3 us
    ppermute x19, starting transfers between devices, shift(): lax.ppermute(value, axis, [(i, (i + distance) % size) for i in range(size)])  31.6 us
    pallas_call x1, Pallas kernels, feed(): pl.pallas_call(feed_kernel, grid=(total // step,), in_specs=[whole] + wei...  28.7 us
    pallas_call x4, Pallas kernels, project(): pl.pallas_call(functools.partial(project_kernel, count), grid_spec=pltpu....  23.2 us
    ppermute x9, starting transfers between devices, carry_on(): up = lax.ppermute(up, axis, [(i, i + 1) for i in range(hop - 1, size - 1)])  20.5 us
  transfers between devices with their start and end apart: 64, of which 27 were waited for; matrix products, arithmetic and copies ran while one was open for 11% of the time, Pallas kernels for 28%

profile of v9, /device:TPU:0, one launch (start us, length us, event | category | flops | bytes accessed | tf_op | source)
XLA Modules:
  0.0 547.4 jit_solution(1455862918145944433)
XLA Ops:
  15.9 9.8 %collective-permute-done.14 = bf16[256,1024]{1,0:T(8,128)(2,1)S(1)} collective-permute-done((bf16[256,1024]{1,0:T(8,128)(2,1)S(1)}, bf16[256,1024]{1,0:T(8,128)(2,1)S(1)}, u32[]{:S(2)}, u32[]{:S(2)}) %collective-permute-start.14) | collective-permute-done | bytes 524320 | tf_op jit(solution)/shard_map/ppermute | solution.py:813
  40.1 7.7 %collective-permute-done.2 = bf16[160,1024]{1,0:T(8,128)(2,1)} collective-permute-done((bf16[160,1024]{1,0:T(8,128)(2,1)}, bf16[160,1024]{1,0:T(8,128)(2,1)}, u32[]{:S(2)}, u32[]{:S(2)}) %collective-permute-start.2) | collective-permute-done | bytes 327712 | tf_op jit(solution)/shard_map/ppermute | solution.py:813
  50.4 10.2 %collective-permute-done.3 = bf16[160,1024]{1,0:T(8,128)(2,1)} collective-permute-done((bf16[160,1024]{1,0:T(8,128)(2,1)}, bf16[160,1024]{1,0:T(8,128)(2,1)}, u32[]{:S(2)}, u32[]{:S(2)}) %collective-permute-start.3) | collective-permute-done | bytes 327712 | tf_op jit(solution)/shard_map/ppermute | solution.py:813
  68.7 7.6 %collective-permute-done.19 = bf16[160,1024]{1,0:T(8,128)(2,1)} collective-permute-done((bf16[160,1024]{1,0:T(8,128)(2,1)}, bf16[160,1024]{1,0:T(8,128)(2,1)}, u32[]{:S(2)}, u32[]{:S(2)}) %collective-permute-start.19) | collective-permute-done | bytes 327712 | tf_op jit(solution)/shard_map/ppermute | solution.py:813
  103.5 6.9 %collective-permute-done.4.refs_0_ = bf16[512,1024]{1,0:T(8,128)(2,1)S(1)} collective-permute-done((bf16[512,1024]{1,0:T(8,128)(2,1)S(1)}, bf16[512,1024]{1,0:T(8,128)(2,1)S(1)}, u32[]{:S(2)}, u32[]{:S(2)}) %collective-permute-start.4) | collective-permute-done | bytes 1048608 | tf_op jit(solution)/shard_map/ppermute | solution.py:812
  116.6 22.9 %collective-permute-done.7.refs_1_.refs_6_ = bf16[512,1024]{1,0:T(8,128)(2,1)} collective-permute-done((bf16[512,1024]{1,0:T(8,128)(2,1)S(1)}, bf16[512,1024]{1,0:T(8,128)(2,1)}, u32[]{:S(2)}, u32[]{:S(2)}) %collective-permute-start.7) | collective-permute-done | bytes 1048608 | tf_op jit(solution)/shard_map/ppermute | solution.py:813
  156.8 7.3 %collective-permute-done.9.refs_1_ = bf16[512,1024]{1,0:T(8,128)(2,1)} collective-permute-done((bf16[512,1024]{1,0:T(8,128)(2,1)}, bf16[512,1024]{1,0:T(8,128)(2,1)}, u32[]{:S(2)}, u32[]{:S(2)}) %collective-permute-start.9) | collective-permute-done | bytes 1048608 | tf_op jit(solution)/shard_map/ppermute | solution.py:813
  169.9 5.8 %project.7 = (bf16[2048,256]{1,0:T(8,128)(2,1)}, bf16[2048,256]{1,0:T(8,128)(2,1)}, bf16[2048,256]{1,0:T(8,128)(2,1)}, f32[2048,256]{1,0:T(8,128)}, f32[2048,256]{1,0:T(8,128)}) custom-call(s32[1]{0:T(128)} %bitcast.4.index_ref, ...), custom_call_target="tpu_custom_call", output_to_operand_aliasing={{0}: (9, {}), {1}: (10, {}), {2}: (11, {}), {3}: (12, {}), ... | custom-call | flops 805306368 | bytes 2097152 | tf_op jit(solution)/shard_map/project/pallas_call | solution.py:292
  175.8 20.1 %attend.1 = (bf16[2048,256]{1,0:T(8,128)(2,1)}, f32[2048,256]{1,0:T(8,128)}, f32[4,2048]{1,0:T(4,128)}) custom-call(s32[2,4]{1,0:T(2,128)} %pad_add_fusion.bounds_ref, bf16[2048,256]{1,0:T(8,128)(2,1)} %get-tuple-element.196.q_ref, bf16[2048,256]{1,0:T(8,128)(2,1)} %get-tuple-element.197.k_ref, bf16[2048,256]{1,0:T(8,128)(2,1)} %get-tuple-element.198.v_ref, ...), custom_call_target="tpu_custom_call" | custom-call | flops 20000000000 | bytes 4194304 | tf_op jit(solution)/shard_map/attend/pallas_call | solution.py:124
  206.2 6.6 %collective-permute-done.11.refs_2_ = bf16[512,256]{1,0:T(8,128)(2,1)S(1)} collective-permute-done((bf16[512,256]{1,0:T(8,128)(2,1)S(1)}, bf16[512,256]{1,0:T(8,128)(2,1)S(1)}, u32[]{:S(2)}, u32[]{:S(2)}) %collective-permute-start.11) | collective-permute-done | bytes 262176 | tf_op jit(solution)/shard_map/ppermute | solution.py:808
  212.9 8.0 %all-gather.5.cloned.1.call-done = bf16[13312,1024]{1,0:T(8,128)(2,1)} async-done(((bf16[1664,1024]{1,0:T(8,128)(2,1)}), bf16[13312,1024]{1,0:T(8,128)(2,1)}) %all-gather.5.cloned.1.call-update) | async-done | bytes 27262992 | tf_op jit(solution)/shard_map/all_gather | solution.py:917
  220.9 9.0 %mix.1 = (f32[512,1024]{1,0:T(8,128)}, f32[512,1024]{1,0:T(8,128)}, bf16[512,1024]{1,0:T(8,128)(2,1)}, bf16[1024,512]{1,0:T(8,128)(2,1)}, bf16[1024,1024]{1,0:T(8,128)(2,1)}) custom-call(bf16[512,256]{1,0:T(8,128)(2,1)} %get-tuple-element.323.refs_0_, bf16[512,256]{1,0:T(8,128)(2,1)} %copy-done.12, bf16[512,256]{1,0:T(8,128)(2,1)} %copy-done.13, ...), custom_call_target="tpu_custom_call" | custom-call | flops 1073741824 | bytes 7340032 | tf_op jit(solution)/shard_map/mix/pallas_call | solution.py:522
  229.8 28.7 %feed.1 = (f32[512,4096]{1,0:T(8,128)}, f32[512,4096]{1,0:T(8,128)}, bf16[512,4096]{1,0:T(8,128)(2,1)}, bf16[512,1024]{1,0:T(8,128)(2,1)}, f32[512,1024]{1,0:T(8...) custom-call(bf16[512,1024]{1,0:T(8,128)(2,1)} %get-tuple-element.202.m_ref, ...), custom_call_target="tpu_custom_call" | custom-call | flops 12884901888 | bytes 46137344 | tf_op jit(solution)/shard_map/feed/pallas_call | solution.py:640
  258.5 15.1 %feed_back_first.1 = (bf16[3,1024,1024]{2,1,0:T(8,128)(2,1)}, f32[2,1024]{1,0:T(2,128)}, f32[512,1024]{1,0:T(8,128)}) custom-call(bf16[512,1024]{1,0:T(8,128)(2,1)} %get-tuple-element.205.refs_0_, bf16[1024,512]{1,0:T(8,128)(2,1)} %get-tuple-element.206.refs_1_, bf16[1024,512]{1,0:T(8,128)(2,1)} %get-tuple-element.207.refs_2_, ...), custom_call_target="tpu_custom_call" | custom-call | flops 6442450944 | bytes 17825792 | tf_op jit(solution)/shard_map/feed_back_first/pallas_call | solution.py:765
  273.8 36.0 %feed_back_last.1 = (bf16[3,1024,3072]{2,1,0:T(8,128)(2,1)}, f32[2,3072]{1,0:T(2,128)}, f32[512,1024]{1,0:T(8,128)}, bf16[512,1024]{1,0:T(8,128)(2,1)}, f32[1,1024]{1,0:T(1,128)}) custom-call(bf16[512,1024]{1,0:T(8,128)(2,1)} %get-tuple-element.205.refs_0_, bf16[1024,512]{1,0:T(8,128)(2,1)} %get-tuple-element.206.refs_1_, ...), custom_call_target="tpu_custom_call" | custom-call | flops 19327352832 | bytes 53477376 | tf_op jit(solution)/shard_map/feed_back_last/pallas_call | solution.py:765
  331.5 8.3 %collective-permute-done.25 = bf16[512,256]{1,0:T(8,128)(2,1)} collective-permute-done((bf16[512,256]{1,0:T(8,128)(2,1)}, bf16[512,256]{1,0:T(8,128)(2,1)}, u32[]{:S(2)}, u32[]{:S(2)}) %collective-permute-start.25) | collective-permute-done | bytes 262176 | tf_op jit(solution)/shard_map/ppermute | solution.py:808
  345.4 20.1 %attend_back.2 = (f32[2048,128]{1,0:T(8,128)}, f32[2048,128]{1,0:T(8,128)}, f32[2048,128]{1,0:T(8,128)}) custom-call(s32[2,4]{1,0:T(2,128)} %pad_add_fusion.bounds_ref, bf16[2048,256]{1,0:T(8,128)(2,1)} %get-tuple-element.196.q_ref, bf16[2048,256]{1,0:T(8,128)(2,1)} %constant_dynamic-update-slice_fusion.11.do_ref, ...), custom_call_target="tpu_custom_call" | custom-call | flops 40000000000 | bytes 5242880 | tf_op jit(solution)/shard_map/attend_back/pallas_call | solution.py:209
  369.0 20.2 %attend_back.3 = (f32[2048,128]{1,0:T(8,128)}, f32[2048,128]{1,0:T(8,128)}, f32[2048,128]{1,0:T(8,128)}) custom-call(s32[2,4]{1,0:T(2,128)} %pad_add_fusion.bounds_ref, bf16[2048,256]{1,0:T(8,128)(2,1)} %get-tuple-element.196.q_ref, bf16[2048,256]{1,0:T(8,128)(2,1)} %constant_dynamic-update-slice_fusion.11.do_ref, ...), custom_call_target="tpu_custom_call" | custom-call | flops 40000000000 | bytes 5242880 | tf_op jit(solution)/shard_map/attend_back/pallas_call | solution.py:209
  398.4 10.3 %project_back.2 = (bf16[1024,768]{1,0:T(8,128)(2,1)}, f32[1,256]{1,0:T(1,128)}, bf16[512,1024]{1,0:T(8,128)(2,1)}, bf16[512,1024]{1,0:T(8,128)(2,1)}) custom-call(s32[2]{0:T(128)} %get-tuple-element.343.index_ref, f32[2048,128]{1,0:T(8,128)} %get-tuple-element.254.refs_0_, f32[2048,128]{1,0:T(8,128)} %get-tuple-element.255.refs_1_, ...), custom_call_target="tpu_custom_call" | custom-call | flops 131072 | bytes 131072 | tf_op jit(solution)/shard_map/project_back/pallas_call | solution.py:389
  415.0 10.0 %project_back.3 = (bf16[1024,768]{1,0:T(8,128)(2,1)}, f32[1,256]{1,0:T(1,128)}, bf16[512,1024]{1,0:T(8,128)(2,1)}, bf16[512,1024]{1,0:T(8,128)(2,1)}) custom-call(s32[2]{0:T(128)} %get-tuple-element.342.index_ref, f32[2048,128]{1,0:T(8,128)} %get-tuple-element.254.refs_0_, f32[2048,128]{1,0:T(8,128)} %get-tuple-element.255.refs_1_, ...), custom_call_target="tpu_custom_call" | custom-call | flops 131072 | bytes 131072 | tf_op jit(solution)/shard_map/project_back/pallas_call | solution.py:389
  425.8 8.4 %projection_grads.1 = bf16[1024,768]{1,0:T(8,128)(2,1)} custom-call(bf16[512,1024]{1,0:T(8,128)(2,1)} %copy-done.4, bf16[512,1024]{1,0:T(8,128)(2,1)} %collective-permute-done.9.refs_1_, bf16[512,1024]{1,0:T(8,128)(2,1)} %collective-permute-done.8.refs_0_.refs_2_, bf16[512,1024]{1,0:T(8,128)(2,1)} %copy-done.5, bf16[512,1024]{1,0:T(8,128)(2,1)} %refs_4_, ...), custom_call_target="tpu_custom_call" | custom-call | flops 3221225472 | bytes 16777216 | tf_op jit(solution)/shard_map/projection_grads/pallas_call | solution.py:436
  451.4 15.5 %collective-permute-done.43 = bf16[2,128,768]{2,1,0:T(8,128)(2,1)S(1)} collective-permute-done((bf16[2,128,768]{2,1,0:T(8,128)(2,1)S(1)}, bf16[2,128,768]{2,1,0:T(8,128)(2,1)S(1)}, u32[]{:S(2)}, u32[]{:S(2)}) %collective-permute-start.43) | collective-permute-done | bytes 393248 | tf_op jit(solution)/shard_map/ppermute | solution.py:832
  501.9 12.9 %collective-permute-done.48 = bf16[3,128,1024]{2,1,0:T(8,128)(2,1)S(1)} collective-permute-done((bf16[3,128,1024]{2,1,0:T(8,128)(2,1)S(1)}, bf16[3,128,1024]{2,1,0:T(8,128)(2,1)S(1)}, u32[]{:S(2)}, u32[]{:S(2)}) %collective-permute-start.48) | collective-permute-done | bytes 786464 | tf_op jit(solution)/shard_map/ppermute | solution.py:808
  526.6 8.4 %collective-permute-done.58 = bf16[512,1024]{1,0:T(8,128)(2,1)} collective-permute-done((bf16[512,1024]{1,0:T(8,128)(2,1)}, bf16[512,1024]{1,0:T(8,128)(2,1)}, u32[]{:S(2)}, u32[]{:S(2)}) %collective-permute-start.58) | collective-permute-done | bytes 1048608 | tf_op jit(solution)/shard_map/ppermute | solution.py:821
  (327 shorter events, 216.3 us)
Async XLA Ops:
  7.2 90.5 %all-gather.3.cloned.1.call-start = ((), (), s32[]{:S(2)}) async-start(), calls=%async_computation.2 | async-start | bytes 1769472 | tf_op jit(solution)/shard_map/all_gather | solution.py:893
  10.2 24.9 %collective-permute-start.13 = (bf16[256,1024]{1,0:T(8,128)(2,1)S(1)}, bf16[256,1024]{1,0:T(8,128)(2,1)S(1)}, u32[]{:S(2)}, u32[]{:S(2)}) collective-permute-start(bf16[256,1024]{1,0:T(8,128)(2,1)S(1)} %bitcast.108), channel_id=1, source_target_pairs={{0,1},{1,2},{2,3},{4,5},{5,6},{6,7},{8,9},{9,10},{10,11},{12,13},{... | collective-permute-start | bytes 1572872 | tf_op jit(solution)/shard_map/ppermute | solution.py:812
  25.7 23.4 %collective-permute-start.15 = (bf16[256,1024]{1,0:T(8,128)(2,1)S(1)}, bf16[256,1024]{1,0:T(8,128)(2,1)S(1)}, u32[]{:S(2)}, u32[]{:S(2)}) collective-permute-start(bf16[256,1024]{1,0:T(8,128)(2,1)S(1)} %collective-permute-done.14), channel_id=1, source_target_pairs={{1,0},{2,1},{5,4},{6,5},{9,8},{10,9},{13,12},{14,13},{17,16},{18,1... | collective-permute-start | bytes 1572872 | tf_op jit(solution)/shard_map/ppermute | solution.py:813
  35.1 185.8 %all-gather.5.cloned.1.call-start = ((), (), s32[]{:S(2)}) async-start(), calls=%async_computation.3 | async-start | bytes 30670848 | tf_op jit(solution)/shard_map/all_gather | solution.py:917
  35.1 28.2 %collective-permute-start.17 = (bf16[256,1024]{1,0:T(8,128)(2,1)S(1)}, bf16[256,1024]{1,0:T(8,128)(2,1)}, u32[]{:S(2)}, u32[]{:S(2)}) collective-permute-start(bf16[256,1024]{1,0:T(8,128)(2,1)S(1)} %collective-permute-done.13), channel_id=1, source_target_pairs={{1,2},{2,3},{5,6},{6,7},{9,10},{10,11},{13,14},{14,15},{17,18},{18... | collective-permute-start | bytes 1572872 | tf_op jit(solution)/shard_map/ppermute | solution.py:812
  49.1 29.0 %collective-permute-start.16 = (bf16[256,1024]{1,0:T(8,128)(2,1)S(1)}, bf16[256,1024]{1,0:T(8,128)(2,1)}, u32[]{:S(2)}, u32[]{:S(2)}) collective-permute-start(bf16[256,1024]{1,0:T(8,128)(2,1)S(1)} %collective-permute-done.15), channel_id=1, source_target_pairs={{1,0},{5,4},{9,8},{13,12},{17,16},{21,20},{25,24},{29,28}} | collective-permute-start | bytes 1572872 | tf_op jit(solution)/shard_map/ppermute | solution.py:813
  88.1 255.7 %reduce-scatter.3.cloned.1.call-start = ((), (), s32[]{:S(2)}) async-start(), calls=%async_computation.4 | async-start | bytes 7077888 | tf_op jit(solution)/shard_map/reduce_scatter | solution.py:1002
  90.2 24.3 %collective-permute-start.5 = (bf16[512,1024]{1,0:T(8,128)(2,1)S(1)}, bf16[512,1024]{1,0:T(8,128)(2,1)S(1)}, u32[]{:S(2)}, u32[]{:S(2)}) collective-permute-start(bf16[512,1024]{1,0:T(8,128)(2,1)S(1)} %copy-done), channel_id=1, source_target_pairs={{1,0},{2,1},{3,2},{5,4},{6,5},{7,6},{9,8},{10,9},{11,10},{13,12},{... | collective-permute-start | bytes 3145736 | tf_op jit(solution)/shard_map/ppermute | solution.py:813
  115.2 24.3 %collective-permute-start.7 = (bf16[512,1024]{1,0:T(8,128)(2,1)S(1)}, bf16[512,1024]{1,0:T(8,128)(2,1)}, u32[]{:S(2)}, u32[]{:S(2)}) collective-permute-start(bf16[512,1024]{1,0:T(8,128)(2,1)S(1)} %collective-permute-done.5.refs_1_.refs_3_), channel_id=1, source_target_pairs={{1,0},{2,1},{5,4},{6,5},{9,8},{10,9},{13,12},{14,13},{17,16},{18,1... | collective-permute-start | bytes 3145736 | tf_op jit(solution)/shard_map/ppermute | solution.py:813
  142.5 55.4 %collective-permute-start.21 = (f32[2,1024]{1,0:T(2,128)S(1)}, f32[2,1024]{1,0:T(2,128)S(1)}, u32[]{:S(2)}, u32[]{:S(2)}) collective-permute-start(f32[2,1024]{1,0:T(2,128)S(1)} %copy-done.38), channel_id=1, source_target_pairs={{0,1},{1,2},{2,3},{3,0},{4,5},{5,6},{6,7},{7,4},{8,9},{9,10},{10,1... | collective-permute-start | bytes 24584 | tf_op jit(solution)/shard_map/ppermute | solution.py:808
  146.1 56.1 %collective-permute-start.22 = (f32[2,1024]{1,0:T(2,128)S(1)}, f32[2,1024]{1,0:T(2,128)S(1)}, u32[]{:S(2)}, u32[]{:S(2)}) collective-permute-start(f32[2,1024]{1,0:T(2,128)S(1)} %copy-done.38), channel_id=1, source_target_pairs={{0,3},{1,0},{2,1},{3,2},{4,7},{5,4},{6,5},{7,6},{8,11},{9,8},{10,9... | collective-permute-start | bytes 24584 | tf_op jit(solution)/shard_map/ppermute | solution.py:808
  146.6 55.6 %collective-permute-start.23 = (f32[2,1024]{1,0:T(2,128)S(1)}, f32[2,1024]{1,0:T(2,128)S(1)}, u32[]{:S(2)}, u32[]{:S(2)}) collective-permute-start(f32[2,1024]{1,0:T(2,128)S(1)} %copy-done.38), channel_id=1, source_target_pairs={{0,2},{1,3},{2,0},{3,1},{4,6},{5,7},{6,4},{7,5},{8,10},{9,11},{10,... | collective-permute-start | bytes 24584 | tf_op jit(solution)/shard_map/ppermute | solution.py:808
  273.7 200.6 %reduce-scatter.5.cloned.1.call-start = ((), (), s32[]{:S(2)}) async-start(), calls=%async_computation.5 | async-start | bytes 21233664 | tf_op jit(solution)/shard_map/reduce_scatter | solution.py:1006
  365.8 23.5 %collective-permute-start.30 = (f32[10,1024]{1,0:T(8,128)S(1)}, f32[10,1024]{1,0:T(8,128)S(1)}, u32[]{:S(2)}, u32[]{:S(2)}) collective-permute-start(f32[10,1024]{1,0:T(8,128)S(1)} %add.366), channel_id=1, source_target_pairs={{0,2},{1,3},{2,0},{3,1},{4,6},{5,7},{6,4},{7,5},{8,10},{9,11},{10,... | collective-permute-start | bytes 122888 | tf_op jit(solution)/shard_map/ppermute | solution.py:838
  367.6 25.2 %collective-permute-start.32 = (bf16[2,128,1024]{2,1,0:T(8,128)(2,1)S(1)}, bf16[2,128,1024]{2,1,0:T(8,128)(2,1)S(1)}, u32[]{:S(2)}, u32[]{:S(2)}) collective-permute-start(bf16[2,128,1024]{2,1,0:T(8,128)(2,1)S(1)} %slice.149), channel_id=1, source_target_pairs={{0,2},{1,3},{2,0},{3,1},{4,6},{5,7},{6,4},{7,5},{8,10},{9,11},{10,... | collective-permute-start | bytes 1572872 | tf_op jit(solution)/shard_map/ppermute | solution.py:808
  412.9 24.5 %collective-permute-start.38 = (bf16[512,1024]{1,0:T(8,128)(2,1)}, bf16[512,1024]{1,0:T(8,128)(2,1)S(1)}, u32[]{:S(2)}, u32[]{:S(2)}) collective-permute-start(bf16[512,1024]{1,0:T(8,128)(2,1)} %get-tuple-element.262), channel_id=1, source_target_pairs={{0,1},{4,5},{8,9},{12,13},{16,17},{20,21},{24,25},{28,29}} | collective-permute-start | bytes 3145736 | tf_op jit(solution)/shard_map/ppermute | solution.py:821
  440.3 34.0 %collective-permute-start.40 = (bf16[512,1024]{1,0:T(8,128)(2,1)}, bf16[512,1024]{1,0:T(8,128)(2,1)}, u32[]{:S(2)}, u32[]{:S(2)}) collective-permute-start(bf16[512,1024]{1,0:T(8,128)(2,1)} %get-tuple-element.319), channel_id=1, source_target_pairs={{0,1},{1,2},{4,5},{5,6},{8,9},{9,10},{12,13},{13,14},{16,17},{17,1... | collective-permute-start | bytes 3145736 | tf_op jit(solution)/shard_map/ppermute | solution.py:821
  445.7 28.7 %collective-permute-start.41 = (bf16[512,1024]{1,0:T(8,128)(2,1)}, bf16[512,1024]{1,0:T(8,128)(2,1)S(1)}, u32[]{:S(2)}, u32[]{:S(2)}) collective-permute-start(bf16[512,1024]{1,0:T(8,128)(2,1)} %get-tuple-element.318), channel_id=1, source_target_pairs={{2,1},{3,2},{6,5},{7,6},{10,9},{11,10},{14,13},{15,14},{18,17},{19... | collective-permute-start | bytes 3145736 | tf_op jit(solution)/shard_map/ppermute | solution.py:822
  446.8 26.5 %collective-permute-start.44 = (f32[1,256]{1,0:T(1,128)S(1)}, f32[1,256]{1,0:T(1,128)S(1)}, u32[]{:S(2)}, u32[]{:S(2)}) collective-permute-start(f32[1,256]{1,0:T(1,128)S(1)} %add.378), channel_id=1, source_target_pairs={{0,1},{1,2},{2,3},{3,0},{4,5},{5,6},{6,7},{7,4},{8,9},{9,10},{10,1... | collective-permute-start | bytes 3080 | tf_op jit(solution)/shard_map/ppermute | solution.py:808
  449.2 25.1 %collective-permute-start.45 = (f32[1,256]{1,0:T(1,128)S(1)}, f32[1,256]{1,0:T(1,128)S(1)}, u32[]{:S(2)}, u32[]{:S(2)}) collective-permute-start(f32[1,256]{1,0:T(1,128)S(1)} %add.378), channel_id=1, source_target_pairs={{0,2},{1,3},{2,0},{3,1},{4,6},{5,7},{6,4},{7,5},{8,10},{9,11},{10,... | collective-permute-start | bytes 3080 | tf_op jit(solution)/shard_map/ppermute | solution.py:808
  476.2 25.7 %collective-permute-start.47 = (bf16[3,128,1024]{2,1,0:T(8,128)(2,1)S(1)}, bf16[3,128,1024]{2,1,0:T(8,128)(2,1)S(1)}, u32[]{:S(2)}, u32[]{:S(2)}) collective-permute-start(bf16[3,128,1024]{2,1,0:T(8,128)(2,1)S(1)} %get-tuple-element.277), channel_id=1, source_target_pairs={{0,3},{1,0},{2,1},{3,2},{4,7},{5,4},{6,5},{7,6},{8,11},{9,8},{10,9... | collective-permute-start | bytes 2359304 | tf_op jit(solution)/shard_map/ppermute | solution.py:808
  478.9 35.8 %collective-permute-start.48 = (bf16[3,128,1024]{2,1,0:T(8,128)(2,1)S(1)}, bf16[3,128,1024]{2,1,0:T(8,128)(2,1)S(1)}, u32[]{:S(2)}, u32[]{:S(2)}) collective-permute-start(bf16[3,128,1024]{2,1,0:T(8,128)(2,1)S(1)} %get-tuple-element.278), channel_id=1, source_target_pairs={{0,1},{1,2},{2,3},{3,0},{4,5},{5,6},{6,7},{7,4},{8,9},{9,10},{10,1... | collective-permute-start | bytes 2359304 | tf_op jit(solution)/shard_map/ppermute | solution.py:808
  496.2 38.9 %collective-permute-start.58 = (bf16[512,1024]{1,0:T(8,128)(2,1)}, bf16[512,1024]{1,0:T(8,128)(2,1)}, u32[]{:S(2)}, u32[]{:S(2)}) collective-permute-start(bf16[512,1024]{1,0:T(8,128)(2,1)} %add.410), channel_id=1, source_target_pairs={{0,1},{1,2},{2,3},{4,5},{5,6},{6,7},{8,9},{9,10},{10,11},{12,13},{... | collective-permute-start | bytes 3145736 | tf_op jit(solution)/shard_map/ppermute | solution.py:821
  500.6 35.4 %collective-permute-start.59 = (bf16[512,1024]{1,0:T(8,128)(2,1)}, bf16[512,1024]{1,0:T(8,128)(2,1)}, u32[]{:S(2)}, u32[]{:S(2)}) collective-permute-start(bf16[512,1024]{1,0:T(8,128)(2,1)} %add.411), channel_id=1, source_target_pairs={{1,0},{2,1},{3,2},{5,4},{6,5},{7,6},{9,8},{10,9},{11,10},{13,12},{... | collective-permute-start | bytes 3145736 | tf_op jit(solution)/shard_map/ppermute | solution.py:822
  (84 other events, 1134.4 us)
Sparse Core Ops, SparseCore 0:
  35.2 26.5 all-gather.2
  88.2 132.6 all-gather.4
  273.8 61.6 reduce-scatter.2
  339.0 134.6 reduce-scatter.4

commit v10 on v8

--- a/solution.py
+++ b/solution.py
@@ -474,6 +474,42 @@
         ),
         name="out_grads",
     )(*attended, branch_grad)
+
+
+def assemble_kernel(order, wide_counts, shard, width, *refs):
+    out_ref = refs[-1]
+    size = len(order)
+    hidden_width = out_ref.shape[1]
+    wide, low = [], []
+    for blocks in (wide, low):
+        for count in wide_counts:
+            blocks.append(refs[:count])
+            refs = refs[count:]
+    for p, d in enumerate(order):
+        out_ref[2 * p * shard : 2 * (p + 1) * shard, :] = added(wide[d])
+    packed = shard * width // hidden_width
+    per = hidden_width // width
+    for p, d in enumerate(order):
+        down = [ref[:shard, :] for ref in low[d]]
+        out_ref[(2 * size + p) * shard : (2 * size + p + 1) * shard, :] = sum(down[1:], down[0])
+    for d in range(size):
+        outs = [ref[shard:, :] for ref in low[d]]
+        block = sum(outs[1:], outs[0])
+        columns = slice((d % per) * width, (d % per + 1) * width)
+        for c in range(per):
+            row = (3 * size + d // per) * shard + c * packed
+            out_ref[row : row + packed, columns] = block[:, c * width : (c + 1) * width]
+
+
+def assemble(order, wide, low, shard, width):
+    hidden_width = wide[0][0].shape[1]
+    counts = tuple(len(parts) for parts in wide)
+    blocks = 3 * len(order) + len(order) * width // hidden_width
+    return pl.pallas_call(
+        functools.partial(assemble_kernel, tuple(order), counts, shard, width),
+        out_shape=jax.ShapeDtypeStruct((blocks * shard, hidden_width), bf16),
+        name="assemble",
+    )(*[x for parts in list(wide) + list(low) for x in parts])
 
 
 def rms_scale(x):
@@ -615,14 +651,16 @@
             turned_ref[:, rows] = low_ref[rows, :].T
 
 
-def weight_specs(weights, step, base=0):
+def weight_specs(weights, step, total, base=0):
     nd, _, shard, local_width = weights.shape
     per = local_width // step
 
     def spec(m):
-        return pl.BlockSpec(
-            (nd, 1, shard, step), lambda i: (0, 3 * ((i + base) // per) + m, 0, (i + base) % per)
-        )
+        def place(i):
+            p = (i + base) // per
+            return (0, 2 * p + m if m < 2 else 2 * (total // local_width) + p, 0, (i + base) % per)
+
+        return pl.BlockSpec((nd, 1, shard, step), place)
 
     return [spec(0), spec(1), spec(2)]
 
@@ -636,7 +674,7 @@
         feed_kernel,
         grid=(total // step,),
         in_specs=[whole]
-        + weight_specs(weights, step)
+        + weight_specs(weights, step, total)
         + [
             pl.BlockSpec((2, step), lambda i: (0, i)),
             whole,
@@ -761,7 +799,7 @@
         feed_back_last_kernel if last else feed_back_first_kernel,
         grid=(count,),
         in_specs=[whole, turned, turned]
-        + weight_specs(weights, step, base)
+        + weight_specs(weights, step, scales.shape[1], base)
         + [pl.BlockSpec((2, step), lambda i: (0, i + base)), columns, columns, columns, whole]
         + ([whole, whole, pl.BlockSpec((2, model), lambda i: (0, 0))] if last else []),
         out_specs=grads_specs
@@ -888,37 +926,28 @@
     qkv_full = lax.all_gather(
         jnp.concatenate([attn_low[0], attn_low[1], attn_low[2]], axis=1), "dp", axis=0, tiled=True
     )
-    low_block = jnp.concatenate(
-        [
-            mlp_weight.astype(bf16).reshape(3 * shard, hidden_width),
-            attn_low[3].reshape(-1, hidden_width),
-        ],
-        axis=0,
-    )
-    ups, downs = [low_block], [low_block]
+    mlp_low = mlp_weight.astype(bf16)
+    splits = hidden_width // heads_width
+    packed = jnp.concatenate(jnp.split(attn_low[3], splits, axis=0), axis=1)
+    chunks = [
+        mlp_low[:2].reshape(2 * shard, hidden_width),
+        jnp.concatenate([mlp_low[2], packed], axis=0),
+    ]
+    lines = [([chunk], [chunk]) for chunk in chunks]
     for hop in range(1, nt):
-        if hop == nt - 1:
-            ups[-1], downs[-1], hidden_in = lax.optimization_barrier((ups[-1], downs[-1], hidden_in))
-        up, down = carry_on(ups[-1], downs[-1], hop, "tensor", nt)
-        ups.append(up)
-        downs.append(down)
-    low_blocks = [sum(both(ups, downs, d)) for d in range(nt)]
-    out_low = jnp.concatenate(
-        [low[3 * shard :].reshape(shard, heads_width) for low in low_blocks], axis=1
-    )
-    mlp_full = lax.all_gather(
-        jnp.concatenate(
-            [low_blocks[d][: 3 * shard] for d in order]
-            + [
-                out_low[:, at : at + hidden_width]
-                for at in range(0, nt * heads_width, hidden_width)
-            ],
-            axis=0,
-        ),
-        "dp",
-        axis=0,
-        tiled=True,
-    )
+        for c, (ups, downs) in enumerate(lines):
+            if hop == nt - 1 and c == 1:
+                ups[-1], downs[-1], hidden_in = lax.optimization_barrier(
+                    (ups[-1], downs[-1], hidden_in)
+                )
+            up, down = carry_on(ups[-1], downs[-1], hop, "tensor", nt)
+            ups.append(up)
+            downs.append(down)
+    wide_blocks, low_blocks = [
+        [both(ups, downs, d) for d in range(nt)] for ups, downs in lines
+    ]
+    operand = assemble(order, wide_blocks, low_blocks, shard, heads_width)
+    mlp_full = lax.all_gather(operand, "dp", axis=0, tiled=True)
     mlp_full = mlp_full.reshape(nd, -1, shard, hidden_width)
     scales_parts = gather(mlp_scales)
     scales_row = jnp.concatenate([scales_parts[d] for d in order], axis=1)

time: 556 us -> 553 us (level)
  starting transfers between devices: 69.1 us -> 87.4 us
  waiting for transfers between devices: 199 us -> 182 us
  other arithmetic: 34.6 us -> 26.9 us
    ppermute x6 -> x9, waiting for transfers between devices: 22.7 us -> 10.1 us  [carry_on(): up = lax.ppermute(up, axis, [(i, i + 1) for i in range(hop - 1, size - 1)])]
    ppermute x6 -> x9, starting transfers between devices: 11.2 us -> 20.6 us  [carry_on(): up = lax.ppermute(up, axis, [(i, i + 1) for i in range(hop - 1, size - 1)])]
    ppermute x6 -> x9, waiting for transfers between devices: 73.5 us -> 78.3 us  [carry_on(): lax.ppermute(down, axis, [(i, i - 1) for i in range(1, size - hop + 1)])]
    ppermute x6 -> x9, starting transfers between devices: 7.72 us -> 11.6 us  [carry_on(): lax.ppermute(down, axis, [(i, i - 1) for i in range(1, size - hop + 1)])]
  transfers between devices with their start and end apart: 58 -> 64, of which waited for: 27 -> 25; matrix products, arithmetic and copies ran while one was open for 9% -> 7% of each run, Pallas kernels for 27% -> 28%
where the time goes in v10:
time: 553 us; the launch traced here: 547 us
  Pallas kernels  208 us (38%)
  waiting for transfers between devices  182 us (33%)
  starting transfers between devices  87.4 us (16%)
  other arithmetic  26.9 us (5%)
  local copies, waits for them, and re-layouts  21.6 us (4%)
  between operations  15.4 us (3%)
  matrix products  5.82 us (1%)
    ppermute x9, waiting for transfers between devices, carry_on(): lax.ppermute(down, axis, [(i, i - 1) for i in range(1, size - hop + 1)])  78.3 us
    pallas_call x2, Pallas kernels, feed_back(): pl.pallas_call(feed_back_last_kernel if last else feed_back_first_kernel,...  51.1 us
    pallas_call x2, Pallas kernels, attend_back(): pl.pallas_call(functools.partial(attend_back_kernel, group * heads, heads...  40.4 us
    ppermute x19, waiting for transfers between devices, shift(): lax.ppermute(value, axis, [(i, (i + distance) % size) for i in range(size)])  33.4 us
    pallas_call x1, Pallas kernels, feed(): pl.pallas_call(feed_kernel, grid=(total // step,), in_specs=[whole] + wei...  28.7 us
    ppermute x19, starting transfers between devices, shift(): lax.ppermute(value, axis, [(i, (i + distance) % size) for i in range(size)])  26.1 us
    pallas_call x4, Pallas kernels, project(): pl.pallas_call(functools.partial(project_kernel, count), grid_spec=pltpu....  23.7 us
    ppermute x3, waiting for transfers between devices, line_sum(): up = lax.ppermute(ahead, axis, [(i, i + 1) for i in range(hop)])  22.7 us
  transfers between devices with their start and end apart: 64, of which 25 were waited for; matrix products, arithmetic and copies ran while one was open for 7% of the time, Pallas kernels for 28%

profile of v10, /device:TPU:0, one launch (start us, length us, event | category | flops | bytes accessed | tf_op | source)
XLA Modules:
  0.0 547.2 jit_solution(18017583293931774404)
XLA Ops:
  16.4 9.9 %collective-permute-done.14.refs_6_ = bf16[256,1024]{1,0:T(8,128)(2,1)S(1)} collective-permute-done((bf16[256,1024]{1,0:T(8,128)(2,1)S(1)}, bf16[256,1024]{1,0:T(8,128)(2,1)S(1)}, u32[]{:S(2)}, u32[]{:S(2)}) %collective-permute-start.14) | collective-permute-done | bytes 524320 | tf_op jit(solution)/shard_map/ppermute | solution.py:846
  28.3 7.6 %collective-permute-start = (bf16[160,1024]{1,0:T(8,128)(2,1)S(1)}, bf16[160,1024]{1,0:T(8,128)(2,1)S(1)}, u32[]{:S(2)}, u32[]{:S(2)}) collective-permute-start(bf16[160,1024]{1,0:T(8,128)(2,1)S(1)} %maximum_maximum_fusion.refs_7_), channel_id=1, source_target_pairs={{0,1},{1,2},{2,3},{4,5},{5,6},{6,7},{8,9},{9,10},{10,11},{12,13},{... | collective-permute-start | bytes 983048 | tf_op jit(solution)/shard_map/ppermute | solution.py:845
  42.1 6.2 %collective-permute-done.2.refs_13_ = bf16[160,1024]{1,0:T(8,128)(2,1)S(1)} collective-permute-done((bf16[160,1024]{1,0:T(8,128)(2,1)S(1)}, bf16[160,1024]{1,0:T(8,128)(2,1)S(1)}, u32[]{:S(2)}, u32[]{:S(2)}) %collective-permute-start.2) | collective-permute-done | bytes 327712 | tf_op jit(solution)/shard_map/ppermute | solution.py:846
  52.4 13.5 %collective-permute-done.3.refs_11_ = bf16[160,1024]{1,0:T(8,128)(2,1)S(1)} collective-permute-done((bf16[160,1024]{1,0:T(8,128)(2,1)S(1)}, bf16[160,1024]{1,0:T(8,128)(2,1)S(1)}, u32[]{:S(2)}, u32[]{:S(2)}) %collective-permute-start.3) | collective-permute-done | bytes 327712 | tf_op jit(solution)/shard_map/ppermute | solution.py:846
  67.8 13.2 %collective-permute-done.19.refs_9_ = bf16[160,1024]{1,0:T(8,128)(2,1)S(1)} collective-permute-done((bf16[160,1024]{1,0:T(8,128)(2,1)S(1)}, bf16[160,1024]{1,0:T(8,128)(2,1)S(1)}, u32[]{:S(2)}, u32[]{:S(2)}) %collective-permute-start.19) | collective-permute-done | bytes 327712 | tf_op jit(solution)/shard_map/ppermute | solution.py:846
  97.7 6.2 %project.4 = (bf16[2048,256]{1,0:T(8,128)(2,1)}, bf16[2048,256]{1,0:T(8,128)(2,1)}, bf16[2048,256]{1,0:T(8,128)(2,1)}, f32[2048,256]{1,0:T(8,128)}, f32[2048,256]{1,0:T(8,128)}) custom-call(s32[1]{0:T(128)} %bitcast.10.index_ref, bf16[512,1024]{1,0:T(8,128)(2,1)} %refs_0_.1, ...), custom_call_target="tpu_custom_call" | custom-call | flops 805306368 | bytes 2097152 | tf_op jit(solution)/shard_map/project/pallas_call | solution.py:292
  116.0 23.6 %collective-permute-done.7.refs_1_.refs_4_ = bf16[512,1024]{1,0:T(8,128)(2,1)} collective-permute-done((bf16[512,1024]{1,0:T(8,128)(2,1)S(1)}, bf16[512,1024]{1,0:T(8,128)(2,1)}, u32[]{:S(2)}, u32[]{:S(2)}) %collective-permute-start.7) | collective-permute-done | bytes 1048608 | tf_op jit(solution)/shard_map/ppermute | solution.py:846
  156.9 7.8 %collective-permute-done.9.refs_1_.refs_6_ = bf16[512,1024]{1,0:T(8,128)(2,1)} collective-permute-done((bf16[512,1024]{1,0:T(8,128)(2,1)}, bf16[512,1024]{1,0:T(8,128)(2,1)}, u32[]{:S(2)}, u32[]{:S(2)}) %collective-permute-start.9) | collective-permute-done | bytes 1048608 | tf_op jit(solution)/shard_map/ppermute | solution.py:846
  170.6 5.9 %project.7 = (bf16[2048,256]{1,0:T(8,128)(2,1)}, bf16[2048,256]{1,0:T(8,128)(2,1)}, bf16[2048,256]{1,0:T(8,128)(2,1)}, f32[2048,256]{1,0:T(8,128)}, f32[2048,256]{1,0:T(8,128)}) custom-call(s32[1]{0:T(128)} %bitcast.4.index_ref, ...), custom_call_target="tpu_custom_call", output_to_operand_aliasing={{0}: (9, {}), {1}: (10, {}), {2}: (11, {}), {3}: (12, {}), ... | custom-call | flops 805306368 | bytes 2097152 | tf_op jit(solution)/shard_map/project/pallas_call | solution.py:292
  176.4 20.2 %attend.1 = (bf16[2048,256]{1,0:T(8,128)(2,1)}, f32[2048,256]{1,0:T(8,128)}, f32[4,2048]{1,0:T(4,128)}) custom-call(s32[2,4]{1,0:T(2,128)} %pad_add_fusion.bounds_ref, bf16[2048,256]{1,0:T(8,128)(2,1)} %get-tuple-element.191.q_ref, bf16[2048,256]{1,0:T(8,128)(2,1)} %get-tuple-element.192.k_ref, bf16[2048,256]{1,0:T(8,128)(2,1)} %get-tuple-element.193.v_ref, ...), custom_call_target="tpu_custom_call" | custom-call | flops 20000000000 | bytes 4194304 | tf_op jit(solution)/shard_map/attend/pallas_call | solution.py:124
  211.5 8.4 %all-gather.5.cloned.1.call-done = bf16[13312,1024]{1,0:T(8,128)(2,1)} async-done(((bf16[1664,1024]{1,0:T(8,128)(2,1)}), bf16[13312,1024]{1,0:T(8,128)(2,1)}) %all-gather.5.cloned.1.call-update) | async-done | bytes 27262992 | tf_op jit(solution)/shard_map/all_gather | solution.py:950
  219.9 9.0 %mix.1 = (f32[512,1024]{1,0:T(8,128)}, f32[512,1024]{1,0:T(8,128)}, bf16[512,1024]{1,0:T(8,128)(2,1)}, bf16[1024,512]{1,0:T(8,128)(2,1)}, bf16[1024,1024]{1,0:T(8,128)(2,1)}) custom-call(bf16[512,256]{1,0:T(8,128)(2,1)} %get-tuple-element.313.refs_0_, bf16[512,256]{1,0:T(8,128)(2,1)} %copy-done.14, bf16[512,256]{1,0:T(8,128)(2,1)} %copy-done.15, ...), custom_call_target="tpu_custom_call" | custom-call | flops 1073741824 | bytes 7340032 | tf_op jit(solution)/shard_map/mix/pallas_call | solution.py:555
  228.9 28.7 %feed.1 = (f32[512,4096]{1,0:T(8,128)}, f32[512,4096]{1,0:T(8,128)}, bf16[512,4096]{1,0:T(8,128)(2,1)}, bf16[512,1024]{1,0:T(8,128)(2,1)}, f32[512,1024]{1,0:T(8...) custom-call(bf16[512,1024]{1,0:T(8,128)(2,1)} %get-tuple-element.197.m_ref, ...), custom_call_target="tpu_custom_call" | custom-call | flops 12884901888 | bytes 46137344 | tf_op jit(solution)/shard_map/feed/pallas_call | solution.py:673
  257.6 15.1 %feed_back_first.1 = (bf16[3,1024,1024]{2,1,0:T(8,128)(2,1)}, f32[2,1024]{1,0:T(2,128)}, f32[512,1024]{1,0:T(8,128)}) custom-call(bf16[512,1024]{1,0:T(8,128)(2,1)} %get-tuple-element.200.refs_0_, bf16[1024,512]{1,0:T(8,128)(2,1)} %get-tuple-element.201.refs_1_, bf16[1024,512]{1,0:T(8,128)(2,1)} %get-tuple-element.202.refs_2_, ...), custom_call_target="tpu_custom_call" | custom-call | flops 6442450944 | bytes 17825792 | tf_op jit(solution)/shard_map/feed_back_first/pallas_call | solution.py:798
  272.8 36.0 %feed_back_last.1 = (bf16[3,1024,3072]{2,1,0:T(8,128)(2,1)}, f32[2,3072]{1,0:T(2,128)}, f32[512,1024]{1,0:T(8,128)}, bf16[512,1024]{1,0:T(8,128)(2,1)}, f32[1,1024]{1,0:T(1,128)}) custom-call(bf16[512,1024]{1,0:T(8,128)(2,1)} %get-tuple-element.200.refs_0_, bf16[1024,512]{1,0:T(8,128)(2,1)} %get-tuple-element.201.refs_1_, ...), custom_call_target="tpu_custom_call" | custom-call | flops 19327352832 | bytes 53477376 | tf_op jit(solution)/shard_map/feed_back_last/pallas_call | solution.py:798
  330.5 8.2 %collective-permute-done.25 = bf16[512,256]{1,0:T(8,128)(2,1)} collective-permute-done((bf16[512,256]{1,0:T(8,128)(2,1)}, bf16[512,256]{1,0:T(8,128)(2,1)}, u32[]{:S(2)}, u32[]{:S(2)}) %collective-permute-start.25) | collective-permute-done | bytes 262176 | tf_op jit(solution)/shard_map/ppermute | solution.py:841
  344.5 20.1 %attend_back.2 = (f32[2048,128]{1,0:T(8,128)}, f32[2048,128]{1,0:T(8,128)}, f32[2048,128]{1,0:T(8,128)}) custom-call(s32[2,4]{1,0:T(2,128)} %pad_add_fusion.bounds_ref, bf16[2048,256]{1,0:T(8,128)(2,1)} %get-tuple-element.191.q_ref, bf16[2048,256]{1,0:T(8,128)(2,1)} %constant_dynamic-update-slice_fusion.9.do_ref, ...), custom_call_target="tpu_custom_call" | custom-call | flops 40000000000 | bytes 5242880 | tf_op jit(solution)/shard_map/attend_back/pallas_call | solution.py:209
  369.4 20.2 %attend_back.3 = (f32[2048,128]{1,0:T(8,128)}, f32[2048,128]{1,0:T(8,128)}, f32[2048,128]{1,0:T(8,128)}) custom-call(s32[2,4]{1,0:T(2,128)} %pad_add_fusion.bounds_ref, bf16[2048,256]{1,0:T(8,128)(2,1)} %get-tuple-element.191.q_ref, bf16[2048,256]{1,0:T(8,128)(2,1)} %constant_dynamic-update-slice_fusion.9.do_ref, ...), custom_call_target="tpu_custom_call" | custom-call | flops 40000000000 | bytes 5242880 | tf_op jit(solution)/shard_map/attend_back/pallas_call | solution.py:209
  395.0 16.4 %project_back.1 = (bf16[2048,768]{1,0:T(8,128)(2,1)}, f32[1,256]{1,0:T(1,128)}, bf16[512,1024]{1,0:T(8,128)(2,1)}, bf16[512,1024]{1,0:T(8,128)(2,1)}, bf16[512,1...) custom-call(s32[1]{0:T(128)} %bitcast.21.index_ref, f32[2048,128]{1,0:T(8,128)} %get-tuple-element.236.refs_0_, ...), custom_call_target="tpu_custom_call" | custom-call | flops 524288 | bytes 524288 | tf_op jit(solution)/shard_map/project_back/pallas_call | solution.py:389
  416.8 8.6 %projection_grads.1 = bf16[1024,768]{1,0:T(8,128)(2,1)} custom-call(bf16[512,1024]{1,0:T(8,128)(2,1)} %refs_0_.1, bf16[512,1024]{1,0:T(8,128)(2,1)} %collective-permute-done.8.refs_0_.refs_1_, bf16[512,1024]{1,0:T(8,128)(2,1)} %copy-done.6, bf16[512,1024]{1,0:T(8,128)(2,1)} %copy-done.7, bf16[512,1024]{1,0:T(8,128)(2,1)} %collective-permute-done.7.refs_1_.refs_4_, ...), custom_call_target="tpu_custom_call" | custom-call | flops 3221225472 | bytes 16777216 | tf_op jit(solution)/shard_map/projection_grads/pallas_call | solution.py:433
  425.4 14.3 %collective-permute-done.38 = bf16[512,1024]{1,0:T(8,128)(2,1)S(1)} collective-permute-done((bf16[512,1024]{1,0:T(8,128)(2,1)}, bf16[512,1024]{1,0:T(8,128)(2,1)S(1)}, u32[]{:S(2)}, u32[]{:S(2)}) %collective-permute-start.38) | collective-permute-done | bytes 1048608 | tf_op jit(solution)/shard_map/ppermute | solution.py:854
  451.7 17.6 %collective-permute-done.43 = bf16[2,128,768]{2,1,0:T(8,128)(2,1)S(1)} collective-permute-done((bf16[2,128,768]{2,1,0:T(8,128)(2,1)S(1)}, bf16[2,128,768]{2,1,0:T(8,128)(2,1)S(1)}, u32[]{:S(2)}, u32[]{:S(2)}) %collective-permute-start.43) | collective-permute-done | bytes 393248 | tf_op jit(solution)/shard_map/ppermute | solution.py:865
  501.3 12.5 %collective-permute-done.48 = bf16[3,128,1024]{2,1,0:T(8,128)(2,1)S(1)} collective-permute-done((bf16[3,128,1024]{2,1,0:T(8,128)(2,1)S(1)}, bf16[3,128,1024]{2,1,0:T(8,128)(2,1)S(1)}, u32[]{:S(2)}, u32[]{:S(2)}) %collective-permute-start.48) | collective-permute-done | bytes 786464 | tf_op jit(solution)/shard_map/ppermute | solution.py:841
  525.7 8.4 %collective-permute-done.58 = bf16[512,1024]{1,0:T(8,128)(2,1)} collective-permute-done((bf16[512,1024]{1,0:T(8,128)(2,1)}, bf16[512,1024]{1,0:T(8,128)(2,1)}, u32[]{:S(2)}, u32[]{:S(2)}) %collective-permute-start.58) | collective-permute-done | bytes 1048608 | tf_op jit(solution)/shard_map/ppermute | solution.py:854
  (329 shorter events, 194.2 us)
Async XLA Ops:
  7.2 90.5 %all-gather.3.cloned.1.call-start = ((), (), s32[]{:S(2)}) async-start(), calls=%async_computation.2 | async-start | bytes 1769472 | tf_op jit(solution)/shard_map/all_gather | solution.py:926
  9.2 210.7 %all-gather.5.cloned.1.call-start = ((), (), s32[]{:S(2)}) async-start(), calls=%async_computation.3 | async-start | bytes 30670848 | tf_op jit(solution)/shard_map/all_gather | solution.py:950
  27.6 23.3 %collective-permute-start.17 = (bf16[256,1024]{1,0:T(8,128)(2,1)S(1)}, bf16[256,1024]{1,0:T(8,128)(2,1)S(1)}, u32[]{:S(2)}, u32[]{:S(2)}) collective-permute-start(bf16[256,1024]{1,0:T(8,128)(2,1)S(1)} %collective-permute-done.13.refs_1_), channel_id=1, source_target_pairs={{1,2},{2,3},{5,6},{6,7},{9,10},{10,11},{13,14},{14,15},{17,18},{18... | collective-permute-start | bytes 1572872 | tf_op jit(solution)/shard_map/ppermute | solution.py:845
  49.6 31.4 %collective-permute-start.16 = (bf16[256,1024]{1,0:T(8,128)(2,1)S(1)}, bf16[256,1024]{1,0:T(8,128)(2,1)S(1)}, u32[]{:S(2)}, u32[]{:S(2)}) collective-permute-start(bf16[256,1024]{1,0:T(8,128)(2,1)S(1)} %collective-permute-done.15.refs_4_), channel_id=1, source_target_pairs={{1,0},{5,4},{9,8},{13,12},{17,16},{21,20},{25,24},{29,28}} | collective-permute-start | bytes 1572872 | tf_op jit(solution)/shard_map/ppermute | solution.py:846
  50.9 31.7 %collective-permute-start.18 = (bf16[256,1024]{1,0:T(8,128)(2,1)S(1)}, bf16[256,1024]{1,0:T(8,128)(2,1)}, u32[]{:S(2)}, u32[]{:S(2)}) collective-permute-start(bf16[256,1024]{1,0:T(8,128)(2,1)S(1)} %collective-permute-done.17.refs_3_), channel_id=1, source_target_pairs={{2,3},{6,7},{10,11},{14,15},{18,19},{22,23},{26,27},{30,31}} | collective-permute-start | bytes 1572872 | tf_op jit(solution)/shard_map/ppermute | solution.py:845
  87.4 255.4 %reduce-scatter.3.cloned.1.call-start = ((), (), s32[]{:S(2)}) async-start(), calls=%async_computation.4 | async-start | bytes 7077888 | tf_op jit(solution)/shard_map/reduce_scatter | solution.py:1022
  90.2 23.8 %collective-permute-start.5 = (bf16[512,1024]{1,0:T(8,128)(2,1)S(1)}, bf16[512,1024]{1,0:T(8,128)(2,1)S(1)}, u32[]{:S(2)}, u32[]{:S(2)}) collective-permute-start(bf16[512,1024]{1,0:T(8,128)(2,1)S(1)} %copy-done), channel_id=1, source_target_pairs={{1,0},{2,1},{3,2},{5,4},{6,5},{7,6},{9,8},{10,9},{11,10},{13,12},{... | collective-permute-start | bytes 3145736 | tf_op jit(solution)/shard_map/ppermute | solution.py:846
  114.7 24.9 %collective-permute-start.7 = (bf16[512,1024]{1,0:T(8,128)(2,1)S(1)}, bf16[512,1024]{1,0:T(8,128)(2,1)}, u32[]{:S(2)}, u32[]{:S(2)}) collective-permute-start(bf16[512,1024]{1,0:T(8,128)(2,1)S(1)} %collective-permute-done.5.refs_1_.refs_2_), channel_id=1, source_target_pairs={{1,0},{2,1},{5,4},{6,5},{9,8},{10,9},{13,12},{14,13},{17,16},{18,1... | collective-permute-start | bytes 3145736 | tf_op jit(solution)/shard_map/ppermute | solution.py:846
  141.3 23.4 %collective-permute-start.9 = (bf16[512,1024]{1,0:T(8,128)(2,1)}, bf16[512,1024]{1,0:T(8,128)(2,1)}, u32[]{:S(2)}, u32[]{:S(2)}) collective-permute-start(bf16[512,1024]{1,0:T(8,128)(2,1)} %collective-permute-done.7.refs_1_.refs_4_), channel_id=1, source_target_pairs={{1,0},{5,4},{9,8},{13,12},{17,16},{21,20},{25,24},{29,28}} | collective-permute-start | bytes 3145736 | tf_op jit(solution)/shard_map/ppermute | solution.py:846
  142.6 56.0 %collective-permute-start.21 = (f32[2,1024]{1,0:T(2,128)S(1)}, f32[2,1024]{1,0:T(2,128)S(1)}, u32[]{:S(2)}, u32[]{:S(2)}) collective-permute-start(f32[2,1024]{1,0:T(2,128)S(1)} %copy-done.49), channel_id=1, source_target_pairs={{0,1},{1,2},{2,3},{3,0},{4,5},{5,6},{6,7},{7,4},{8,9},{9,10},{10,1... | collective-permute-start | bytes 24584 | tf_op jit(solution)/shard_map/ppermute | solution.py:841
  146.2 56.7 %collective-permute-start.22 = (f32[2,1024]{1,0:T(2,128)S(1)}, f32[2,1024]{1,0:T(2,128)S(1)}, u32[]{:S(2)}, u32[]{:S(2)}) collective-permute-start(f32[2,1024]{1,0:T(2,128)S(1)} %copy-done.49), channel_id=1, source_target_pairs={{0,3},{1,0},{2,1},{3,2},{4,7},{5,4},{6,5},{7,6},{8,11},{9,8},{10,9... | collective-permute-start | bytes 24584 | tf_op jit(solution)/shard_map/ppermute | solution.py:841
  146.8 56.2 %collective-permute-start.23 = (f32[2,1024]{1,0:T(2,128)S(1)}, f32[2,1024]{1,0:T(2,128)S(1)}, u32[]{:S(2)}, u32[]{:S(2)}) collective-permute-start(f32[2,1024]{1,0:T(2,128)S(1)} %copy-done.49), channel_id=1, source_target_pairs={{0,2},{1,3},{2,0},{3,1},{4,6},{5,7},{6,4},{7,5},{8,10},{9,11},{10,... | collective-permute-start | bytes 24584 | tf_op jit(solution)/shard_map/ppermute | solution.py:841
  272.8 201.5 %reduce-scatter.5.cloned.1.call-start = ((), (), s32[]{:S(2)}) async-start(), calls=%async_computation.5 | async-start | bytes 21233664 | tf_op jit(solution)/shard_map/reduce_scatter | solution.py:1026
  364.9 24.7 %collective-permute-start.30 = (f32[10,1024]{1,0:T(8,128)S(1)}, f32[10,1024]{1,0:T(8,128)S(1)}, u32[]{:S(2)}, u32[]{:S(2)}) collective-permute-start(f32[10,1024]{1,0:T(8,128)S(1)} %add.332), channel_id=1, source_target_pairs={{0,2},{1,3},{2,0},{3,1},{4,6},{5,7},{6,4},{7,5},{8,10},{9,11},{10,... | collective-permute-start | bytes 122888 | tf_op jit(solution)/shard_map/ppermute | solution.py:871
  411.5 28.2 %collective-permute-start.38 = (bf16[512,1024]{1,0:T(8,128)(2,1)}, bf16[512,1024]{1,0:T(8,128)(2,1)S(1)}, u32[]{:S(2)}, u32[]{:S(2)}) collective-permute-start(bf16[512,1024]{1,0:T(8,128)(2,1)} %get-tuple-element.254), channel_id=1, source_target_pairs={{0,1},{4,5},{8,9},{12,13},{16,17},{20,21},{24,25},{28,29}} | collective-permute-start | bytes 3145736 | tf_op jit(solution)/shard_map/ppermute | solution.py:854
  416.0 23.7 %collective-permute-start.39 = (bf16[512,1024]{1,0:T(8,128)(2,1)}, bf16[512,1024]{1,0:T(8,128)(2,1)S(1)}, u32[]{:S(2)}, u32[]{:S(2)}) collective-permute-start(bf16[512,1024]{1,0:T(8,128)(2,1)} %get-tuple-element.255), channel_id=1, source_target_pairs={{3,2},{7,6},{11,10},{15,14},{19,18},{23,22},{27,26},{31,30}} | collective-permute-start | bytes 3145736 | tf_op jit(solution)/shard_map/ppermute | solution.py:855
  442.5 31.7 %collective-permute-start.40 = (bf16[512,1024]{1,0:T(8,128)(2,1)}, bf16[512,1024]{1,0:T(8,128)(2,1)}, u32[]{:S(2)}, u32[]{:S(2)}) collective-permute-start(bf16[512,1024]{1,0:T(8,128)(2,1)} %get-tuple-element.309), channel_id=1, source_target_pairs={{0,1},{1,2},{4,5},{5,6},{8,9},{9,10},{12,13},{13,14},{16,17},{17,1... | collective-permute-start | bytes 3145736 | tf_op jit(solution)/shard_map/ppermute | solution.py:854
  447.9 26.3 %collective-permute-start.41 = (bf16[512,1024]{1,0:T(8,128)(2,1)}, bf16[512,1024]{1,0:T(8,128)(2,1)S(1)}, u32[]{:S(2)}, u32[]{:S(2)}) collective-permute-start(bf16[512,1024]{1,0:T(8,128)(2,1)} %get-tuple-element.308), channel_id=1, source_target_pairs={{2,1},{3,2},{6,5},{7,6},{10,9},{11,10},{14,13},{15,14},{18,17},{19... | collective-permute-start | bytes 3145736 | tf_op jit(solution)/shard_map/ppermute | solution.py:855
  449.2 24.1 %collective-permute-start.44 = (f32[1,256]{1,0:T(1,128)S(1)}, f32[1,256]{1,0:T(1,128)S(1)}, u32[]{:S(2)}, u32[]{:S(2)}) collective-permute-start(f32[1,256]{1,0:T(1,128)S(1)} %copy-done.53), channel_id=1, source_target_pairs={{0,1},{1,2},{2,3},{3,0},{4,5},{5,6},{6,7},{7,4},{8,9},{9,10},{10,1... | collective-permute-start | bytes 3080 | tf_op jit(solution)/shard_map/ppermute | solution.py:841
  449.5 24.7 %collective-permute-start.45 = (f32[1,256]{1,0:T(1,128)S(1)}, f32[1,256]{1,0:T(1,128)S(1)}, u32[]{:S(2)}, u32[]{:S(2)}) collective-permute-start(f32[1,256]{1,0:T(1,128)S(1)} %copy-done.53), channel_id=1, source_target_pairs={{0,2},{1,3},{2,0},{3,1},{4,6},{5,7},{6,4},{7,5},{8,10},{9,11},{10,... | collective-permute-start | bytes 3080 | tf_op jit(solution)/shard_map/ppermute | solution.py:841
  476.2 25.1 %collective-permute-start.47 = (bf16[3,128,1024]{2,1,0:T(8,128)(2,1)S(1)}, bf16[3,128,1024]{2,1,0:T(8,128)(2,1)S(1)}, u32[]{:S(2)}, u32[]{:S(2)}) collective-permute-start(bf16[3,128,1024]{2,1,0:T(8,128)(2,1)S(1)} %get-tuple-element.267), channel_id=1, source_target_pairs={{0,3},{1,0},{2,1},{3,2},{4,7},{5,4},{6,5},{7,6},{8,11},{9,8},{10,9... | collective-permute-start | bytes 2359304 | tf_op jit(solution)/shard_map/ppermute | solution.py:841
  478.0 35.8 %collective-permute-start.48 = (bf16[3,128,1024]{2,1,0:T(8,128)(2,1)S(1)}, bf16[3,128,1024]{2,1,0:T(8,128)(2,1)S(1)}, u32[]{:S(2)}, u32[]{:S(2)}) collective-permute-start(bf16[3,128,1024]{2,1,0:T(8,128)(2,1)S(1)} %get-tuple-element.268), channel_id=1, source_target_pairs={{0,1},{1,2},{2,3},{3,0},{4,5},{5,6},{6,7},{7,4},{8,9},{9,10},{10,1... | collective-permute-start | bytes 2359304 | tf_op jit(solution)/shard_map/ppermute | solution.py:841
  495.2 38.8 %collective-permute-start.58 = (bf16[512,1024]{1,0:T(8,128)(2,1)}, bf16[512,1024]{1,0:T(8,128)(2,1)}, u32[]{:S(2)}, u32[]{:S(2)}) collective-permute-start(bf16[512,1024]{1,0:T(8,128)(2,1)} %add.375), channel_id=1, source_target_pairs={{0,1},{1,2},{2,3},{4,5},{5,6},{6,7},{8,9},{9,10},{10,11},{12,13},{... | collective-permute-start | bytes 3145736 | tf_op jit(solution)/shard_map/ppermute | solution.py:854
  499.9 35.0 %collective-permute-start.59 = (bf16[512,1024]{1,0:T(8,128)(2,1)}, bf16[512,1024]{1,0:T(8,128)(2,1)S(1)}, u32[]{:S(2)}, u32[]{:S(2)}) collective-permute-start(bf16[512,1024]{1,0:T(8,128)(2,1)} %add.376), channel_id=1, source_target_pairs={{1,0},{2,1},{3,2},{5,4},{6,5},{7,6},{9,8},{10,9},{11,10},{13,12},{... | collective-permute-start | bytes 3145736 | tf_op jit(solution)/shard_map/ppermute | solution.py:855
  (95 other events, 1520.1 us)
Sparse Core Ops, SparseCore 0:
  9.9 28.2 all-gather.2
  87.6 132.2 all-gather.4
  272.9 61.6 reduce-scatter.2
  338.0 134.6 reduce-scatter.4
